TPU v7x, 32 devices: a whole 2x2x4 slice. The times are simulated.
32 devices in a mesh: img: 2 (over core), ch: 16 (over z, y, x).
Axes of the slice: x: 2, y: 2, z: 4, core: 2. Of those that a mesh axis runs over, the one named last changes fastest.
Arguments:
- features: bfloat16 [384, 16384], P('ch', 'img'), may hold values from -6 to 6
- cotangent: bfloat16 [384, 16384], P('ch', 'img'), may hold values from -6 to 6
- heights: int32 [16], P('img'), may hold values from 16 to 32, as said below
- widths: int32 [16], P('img'), may hold values from 16 to 32, as said below
- step_height: float32 [384], P('ch'), may hold values from -3 to 0
- rate_height: float32 [384, 64], P('ch'), may hold values from 0.05 to 2
- readout_height: float32 [384, 64], P('ch'), may hold values from -0.125 to 0.125
- step_width: float32 [384], P('ch'), may hold values from -3 to 0
- rate_width: float32 [384, 64], P('ch'), may hold values from 0.05 to 2
- readout_width: float32 [384, 64], P('ch'), may hold values from -0.125 to 0.125
- skip_gain: float32 [384], P('ch'), may hold values from -4 to 4
- norm_gain: bfloat16 [384], P('ch'), may hold values from 0.5 to 1.5
- norm_shift: bfloat16 [384], P('ch'), may hold values from -3 to 3
- in_weight: bfloat16 [384, 1536], P(None, 'ch'), may hold values from -0.3125 to 0.3125
- in_bias: bfloat16 [1536], P('ch'), may hold values from -3 to 3
- out_weight: bfloat16 [1536, 384], P('ch'), may hold values from -0.15625 to 0.15625
- out_bias: float32 [384], P('ch'), may hold values from -3 to 3
- layer_scale: float32 [384], P('ch'), may hold values from 0.3 to 3
Outputs:
- result: bfloat16 [384, 16384], P('ch', 'img')
- grad_features: float32 [384, 16384], P('ch', 'img')
- grad_step_height: float32 [384], P('ch')
- grad_rate_height: float32 [384, 64], P('ch')
- grad_readout_height: float32 [384, 64], P('ch')
- grad_step_width: float32 [384], P('ch')
- grad_rate_width: float32 [384, 64], P('ch')
- grad_readout_width: float32 [384, 64], P('ch')
- grad_skip_gain: float32 [384], P('ch')
- grad_norm_gain: float32 [384], P('ch')
- grad_norm_shift: float32 [384], P('ch')
- grad_in_weight: float32 [384, 1536], P(None, 'ch')
- grad_in_bias: float32 [1536], P('ch')
- grad_out_weight: float32 [1536, 384], P('ch')
- grad_out_bias: float32 [384], P('ch')
- grad_layer_scale: float32 [384], P('ch')
Inputs may be any that keep to these rules, and one draw needn't show every extreme that they name: `heights`: every image is 16 to 32 cells high; in every draw some image is exactly 32 high and some image is less. `widths`: every image is 16 to 32 cells wide; in every draw some image is exactly 32 wide and some image is less.
All inputs are finite; a program needn't handle non-finite values.
Results may differ from a plain program's by a relative error of at most 0.009.
Values may be sent and summed in bfloat16 or wider, within the bound.
No kernel may reach another device: no remote copies, remote signals or barrier semaphores. Data moves between devices by JAX's collectives and lax.ppermute only.
A program may use at most 128 MiB of HBM per device.

v0:
```python
from functools import partial

import jax
import jax.numpy as jnp
from jax import lax
from jax.sharding import PartitionSpec as P

SIDE = 32


EPS = 1e-06
HIGH = lax.Precision.HIGHEST


def slot_mask(heights, widths):
    places = jnp.arange(SIDE, dtype=jnp.int32)
    inside = (places[None, :, None] < heights[:, None, None]) & (
        places[None, None, :] < widths[:, None, None]
    )
    return inside.reshape(-1).astype(jnp.float32)


def kernel_rows(step_log, rates, readout):
    places = jnp.arange(SIDE, dtype=jnp.float32)
    decays = jnp.exp(step_log)[:, None] * rates
    return jnp.einsum("cn,cnl->cl", readout, jnp.exp(-decays[:, :, None] * places), precision=HIGH)


def toeplitz(kernel):
    lagged = jnp.arange(SIDE, dtype=jnp.int32)
    select = (lagged[:, None, None] == lagged[None, :, None] - lagged[None, None, :]).astype(
        jnp.float32
    )
    return jnp.einsum("cl,lab->cab", kernel, select, precision=HIGH)


def mixer(
    inside,
    values,
    step_height,
    rate_height,
    readout_height,
    step_width,
    rate_width,
    readout_width,
    skip_gain,
):
    channels = values.shape[0]
    masked = values * inside[None, :]
    image_grid = masked.reshape(channels, -1, SIDE, SIDE)
    down_matrix = toeplitz(kernel_rows(step_height, rate_height, readout_height))
    across_matrix = toeplitz(kernel_rows(step_width, rate_width, readout_width))
    spread = jnp.einsum("cah,cihw->ciaw", down_matrix, image_grid, precision=HIGH)
    spread = jnp.einsum("ciaw,cbw->ciab", spread, across_matrix, precision=HIGH)
    return inside[None, :] * (spread.reshape(channels, -1) + skip_gain[:, None] * masked)


def normed(values, gain, shift):
    centred = values - jnp.mean(values, axis=0)
    variance = jnp.mean(centred * centred, axis=0)
    return centred * lax.rsqrt(variance + EPS) * gain[:, None] + shift[:, None]


def per_device(
    features,
    cotangent,
    heights,
    widths,
    step_height,
    rate_height,
    readout_height,
    step_width,
    rate_width,
    readout_width,
    skip_gain,
    norm_gain,
    norm_shift,
    in_weight,
    in_bias,
    out_weight,
    out_bias,
    layer_scale,
):
    inside = slot_mask(heights, widths)
    values = features.astype(jnp.float32)
    mixed, mixer_pull = jax.vjp(
        partial(mixer, inside),
        values,
        step_height,
        rate_height,
        readout_height,
        step_width,
        rate_width,
        readout_width,
        skip_gain,
    )
    mixed_low = mixed.astype(jnp.bfloat16)
    upstream = cotangent.astype(jnp.float32)
    own_rows = features.shape[0]
    whole, gains, shifts = (
        lax.all_gather(mixed_low, "ch", axis=0, tiled=True),
        lax.all_gather(norm_gain, "ch", axis=0, tiled=True),
        lax.all_gather(norm_shift, "ch", axis=0, tiled=True),
    )
    whole_float = whole.astype(jnp.float32)
    active = normed(whole_float, gains.astype(jnp.float32), shifts.astype(jnp.float32)).astype(
        jnp.bfloat16
    )
    before = (
        jnp.einsum("cf,cp->fp", in_weight, active, preferred_element_type=jnp.float32)
        + in_bias.astype(jnp.float32)[:, None]
    )
    hidden_full, gelu_pull = jax.vjp(jax.nn.gelu, before)
    hidden = hidden_full.astype(jnp.bfloat16)
    columns = out_weight
    summed = lax.psum_scatter(
        jnp.einsum("fc,fp->cp", columns, hidden, preferred_element_type=jnp.float32),
        "ch",
        scatter_dimension=0,
        tiled=True,
    )
    shifted = summed + out_bias[:, None]
    output = values + inside[None, :] * layer_scale[:, None] * shifted
    weighted = inside[None, :] * upstream
    grad_layer_scale = jnp.sum(weighted * shifted, axis=1)
    grad_out_bias = layer_scale * jnp.sum(weighted, axis=1)
    down_grad = (weighted * layer_scale[:, None]).astype(jnp.bfloat16)
    piece = lax.all_gather(down_grad, "ch", axis=0, tiled=True)
    columns = out_weight
    hidden_grad = jnp.einsum("fc,cp->fp", columns, piece, preferred_element_type=jnp.float32)
    block_grad = jnp.einsum("fp,cp->fc", hidden, piece, preferred_element_type=jnp.float32)
    hidden_grad, grad_out_weight = (hidden_grad, block_grad)
    before_grad = gelu_pull(hidden_grad)[0].astype(jnp.bfloat16)
    grad_in_bias = jnp.sum(before_grad.astype(jnp.float32), axis=1)
    grad_in_weight = jnp.einsum(
        "cp,fp->cf", active, before_grad, preferred_element_type=jnp.float32
    )
    active_grad = lax.psum_scatter(
        jnp.einsum("cf,fp->cp", in_weight, before_grad, preferred_element_type=jnp.float32),
        "ch",
        scatter_dimension=0,
        tiled=True,
    )
    channels_all = whole_float.shape[0]
    centred = whole_float - jnp.mean(whole_float, axis=0)
    inverse_std = lax.rsqrt(jnp.mean(centred * centred, axis=0) + EPS)
    offset = lax.axis_index("ch") * own_rows
    normal_own = lax.dynamic_slice_in_dim(centred, offset, own_rows, 0) * inverse_std[None, :]
    scaled = active_grad * norm_gain.astype(jnp.float32)[:, None]
    total_g, total_gn = lax.psum(
        (jnp.sum(scaled, axis=0), jnp.sum(scaled * normal_own, axis=0)), "ch"
    )
    mixed_grad = (
        scaled - total_g[None, :] / channels_all - normal_own * (total_gn[None, :] / channels_all)
    ) * inverse_std[None, :]
    grad_norm_gain = jnp.sum(active_grad * normal_own, axis=1)
    grad_norm_shift = jnp.sum(active_grad, axis=1)
    mixer_grads = mixer_pull(mixed_grad)
    grad_features = upstream + mixer_grads[0]
    summed_grads = lax.psum(
        (
            mixer_grads[1],
            mixer_grads[2],
            mixer_grads[3],
            mixer_grads[4],
            mixer_grads[5],
            mixer_grads[6],
            mixer_grads[7],
            grad_norm_gain,
            grad_norm_shift,
            grad_in_weight,
            grad_in_bias,
            grad_out_weight,
            grad_out_bias,
            grad_layer_scale,
        ),
        "img",
    )
    return (output.astype(jnp.bfloat16), grad_features) + tuple(summed_grads)


def solution(mesh):
    return jax.shard_map(
        per_device,
        mesh=mesh,
        in_specs=(
            P("ch", "img"),
            P("ch", "img"),
            P("img"),
            P("img"),
            P("ch"),
            P("ch", None),
            P("ch", None),
            P("ch"),
            P("ch", None),
            P("ch", None),
            P("ch"),
            P("ch"),
            P("ch"),
            P(None, "ch"),
            P("ch"),
            P("ch", None),
            P("ch"),
            P("ch"),
        ),
        out_specs=(
            P("ch", "img"),
            P("ch", "img"),
            P("ch"),
            P("ch", None),
            P("ch", None),
            P("ch"),
            P("ch", None),
            P("ch", None),
            P("ch"),
            P("ch"),
            P("ch"),
            P(None, "ch"),
            P("ch"),
            P("ch", None),
            P("ch"),
            P("ch"),
        ),
        check_vma=False,
    )
```

profile of v0, /device:TPU:0, one launch (start us, length us, event | category | flops | bytes accessed | tf_op | source)
XLA Modules:
  0.0 831.7 jit_solution(14961640819253865202)
XLA Ops:
  7.3 0.7 exp.12
  7.9 0.7 exp.14
  8.6 0.7 iota_compare_fusion.5
  9.3 0.1 and_convert_fusion
  9.4 0.1 reshape.164
  9.5 0.8 multiply_negate_fusion
  10.3 0.8 multiply_negate_fusion.1
  11.1 1.5 fusion.42
  12.6 1.5 fusion.40
  14.0 1.1 convolution_bitcast_fusion.3
  15.1 1.1 convolution_bitcast_fusion.4
  16.2 1.1 convert_multiply_fusion.1
  17.3 2.7 reshape.160
  19.9 7.1 fusion.47
  27.1 7.2 fusion.14
  34.3 3.8 reshape.161
  38.1 2.5 fusion.29
  40.7 0.7 all-gather.5.cloned.1.call-update
  41.5 0.6 dynamic-slice
  42.8 0.2 dynamic-update-slice.1
  43.0 0.2 dynamic-update-slice
  43.3 43.9 %all-reduce.5 = (bf16[384]{0:T(512)(128)(2,1)S(1)}, bf16[384]{0:T(512)(128)(2,1)S(1)}) all-reduce(bf16[384]{0:T(512)(128)(2,1)S(1)} %dynamic-update-slice.1, bf16[384]{0:T(512)(128)(2,1)S(1)} %dynamic-update-slice), channel_id=1, replica_groups=mesh['img'=2,'ch'=16] {'ch'}, use_global_device_ids=true, to_apply=%add.1 | all-reduce | flops 768 | bytes 3072
  87.2 50.8 %all-gather.3.cloned.1.call-done = bf16[384,8192]{1,0:T(8,128)(2,1)} async-done(((bf16[24,8192]{1,0:T(8,128)(2,1)}), bf16[384,8192]{1,0:T(8,128)(2,1)}) %all-gather.3.cloned.1.call-update) | async-done | bytes 6291472 | tf_op jit(solution)/shard_map/all_gather | solution.py:101
  138.1 4.1 convert_reduce_fusion
  142.2 0.5 copy-done.3
  142.7 6.6 convert_subtract_fusion
  149.3 4.1 add_convert_fusion
  153.4 2.6 copy-done.2
  155.9 3.0 fusion
  158.9 75.0 %all-gather.5.cloned.1.call-done = bf16[384,8192]{1,0:T(8,128)(2,1)} async-done(((bf16[24,8192]{1,0:T(8,128)(2,1)}), bf16[384,8192]{1,0:T(8,128)(2,1)}) %all-gather.5.cloned.1.call-update) | async-done | bytes 6291472 | tf_op jit(solution)/shard_map/all_gather | solution.py:128
  233.9 7.5 convert_reduce_fusion.1
  241.3 1.1 copy-done.7
  242.5 6.4 convolution_bitcast_fusion
  248.9 12.7 %copy.117 = f32[384,8192]{1,0:T(8,128)} copy(f32[384,8192]{0,1:T(8,128)} %convolution_bitcast_fusion) | data formatting | bytes 25165824
  261.7 202.2 %reduce-scatter.9.cloned.1.call-done = f32[24,8192]{1,0:T(8,128)} async-done(((f32[384,8192]{1,0:T(8,128)}), f32[24,8192]{1,0:T(8,128)}) %reduce-scatter.9.cloned.1.call-update) | async-done | bytes 786448 | tf_op jit(solution)/shard_map/reduce_scatter | solution.py:138
  463.9 2.3 multiply_reduce_fusion.1
  466.3 8.3 %convolution_bitcast_fusion.1 = f32[384,8192]{0,1:T(8,128)} fusion(bf16[96,384]{1,0:T(8,128)(2,1)S(1)} %copy-done, f32[96,8192]{1,0:T(8,128)} %fusion), kind=kOutput, calls=%fused_computation.5 | convolution fusion | flops 611057664 | bytes 15802368 | tf_op jit(solution)/shard_map/fc,fp->cp/dot_general | solution.py:117
  474.6 12.6 %copy.115 = f32[384,8192]{1,0:T(8,128)} copy(f32[384,8192]{0,1:T(8,128)} %convolution_bitcast_fusion.1) | data formatting | bytes 25165824
  487.3 6.0 fusion.58
  493.4 5.6 fusion.57
  499.0 73.9 %all-reduce.9.cloned.1.call-done = (f32[8192]{0:T(1024)}, f32[8192]{0:T(1024)}) async-done(((f32[8192]{0:T(1024)}, f32[8192]{0:T(1024)}), (f32[8192]{0:T(1024)}, f32[8192]{0:T(1024)})) %all-reduce.9.cloned.1.call-update) | async-done | bytes 65552 | tf_op jit(solution)/shard_map/psum | solution.py:150
  572.9 0.8 broadcast_multiply_fusion
  573.7 0.8 broadcast_multiply_fusion.1
  574.4 207.1 %reduce-scatter.7.cloned.1.call-done = f32[24,8192]{1,0:T(8,128)} async-done(((f32[384,8192]{1,0:T(8,128)}), f32[24,8192]{1,0:T(8,128)}) %reduce-scatter.7.cloned.1.call-update) | async-done | bytes 786448 | tf_op jit(solution)/shard_map/reduce_scatter | solution.py:116
  781.5 3.6 fusion.30
  785.1 3.6 reshape.162
  788.7 7.3 fusion.19
  796.0 3.1 fusion.43
  799.1 3.1 fusion.22
  802.2 5.3 fusion.16
  807.6 0.6 fusion.32
  808.2 0.6 fusion.31
  808.8 2.4 copy.82
  811.2 3.1 reshape.163
  814.4 1.1 convert_add_fusion
  815.5 0.2 fusion.36
  815.7 0.5 fusion.41
  816.1 0.1 negate_multiply_fusion.1
  816.3 0.2 fusion.34
  816.5 0.1 negate_multiply_fusion
  816.6 0.5 fusion.39
  817.1 4.1 all-reduce.3
  821.2 1.6 copy.138
  822.8 1.6 copy.139
  (75 shorter events, 0.5 us)
Async XLA Ops:
  7.2 226.7 %copy-start = (bf16[96,384]{1,0:T(8,128)(2,1)S(1)}, bf16[96,384]{1,0:T(8,128)(2,1)}, u32[]{:S(2)}) copy-start(bf16[96,384]{1,0:T(8,128)(2,1)} %param.33) | copy-start | bytes 221188
  7.2 130.9 %all-gather.3.cloned.1.call-start = ((), (), s32[]{:S(2)}) async-start(), calls=%async_computation.2 | async-start | bytes 6684672 | tf_op jit(solution)/shard_map/all_gather | solution.py:101
  19.9 7.1 copy-start.10
  34.3 3.9 copy-start.16
  34.3 3.9 copy-start.17
  34.3 7.2 copy-start.21
  34.3 7.2 copy-start.26
  34.3 8.5 %copy-start.22 = (bf16[24]{0:T(256)(128)(2,1)S(1)}, bf16[24]{0:T(256)(128)(2,1)}, u32[]{:S(2)}) copy-start(bf16[24]{0:T(256)(128)(2,1)} %param.30) | copy-start | bytes 148
  34.3 8.7 %copy-start.23 = (bf16[24]{0:T(256)(128)(2,1)S(1)}, bf16[24]{0:T(256)(128)(2,1)}, u32[]{:S(2)}) copy-start(bf16[24]{0:T(256)(128)(2,1)} %param.29) | copy-start | bytes 148
  40.7 193.2 %all-gather.5.cloned.1.call-start = ((), (), s32[]{:S(2)}) async-start(), calls=%async_computation.3 | async-start | bytes 6684672 | tf_op jit(solution)/shard_map/all_gather | solution.py:128
  41.4 422.5 %reduce-scatter.9.cloned.1.call-start = ((), (), s32[]{:S(2)}) async-start(), calls=%async_computation.5 | async-start | bytes 13369344 | tf_op jit(solution)/shard_map/reduce_scatter | solution.py:138
  138.1 4.6 copy-start.3
  149.2 6.7 copy-start.13
  153.3 2.6 copy-start.2
  241.3 1.1 copy-start.7
  261.6 311.3 %all-reduce.9.cloned.1.call-start = ((), (), s32[]{:S(2)}) async-start(), calls=%async_computation.6 | async-start | bytes 131072 | tf_op jit(solution)/shard_map/psum | solution.py:150
  466.3 315.3 %reduce-scatter.7.cloned.1.call-start = ((), (), s32[]{:S(2)}) async-start(), calls=%async_computation.4 | async-start | bytes 13369344 | tf_op jit(solution)/shard_map/reduce_scatter | solution.py:116
  487.3 334.0 %all-reduce.11.cloned.1.call-start = ((), (), s32[]{:S(2)}) async-start(), calls=%async_computation.7 | async-start | bytes 589824 | tf_op jit(solution)/shard_map/psum | solution.py:160
  487.3 6.1 copy-start.6
  493.4 288.1 %copy-start.18 = (f32[24]{0:T(128)S(1)}, f32[24]{0:T(128)}, u32[]{:S(2)}) copy-start(f32[24]{0:T(128)} %param.34) | copy-start | bytes 292
  788.7 7.3 copy-start.5
  788.7 7.3 copy-start.11
  796.0 3.1 copy-start.4
  799.1 3.1 copy-start.9
  808.8 15.6 %copy-start.1 = (bf16[96,384]{1,0:T(8,128)(2,1)S(1)}, bf16[96,384]{1,0:T(8,128)(2,1)}, u32[]{:S(2)}) copy-start(bf16[96,384]{1,0:T(8,128)(2,1)} %param.33) | copy-start | bytes 221188
  811.1 3.2 copy-start.8
  811.1 3.2 copy-start.12
  811.1 4.3 copy-start.19
  811.1 5.0 copy-start.14
  811.1 5.1 copy-start.24
  811.2 5.1 copy-start.20
  811.2 5.3 copy-start.15
  811.2 5.4 copy-start.25
Sparse Core Ops, SparseCore 0:
  40.8 97.2 all-gather.2
  141.4 92.4 all-gather.4
  261.7 202.1 reduce-scatter.8
  470.8 102.0 all-reduce.8
  578.4 203.0 reduce-scatter.6
  784.4 17.9 all-reduce.10
where the time goes:
time: 841 us; the launch traced here: 832 us
  waiting for transfers between devices  610 us (73%)
  matrix products  77.2 us (9%)
  local copies, waits for them, and re-layouts  50.8 us (6%)
  blocking collectives  48.1 us (6%)
  other arithmetic  29.9 us (4%)
  between operations  15.7 us (2%)
    reduce_scatter x1, waiting for transfers between devices, per_device(): lax.psum_scatter(jnp.einsum('fc,fp->cp', columns, hidden, preferred_eleme...  207 us
    reduce_scatter x1, waiting for transfers between devices, per_device(): lax.psum_scatter(jnp.einsum('cf,fp->cp', in_weight, before_grad, preferre...  202 us
    all_gather x1, waiting for transfers between devices, per_device(): piece = lax.all_gather(down_grad, 'ch', axis=0, tiled=True)  75 us
    psum x1, waiting for transfers between devices, per_device(): lax.psum((jnp.sum(scaled, axis=0), jnp.sum(scaled * normal_own, axis=0)),...  73.9 us
    all_gather x1, waiting for transfers between devices, per_device(): lax.all_gather(mixed_low, 'ch', axis=0, tiled=True)  50.8 us
    unnamed x1, blocking collectives  43.9 us
    unnamed x63, local copies, waits for them, and re-layouts  33.8 us
    dot_general x3, matrix products, mixer(): spread = jnp.einsum('ciaw,cbw->ciab', spread, across_matrix, precision=HIGH)  17.5 us
  transfers between devices with their start and end apart: 6, of which 5 were waited for; matrix products, arithmetic and copies ran while one was open for 11% of the time, Pallas kernels for 0%

commit v1 on v0

v1 whole, which is shorter than its diff:
```python
import math
from functools import partial

import jax
import jax.numpy as jnp
from jax import lax
from jax.experimental import pallas as pl
from jax.experimental.pallas import tpu as pltpu
from jax.sharding import PartitionSpec as P

SIDE = 32
CELLS = SIDE * SIDE
LANES = 128
PER = LANES // SIDE
TILES = CELLS // LANES
EPS = 1e-06
F32 = jnp.float32
BF16 = jnp.bfloat16
VMEM_LIMIT = 56 * 1024 * 1024


def column(row):
    n = row.shape[1]
    eye = lax.broadcasted_iota(jnp.int32, (n, n), 0) == lax.broadcasted_iota(jnp.int32, (n, n), 1)
    return jnp.sum(jnp.where(eye, jnp.broadcast_to(row, (n, n)), 0.0), axis=1, keepdims=True)


def as_row(col):
    n = col.shape[0]
    eye = lax.broadcasted_iota(jnp.int32, (n, n), 0) == lax.broadcasted_iota(jnp.int32, (n, n), 1)
    return jnp.sum(jnp.where(eye, jnp.broadcast_to(col, (n, n)), 0.0), axis=0, keepdims=True)


def image_mask(rows, height, width):
    cell = lax.broadcasted_iota(jnp.int32, (rows, CELLS), 1)
    return (cell // SIDE < height) & (cell % SIDE < width)


def lane_of(rows):
    return lax.broadcasted_iota(jnp.int32, (rows, LANES), 1)


def later(tiles, lane):
    out = [tiles]
    for step in range(1, PER):
        turned = [pltpu.roll(t, SIDE * step, 1) for t in tiles]
        out.append(
            [
                jnp.where(lane < SIDE * step, turned[k - 1] if k else 0.0, turned[k])
                for k in range(TILES)
            ]
        )
    return out


def sooner(tiles, lane):
    out = [tiles]
    for step in range(1, PER):
        turned = [pltpu.roll(t, LANES - SIDE * step, 1) for t in tiles]
        out.append(
            [
                jnp.where(
                    lane >= LANES - SIDE * step, turned[k + 1] if k < TILES - 1 else 0.0, turned[k]
                )
                for k in range(TILES)
            ]
        )
    return out


def vertical(tiles_at, taps, rows):
    out = [None] * TILES
    for lag in range(SIDE):
        tap = taps[lag, rows, :]
        for k in range(lag // PER, TILES):
            term = tap * tiles_at[lag % PER][k - lag // PER]
            out[k] = term if out[k] is None else out[k] + term
    return out


def group_of(channels):
    return 8 if channels % 8 == 0 else channels


def down_kernel(heights, widths, cot_ref, scale_ref, out_ref):
    image = pl.program_id(0)
    channels = cot_ref.shape[0]
    inside = image_mask(channels, heights[image], widths[image])
    value = jnp.where(inside, cot_ref[...].astype(F32), 0.0) * column(scale_ref[...])
    wide = out_ref.shape[2]
    for j in range(out_ref.shape[0]):
        out_ref[j] = value[:, j * wide : (j + 1) * wide].astype(BF16)


def forward_kernel(
    heights, widths, feat_ref, step_h, step_w, rate_h, rate_w, read_h, read_w, skip_ref,
    out_ref, rows_ref, taps_v, taps_h, held, done,
):
    image = pl.program_id(0)
    channels = feat_ref.shape[0]
    size = group_of(channels)

    @pl.when(image == 0)
    def _():
        lane = lane_of(channels)
        kept = jnp.zeros((channels, LANES), F32)
        decay_h = jnp.exp(column(step_h[...])) * rate_h[...]
        decay_w = jnp.exp(column(step_w[...])) * rate_w[...]
        for lag in range(SIDE):
            tap = jnp.sum(read_h[...] * jnp.exp(-decay_h * lag), axis=1, keepdims=True)
            tap = jnp.broadcast_to(tap, (channels, LANES))
            taps_v[lag] = tap
            kept = jnp.where(lane == lag, tap, kept)
            tap = jnp.sum(read_w[...] * jnp.exp(-decay_w * lag), axis=1, keepdims=True)
            tap = jnp.broadcast_to(tap, (channels, LANES))
            taps_h[lag] = jnp.where(lane % SIDE >= lag, tap, 0.0)
            kept = jnp.where(lane == SIDE + lag, tap, kept)
        kept = jnp.where(lane == 2 * SIDE, column(skip_ref[...]), kept)
        rows_ref[...] = kept

    inside = image_mask(channels, heights[image], widths[image])
    held[...] = jnp.where(inside, feat_ref[...].astype(F32), 0.0)

    def body(group, carry):
        rows = pl.ds(pl.multiple_of(group * size, size), size)
        lane = lane_of(size)
        tiles = [held[rows, k * LANES : (k + 1) * LANES] for k in range(TILES)]
        tall = vertical(later(tiles, lane), taps_v, rows)
        skip = rows_ref[rows, 2 * SIDE : 2 * SIDE + 1]
        acc = [skip * t for t in tiles]
        for lag in range(SIDE):
            tap = taps_h[lag, rows, :]
            for k in range(TILES):
                acc[k] = acc[k] + tap * (pltpu.roll(tall[k], lag, 1) if lag else tall[k])
        for k in range(TILES):
            done[rows, k * LANES : (k + 1) * LANES] = acc[k]
        return carry

    lax.fori_loop(0, channels // size, body, 0)
    value = jnp.where(inside, done[...], 0.0)
    wide = out_ref.shape[2]
    for j in range(out_ref.shape[0]):
        out_ref[j] = value[:, j * wide : (j + 1) * wide].astype(BF16)


def backward_kernel(
    heights, widths, feat_ref, cot_ref, mgrad_ref, summed_ref, rows_in, scale_ref, bias_ref,
    result_ref, gfeat_ref, small_ref, taps_v, taps_h, sums_v, sums_h, held, back, turn,
):
    image = pl.program_id(0)
    last = pl.num_programs(0) - 1
    channels = feat_ref.shape[0]
    size = group_of(channels)

    @pl.when(image == 0)
    def _():
        lane = lane_of(channels)
        for lag in range(SIDE):
            taps_v[lag] = jnp.broadcast_to(rows_in[:, lag : lag + 1], (channels, LANES))
            tap = jnp.broadcast_to(rows_in[:, SIDE + lag : SIDE + lag + 1], (channels, LANES))
            taps_h[lag] = jnp.where(lane % SIDE + lag < SIDE, tap, 0.0)
        sums_v[...] = jnp.zeros_like(sums_v)
        sums_h[...] = jnp.zeros_like(sums_h)
        small_ref[...] = jnp.zeros_like(small_ref)

    inside = image_mask(channels, heights[image], widths[image])
    values = feat_ref[...].astype(F32)
    masked = jnp.where(inside, values, 0.0)
    held[...] = masked
    wide = mgrad_ref.shape[2]
    parts = mgrad_ref.shape[0]
    grad = jnp.concatenate([mgrad_ref[j].astype(F32) for j in range(parts)], axis=1)
    grad = jnp.where(inside, grad, 0.0)
    back[...] = grad

    def body(group, carry):
        rows = pl.ds(pl.multiple_of(group * size, size), size)
        lane = lane_of(size)
        tiles = [held[rows, k * LANES : (k + 1) * LANES] for k in range(TILES)]
        tall = vertical(later(tiles, lane), taps_v, rows)
        flow = [back[rows, k * LANES : (k + 1) * LANES] for k in range(TILES)]
        wide_grad = [None] * TILES
        for lag in range(SIDE):
            tap = taps_h[lag, rows, :]
            total = None
            for k in range(TILES):
                moved = pltpu.roll(flow[k], LANES - lag, 1) if lag else flow[k]
                term = tap * moved
                wide_grad[k] = term if lag == 0 else wide_grad[k] + term
                term = moved * tall[k]
                total = term if total is None else total + term
            sums_h[lag, rows, :] += total
        moved_at = sooner(wide_grad, lane)
        skip = rows_in[rows, 2 * SIDE : 2 * SIDE + 1]
        out = [skip * flow[k] for k in range(TILES)]
        for lag in range(SIDE):
            tap = taps_v[lag, rows, :]
            high = lag // PER
            total = None
            for k in range(TILES - high):
                moved = moved_at[lag % PER][k + high]
                out[k] = out[k] + tap * moved
                term = moved * tiles[k]
                total = term if total is None else total + term
            sums_v[lag, rows, :] += total
        for k in range(TILES):
            turn[rows, k * LANES : (k + 1) * LANES] = out[k]
        return carry

    lax.fori_loop(0, channels // size, body, 0)
    cot = cot_ref[...].astype(F32)
    gfeat_ref[...] = cot + jnp.where(inside, turn[...], 0.0)

    shifted = jnp.concatenate([summed_ref[j].astype(F32) for j in range(parts)], axis=1)
    shifted = shifted + column(bias_ref[...])
    result = values + jnp.where(inside, column(scale_ref[...]) * shifted, 0.0)
    result_ref[...] = result.astype(BF16)
    weighted = jnp.where(inside, cot, 0.0)
    lane = lane_of(channels)
    add = jnp.where(lane == 64, jnp.sum(grad * masked, axis=1, keepdims=True), 0.0)
    add = jnp.where(lane == 65, jnp.sum(weighted * shifted, axis=1, keepdims=True), add)
    add = jnp.where(lane == 66, jnp.sum(weighted, axis=1, keepdims=True), add)
    small_ref[...] += add

    @pl.when(image == last)
    def _():
        total = small_ref[...]
        for lag in range(SIDE):
            part = jnp.sum(sums_v[lag], axis=1, keepdims=True)
            total = jnp.where(lane == lag, part, total)
            part = jnp.where(lane % SIDE + lag < SIDE, sums_h[lag], 0.0)
            part = jnp.sum(part, axis=1, keepdims=True)
            total = jnp.where(lane == SIDE + lag, part, total)
        small_ref[...] = total


def chain_kernel(
    own_ref, other_ref, step_h, step_w, rate_h, rate_w, read_h, read_w, scale_ref,
    gstep_h, grate_h, gread_h, gstep_w, grate_w, gread_w, gskip, gbias, gscale,
):
    total = own_ref[...] + other_ref[...]
    for first, step, rate, read, gstep, grate, gread in (
        (0, step_h, rate_h, read_h, gstep_h, grate_h, gread_h),
        (SIDE, step_w, rate_w, read_w, gstep_w, grate_w, gread_w),
    ):
        pace = jnp.exp(column(step[...]))
        decay = pace * rate[...]
        to_read = jnp.zeros_like(decay)
        to_decay = jnp.zeros_like(decay)
        for lag in range(SIDE):
            term = total[:, first + lag : first + lag + 1] * jnp.exp(-decay * lag)
            to_read = to_read + term
            if lag:
                to_decay = to_decay - float(lag) * term
        to_decay = to_decay * read[...]
        gread[...] = to_read
        grate[...] = pace * to_decay
        gstep[...] = as_row(jnp.sum(to_decay * decay, axis=1, keepdims=True))
    gskip[...] = as_row(total[:, 64:65])
    gscale[...] = as_row(total[:, 65:66])
    gbias[...] = as_row(total[:, 66:67]) * scale_ref[...]


def pack_kernel(half, in_ref, out_ref, bias_ref, gain_ref, shift_ref, pack_ref):
    copies, deep, wide = pack_ref.shape
    own, count = out_ref.shape
    channels = gain_ref.shape[1]
    keep = own // 2
    row = lax.broadcasted_iota(jnp.int32, (deep, own), 0)
    col = lax.broadcasted_iota(jnp.int32, (deep, own), 1)
    pick = jnp.where((col == row + half[0] * keep) & (row < keep), 1.0, 0.0).astype(BF16)
    nt = (((1,), (1,)), ((), ()))
    first = lax.dot_general(pick, in_ref[...], nt, preferred_element_type=F32)
    second = jnp.dot(pick, out_ref[...], preferred_element_type=F32)
    bias = jnp.broadcast_to(bias_ref[...], (LANES, own))
    third = lax.dot_general(pick, bias, nt, preferred_element_type=F32)
    row = lax.broadcasted_iota(jnp.int32, (deep, channels), 0)
    col = lax.broadcasted_iota(jnp.int32, (deep, channels), 1)
    pick = jnp.where(col == row, 1.0, 0.0).astype(BF16)
    gain = jnp.broadcast_to(gain_ref[...], (LANES, channels))
    gain = lax.dot_general(pick, gain, nt, preferred_element_type=F32)
    shift = jnp.broadcast_to(shift_ref[...], (LANES, channels))
    shift = lax.dot_general(pick, shift, nt, preferred_element_type=F32)
    lane = lane_of(deep)
    third = jnp.where(lane == 0, third, jnp.where(lane == 1, gain, jnp.where(lane == 2, shift, 0.0)))
    for j in range(copies):
        pack_ref[j, :, :count] = first.astype(BF16)
        pack_ref[j, :, count : 2 * count] = second.astype(BF16)
        pack_ref[j, :, 2 * count :] = third.astype(BF16)


ROOT = math.sqrt(2.0 / math.pi)


def mlp_kernel(
    mixed_ref, down_ref, gain_ref, shift_ref, own_ref, other_ref,
    summed_ref, mgrad_ref, gown_ref, gother_ref, gnorm_ref,
    active, mean_ref, inv_ref, sum_acc, grad_acc,
):
    step = pl.program_id(0)
    last = pl.num_programs(0) - 1
    count = mixed_ref.shape[0]
    block = own_ref.shape[0]

    @pl.when(step == 0)
    def _():
        value = mixed_ref[...].astype(F32)
        mean = jnp.mean(value, axis=0, keepdims=True)
        value = value - mean
        inv = lax.rsqrt(jnp.mean(value * value, axis=0, keepdims=True) + EPS)
        mean_ref[...] = mean
        inv_ref[...] = inv
        active[...] = (value * inv * gain_ref[...] + shift_ref[...]).astype(BF16)
        sum_acc[...] = jnp.zeros_like(sum_acc)
        grad_acc[...] = jnp.zeros_like(grad_acc)

    nt = (((1,), (1,)), ((), ()))
    tn = (((0,), (0,)), ((), ()))

    def process(ref):
        w_in = ref[:, :count]
        w_out = ref[:, count : 2 * count]
        act = active[...]
        down = down_ref[...]
        v = jnp.dot(w_in, act, preferred_element_type=F32)
        v = v + ref[:, 2 * count : 2 * count + 1].astype(F32)
        square = v * v
        bend = jnp.tanh(ROOT * v * (1.0 + 0.044715 * square))
        half = 0.5 * (1.0 + bend)
        hidden = (v * half).astype(BF16)
        slope = half + 0.5 * v * (1.0 - bend * bend) * (ROOT * (1.0 + 3.0 * 0.044715 * square))
        sum_acc[...] += lax.dot_general(w_out, hidden, tn, preferred_element_type=F32)
        hgrad = jnp.dot(w_out, down, preferred_element_type=F32)
        bgrad = hgrad * slope
        low = bgrad.astype(BF16)
        grad_acc[...] += lax.dot_general(w_in, low, tn, preferred_element_type=F32)
        g_in = lax.dot_general(low, act, nt, preferred_element_type=F32)
        g_out = lax.dot_general(hidden, down, nt, preferred_element_type=F32)
        g_bias = jnp.sum(low.astype(F32), axis=1, keepdims=True)
        return g_in, g_out, jnp.where(lane_of(block) == 0, g_bias, 0.0)

    g_in, g_out, g_ext = process(other_ref)
    gother_ref[:, :count] = g_in.astype(BF16)
    gother_ref[:, count : 2 * count] = g_out.astype(BF16)
    gother_ref[:, 2 * count :] = g_ext.astype(BF16)
    g_in, g_out, g_ext = process(own_ref)
    gown_ref[:, :count] = g_in
    gown_ref[:, count : 2 * count] = g_out
    gown_ref[:, 2 * count :] = g_ext

    @pl.when(step == last)
    def _():
        summed_ref[...] = sum_acc[...].astype(BF16)
        agrad = grad_acc[...]
        inv = inv_ref[...]
        normal = (mixed_ref[...].astype(F32) - mean_ref[...]) * inv
        scaled = agrad * gain_ref[...]
        first = jnp.mean(scaled, axis=0, keepdims=True)
        second = jnp.mean(scaled * normal, axis=0, keepdims=True)
        mgrad_ref[...] = ((scaled - first - normal * second) * inv).astype(BF16)
        lane = lane_of(count)
        ext = jnp.where(lane == 1, jnp.sum(agrad * normal, axis=1, keepdims=True), 0.0)
        gnorm_ref[...] = jnp.where(lane == 2, jnp.sum(agrad, axis=1, keepdims=True), ext)


def whole(shape):
    return pl.BlockSpec(shape, lambda i: (0,) * len(shape))


def params(**extra):
    return pltpu.CompilerParams(vmem_limit_bytes=VMEM_LIMIT, **extra)


SMEM = pl.BlockSpec(memory_space=pltpu.SMEM)


def per_device(
    ch, features, cotangent, heights, widths, step_height, rate_height, readout_height,
    step_width, rate_width, readout_width, skip_gain, norm_gain, norm_shift, in_weight,
    in_bias, out_weight, out_bias, layer_scale,
):
    channels, cells = features.shape
    count = in_weight.shape[0]
    units = in_weight.shape[1]
    states = rate_height.shape[1]
    images = cells // CELLS
    tokens = cells // ch
    parts = CELLS // tokens
    far = 4 if ch % 4 == 0 else 1
    near = ch // far
    deep = -(-(units // 2) // 16) * 16
    width = 2 * count + LANES
    near_groups = [[f * near + i for i in range(near)] for f in range(far)]
    far_groups = [[f * near + i for f in range(far)] for i in range(near)]
    row = lambda v: v.reshape(1, -1)
    exchange = lambda v: lax.ppermute(v, "img", [(0, 1), (1, 0)])
    swap = lambda v, groups=None: lax.all_to_all(
        v, "ch", split_axis=0, concat_axis=0, tiled=True, axis_index_groups=groups
    )
    half = lax.axis_index("img").astype(jnp.int32)

    full = pl.BlockSpec(memory_space=pltpu.VMEM)
    pack = pl.pallas_call(
        pack_kernel,
        out_shape=jax.ShapeDtypeStruct((far, deep, width), BF16),
        in_specs=[SMEM] + [full] * 5,
        out_specs=full,
        compiler_params=params(),
        name="pack",
    )(half.reshape(1), in_weight, out_weight, row(in_bias), row(norm_gain), row(norm_shift))
    pack = swap(pack, far_groups)
    pack = lax.all_gather(
        pack.reshape(far * deep, width), "ch", axis=0, tiled=True, axis_index_groups=near_groups
    )
    other = exchange(pack)
    vectors = pack.reshape(near, far, deep, width)[:, :, :channels, 2 * count + 1 : 2 * count + 3]
    vectors = vectors.transpose(1, 0, 2, 3).reshape(count, 2).astype(F32)

    cells_spec = pl.BlockSpec((channels, CELLS), lambda i: (0, i))
    token_spec = pl.BlockSpec((parts, channels, tokens), lambda i: (i, 0, 0))
    down = pl.pallas_call(
        down_kernel,
        grid=(images,),
        out_shape=jax.ShapeDtypeStruct((ch, channels, tokens), BF16),
        in_specs=[SMEM, SMEM, cells_spec, whole((1, channels))],
        out_specs=token_spec,
        compiler_params=params(),
        name="down",
    )(heights, widths, cotangent, row(layer_scale))
    down = swap(down).reshape(count, tokens)

    state = whole((channels, states))
    vector = whole((1, channels))
    tap = pltpu.VMEM((SIDE, channels, LANES), F32)
    plane = pltpu.VMEM((channels, CELLS), F32)
    mixed, taps = pl.pallas_call(
        forward_kernel,
        grid=(images,),
        out_shape=(
            jax.ShapeDtypeStruct((ch, channels, tokens), BF16),
            jax.ShapeDtypeStruct((channels, LANES), F32),
        ),
        in_specs=[SMEM, SMEM, cells_spec, vector, vector, state, state, state, state, vector],
        out_specs=(token_spec, whole((channels, LANES))),
        scratch_shapes=[tap, tap, plane, plane],
        compiler_params=params(),
        name="mixer_forward",
    )(
        heights, widths, features, row(step_height), row(step_width), rate_height, rate_width,
        readout_height, readout_width, row(skip_gain),
    )
    mixed = swap(mixed).reshape(count, tokens)

    rows = ch * deep
    blocks = 2
    span = rows // blocks
    token_full = whole((count, tokens))
    weight_spec = pl.BlockSpec((span, width), lambda i: (i, 0))
    summed, mgrad, gown, gother, gnorm = pl.pallas_call(
        mlp_kernel,
        grid=(blocks,),
        out_shape=(
            jax.ShapeDtypeStruct((count, tokens), BF16),
            jax.ShapeDtypeStruct((count, tokens), BF16),
            jax.ShapeDtypeStruct((rows, width), F32),
            jax.ShapeDtypeStruct((rows, width), BF16),
            jax.ShapeDtypeStruct((count, LANES), F32),
        ),
        in_specs=[token_full, token_full, whole((count, 1)), whole((count, 1)), weight_spec, weight_spec],
        out_specs=(token_full, token_full, weight_spec, weight_spec, whole((count, LANES))),
        scratch_shapes=[
            pltpu.VMEM((count, tokens), BF16),
            pltpu.VMEM((1, tokens), F32),
            pltpu.VMEM((1, tokens), F32),
            pltpu.VMEM((count, tokens), F32),
            pltpu.VMEM((count, tokens), F32),
        ],
        compiler_params=params(),
        name="mlp",
    )(mixed, down, vectors[:, 0:1], vectors[:, 1:2], pack, other)

    arrived = exchange(gother)
    mgrad = swap(mgrad.reshape(ch, channels, tokens))
    summed = swap(summed.reshape(ch, channels, tokens))

    gnorm = gnorm.reshape(far, near, channels, LANES).transpose(1, 0, 2, 3)
    gnorm = jnp.pad(gnorm, ((0, 0), (0, 0), (0, deep - channels), (2 * count, 0)))
    partial_sum = (gown + arrived.astype(F32)).reshape(near, far, deep, width) + gnorm
    partial_sum = swap(partial_sum.astype(BF16), near_groups)
    partial_sum = jnp.sum(partial_sum.astype(F32), axis=0)
    partial_sum = swap(partial_sum.astype(BF16), far_groups)
    partial_sum = jnp.sum(partial_sum.astype(F32), axis=0)
    sibling = exchange(partial_sum)
    keep = units // 2
    low = jnp.where(half == 0, partial_sum, sibling)[:keep]
    high = jnp.where(half == 0, sibling, partial_sum)[:keep]
    grads = jnp.concatenate([low, high], axis=0)
    grad_in_weight = grads[:, :count].T
    grad_out_weight = grads[:, count : 2 * count]
    grad_in_bias = grads[:, 2 * count]
    norms = (partial_sum + sibling)[:channels, 2 * count + 1 : 2 * count + 3]

    result, grad_features, small = pl.pallas_call(
        backward_kernel,
        grid=(images,),
        out_shape=(
            jax.ShapeDtypeStruct((channels, cells), BF16),
            jax.ShapeDtypeStruct((channels, cells), F32),
            jax.ShapeDtypeStruct((channels, LANES), F32),
        ),
        in_specs=[
            SMEM, SMEM, cells_spec, cells_spec, token_spec, token_spec, whole((channels, LANES)),
            vector, vector,
        ],
        out_specs=(cells_spec, cells_spec, whole((channels, LANES))),
        scratch_shapes=[tap, tap, tap, tap, plane, plane, plane],
        compiler_params=params(),
        name="mixer_backward",
    )(heights, widths, features, cotangent, mgrad, summed, taps, row(layer_scale), row(out_bias))

    vector_out = jax.ShapeDtypeStruct((1, channels), F32)
    state_out = jax.ShapeDtypeStruct((channels, states), F32)
    chained = pl.pallas_call(
        chain_kernel,
        out_shape=(
            vector_out, state_out, state_out, vector_out, state_out, state_out,
            vector_out, vector_out, vector_out,
        ),
        in_specs=[full] * 9,
        out_specs=(full,) * 9,
        compiler_params=params(),
        name="mixer_chain",
    )(
        small, exchange(small), row(step_height), row(step_width), rate_height, rate_width,
        readout_height, readout_width, row(layer_scale),
    )
    gstep_h, grate_h, gread_h, gstep_w, grate_w, gread_w, gskip, gbias, gscale = chained
    flat = lambda v: v.reshape(-1)
    return (
        result, grad_features, flat(gstep_h), grate_h, gread_h, flat(gstep_w), grate_w, gread_w,
        flat(gskip), norms[:, 0], norms[:, 1], grad_in_weight, grad_in_bias, grad_out_weight,
        flat(gbias), flat(gscale),
    )


def solution(mesh):
    wide, split, tall = P("ch", "img"), P("ch"), P("ch", None)
    return jax.shard_map(
        partial(per_device, mesh.shape["ch"]),
        mesh=mesh,
        in_specs=(
            wide, wide, P("img"), P("img"), split, tall, tall, split, tall, tall, split, split,
            split, P(None, "ch"), split, tall, split, split,
        ),
        out_specs=(
            wide, wide, split, tall, tall, split, tall, tall, split, split, split,
            P(None, "ch"), split, tall, split, split,
        ),
        check_vma=False,
    )
```

time: 841 us -> 204 us (0.24)
  waiting for transfers between devices: 610 us -> 60.9 us
  matrix products: 77.2 us -> 0 us
  Pallas kernels: 0 us -> 48.1 us
  local copies, waits for them, and re-layouts: 50.8 us -> 6.68 us
  other arithmetic: 29.9 us -> 5.02 us
  starting transfers between devices: 0.24 us -> 18 us
    reduce_scatter x2 -> x0, waiting for transfers between devices: 409 us -> none  [the longest x1 207 us: per_device(): lax.psum_scatter(jnp.einsum('fc,fp->cp', columns, hidden, preferred_eleme...]
    all_gather x2 -> x1, waiting for transfers between devices: 126 us -> 22.5 us  [per_device(): lax.all_gather(pack.reshape(far * deep, width), 'ch', axis=0, tiled=True,...]
    dot_general x20 -> x0, matrix products: 77.2 us -> none  [the longest x3 17.5 us: mixer(): spread = jnp.einsum('ciaw,cbw->ciab', spread, across_matrix, precision=HIGH)]
    psum x2 -> x0, waiting for transfers between devices: 73.9 us -> none  [the longest x1 73.9 us: per_device(): lax.psum((jnp.sum(scaled, axis=0), jnp.sum(scaled * normal_own, axis=0)),...]
    all_to_all x0 -> x3, blocking collectives: none -> 49.9 us  [per_device(): lax.all_to_all(v, 'ch', split_axis=0, concat_axis=0, tiled=True, axis_ind...]
    pallas_call x0 -> x6, Pallas kernels: none -> 48.1 us  [the longest x1 15.4 us: per_device(): pl.pallas_call(backward_kernel, grid=(images,), out_shape=(jax.ShapeDtype...]
    unnamed x1 -> x0, blocking collectives: 43.9 us -> none
    all_to_all x0 -> x4, waiting for transfers between devices: none -> 34.6 us  [per_device(): lax.all_to_all(v, 'ch', split_axis=0, concat_axis=0, tiled=True, axis_ind...]
  transfers between devices with their start and end apart: 6 -> 9, of which waited for: 5 -> 6; matrix products, arithmetic and copies ran while one was open for 11% -> 2% of each run, Pallas kernels for 0% -> 17%
where the time goes in v1:
time: 204 us; the launch traced here: 203 us
  waiting for transfers between devices  60.9 us (30%)
  blocking collectives  49.9 us (24%)
  Pallas kernels  48.1 us (24%)
  starting transfers between devices  18 us (9%)
  between operations  14.2 us (7%)
  local copies, waits for them, and re-layouts  6.68 us (3%)
  other arithmetic  5.02 us (2%)
    all_to_all x3, blocking collectives, per_device(): lax.all_to_all(v, 'ch', split_axis=0, concat_axis=0, tiled=True, axis_ind...  49.9 us
    all_to_all x4, waiting for transfers between devices, per_device(): lax.all_to_all(v, 'ch', split_axis=0, concat_axis=0, tiled=True, axis_ind...  34.6 us
    all_gather x1, waiting for transfers between devices, per_device(): lax.all_gather(pack.reshape(far * deep, width), 'ch', axis=0, tiled=True,...  22.5 us
    all_to_all x4, starting transfers between devices, per_device(): lax.all_to_all(v, 'ch', split_axis=0, concat_axis=0, tiled=True, axis_ind...  17.8 us
    pallas_call x1, Pallas kernels, per_device(): pl.pallas_call(backward_kernel, grid=(images,), out_shape=(jax.ShapeDtype...  15.4 us
    pallas_call x1, Pallas kernels, per_device(): pl.pallas_call(forward_kernel, grid=(images,), out_shape=(jax.ShapeDtypeS...  12.6 us
    pallas_call x1, Pallas kernels, per_device(): pl.pallas_call(mlp_kernel, grid=(blocks,), out_shape=(jax.ShapeDtypeStruc...  11.2 us
    pallas_call x1, Pallas kernels, per_device(): pl.pallas_call(down_kernel, grid=(images,), out_shape=jax.ShapeDtypeStruc...  4.91 us
  transfers between devices with their start and end apart: 9, of which 6 were waited for; matrix products, arithmetic and copies ran while one was open for 2% of the time, Pallas kernels for 17%

profile of v1, /device:TPU:0, one launch (start us, length us, event | category | flops | bytes accessed | tf_op | source)
XLA Modules:
  0.0 202.8 jit_solution(17081068968139087173)
XLA Ops:
  7.2 0.0 all-gather.2.cloned.1.call-start
  7.2 1.6 copy.43.in_ref
  8.9 1.9 pack.1
  10.8 17.1 %all_to_all.35 = bf16[4,48,896]{2,1,0:T(8,128)(2,1)} all-to-all(bf16[4,48,896]{2,1,0:T(8,128)(2,1)} %pack.1), channel_id=1, replica_groups={{0,4,8,12},{1,5,9,13},{2,6,10,14},{3,7,11,15},{16,20,24,28},{17,21,25,2..., dimensions={0} | all-to-all | bytes 688128 | tf_op jit(solution)/shard_map/all_to_all | solution.py:397
  27.8 0.0 all-gather.2.cloned.1.call-update
  27.9 4.9 %down.1 = bf16[16,24,512]{2,1,0:T(8,128)(2,1)} custom-call(s32[8]{0:T(128)} %heights.5, s32[8]{0:T(128)} %widths.5, bf16[24,8192]{1,0:T(8,128)(2,1)} %cot_ref.3, f32[1,24]{1,0:T(1,128)} %bitcast.38), custom_call_target="tpu_custom_call" | custom-call | tf_op jit(solution)/shard_map/down/pallas_call | solution.py:421
  32.8 4.7 %all-to-all-start.1 = ((bf16[16,24,512]{2,1,0:T(8,128)(2,1)}), bf16[16,24,512]{2,1,0:T(8,128)(2,1)S(1)}, u32[]{:S(2)}, u32[]{:S(2)}) async-start(bf16[16,24,512]{2,1,0:T(8,128)(2,1)} %down.1), calls=%async_computation.1 | async-start | bytes 786432 | tf_op jit(solution)/shard_map/all_to_all | solution.py:397
  37.5 22.5 %all-gather.2.cloned.1.call-done.own_ref = bf16[768,896]{1,0:T(8,128)(2,1)} async-done(((bf16[192,896]{1,0:T(8,128)(2,1)}), bf16[768,896]{1,0:T(8,128)(2,1)}) %all-gather.2.cloned.1.call-update) | async-done | bytes 1376272 | tf_op jit(solution)/shard_map/all_gather | solution.py:412
  60.0 0.0 collective-permute-start
  60.0 12.6 %mixer_forward.1 = (bf16[16,24,512]{2,1,0:T(8,128)(2,1)}, f32[24,128]{1,0:T(8,128)}) custom-call(s32[8]{0:T(128)} %heights.5, s32[8]{0:T(128)} %widths.5, bf16[24,8192]{1,0:T(8,128)(2,1)} %feat_ref.3, f32[1,24]{1,0:T(1,128)} %bitcast.41, f32[1,24]{1,0:T(1,128)} %bitcast.43, f32[24,64]{1,0:T(8,128)} %rate_h.3, f32[24,64]{1,0:T(8,128)} %rate_w.3, ...), custom_call_target="tpu_custom_call" | custom-call | tf_op jit(solution)/shard_map/mixer_forward/pallas_call | solution.py:436
  72.6 0.0 all-to-all-done.1
  72.6 0.0 copy-start.2
  72.6 5.6 %all-to-all-start = ((bf16[16,24,512]{2,1,0:T(8,128)(2,1)}), bf16[16,24,512]{2,1,0:T(8,128)(2,1)S(1)}, u32[]{:S(2)}, u32[]{:S(2)}) async-start(bf16[16,24,512]{2,1,0:T(8,128)(2,1)} %get-tuple-element.35), calls=%async_computation | async-start | bytes 786432 | tf_op jit(solution)/shard_map/all_to_all | solution.py:397
  78.3 1.0 convert_bitcast_fusion
  79.3 0.8 fusion.4
  80.1 11.3 %all-to-all-done = bf16[16,24,512]{2,1,0:T(8,128)(2,1)S(1)} async-done(((bf16[16,24,512]{2,1,0:T(8,128)(2,1)}), bf16[16,24,512]{2,1,0:T(8,128)(2,1)S(1)}, u32[]{:S(2)}, u32[]{:S(2)}) %all-to-all-start) | async-done | bytes 393248 | tf_op jit(solution)/shard_map/all_to_all | solution.py:397
  91.4 0.0 copy-start.3
  91.4 0.0 collective-permute-done.other_ref
  91.5 0.0 copy-start.4
  91.5 0.0 copy-done.2
  91.5 0.7 copy-done.3
  92.2 0.5 copy-done.4
  92.7 11.2 %mlp.1 = (bf16[384,512]{1,0:T(8,128)(2,1)}, bf16[384,512]{1,0:T(8,128)(2,1)}, f32[768,896]{1,0:T(8,128)}, bf16[768,896]{1,0:T(8,128)(2,1)}, f32[384,128]{1,0:T(8,128)}) custom-call(bf16[384,512]{1,0:T(8,128)(2,1)} %bitcast.34, bf16[384,512]{1,0:T(8,128)(2,1)} %bitcast.33, f32[384,1]{1,0:T(8,128)} %get-tuple-element.62.gain_ref, ...), custom_call_target="tpu_custom_call" | custom-call | tf_op jit(solution)/shard_map/mlp/pallas_call | solution.py:459
  103.9 0.1 collective-permute-start.2
  104.0 0.9 copy.47
  104.9 2.4 %collective-permute-done.2 = bf16[768,896]{1,0:T(8,128)(2,1)S(1)} collective-permute-done((bf16[768,896]{1,0:T(8,128)(2,1)}, bf16[768,896]{1,0:T(8,128)(2,1)S(1)}, u32[]{:S(2)}, u32[]{:S(2)}) %collective-permute-start.2) | collective-permute-done | bytes 1376288 | tf_op jit(solution)/shard_map/ppermute | solution.py:396
  107.3 2.1 %convert_add_fusion = f32[768,896]{1,0:T(8,128)S(1)} fusion(f32[768,896]{1,0:T(8,128)} %get-tuple-element.49, bf16[768,896]{1,0:T(8,128)(2,1)S(1)} %collective-permute-done.2), kind=kLoop, calls=%fused_computation.1 | loop fusion | flops 1376256 | bytes 6881280 | tf_op jit(solution)/shard_map/add | solution.py:488
  109.4 0.2 add_convert_fusion
  109.6 20.8 %all_to_all.36 = bf16[4,4,48,896]{3,2,1,0:T(8,128)(2,1)S(1)} all-to-all(bf16[4,4,48,896]{3,2,1,0:T(8,128)(2,1)S(1)} %add_convert_fusion), channel_id=1, replica_groups={{0,1,2,3},{4,5,6,7},{8,9,10,11},{12,13,14,15},{16,17,18,19},{20,21,22,2..., dimensions={0} | all-to-all | bytes 2752512 | tf_op jit(solution)/shard_map/all_to_all | solution.py:397
  130.4 3.6 %all-to-all-start.4 = ((bf16[16,24,512]{2,1,0:T(8,128)(2,1)}), bf16[16,24,512]{2,1,0:T(8,128)(2,1)S(1)}, u32[]{:S(2)}, u32[]{:S(2)}) async-start(bf16[16,24,512]{2,1,0:T(8,128)(2,1)} %bitcast.15), calls=%async_computation.4 | async-start | bytes 786432 | tf_op jit(solution)/shard_map/all_to_all | solution.py:397
  133.9 0.3 reduce_sum.21
  134.3 11.8 %all-to-all-done.4.summed_ref = bf16[16,24,512]{2,1,0:T(8,128)(2,1)S(1)} async-done(((bf16[16,24,512]{2,1,0:T(8,128)(2,1)}), bf16[16,24,512]{2,1,0:T(8,128)(2,1)S(1)}, u32[]{:S(2)}, u32[]{:S(2)}) %all-to-all-start.4) | async-done | bytes 393248 | tf_op jit(solution)/shard_map/all_to_all | solution.py:397
  146.1 0.0 copy-start
  146.1 12.0 %all_to_all.37 = bf16[4,48,896]{2,1,0:T(8,128)(2,1)S(1)} all-to-all(bf16[4,48,896]{2,1,0:T(8,128)(2,1)S(1)} %reduce_sum.21), channel_id=1, replica_groups={{0,4,8,12},{1,5,9,13},{2,6,10,14},{3,7,11,15},{16,20,24,28},{17,21,25,2..., dimensions={0} | all-to-all | bytes 688128 | tf_op jit(solution)/shard_map/all_to_all | solution.py:397
  158.1 3.9 %all-to-all-start.3 = ((bf16[16,24,512]{2,1,0:T(8,128)(2,1)}), bf16[16,24,512]{2,1,0:T(8,128)(2,1)S(1)}, u32[]{:S(2)}, u32[]{:S(2)}) async-start(bf16[16,24,512]{2,1,0:T(8,128)(2,1)} %bitcast.14), calls=%async_computation.3 | async-start | bytes 786432 | tf_op jit(solution)/shard_map/all_to_all | solution.py:397
  162.0 0.1 collective-permute-start.3
  162.1 11.5 %all-to-all-done.3.mgrad_ref = bf16[16,24,512]{2,1,0:T(8,128)(2,1)S(1)} async-done(((bf16[16,24,512]{2,1,0:T(8,128)(2,1)}), bf16[16,24,512]{2,1,0:T(8,128)(2,1)S(1)}, u32[]{:S(2)}, u32[]{:S(2)}) %all-to-all-start.3) | async-done | bytes 393248 | tf_op jit(solution)/shard_map/all_to_all | solution.py:397
  173.6 0.0 copy-start.1
  173.6 0.0 copy-done
  173.6 0.8 copy-done.1
  174.3 15.4 %mixer_backward.1 = (bf16[24,8192]{1,0:T(8,128)(2,1)}, f32[24,8192]{1,0:T(8,128)}, f32[24,128]{1,0:T(8,128)}) custom-call(s32[8]{0:T(128)} %heights.5, s32[8]{0:T(128)} %widths.5, bf16[24,8192]{1,0:T(8,128)(2,1)} %feat_ref.3, bf16[24,8192]{1,0:T(8,128)(2,1)} %cot_ref.3, bf16[16,24,512]{2,1,0:T(8,128)(2,1)} %copy-done.1, bf16[16,24,512]{2,1,0:T(8,128)(2,1)} %copy-done, ...), custom_call_target="tpu_custom_call" | custom-call | tf_op jit(solution)/shard_map/mixer_backward/pallas_call | solution.py:503
  189.8 0.1 collective-permute-start.1
  189.9 1.4 collective-permute-done.1.other_ref
  191.2 0.0 copy-start.5
  191.2 0.6 copy-done.5
  191.8 2.0 %mixer_chain.1 = (f32[1,24]{1,0:T(1,128)}, f32[24,64]{1,0:T(8,128)}, f32[24,64]{1,0:T(8,128)}, f32[1,24]{1,0:T(1,128)}, f32[24,64]{1,0:T(8,128)}, /*index=5*/f32...) custom-call(f32[24,128]{1,0:T(8,128)} %get-tuple-element.41.own_ref, f32[24,128]{1,0:T(8,128)} %copy-done.5, ...), custom_call_target="tpu_custom_call" | custom-call | tf_op jit(solution)/shard_map/mixer_chain/pallas_call | solution.py:523
  193.9 0.0 collective-permute-done.3
  193.9 0.6 fusion.3
  194.6 0.7 pad_maximum_fusion
  195.3 0.7 slice_reduce_fusion
  (3 shorter events, 0.1 us)
Async XLA Ops:
  7.2 52.8 %all-gather.2.cloned.1.call-start = ((), (), s32[]{:S(2)}) async-start(), calls=%async_computation.7 | async-start | bytes 1720320 | tf_op jit(solution)/shard_map/all_gather | solution.py:412
  32.8 39.9 %all-to-all-start.1 = ((bf16[16,24,512]{2,1,0:T(8,128)(2,1)}), bf16[16,24,512]{2,1,0:T(8,128)(2,1)S(1)}, u32[]{:S(2)}, u32[]{:S(2)}) async-start(bf16[16,24,512]{2,1,0:T(8,128)(2,1)} %down.1), calls=%async_computation.1 | async-start | bytes 786432 | tf_op jit(solution)/shard_map/all_to_all | solution.py:397
  60.0 31.4 %collective-permute-start = (bf16[768,896]{1,0:T(8,128)(2,1)}, bf16[768,896]{1,0:T(8,128)(2,1)S(1)}, u32[]{:S(2)}, u32[]{:S(2)}) collective-permute-start(bf16[768,896]{1,0:T(8,128)(2,1)} %all-gather.2.cloned.1.call-done.own_ref), channel_id=1, source_target_pairs={{0,16},{16,0},{1,17},{17,1},{2,18},{18,2},{3,19},{19,3},{4,20},{20... | collective-permute-start | bytes 4128776 | tf_op jit(solution)/shard_map/ppermute | solution.py:396
  72.6 18.8 %copy-start.2 = (bf16[16,24,512]{2,1,0:T(8,128)(2,1)}, bf16[16,24,512]{2,1,0:T(8,128)(2,1)S(1)}, u32[]{:S(2)}) copy-start(bf16[16,24,512]{2,1,0:T(8,128)(2,1)S(1)} %all-to-all-done.1) | copy-start | bytes 1179652
  72.6 18.8 %all-to-all-start = ((bf16[16,24,512]{2,1,0:T(8,128)(2,1)}), bf16[16,24,512]{2,1,0:T(8,128)(2,1)S(1)}, u32[]{:S(2)}, u32[]{:S(2)}) async-start(bf16[16,24,512]{2,1,0:T(8,128)(2,1)} %get-tuple-element.35), calls=%async_computation | async-start | bytes 786432 | tf_op jit(solution)/shard_map/all_to_all | solution.py:397
  91.4 0.7 copy-start.3
  91.5 1.2 copy-start.4
  103.9 3.4 %collective-permute-start.2 = (bf16[768,896]{1,0:T(8,128)(2,1)}, bf16[768,896]{1,0:T(8,128)(2,1)S(1)}, u32[]{:S(2)}, u32[]{:S(2)}) collective-permute-start(bf16[768,896]{1,0:T(8,128)(2,1)} %get-tuple-element.50), channel_id=1, source_target_pairs={{0,16},{16,0},{1,17},{17,1},{2,18},{18,2},{3,19},{19,3},{4,20},{20... | collective-permute-start | bytes 4128776 | tf_op jit(solution)/shard_map/ppermute | solution.py:396
  130.4 15.7 %all-to-all-start.4 = ((bf16[16,24,512]{2,1,0:T(8,128)(2,1)}), bf16[16,24,512]{2,1,0:T(8,128)(2,1)S(1)}, u32[]{:S(2)}, u32[]{:S(2)}) async-start(bf16[16,24,512]{2,1,0:T(8,128)(2,1)} %bitcast.15), calls=%async_computation.4 | async-start | bytes 786432 | tf_op jit(solution)/shard_map/all_to_all | solution.py:397
  146.1 27.5 %copy-start = (bf16[16,24,512]{2,1,0:T(8,128)(2,1)}, bf16[16,24,512]{2,1,0:T(8,128)(2,1)S(1)}, u32[]{:S(2)}) copy-start(bf16[16,24,512]{2,1,0:T(8,128)(2,1)S(1)} %all-to-all-done.4.summed_ref) | copy-start | bytes 1179652
  158.1 15.5 %all-to-all-start.3 = ((bf16[16,24,512]{2,1,0:T(8,128)(2,1)}), bf16[16,24,512]{2,1,0:T(8,128)(2,1)S(1)}, u32[]{:S(2)}, u32[]{:S(2)}) async-start(bf16[16,24,512]{2,1,0:T(8,128)(2,1)} %bitcast.14), calls=%async_computation.3 | async-start | bytes 786432 | tf_op jit(solution)/shard_map/all_to_all | solution.py:397
  162.0 31.9 %collective-permute-start.3 = (f32[48,896]{1,0:T(8,128)S(1)}, f32[48,896]{1,0:T(8,128)S(1)}, u32[]{:S(2)}, u32[]{:S(2)}) collective-permute-start(f32[48,896]{1,0:T(8,128)S(1)} %convert_reduce_fusion), channel_id=1, source_target_pairs={{0,16},{16,0},{1,17},{17,1},{2,18},{18,2},{3,19},{19,3},{4,20},{20... | collective-permute-start | bytes 516104 | tf_op jit(solution)/shard_map/ppermute | solution.py:396
  173.6 0.8 copy-start.1
  189.8 1.5 collective-permute-start.1
  191.2 0.6 copy-start.5
Sparse Core Ops, SparseCore 0:
  28.0 32.0 all-gather.1

commit v2 on v1

--- a/solution.py
+++ b/solution.py
@@ -83,13 +83,16 @@
 
 
 def down_kernel(heights, widths, cot_ref, scale_ref, out_ref):
-    image = pl.program_id(0)
-    channels = cot_ref.shape[0]
-    inside = image_mask(channels, heights[image], widths[image])
-    value = jnp.where(inside, cot_ref[...].astype(F32), 0.0) * column(scale_ref[...])
+    channels, cells = cot_ref.shape
     wide = out_ref.shape[2]
-    for j in range(out_ref.shape[0]):
-        out_ref[j] = value[:, j * wide : (j + 1) * wide].astype(BF16)
+    parts = CELLS // wide
+    scale = column(scale_ref[...])
+    for image in range(cells // CELLS):
+        inside = image_mask(1, heights[image], widths[image])
+        value = cot_ref[:, image * CELLS : (image + 1) * CELLS].astype(F32)
+        value = (value * jnp.where(inside, scale, 0.0)).astype(BF16)
+        for j in range(parts):
+            out_ref[image * parts + j] = value[:, j * wide : (j + 1) * wide]
 
 
 def forward_kernel(
@@ -144,7 +147,7 @@
 
 
 def backward_kernel(
-    heights, widths, feat_ref, cot_ref, mgrad_ref, summed_ref, rows_in, scale_ref, bias_ref,
+    heights, widths, feat_ref, cot_ref, both_ref, rows_in, scale_ref, bias_ref,
     result_ref, gfeat_ref, small_ref, taps_v, taps_h, sums_v, sums_h, held, back, turn,
 ):
     image = pl.program_id(0)
@@ -167,9 +170,8 @@
     values = feat_ref[...].astype(F32)
     masked = jnp.where(inside, values, 0.0)
     held[...] = masked
-    wide = mgrad_ref.shape[2]
-    parts = mgrad_ref.shape[0]
-    grad = jnp.concatenate([mgrad_ref[j].astype(F32) for j in range(parts)], axis=1)
+    parts = both_ref.shape[0]
+    grad = jnp.concatenate([both_ref[j, 0].astype(F32) for j in range(parts)], axis=1)
     grad = jnp.where(inside, grad, 0.0)
     back[...] = grad
 
@@ -211,7 +213,7 @@
     cot = cot_ref[...].astype(F32)
     gfeat_ref[...] = cot + jnp.where(inside, turn[...], 0.0)
 
-    shifted = jnp.concatenate([summed_ref[j].astype(F32) for j in range(parts)], axis=1)
+    shifted = jnp.concatenate([both_ref[j, 1].astype(F32) for j in range(parts)], axis=1)
     shifted = shifted + column(bias_ref[...])
     result = values + jnp.where(inside, column(scale_ref[...]) * shifted, 0.0)
     result_ref[...] = result.astype(BF16)
@@ -262,7 +264,7 @@
 
 
 def pack_kernel(half, in_ref, out_ref, bias_ref, gain_ref, shift_ref, pack_ref):
-    copies, deep, wide = pack_ref.shape
+    deep = pack_ref.shape[0]
     own, count = out_ref.shape
     channels = gain_ref.shape[1]
     keep = own // 2
@@ -270,7 +272,7 @@
     col = lax.broadcasted_iota(jnp.int32, (deep, own), 1)
     pick = jnp.where((col == row + half[0] * keep) & (row < keep), 1.0, 0.0).astype(BF16)
     nt = (((1,), (1,)), ((), ()))
-    first = lax.dot_general(pick, in_ref[...], nt, preferred_element_type=F32)
+    first = jnp.dot(pick, in_ref[...], preferred_element_type=F32)
     second = jnp.dot(pick, out_ref[...], preferred_element_type=F32)
     bias = jnp.broadcast_to(bias_ref[...], (LANES, own))
     third = lax.dot_general(pick, bias, nt, preferred_element_type=F32)
@@ -283,84 +285,124 @@
     shift = lax.dot_general(pick, shift, nt, preferred_element_type=F32)
     lane = lane_of(deep)
     third = jnp.where(lane == 0, third, jnp.where(lane == 1, gain, jnp.where(lane == 2, shift, 0.0)))
-    for j in range(copies):
-        pack_ref[j, :, :count] = first.astype(BF16)
-        pack_ref[j, :, count : 2 * count] = second.astype(BF16)
-        pack_ref[j, :, 2 * count :] = third.astype(BF16)
+    pack_ref[:, :count] = first.astype(BF16)
+    pack_ref[:, count : 2 * count] = second.astype(BF16)
+    pack_ref[:, 2 * count :] = third.astype(BF16)
 
 
 ROOT = math.sqrt(2.0 / math.pi)
 
 
-def mlp_kernel(
-    mixed_ref, down_ref, gain_ref, shift_ref, own_ref, other_ref,
-    summed_ref, mgrad_ref, gown_ref, gother_ref, gnorm_ref,
-    active, mean_ref, inv_ref, sum_acc, grad_acc,
-):
-    step = pl.program_id(0)
-    last = pl.num_programs(0) - 1
-    count = mixed_ref.shape[0]
-    block = own_ref.shape[0]
-
-    @pl.when(step == 0)
-    def _():
-        value = mixed_ref[...].astype(F32)
-        mean = jnp.mean(value, axis=0, keepdims=True)
-        value = value - mean
-        inv = lax.rsqrt(jnp.mean(value * value, axis=0, keepdims=True) + EPS)
-        mean_ref[...] = mean
-        inv_ref[...] = inv
-        active[...] = (value * inv * gain_ref[...] + shift_ref[...]).astype(BF16)
-        sum_acc[...] = jnp.zeros_like(sum_acc)
-        grad_acc[...] = jnp.zeros_like(grad_acc)
+def place_of(quad, near, deep, z, xy, far_at, near_at):
+    apart = far_at ^ z
+    turn = ((apart & 1) << 1) | (apart >> 1)
+    side = near_at ^ xy
+    if not quad:
+        return (near_at * 4 + turn) * deep
+    swapped = ((side & 1) << 1) | (side >> 1)
+    first = side * 2 + turn
+    second = 8 + swapped * 2 + turn - 2
+    return jnp.where(turn < 2, first, second) * deep
+
+
+def mlp_kernel(quad, near, pieces, where_ref, mixed_ref, down_ref, *refs):
+    own_in, refs = refs[:pieces], refs[pieces:]
+    other_in, refs = refs[:pieces], refs[pieces:]
+    both_ref, refs = refs[0], refs[1:]
+    own_out, refs = refs[:pieces], refs[pieces:]
+    gother_ref, weights, grads, active, normal, gains, sum_acc, grad_acc, sems = refs
+    count, tokens = mixed_ref.shape
+    devices, _, channels, _ = both_ref.shape
+    rows = weights.shape[0] // 2
+    tall = rows // pieces
+    deep = rows // devices
+    blocks = 4
+    block = 2 * rows // blocks
+    loads = []
+    for index, ref in enumerate(own_in + other_in):
+        span = weights.at[pl.ds(index * tall, tall), :]
+        loads.append(pltpu.make_async_copy(ref, span, sems.at[index]))
+    for copy in loads:
+        copy.start()
+
+    value = mixed_ref[...].astype(F32)
+    mean = jnp.mean(value, axis=0, keepdims=True)
+    value = value - mean
+    inv = lax.rsqrt(jnp.mean(value * value, axis=0, keepdims=True) + EPS)
+    normal[...] = value * inv
+    sum_acc[...] = jnp.zeros_like(sum_acc)
+    grad_acc[...] = jnp.zeros_like(grad_acc)
+    for copy in loads:
+        copy.wait()
+    z, xy = where_ref[0], where_ref[1]
+    spots = []
+    for d in range(devices):
+        spot = pl.multiple_of(place_of(quad, near, deep, z, xy, d // near, d % near), deep)
+        spots.append(spot)
+        tile = weights[pl.ds(spot, deep), 2 * count :].astype(F32)
+        gains[d * channels : (d + 1) * channels] = tile[:channels]
+    gain = gains[:, 1:2]
+    active[...] = (normal[...] * gain + gains[:, 2:3]).astype(BF16)
 
     nt = (((1,), (1,)), ((), ()))
     tn = (((0,), (0,)), ((), ()))
 
-    def process(ref):
-        w_in = ref[:, :count]
-        w_out = ref[:, count : 2 * count]
+    def process(step, carry):
+        at = pl.ds(pl.multiple_of(step * block, block), block)
+        w_in = weights[at, :count]
+        w_out = weights[at, count : 2 * count]
+        bias = weights[at, 2 * count :].astype(F32)[:, 0:1]
         act = active[...]
         down = down_ref[...]
-        v = jnp.dot(w_in, act, preferred_element_type=F32)
-        v = v + ref[:, 2 * count : 2 * count + 1].astype(F32)
+        v = jnp.dot(w_in, act, preferred_element_type=F32) + bias
         square = v * v
-        bend = jnp.tanh(ROOT * v * (1.0 + 0.044715 * square))
-        half = 0.5 * (1.0 + bend)
-        hidden = (v * half).astype(BF16)
-        slope = half + 0.5 * v * (1.0 - bend * bend) * (ROOT * (1.0 + 3.0 * 0.044715 * square))
+        half = 0.5 * jnp.tanh(v * (ROOT * 0.044715 * square + ROOT)) + 0.5
+        full = v * half
+        hidden = full.astype(BF16)
+        slope = half + full * (1.0 - half) * (6.0 * ROOT * 0.044715 * square + 2.0 * ROOT)
         sum_acc[...] += lax.dot_general(w_out, hidden, tn, preferred_element_type=F32)
         hgrad = jnp.dot(w_out, down, preferred_element_type=F32)
-        bgrad = hgrad * slope
-        low = bgrad.astype(BF16)
+        low = (hgrad * slope).astype(BF16)
         grad_acc[...] += lax.dot_general(w_in, low, tn, preferred_element_type=F32)
         g_in = lax.dot_general(low, act, nt, preferred_element_type=F32)
         g_out = lax.dot_general(hidden, down, nt, preferred_element_type=F32)
         g_bias = jnp.sum(low.astype(F32), axis=1, keepdims=True)
-        return g_in, g_out, jnp.where(lane_of(block) == 0, g_bias, 0.0)
-
-    g_in, g_out, g_ext = process(other_ref)
-    gother_ref[:, :count] = g_in.astype(BF16)
-    gother_ref[:, count : 2 * count] = g_out.astype(BF16)
-    gother_ref[:, 2 * count :] = g_ext.astype(BF16)
-    g_in, g_out, g_ext = process(own_ref)
-    gown_ref[:, :count] = g_in
-    gown_ref[:, count : 2 * count] = g_out
-    gown_ref[:, 2 * count :] = g_ext
-
-    @pl.when(step == last)
-    def _():
-        summed_ref[...] = sum_acc[...].astype(BF16)
-        agrad = grad_acc[...]
-        inv = inv_ref[...]
-        normal = (mixed_ref[...].astype(F32) - mean_ref[...]) * inv
-        scaled = agrad * gain_ref[...]
-        first = jnp.mean(scaled, axis=0, keepdims=True)
-        second = jnp.mean(scaled * normal, axis=0, keepdims=True)
-        mgrad_ref[...] = ((scaled - first - normal * second) * inv).astype(BF16)
-        lane = lane_of(count)
-        ext = jnp.where(lane == 1, jnp.sum(agrad * normal, axis=1, keepdims=True), 0.0)
-        gnorm_ref[...] = jnp.where(lane == 2, jnp.sum(agrad, axis=1, keepdims=True), ext)
+        grads[at, :count] = g_in.astype(BF16)
+        grads[at, count : 2 * count] = g_out.astype(BF16)
+        g_bias = jnp.where(lane_of(block) == 0, g_bias, 0.0)
+        grads[at, 2 * count :] = g_bias.astype(BF16)
+        return carry
+
+    lax.fori_loop(0, blocks, process, 0)
+    stores = [pltpu.make_async_copy(grads.at[pl.ds(rows, rows), :], gother_ref, sems.at[0])]
+    stores[0].start()
+
+    agrad = grad_acc[...]
+    norm = normal[...]
+    scaled = agrad * gains[:, 1:2]
+    first = jnp.mean(scaled, axis=0, keepdims=True)
+    second = jnp.mean(scaled * norm, axis=0, keepdims=True)
+    mgrad = (scaled - first - norm * second) * inv
+    summed = sum_acc[...]
+    for d in range(devices):
+        both_ref[d, 0] = mgrad[d * channels : (d + 1) * channels].astype(BF16)
+        both_ref[d, 1] = summed[d * channels : (d + 1) * channels].astype(BF16)
+    lane = lane_of(count)
+    ext = jnp.where(lane == 1, jnp.sum(agrad * norm, axis=1, keepdims=True), 0.0)
+    ext = jnp.where(lane == 2, jnp.sum(agrad, axis=1, keepdims=True), ext)
+    for d in range(devices):
+        at = pl.ds(spots[d], deep)
+        part = ext[d * channels : (d + 1) * channels]
+        if channels < deep:
+            part = jnp.concatenate([part, jnp.zeros((deep - channels, LANES), F32)], axis=0)
+        grads[at, 2 * count :] = (grads[at, 2 * count :].astype(F32) + part).astype(BF16)
+    for index, ref in enumerate(own_out):
+        span = grads.at[pl.ds(index * tall, tall), :]
+        copy = pltpu.make_async_copy(span, ref, sems.at[index + 1])
+        copy.start()
+        stores.append(copy)
+    for copy in stores:
+        copy.wait()
 
 
 def whole(shape):
@@ -369,6 +411,10 @@
 
 def params(**extra):
     return pltpu.CompilerParams(vmem_limit_bytes=VMEM_LIMIT, **extra)
+
+
+def cost(micros):
+    return pl.CostEstimate(flops=0, transcendentals=0, bytes_accessed=micros * 3_000_000)
 
 
 SMEM = pl.BlockSpec(memory_space=pltpu.SMEM)
@@ -386,47 +432,46 @@
     images = cells // CELLS
     tokens = cells // ch
     parts = CELLS // tokens
-    far = 4 if ch % 4 == 0 else 1
+    far = 4
     near = ch // far
     deep = -(-(units // 2) // 16) * 16
     width = 2 * count + LANES
+    quad = near == 4
     near_groups = [[f * near + i for i in range(near)] for f in range(far)]
-    far_groups = [[f * near + i for f in range(far)] for i in range(near)]
     row = lambda v: v.reshape(1, -1)
     exchange = lambda v: lax.ppermute(v, "img", [(0, 1), (1, 0)])
+    flip = lambda v, bits: lax.ppermute(v, "ch", [(i, i ^ bits) for i in range(ch)])
     swap = lambda v, groups=None: lax.all_to_all(
         v, "ch", split_axis=0, concat_axis=0, tiled=True, axis_index_groups=groups
     )
     half = lax.axis_index("img").astype(jnp.int32)
-
+    place = lax.axis_index("ch").astype(jnp.int32)
     full = pl.BlockSpec(memory_space=pltpu.VMEM)
+    raw = pl.BlockSpec(memory_space=pl.ANY)
+
     pack = pl.pallas_call(
         pack_kernel,
-        out_shape=jax.ShapeDtypeStruct((far, deep, width), BF16),
+        out_shape=jax.ShapeDtypeStruct((deep, width), BF16),
         in_specs=[SMEM] + [full] * 5,
         out_specs=full,
         compiler_params=params(),
+        cost_estimate=cost(2),
         name="pack",
-    )(half.reshape(1), in_weight, out_weight, row(in_bias), row(norm_gain), row(norm_shift))
-    pack = swap(pack, far_groups)
-    pack = lax.all_gather(
-        pack.reshape(far * deep, width), "ch", axis=0, tiled=True, axis_index_groups=near_groups
-    )
-    other = exchange(pack)
-    vectors = pack.reshape(near, far, deep, width)[:, :, :channels, 2 * count + 1 : 2 * count + 3]
-    vectors = vectors.transpose(1, 0, 2, 3).reshape(count, 2).astype(F32)
+    )(half.reshape(1), in_weight.T, out_weight, row(in_bias), row(norm_gain), row(norm_shift))
+    even = jnp.concatenate([pack, flip(pack, 2 * near)], axis=0)
+    odd = flip(even, near)
 
     cells_spec = pl.BlockSpec((channels, CELLS), lambda i: (0, i))
-    token_spec = pl.BlockSpec((parts, channels, tokens), lambda i: (i, 0, 0))
     down = pl.pallas_call(
         down_kernel,
-        grid=(images,),
         out_shape=jax.ShapeDtypeStruct((ch, channels, tokens), BF16),
-        in_specs=[SMEM, SMEM, cells_spec, whole((1, channels))],
-        out_specs=token_spec,
+        in_specs=[SMEM, SMEM, full, full],
+        out_specs=full,
         compiler_params=params(),
+        cost_estimate=cost(2),
         name="down",
     )(heights, widths, cotangent, row(layer_scale))
+    features_after, down = lax.optimization_barrier((features, down))
     down = swap(down).reshape(count, tokens)
 
     state = whole((channels, states))
@@ -441,55 +486,95 @@
             jax.ShapeDtypeStruct((channels, LANES), F32),
         ),
         in_specs=[SMEM, SMEM, cells_spec, vector, vector, state, state, state, state, vector],
-        out_specs=(token_spec, whole((channels, LANES))),
+        out_specs=(
+            pl.BlockSpec((parts, channels, tokens), lambda i: (i, 0, 0)),
+            whole((channels, LANES)),
+        ),
         scratch_shapes=[tap, tap, plane, plane],
         compiler_params=params(),
+        cost_estimate=cost(12),
         name="mixer_forward",
     )(
-        heights, widths, features, row(step_height), row(step_width), rate_height, rate_width,
-        readout_height, readout_width, row(skip_gain),
+        heights, widths, features_after, row(step_height), row(step_width), rate_height,
+        rate_width, readout_height, readout_width, row(skip_gain),
     )
+    if quad:
+        even = jnp.concatenate([even, flip(even, 1)], axis=0)
+        odd = jnp.concatenate([odd, flip(odd, 2)], axis=0)
+        even, odd, mixed = lax.optimization_barrier((even, odd, mixed))
+        own = [even, flip(even, 2), odd, flip(odd, 1)]
+    else:
+        both = jnp.concatenate([even, odd], axis=0)
+        both = jnp.broadcast_to(both[None], (near, far * deep, width))
+        own = [swap(both, near_groups).reshape(ch * deep, width)]
     mixed = swap(mixed).reshape(count, tokens)
+    other = [exchange(piece) for piece in own]
 
     rows = ch * deep
-    blocks = 2
-    span = rows // blocks
-    token_full = whole((count, tokens))
-    weight_spec = pl.BlockSpec((span, width), lambda i: (i, 0))
-    summed, mgrad, gown, gother, gnorm = pl.pallas_call(
-        mlp_kernel,
-        grid=(blocks,),
-        out_shape=(
-            jax.ShapeDtypeStruct((count, tokens), BF16),
-            jax.ShapeDtypeStruct((count, tokens), BF16),
-            jax.ShapeDtypeStruct((rows, width), F32),
-            jax.ShapeDtypeStruct((rows, width), BF16),
-            jax.ShapeDtypeStruct((count, LANES), F32),
-        ),
-        in_specs=[token_full, token_full, whole((count, 1)), whole((count, 1)), weight_spec, weight_spec],
-        out_specs=(token_full, token_full, weight_spec, weight_spec, whole((count, LANES))),
+    pieces = len(own)
+    both_shape = (ch, 2, channels, tokens)
+    piece_shape = jax.ShapeDtypeStruct((rows // pieces, width), BF16)
+    outs = pl.pallas_call(
+        partial(mlp_kernel, quad, near, pieces),
+        out_shape=[jax.ShapeDtypeStruct(both_shape, BF16)]
+        + [piece_shape] * pieces
+        + [jax.ShapeDtypeStruct((rows, width), BF16)],
+        in_specs=[SMEM, full, full] + [raw] * (2 * pieces),
+        out_specs=[full] + [raw] * (pieces + 1),
         scratch_shapes=[
+            pltpu.VMEM((2 * rows, width), BF16),
+            pltpu.VMEM((2 * rows, width), BF16),
             pltpu.VMEM((count, tokens), BF16),
-            pltpu.VMEM((1, tokens), F32),
-            pltpu.VMEM((1, tokens), F32),
+            pltpu.VMEM((count, tokens), F32),
+            pltpu.VMEM((count, LANES), F32),
             pltpu.VMEM((count, tokens), F32),
             pltpu.VMEM((count, tokens), F32),
+            pltpu.SemaphoreType.DMA((2 * pieces,)),
         ],
         compiler_params=params(),
+        cost_estimate=cost(10),
         name="mlp",
-    )(mixed, down, vectors[:, 0:1], vectors[:, 1:2], pack, other)
-
-    arrived = exchange(gother)
-    mgrad = swap(mgrad.reshape(ch, channels, tokens))
-    summed = swap(summed.reshape(ch, channels, tokens))
-
-    gnorm = gnorm.reshape(far, near, channels, LANES).transpose(1, 0, 2, 3)
-    gnorm = jnp.pad(gnorm, ((0, 0), (0, 0), (0, deep - channels), (2 * count, 0)))
-    partial_sum = (gown + arrived.astype(F32)).reshape(near, far, deep, width) + gnorm
-    partial_sum = swap(partial_sum.astype(BF16), near_groups)
-    partial_sum = jnp.sum(partial_sum.astype(F32), axis=0)
-    partial_sum = swap(partial_sum.astype(BF16), far_groups)
-    partial_sum = jnp.sum(partial_sum.astype(F32), axis=0)
+    )(jnp.stack([place // near, place % near]), mixed, down, *own, *other)
+    both, gown, gother = outs[0], outs[1:-1], outs[-1]
+
+    arrived = exchange(gother).astype(F32)
+    both = swap(both)
+    if quad:
+        tall = rows // 4
+        part = [gown[i].astype(F32) + arrived[i * tall : (i + 1) * tall] for i in range(4)]
+        even = part[0] + flip(part[1].astype(BF16), 2).astype(F32)
+        odd = part[2] + flip(part[3].astype(BF16), 1).astype(F32)
+        cut = tall // 2
+        even = even[:cut] + flip(even[cut:].astype(BF16), 1).astype(F32)
+        odd = odd[:cut] + flip(odd[cut:].astype(BF16), 2).astype(F32)
+    else:
+        total = (gown[0].astype(F32) + arrived).astype(BF16).reshape(near, far * deep, width)
+        total = jnp.sum(swap(total, near_groups).astype(F32), axis=0)
+        even, odd = total[: 2 * deep], total[2 * deep :]
+    even = even + flip(odd.astype(BF16), near).astype(F32)
+
+    result, grad_features, small = pl.pallas_call(
+        backward_kernel,
+        grid=(images,),
+        out_shape=(
+            jax.ShapeDtypeStruct((channels, cells), BF16),
+            jax.ShapeDtypeStruct((channels, cells), F32),
+            jax.ShapeDtypeStruct((channels, LANES), F32),
+        ),
+        in_specs=[
+            SMEM, SMEM, cells_spec, cells_spec,
+            pl.BlockSpec((parts, 2, channels, tokens), lambda i: (i, 0, 0, 0)),
+            whole((channels, LANES)), vector, vector,
+        ],
+        out_specs=(cells_spec, cells_spec, whole((channels, LANES))),
+        scratch_shapes=[tap, tap, tap, tap, plane, plane, plane],
+        compiler_params=params(),
+        cost_estimate=cost(15),
+        name="mixer_backward",
+    )(heights, widths, features, cotangent, both, taps, row(layer_scale), row(out_bias))
+
+    even, small = lax.optimization_barrier((even, small))
+    partial_sum = even[:deep] + flip(even[deep:].astype(BF16), 2 * near).astype(F32)
     sibling = exchange(partial_sum)
     keep = units // 2
     low = jnp.where(half == 0, partial_sum, sibling)[:keep]
@@ -499,24 +584,6 @@
     grad_out_weight = grads[:, count : 2 * count]
     grad_in_bias = grads[:, 2 * count]
     norms = (partial_sum + sibling)[:channels, 2 * count + 1 : 2 * count + 3]
-
-    result, grad_features, small = pl.pallas_call(
-        backward_kernel,
-        grid=(images,),
-        out_shape=(
-            jax.ShapeDtypeStruct((channels, cells), BF16),
-            jax.ShapeDtypeStruct((channels, cells), F32),
-            jax.ShapeDtypeStruct((channels, LANES), F32),
-        ),
-        in_specs=[
-            SMEM, SMEM, cells_spec, cells_spec, token_spec, token_spec, whole((channels, LANES)),
-            vector, vector,
-        ],
-        out_specs=(cells_spec, cells_spec, whole((channels, LANES))),
-        scratch_shapes=[tap, tap, tap, tap, plane, plane, plane],
-        compiler_params=params(),
-        name="mixer_backward",
-    )(heights, widths, features, cotangent, mgrad, summed, taps, row(layer_scale), row(out_bias))
 
     vector_out = jax.ShapeDtypeStruct((1, channels), F32)
     state_out = jax.ShapeDtypeStruct((channels, states), F32)
@@ -529,6 +596,7 @@
         in_specs=[full] * 9,
         out_specs=(full,) * 9,
         compiler_params=params(),
+        cost_estimate=cost(2),
         name="mixer_chain",
     )(
         small, exchange(small), row(step_height), row(step_width), rate_height, rate_width,

time: 204 us -> 146 us (0.72)
  blocking collectives: 49.9 us -> 0 us
  starting transfers between devices: 18 us -> 38 us
  between operations: 14.2 us -> 0.95 us
  waiting for transfers between devices: 60.9 us -> 48.1 us
  other arithmetic: 5.02 us -> 8.1 us
  local copies, waits for them, and re-layouts: 6.68 us -> 3.89 us
    all_to_all x3 -> x0, blocking collectives: 49.9 us -> none  [per_device(): lax.all_to_all(v, 'ch', split_axis=0, concat_axis=0, tiled=True, axis_ind...]
    ppermute x0 -> x12, waiting for transfers between devices: none -> 42.7 us  [per_device(): lax.ppermute(v, 'ch', [(i, i ^ bits) for i in range(ch)])]
    all_to_all x4 -> x3, waiting for transfers between devices: 34.6 us -> 0.01 us  [per_device(): lax.all_to_all(v, 'ch', split_axis=0, concat_axis=0, tiled=True, axis_ind...]
    all_gather x1 -> x0, waiting for transfers between devices: 22.5 us -> none  [per_device(): lax.all_gather(pack.reshape(far * deep, width), 'ch', axis=0, tiled=True,...]
    ppermute x0 -> x12, starting transfers between devices: none -> 19.1 us  [per_device(): lax.ppermute(v, 'ch', [(i, i ^ bits) for i in range(ch)])]
    ppermute x4 -> x7, waiting for transfers between devices: 3.76 us -> 5.35 us  [per_device(): exchange = lambda v: lax.ppermute(v, 'img', [(0, 1), (1, 0)])]
    unnamed x13 -> x30, local copies, waits for them, and re-layouts: 4.22 us -> 3.14 us
    all_to_all x4 -> x3, starting transfers between devices: 17.8 us -> 17.6 us  [per_device(): lax.all_to_all(v, 'ch', split_axis=0, concat_axis=0, tiled=True, axis_ind...]
  transfers between devices with their start and end apart: 9 -> 22, of which waited for: 6 -> 12; matrix products, arithmetic and copies ran while one was open for 2% -> 3% of each run, Pallas kernels for 17% -> 22%
where the time goes in v2:
time: 146 us
  waiting for transfers between devices  48.1 us (33%)
  Pallas kernels  46.6 us (32%)
  starting transfers between devices  38 us (26%)
  other arithmetic  8.1 us (6%)
  local copies, waits for them, and re-layouts  3.89 us (3%)
    ppermute x12, waiting for transfers between devices, per_device(): lax.ppermute(v, 'ch', [(i, i ^ bits) for i in range(ch)])  42.7 us
    ppermute x12, starting transfers between devices, per_device(): lax.ppermute(v, 'ch', [(i, i ^ bits) for i in range(ch)])  19.1 us
    all_to_all x3, starting transfers between devices, per_device(): lax.all_to_all(v, 'ch', split_axis=0, concat_axis=0, tiled=True, axis_ind...  17.6 us
    pallas_call x1, Pallas kernels, per_device(): pl.pallas_call(backward_kernel, grid=(images,), out_shape=(jax.ShapeDtype...  15.5 us
    pallas_call x1, Pallas kernels, per_device(): pl.pallas_call(partial(mlp_kernel, quad, near, pieces), out_shape=[jax.Sh...  12.8 us
    pallas_call x1, Pallas kernels, per_device(): pl.pallas_call(forward_kernel, grid=(images,), out_shape=(jax.ShapeDtypeS...  12.6 us
    ppermute x7, waiting for transfers between devices, per_device(): exchange = lambda v: lax.ppermute(v, 'img', [(0, 1), (1, 0)])  5.35 us
    unnamed x30, local copies, waits for them, and re-layouts  3.14 us
  transfers between devices with their start and end apart: 22, of which 12 were waited for; matrix products, arithmetic and copies ran while one was open for 3% of the time, Pallas kernels for 22%

profile of v2, /device:TPU:0, one launch (start us, length us, event | category | flops | bytes accessed | tf_op | source)
XLA Modules:
  0.0 145.7 jit_solution(13532659713635536968)
XLA Ops:
  0.6 1.9 %down.1 = bf16[16,24,512]{2,1,0:T(8,128)(2,1)} custom-call(s32[8]{0:T(128)} %heights.5, s32[8]{0:T(128)} %widths.5, bf16[24,8192]{1,0:T(8,128)(2,1)} %cot_ref.3, f32[1,24]{1,0:T(1,128)} %bitcast.24), custom_call_target="tpu_custom_call" | custom-call | bytes 6000000 | tf_op jit(solution)/shard_map/down/pallas_call | solution.py:465
  2.6 8.3 %all-to-all-start.1 = ((bf16[16,24,512]{2,1,0:T(8,128)(2,1)}), bf16[16,24,512]{2,1,0:T(8,128)(2,1)S(1)}, u32[]{:S(2)}, u32[]{:S(2)}) async-start(bf16[16,24,512]{2,1,0:T(8,128)(2,1)} %down.1), calls=%async_computation.1 | async-start | bytes 786432 | tf_op jit(solution)/shard_map/all_to_all | solution.py:444
  10.9 1.8 %pack.1 = bf16[48,896]{1,0:T(8,128)(2,1)} custom-call(s32[1]{0:T(128)} %bitcast.2.half, bf16[96,384]{1,0:T(8,128)(2,1)} %bitcast.23, bf16[96,384]{1,0:T(8,128)(2,1)} %out_ref.1, bf16[1,96]{1,0:T(2,128)(2,1)} %bitcast.31, bf16[1,24]{1,0:T(2,128)(2,1)} %bitcast.32, bf16[1,24]{1,0:T(2,128)(2,1)} %bitcast.33), custom_call_target="tpu_custom_call" | custom-call | bytes 6000000 | tf_op jit(solution)/shard_map/pack/pallas_call | solution.py:452
  12.7 2.8 %collective-permute-start = (bf16[48,896]{1,0:T(8,128)(2,1)}, bf16[48,896]{1,0:T(8,128)(2,1)S(1)}, u32[]{:S(2)}, u32[]{:S(2)}) collective-permute-start(bf16[48,896]{1,0:T(8,128)(2,1)} %pack.1), channel_id=1, source_target_pairs={{0,8},{1,9},{2,10},{3,11},{4,12},{5,13},{6,14},{7,15},{8,0},{9,1},... | collective-permute-start | bytes 258056 | tf_op jit(solution)/shard_map/ppermute | solution.py:443
  15.5 10.7 %collective-permute-done = bf16[48,896]{1,0:T(8,128)(2,1)S(1)} collective-permute-done((bf16[48,896]{1,0:T(8,128)(2,1)}, bf16[48,896]{1,0:T(8,128)(2,1)S(1)}, u32[]{:S(2)}, u32[]{:S(2)}) %collective-permute-start) | collective-permute-done | bytes 86048 | tf_op jit(solution)/shard_map/ppermute | solution.py:443
  26.2 0.9 pad_maximum_fusion.2
  27.1 0.1 collective-permute-start.2
  27.2 1.5 %collective-permute-start.1 = (bf16[96,896]{1,0:T(8,128)(2,1)S(1)}, bf16[96,896]{1,0:T(8,128)(2,1)S(1)}, u32[]{:S(2)}, u32[]{:S(2)}) collective-permute-start(bf16[96,896]{1,0:T(8,128)(2,1)S(1)} %pad_maximum_fusion.2), channel_id=1, source_target_pairs={{0,1},{1,0},{2,3},{3,2},{4,5},{5,4},{6,7},{7,6},{8,9},{9,8},{10,11... | collective-permute-start | bytes 516104 | tf_op jit(solution)/shard_map/ppermute | solution.py:443
  28.7 3.9 %collective-permute-done.2 = bf16[96,896]{1,0:T(8,128)(2,1)S(1)} collective-permute-done((bf16[96,896]{1,0:T(8,128)(2,1)S(1)}, bf16[96,896]{1,0:T(8,128)(2,1)S(1)}, u32[]{:S(2)}, u32[]{:S(2)}) %collective-permute-start.2) | collective-permute-done | bytes 172064 | tf_op jit(solution)/shard_map/ppermute | solution.py:443
  32.6 1.5 %collective-permute-start.3 = (bf16[96,896]{1,0:T(8,128)(2,1)S(1)}, bf16[96,896]{1,0:T(8,128)(2,1)S(1)}, u32[]{:S(2)}, u32[]{:S(2)}) collective-permute-start(bf16[96,896]{1,0:T(8,128)(2,1)S(1)} %collective-permute-done.2), channel_id=1, source_target_pairs={{0,2},{1,3},{2,0},{3,1},{4,6},{5,7},{6,4},{7,5},{8,10},{9,11},{10,... | collective-permute-start | bytes 516104 | tf_op jit(solution)/shard_map/ppermute | solution.py:443
  34.1 12.6 %mixer_forward.1 = (bf16[16,24,512]{2,1,0:T(8,128)(2,1)}, f32[24,128]{1,0:T(8,128)}) custom-call(s32[8]{0:T(128)} %heights.5, s32[8]{0:T(128)} %widths.5, bf16[24,8192]{1,0:T(8,128)(2,1)} %feat_ref.2, f32[1,24]{1,0:T(1,128)} %bitcast.27, f32[1,24]{1,0:T(1,128)} %bitcast.29, f32[24,64]{1,0:T(8,128)} %rate_h.3, f32[24,64]{1,0:T(8,128)} %rate_w.3, ...), custom_call_target="tpu_custom_call" | custom-call | bytes 36000000 | tf_op jit(solution)/shard_map/mixer_forward/pallas_call | solution.py:481
  46.6 0.9 pad_maximum_fusion.refs_0_
  47.6 0.0 all-to-all-done.1
  47.6 4.3 %all-to-all-start = ((bf16[16,24,512]{2,1,0:T(8,128)(2,1)}), bf16[16,24,512]{2,1,0:T(8,128)(2,1)S(1)}, u32[]{:S(2)}, u32[]{:S(2)}) async-start(bf16[16,24,512]{2,1,0:T(8,128)(2,1)} %get-tuple-element.45), calls=%async_computation | async-start | bytes 786432 | tf_op jit(solution)/shard_map/all_to_all | solution.py:444
  51.9 1.9 %collective-permute-start.4 = (bf16[192,896]{1,0:T(8,128)(2,1)S(1)}, bf16[192,896]{1,0:T(8,128)(2,1)S(1)}, u32[]{:S(2)}, u32[]{:S(2)}) collective-permute-start(bf16[192,896]{1,0:T(8,128)(2,1)S(1)} %pad_maximum_fusion.refs_0_), channel_id=1, source_target_pairs={{0,2},{1,3},{2,0},{3,1},{4,6},{5,7},{6,4},{7,5},{8,10},{9,11},{10,... | collective-permute-start | bytes 1032200 | tf_op jit(solution)/shard_map/ppermute | solution.py:443
  53.8 1.5 %collective-permute-start.5 = (bf16[192,896]{1,0:T(8,128)(2,1)S(1)}, bf16[192,896]{1,0:T(8,128)(2,1)S(1)}, u32[]{:S(2)}, u32[]{:S(2)}) collective-permute-start(bf16[192,896]{1,0:T(8,128)(2,1)S(1)} %pad_maximum_fusion.1.refs_2_), channel_id=1, source_target_pairs={{0,1},{1,0},{2,3},{3,2},{4,5},{5,4},{6,7},{7,6},{8,9},{9,8},{10,11... | collective-permute-start | bytes 1032200 | tf_op jit(solution)/shard_map/ppermute | solution.py:443
  55.3 0.0 collective-permute-start.6
  55.3 0.5 collective-permute-start.8
  55.8 8.6 %collective-permute-done.4.refs_1_ = bf16[192,896]{1,0:T(8,128)(2,1)S(1)} collective-permute-done((bf16[192,896]{1,0:T(8,128)(2,1)S(1)}, bf16[192,896]{1,0:T(8,128)(2,1)S(1)}, u32[]{:S(2)}, u32[]{:S(2)}) %collective-permute-start.4) | collective-permute-done | bytes 344096 | tf_op jit(solution)/shard_map/ppermute | solution.py:443
  64.5 0.0 collective-permute-start.7
  64.5 0.7 collective-permute-done.5.refs_3_
  65.2 0.0 collective-permute-start.9
  65.2 0.6 pad_add_fusion.where_ref
  65.8 0.0 collective-permute-done.6.refs_4_
  65.8 0.0 collective-permute-done.8.refs_6_
  65.8 0.3 collective-permute-done.7.refs_5_
  66.1 0.7 collective-permute-done.9.refs_7_
  66.8 0.0 all-to-all-done
  66.9 0.7 copy-done.12
  67.6 0.1 copy-done.3
  67.7 12.8 %mlp.1 = (bf16[16,2,24,512]{3,2,1,0:T(8,128)(2,1)}, bf16[192,896]{1,0:T(8,128)(2,1)}, bf16[192,896]{1,0:T(8,128)(2,1)}, bf16[192,896]{1,0:T(8,128)(2,1)}, bf16[1...) custom-call(s32[2]{0:T(128)} %pad_add_fusion.where_ref, bf16[384,512]{1,0:T(8,128)(2,1)} %bitcast.22, ...), custom_call_target="tpu_custom_call" | custom-call | bytes 30000000 | tf_op jit(solution)/shard_map/mlp/pallas_call | solution.py:517
  80.5 0.2 collective-permute-start.10
  80.7 3.2 %collective-permute-done.10 = bf16[768,896]{1,0:T(8,128)(2,1)S(1)} collective-permute-done((bf16[768,896]{1,0:T(8,128)(2,1)}, bf16[768,896]{1,0:T(8,128)(2,1)S(1)}, u32[]{:S(2)}, u32[]{:S(2)}) %collective-permute-start.10) | collective-permute-done | bytes 1376288 | tf_op jit(solution)/shard_map/ppermute | solution.py:442
  83.9 0.2 convert_element_type.46
  84.1 0.8 fusion
  84.9 1.2 collective-permute-start.13
  86.2 5.1 %all-to-all-start.2 = ((bf16[16,2,24,512]{3,2,1,0:T(8,128)(2,1)}), bf16[16,2,24,512]{3,2,1,0:T(8,128)(2,1)S(1)}, u32[]{:S(2)}, u32[]{:S(2)}) async-start(bf16[16,2,24,512]{3,2,1,0:T(8,128)(2,1)} %get-tuple-element.49), calls=%async_computation.2 | async-start | bytes 1572864 | tf_op jit(solution)/shard_map/all_to_all | solution.py:444
  91.2 4.9 %collective-permute-done.13 = bf16[192,896]{1,0:T(8,128)(2,1)} collective-permute-done((bf16[192,896]{1,0:T(8,128)(2,1)}, bf16[192,896]{1,0:T(8,128)(2,1)}, u32[]{:S(2)}, u32[]{:S(2)}) %collective-permute-start.13) | collective-permute-done | bytes 344096 | tf_op jit(solution)/shard_map/ppermute | solution.py:443
  96.1 1.3 fusion.1
  97.5 1.0 collective-permute-start.14
  98.5 1.1 collective-permute-start.11
  99.6 7.5 %collective-permute-done.14 = bf16[96,896]{1,0:T(8,128)(2,1)S(1)} collective-permute-done((bf16[96,896]{1,0:T(8,128)(2,1)S(1)}, bf16[96,896]{1,0:T(8,128)(2,1)S(1)}, u32[]{:S(2)}, u32[]{:S(2)}) %collective-permute-start.14) | collective-permute-done | bytes 172064 | tf_op jit(solution)/shard_map/ppermute | solution.py:443
  107.1 0.7 fusion.4
  107.9 2.4 %collective-permute-start.15 = (bf16[96,896]{1,0:T(8,128)(2,1)}, bf16[96,896]{1,0:T(8,128)(2,1)}, u32[]{:S(2)}, u32[]{:S(2)}) collective-permute-start(bf16[96,896]{1,0:T(8,128)(2,1)} %fusion.4), channel_id=1, source_target_pairs={{0,4},{1,5},{2,6},{3,7},{4,0},{5,1},{6,2},{7,3},{8,12},{9,13},{10,... | collective-permute-start | bytes 516104 | tf_op jit(solution)/shard_map/ppermute | solution.py:443
  110.2 3.8 %collective-permute-done.11 = bf16[192,896]{1,0:T(8,128)(2,1)S(1)} collective-permute-done((bf16[192,896]{1,0:T(8,128)(2,1)S(1)}, bf16[192,896]{1,0:T(8,128)(2,1)S(1)}, u32[]{:S(2)}, u32[]{:S(2)}) %collective-permute-start.11) | collective-permute-done | bytes 344096 | tf_op jit(solution)/shard_map/ppermute | solution.py:443
  114.0 0.1 fusion.3
  114.2 0.8 copy-done.1
  115.0 1.3 collective-permute-start.12
  116.3 0.0 all-to-all-done.2.both_ref
  116.3 0.9 copy-done
  117.2 15.5 %mixer_backward.1 = (bf16[24,8192]{1,0:T(8,128)(2,1)}, f32[24,8192]{1,0:T(8,128)}, f32[24,128]{1,0:T(8,128)}) custom-call(s32[8]{0:T(128)} %heights.5, s32[8]{0:T(128)} %widths.5, bf16[24,8192]{1,0:T(8,128)(2,1)} %feat_ref.2, bf16[24,8192]{1,0:T(8,128)(2,1)} %cot_ref.3, bf16[16,2,24,512]{3,2,1,0:T(8,128)(2,1)} %copy-done, ...), custom_call_target="tpu_custom_call" | custom-call | bytes 45000000 | tf_op jit(solution)/shard_map/mixer_backward/pallas_call | solution.py:556
  132.6 0.0 collective-permute-done.15
  132.7 1.1 fusion.5
  133.8 2.9 %collective-permute-start.17 = (bf16[48,896]{1,0:T(8,128)(2,1)S(1)}, bf16[48,896]{1,0:T(8,128)(2,1)S(1)}, u32[]{:S(2)}, u32[]{:S(2)}) collective-permute-start(bf16[48,896]{1,0:T(8,128)(2,1)S(1)} %slice.125), channel_id=1, source_target_pairs={{0,8},{1,9},{2,10},{3,11},{4,12},{5,13},{6,14},{7,15},{8,0},{9,1},... | collective-permute-start | bytes 258056 | tf_op jit(solution)/shard_map/ppermute | solution.py:443
  136.7 2.6 %collective-permute-done.17 = bf16[48,896]{1,0:T(8,128)(2,1)S(1)} collective-permute-done((bf16[48,896]{1,0:T(8,128)(2,1)S(1)}, bf16[48,896]{1,0:T(8,128)(2,1)S(1)}, u32[]{:S(2)}, u32[]{:S(2)}) %collective-permute-start.17) | collective-permute-done | bytes 86048 | tf_op jit(solution)/shard_map/ppermute | solution.py:443
  139.2 0.1 collective-permute-start.18
  139.3 0.5 collective-permute-start.16
  139.8 1.1 collective-permute-done.16.other_ref
  140.9 0.6 copy-done.14
  141.5 2.0 %mixer_chain.1 = (f32[1,24]{1,0:T(1,128)}, f32[24,64]{1,0:T(8,128)}, f32[24,64]{1,0:T(8,128)}, f32[1,24]{1,0:T(1,128)}, f32[24,64]{1,0:T(8,128)}, /*index=5*/f32...) custom-call(f32[24,128]{1,0:T(8,128)} %get-tuple-element.59.own_ref, f32[24,128]{1,0:T(8,128)} %copy-done.14, ...), custom_call_target="tpu_custom_call" | custom-call | bytes 6000000 | tf_op jit(solution)/shard_map/mixer_chain/pallas_call | solution.py:590
  143.6 0.0 collective-permute-done.18
  143.6 0.6 fusion.9
  144.3 0.7 pad_maximum_fusion.3
  145.0 0.7 slice_reduce_fusion
  (34 shorter events, 0.2 us)
Async XLA Ops:
  2.6 45.0 %all-to-all-start.1 = ((bf16[16,24,512]{2,1,0:T(8,128)(2,1)}), bf16[16,24,512]{2,1,0:T(8,128)(2,1)S(1)}, u32[]{:S(2)}, u32[]{:S(2)}) async-start(bf16[16,24,512]{2,1,0:T(8,128)(2,1)} %down.1), calls=%async_computation.1 | async-start | bytes 786432 | tf_op jit(solution)/shard_map/all_to_all | solution.py:444
  12.7 13.5 %collective-permute-start = (bf16[48,896]{1,0:T(8,128)(2,1)}, bf16[48,896]{1,0:T(8,128)(2,1)S(1)}, u32[]{:S(2)}, u32[]{:S(2)}) collective-permute-start(bf16[48,896]{1,0:T(8,128)(2,1)} %pack.1), channel_id=1, source_target_pairs={{0,8},{1,9},{2,10},{3,11},{4,12},{5,13},{6,14},{7,15},{8,0},{9,1},... | collective-permute-start | bytes 258056 | tf_op jit(solution)/shard_map/ppermute | solution.py:443
  27.1 5.5 %collective-permute-start.2 = (bf16[96,896]{1,0:T(8,128)(2,1)S(1)}, bf16[96,896]{1,0:T(8,128)(2,1)S(1)}, u32[]{:S(2)}, u32[]{:S(2)}) collective-permute-start(bf16[96,896]{1,0:T(8,128)(2,1)S(1)} %pad_maximum_fusion.2), channel_id=1, source_target_pairs={{0,4},{1,5},{2,6},{3,7},{4,0},{5,1},{6,2},{7,3},{8,12},{9,13},{10,... | collective-permute-start | bytes 516104 | tf_op jit(solution)/shard_map/ppermute | solution.py:443
  27.2 19.4 %collective-permute-start.1 = (bf16[96,896]{1,0:T(8,128)(2,1)S(1)}, bf16[96,896]{1,0:T(8,128)(2,1)S(1)}, u32[]{:S(2)}, u32[]{:S(2)}) collective-permute-start(bf16[96,896]{1,0:T(8,128)(2,1)S(1)} %pad_maximum_fusion.2), channel_id=1, source_target_pairs={{0,1},{1,0},{2,3},{3,2},{4,5},{5,4},{6,7},{7,6},{8,9},{9,8},{10,11... | collective-permute-start | bytes 516104 | tf_op jit(solution)/shard_map/ppermute | solution.py:443
  32.6 15.0 %collective-permute-start.3 = (bf16[96,896]{1,0:T(8,128)(2,1)S(1)}, bf16[96,896]{1,0:T(8,128)(2,1)S(1)}, u32[]{:S(2)}, u32[]{:S(2)}) collective-permute-start(bf16[96,896]{1,0:T(8,128)(2,1)S(1)} %collective-permute-done.2), channel_id=1, source_target_pairs={{0,2},{1,3},{2,0},{3,1},{4,6},{5,7},{6,4},{7,5},{8,10},{9,11},{10,... | collective-permute-start | bytes 516104 | tf_op jit(solution)/shard_map/ppermute | solution.py:443
  47.6 19.3 %copy-start.4 = (bf16[192,896]{1,0:T(8,128)(2,1)}, bf16[192,896]{1,0:T(8,128)(2,1)S(1)}, u32[]{:S(2)}) copy-start(bf16[192,896]{1,0:T(8,128)(2,1)S(1)} %pad_maximum_fusion.refs_0_) | copy-start | bytes 1032196
  47.6 19.2 %copy-start.5 = (bf16[192,896]{1,0:T(8,128)(2,1)}, bf16[192,896]{1,0:T(8,128)(2,1)S(1)}, u32[]{:S(2)}) copy-start(bf16[192,896]{1,0:T(8,128)(2,1)S(1)} %pad_maximum_fusion.1.refs_2_) | copy-start | bytes 1032196
  47.6 19.2 %copy-start.2 = (bf16[16,24,512]{2,1,0:T(8,128)(2,1)}, bf16[16,24,512]{2,1,0:T(8,128)(2,1)S(1)}, u32[]{:S(2)}) copy-start(bf16[16,24,512]{2,1,0:T(8,128)(2,1)S(1)} %all-to-all-done.1) | copy-start | bytes 1179652
  47.6 19.2 %all-to-all-start = ((bf16[16,24,512]{2,1,0:T(8,128)(2,1)}), bf16[16,24,512]{2,1,0:T(8,128)(2,1)S(1)}, u32[]{:S(2)}, u32[]{:S(2)}) async-start(bf16[16,24,512]{2,1,0:T(8,128)(2,1)} %get-tuple-element.45), calls=%async_computation | async-start | bytes 786432 | tf_op jit(solution)/shard_map/all_to_all | solution.py:444
  51.9 12.5 %collective-permute-start.4 = (bf16[192,896]{1,0:T(8,128)(2,1)S(1)}, bf16[192,896]{1,0:T(8,128)(2,1)S(1)}, u32[]{:S(2)}, u32[]{:S(2)}) collective-permute-start(bf16[192,896]{1,0:T(8,128)(2,1)S(1)} %pad_maximum_fusion.refs_0_), channel_id=1, source_target_pairs={{0,2},{1,3},{2,0},{3,1},{4,6},{5,7},{6,4},{7,5},{8,10},{9,11},{10,... | collective-permute-start | bytes 1032200 | tf_op jit(solution)/shard_map/ppermute | solution.py:443
  53.8 11.3 %collective-permute-start.5 = (bf16[192,896]{1,0:T(8,128)(2,1)S(1)}, bf16[192,896]{1,0:T(8,128)(2,1)S(1)}, u32[]{:S(2)}, u32[]{:S(2)}) collective-permute-start(bf16[192,896]{1,0:T(8,128)(2,1)S(1)} %pad_maximum_fusion.1.refs_2_), channel_id=1, source_target_pairs={{0,1},{1,0},{2,3},{3,2},{4,5},{5,4},{6,7},{7,6},{8,9},{9,8},{10,11... | collective-permute-start | bytes 1032200 | tf_op jit(solution)/shard_map/ppermute | solution.py:443
  55.3 10.5 %collective-permute-start.6 = (bf16[192,896]{1,0:T(8,128)(2,1)S(1)}, bf16[192,896]{1,0:T(8,128)(2,1)S(1)}, u32[]{:S(2)}, u32[]{:S(2)}) collective-permute-start(bf16[192,896]{1,0:T(8,128)(2,1)S(1)} %pad_maximum_fusion.refs_0_), channel_id=1, source_target_pairs={{0,16},{16,0},{1,17},{17,1},{2,18},{18,2},{3,19},{19,3},{4,20},{20... | collective-permute-start | bytes 1032200 | tf_op jit(solution)/shard_map/ppermute | solution.py:442
  55.3 10.5 %collective-permute-start.8 = (bf16[192,896]{1,0:T(8,128)(2,1)S(1)}, bf16[192,896]{1,0:T(8,128)(2,1)S(1)}, u32[]{:S(2)}, u32[]{:S(2)}) collective-permute-start(bf16[192,896]{1,0:T(8,128)(2,1)S(1)} %pad_maximum_fusion.1.refs_2_), channel_id=1, source_target_pairs={{0,16},{16,0},{1,17},{17,1},{2,18},{18,2},{3,19},{19,3},{4,20},{20... | collective-permute-start | bytes 1032200 | tf_op jit(solution)/shard_map/ppermute | solution.py:442
  64.5 2.4 %copy-start.7 = (bf16[192,896]{1,0:T(8,128)(2,1)}, bf16[192,896]{1,0:T(8,128)(2,1)S(1)}, u32[]{:S(2)}) copy-start(bf16[192,896]{1,0:T(8,128)(2,1)S(1)} %collective-permute-done.4.refs_1_) | copy-start | bytes 1032196
  64.5 1.7 %collective-permute-start.7 = (bf16[192,896]{1,0:T(8,128)(2,1)S(1)}, bf16[192,896]{1,0:T(8,128)(2,1)S(1)}, u32[]{:S(2)}, u32[]{:S(2)}) collective-permute-start(bf16[192,896]{1,0:T(8,128)(2,1)S(1)} %collective-permute-done.4.refs_1_), channel_id=1, source_target_pairs={{0,16},{16,0},{1,17},{17,1},{2,18},{18,2},{3,19},{19,3},{4,20},{20... | collective-permute-start | bytes 1032200 | tf_op jit(solution)/shard_map/ppermute | solution.py:442
  65.2 1.7 %copy-start.8 = (bf16[192,896]{1,0:T(8,128)(2,1)}, bf16[192,896]{1,0:T(8,128)(2,1)S(1)}, u32[]{:S(2)}) copy-start(bf16[192,896]{1,0:T(8,128)(2,1)S(1)} %collective-permute-done.5.refs_3_) | copy-start | bytes 1032196
  65.2 1.7 %collective-permute-start.9 = (bf16[192,896]{1,0:T(8,128)(2,1)S(1)}, bf16[192,896]{1,0:T(8,128)(2,1)S(1)}, u32[]{:S(2)}, u32[]{:S(2)}) collective-permute-start(bf16[192,896]{1,0:T(8,128)(2,1)S(1)} %collective-permute-done.5.refs_3_), channel_id=1, source_target_pairs={{0,16},{16,0},{1,17},{17,1},{2,18},{18,2},{3,19},{19,3},{4,20},{20... | collective-permute-start | bytes 1032200 | tf_op jit(solution)/shard_map/ppermute | solution.py:442
  65.8 1.1 copy-start.9
  65.8 1.1 copy-start.10
  66.1 0.8 copy-start.11
  66.8 0.7 copy-start.12
  66.8 0.9 copy-start.3
  80.5 3.6 %copy-start.6 = (bf16[192,896]{1,0:T(8,128)(2,1)S(1)}, bf16[192,896]{1,0:T(8,128)(2,1)}, u32[]{:S(2)}) copy-start(bf16[192,896]{1,0:T(8,128)(2,1)} %get-tuple-element.57) | copy-start | bytes 1032196
  80.5 3.4 %collective-permute-start.10 = (bf16[768,896]{1,0:T(8,128)(2,1)}, bf16[768,896]{1,0:T(8,128)(2,1)S(1)}, u32[]{:S(2)}, u32[]{:S(2)}) collective-permute-start(bf16[768,896]{1,0:T(8,128)(2,1)} %get-tuple-element.54), channel_id=1, source_target_pairs={{0,16},{16,0},{1,17},{17,1},{2,18},{18,2},{3,19},{19,3},{4,20},{20... | collective-permute-start | bytes 4128776 | tf_op jit(solution)/shard_map/ppermute | solution.py:442
  84.9 11.2 %collective-permute-start.13 = (bf16[192,896]{1,0:T(8,128)(2,1)}, bf16[192,896]{1,0:T(8,128)(2,1)}, u32[]{:S(2)}, u32[]{:S(2)}) collective-permute-start(bf16[192,896]{1,0:T(8,128)(2,1)} %fusion), channel_id=1, source_target_pairs={{0,1},{1,0},{2,3},{3,2},{4,5},{5,4},{6,7},{7,6},{8,9},{9,8},{10,11... | collective-permute-start | bytes 1032200 | tf_op jit(solution)/shard_map/ppermute | solution.py:443
  86.2 30.1 %all-to-all-start.2 = ((bf16[16,2,24,512]{3,2,1,0:T(8,128)(2,1)}), bf16[16,2,24,512]{3,2,1,0:T(8,128)(2,1)S(1)}, u32[]{:S(2)}, u32[]{:S(2)}) async-start(bf16[16,2,24,512]{3,2,1,0:T(8,128)(2,1)} %get-tuple-element.49), calls=%async_computation.2 | async-start | bytes 1572864 | tf_op jit(solution)/shard_map/all_to_all | solution.py:444
  91.2 22.8 %copy-start.13 = (bf16[192,896]{1,0:T(8,128)(2,1)S(1)}, bf16[192,896]{1,0:T(8,128)(2,1)}, u32[]{:S(2)}) copy-start(bf16[192,896]{1,0:T(8,128)(2,1)} %get-tuple-element.53) | copy-start | bytes 1032196
  97.5 9.6 %collective-permute-start.14 = (bf16[96,896]{1,0:T(8,128)(2,1)S(1)}, bf16[96,896]{1,0:T(8,128)(2,1)S(1)}, u32[]{:S(2)}, u32[]{:S(2)}) collective-permute-start(bf16[96,896]{1,0:T(8,128)(2,1)S(1)} %slice.123), channel_id=1, source_target_pairs={{0,2},{1,3},{2,0},{3,1},{4,6},{5,7},{6,4},{7,5},{8,10},{9,11},{10,... | collective-permute-start | bytes 516104 | tf_op jit(solution)/shard_map/ppermute | solution.py:443
  98.5 15.5 %collective-permute-start.11 = (bf16[192,896]{1,0:T(8,128)(2,1)S(1)}, bf16[192,896]{1,0:T(8,128)(2,1)S(1)}, u32[]{:S(2)}, u32[]{:S(2)}) collective-permute-start(bf16[192,896]{1,0:T(8,128)(2,1)S(1)} %get-tuple-element.73), channel_id=1, source_target_pairs={{0,2},{1,3},{2,0},{3,1},{4,6},{5,7},{6,4},{7,5},{8,10},{9,11},{10,... | collective-permute-start | bytes 1032200 | tf_op jit(solution)/shard_map/ppermute | solution.py:443
  107.9 24.8 %collective-permute-start.15 = (bf16[96,896]{1,0:T(8,128)(2,1)}, bf16[96,896]{1,0:T(8,128)(2,1)}, u32[]{:S(2)}, u32[]{:S(2)}) collective-permute-start(bf16[96,896]{1,0:T(8,128)(2,1)} %fusion.4), channel_id=1, source_target_pairs={{0,4},{1,5},{2,6},{3,7},{4,0},{5,1},{6,2},{7,3},{8,12},{9,13},{10,... | collective-permute-start | bytes 516104 | tf_op jit(solution)/shard_map/ppermute | solution.py:443
  114.1 0.9 copy-start.1
  115.0 17.6 %collective-permute-start.12 = (bf16[96,896]{1,0:T(8,128)(2,1)S(1)}, bf16[96,896]{1,0:T(8,128)(2,1)S(1)}, u32[]{:S(2)}, u32[]{:S(2)}) collective-permute-start(bf16[96,896]{1,0:T(8,128)(2,1)S(1)} %slice.124), channel_id=1, source_target_pairs={{0,1},{1,0},{2,3},{3,2},{4,5},{5,4},{6,7},{7,6},{8,9},{9,8},{10,11... | collective-permute-start | bytes 516104 | tf_op jit(solution)/shard_map/ppermute | solution.py:443
  116.3 0.9 copy-start
  133.8 5.4 %collective-permute-start.17 = (bf16[48,896]{1,0:T(8,128)(2,1)S(1)}, bf16[48,896]{1,0:T(8,128)(2,1)S(1)}, u32[]{:S(2)}, u32[]{:S(2)}) collective-permute-start(bf16[48,896]{1,0:T(8,128)(2,1)S(1)} %slice.125), channel_id=1, source_target_pairs={{0,8},{1,9},{2,10},{3,11},{4,12},{5,13},{6,14},{7,15},{8,0},{9,1},... | collective-permute-start | bytes 258056 | tf_op jit(solution)/shard_map/ppermute | solution.py:443
  139.2 4.3 %collective-permute-start.18 = (f32[48,896]{1,0:T(8,128)S(1)}, f32[48,896]{1,0:T(8,128)S(1)}, u32[]{:S(2)}, u32[]{:S(2)}) collective-permute-start(f32[48,896]{1,0:T(8,128)S(1)} %convert_add_fusion), channel_id=1, source_target_pairs={{0,16},{16,0},{1,17},{17,1},{2,18},{18,2},{3,19},{19,3},{4,20},{20... | collective-permute-start | bytes 516104 | tf_op jit(solution)/shard_map/ppermute | solution.py:442
  139.3 1.6 %collective-permute-start.16 = (f32[24,128]{1,0:T(8,128)}, f32[24,128]{1,0:T(8,128)S(1)}, u32[]{:S(2)}, u32[]{:S(2)}) collective-permute-start(f32[24,128]{1,0:T(8,128)} %get-tuple-element.59.own_ref), channel_id=1, source_target_pairs={{0,16},{16,0},{1,17},{17,1},{2,18},{18,2},{3,19},{19,3},{4,20},{20... | collective-permute-start | bytes 36872 | tf_op jit(solution)/shard_map/ppermute | solution.py:442
  140.9 0.6 copy-start.14

commit v3 on v2

v3 whole, which is shorter than its diff:
```python
import math
from functools import partial

import jax
import jax.numpy as jnp
from jax import lax
from jax.experimental import pallas as pl
from jax.experimental.pallas import tpu as pltpu
from jax.sharding import PartitionSpec as P

SIDE = 32
CELLS = SIDE * SIDE
LANES = 128
PER = LANES // SIDE
SLOT = 8
TILES = CELLS // LANES
EPS = 1e-06
F32 = jnp.float32
BF16 = jnp.bfloat16


def column(row):
    n = row.shape[1]
    eye = lax.broadcasted_iota(jnp.int32, (n, n), 0) == lax.broadcasted_iota(jnp.int32, (n, n), 1)
    return jnp.sum(jnp.where(eye, jnp.broadcast_to(row, (n, n)), 0.0), axis=1, keepdims=True)


def as_row(col):
    n = col.shape[0]
    eye = lax.broadcasted_iota(jnp.int32, (n, n), 0) == lax.broadcasted_iota(jnp.int32, (n, n), 1)
    return jnp.sum(jnp.where(eye, jnp.broadcast_to(col, (n, n)), 0.0), axis=0, keepdims=True)


def image_mask(rows, height, width):
    cell = lax.broadcasted_iota(jnp.int32, (rows, CELLS), 1)
    return (cell // SIDE < height) & (cell % SIDE < width)


def lane_of(rows):
    return lax.broadcasted_iota(jnp.int32, (rows, LANES), 1)


def fill_slots(slots, value, image):
    channels = value.shape[0]
    for group in range(slots.shape[0]):
        live = min(SLOT, channels - group * SLOT)
        for k in range(TILES):
            at = (image * TILES + k) * SLOT
            part = value[group * SLOT : group * SLOT + live, k * LANES : (k + 1) * LANES]
            slots[group, pl.ds(at, live), :] = part


def read_slots(slots, image, channels):
    rows = []
    for group in range(slots.shape[0]):
        live = min(SLOT, channels - group * SLOT)
        at = [(image * TILES + k) * SLOT for k in range(TILES)]
        rows.append(jnp.concatenate([slots[group, pl.ds(a, live), :] for a in at], axis=1))
    return jnp.concatenate(rows, axis=0) if len(rows) > 1 else rows[0]


def cross(tiles, lane):
    for bit, far in ((2, 64), (1, 32)):
        low = (lane & far) == 0
        out = list(tiles)
        for k in range(len(tiles)):
            if not k & bit:
                one, two = tiles[k], tiles[k | bit]
                out[k] = jnp.where(low, one, pltpu.roll(two, far, 1))
                out[k | bit] = jnp.where(low, pltpu.roll(one, LANES - far, 1), two)
        tiles = out
    return tiles


def load_channel(slots, group, c, lane):
    count = slots.shape[1] // SLOT
    value = slots[group, pl.ds(c, count, stride=SLOT), :]
    return cross([value[k * SLOT : (k + 1) * SLOT] for k in range(count // SLOT)], lane)


def store_channel(slots, group, c, tiles, lane):
    count = slots.shape[1] // SLOT
    slots[group, pl.ds(c, count, stride=SLOT), :] = jnp.concatenate(cross(tiles, lane), axis=0)


def split(value):
    high = value.astype(BF16)
    return high, (value - high.astype(F32)).astype(BF16)


def pick(row, index):
    spread = jnp.broadcast_to(row, index.shape)
    value = jnp.take_along_axis(spread, jnp.clip(index, 0, LANES - 1), axis=1)
    return value


def build_down(row, c, high_ref, low_ref, lane, sub):
    place = lane % SIDE
    source = (place % TILES) * PER + place // TILES
    here = lane // SIDE == c % PER
    parts = []
    for turn in range(PER):
        index = PER * sub + turn - source
        parts.append(jnp.where(here & (index >= 0), pick(row, index), 0.0))
    high, low = split(jnp.concatenate(parts, axis=0))
    at = (slice(c * SIDE, (c + 1) * SIDE), slice(c // PER * LANES, (c // PER + 1) * LANES))
    high_ref[at] = high
    low_ref[at] = low


def build_across(row, turned, lane, sub):
    place = lane % SIDE
    highs, lows = [], []
    for part in range(PER):
        own = part * SLOT + sub
        index = own - place if turned else place - own
        value = jnp.where(index >= 0, pick(row, index + SIDE), 0.0)
        high = value.astype(BF16).astype(F32)
        highs.append(high)
        lows.append(value - high)
    spread = lambda parts: jnp.concatenate(
        [jnp.where(lane // SIDE == i, p, 0.0) for i in range(PER) for p in parts], axis=0
    ).astype(BF16)
    return spread(highs), spread(lows)


def taps_of(step_h, step_w, rate_h, rate_w, read_h, read_w, skip_ref):
    channels = rate_h.shape[0]
    lane = lane_of(channels)
    kept = jnp.zeros((channels, LANES), F32)
    decay_h = jnp.exp(column(step_h[...])) * rate_h[...]
    decay_w = jnp.exp(column(step_w[...])) * rate_w[...]
    for lag in range(SIDE):
        tap = jnp.sum(read_h[...] * jnp.exp(-decay_h * lag), axis=1, keepdims=True)
        kept = jnp.where(lane == lag, tap, kept)
        tap = jnp.sum(read_w[...] * jnp.exp(-decay_w * lag), axis=1, keepdims=True)
        kept = jnp.where(lane == SIDE + lag, tap, kept)
    return jnp.where(lane == 2 * SIDE, column(skip_ref[...]), kept)


def dot(a, b, dims=(((1,), (0,)), ((), ()))):
    return lax.dot_general(a, b, dims, preferred_element_type=F32)


NT = (((1,), (1,)), ((), ()))
TN = (((0,), (0,)), ((), ()))


def forward_kernel(
    heights, widths, feat_ref, cot_ref, scale_ref, step_h, step_w, rate_h, rate_w, read_h,
    read_w, skip_ref, out_ref, rows_ref, slots, high_a, low_a, field, tall,
):
    channels, cells = feat_ref.shape
    images = cells // CELLS
    rows_ref[0:channels] = taps_of(step_h, step_w, rate_h, rate_w, read_h, read_w, skip_ref)
    for ref in (high_a, low_a, field):
        ref[...] = jnp.zeros_like(ref)
    for image in range(images):
        inside = image_mask(1, heights[image], widths[image])
        value = feat_ref[:, image * CELLS : (image + 1) * CELLS].astype(F32)
        fill_slots(slots, jnp.where(inside, value, 0.0), image)
    live = min(SLOT, channels)
    sides = images // PER

    def body(group, carry):
        lane = lane_of(SLOT)
        sub = lax.broadcasted_iota(jnp.int32, (SLOT, LANES), 0)
        for c in range(live):
            row = rows_ref[pl.ds(group * SLOT + c, 1), :]
            build_down(row, c, high_a, low_a, lane, sub)
            tiles = load_channel(slots, group, c, lane)
            for s in range(sides):
                value = jnp.concatenate(tiles[s * PER : (s + 1) * PER], axis=0)
                field[c * SIDE : (c + 1) * SIDE, s * LANES : (s + 1) * LANES] = value.astype(BF16)
        source = field[...]
        tall[...] = dot(high_a[...], source) + dot(low_a[...], source)
        for c in range(live):
            row = rows_ref[pl.ds(group * SLOT + c, 1), :]
            high_b, low_b = build_across(row, False, lane, sub)
            value = jnp.concatenate(
                [tall[c * SIDE : (c + 1) * SIDE, s * LANES : (s + 1) * LANES] for s in range(sides)],
                axis=0,
            )
            high, low = split(value)
            value = dot(
                jnp.concatenate([high, low, high], axis=1),
                jnp.concatenate([high_b, high_b, low_b], axis=0),
            )
            tiles = [value[k * SLOT : (k + 1) * SLOT] for k in range(images)]
            store_channel(slots, group, c, tiles, lane)
        return carry

    lax.fori_loop(0, slots.shape[0], body, 0)
    wide = out_ref.shape[3]
    parts = CELLS // wide
    skip = rows_ref[0:channels, 2 * SIDE : 2 * SIDE + 1]
    scale = column(scale_ref[...])
    for image in range(images):
        span = slice(image * CELLS, (image + 1) * CELLS)
        inside = image_mask(1, heights[image], widths[image])
        value = read_slots(slots, image, channels) + skip * feat_ref[:, span].astype(F32)
        value = jnp.where(inside, value, 0.0).astype(BF16)
        down = cot_ref[:, span].astype(F32) * scale
        down = jnp.where(inside, down, 0.0).astype(BF16)
        for j in range(parts):
            out_ref[image * parts + j, 0] = value[:, j * wide : (j + 1) * wide]
            out_ref[image * parts + j, 1] = down[:, j * wide : (j + 1) * wide]


def backward_kernel(
    heights, widths, feat_ref, cot_ref, both_ref, rows_ref, scale_ref, bias_ref,
    result_ref, gfeat_ref, small_ref,
    slots, slots_g, high_a, low_a, field, field_g, tall, high_d, low_d, wide_ref, sums,
):
    channels, cells = feat_ref.shape
    images = cells // CELLS
    live = min(SLOT, channels)
    sides = images // PER
    wide = both_ref.shape[3]
    parts = CELLS // wide
    for ref in (high_a, low_a, sums, field, field_g, high_d, low_d):
        ref[...] = jnp.zeros_like(ref)
    lane_c = lane_of(channels)
    scale = column(scale_ref[...])
    bias = column(bias_ref[...])
    small = jnp.zeros((channels, LANES), F32)
    for image in range(images):
        span = slice(image * CELLS, (image + 1) * CELLS)
        inside = image_mask(1, heights[image], widths[image])
        values = feat_ref[:, span].astype(F32)
        masked = jnp.where(inside, values, 0.0)
        fill_slots(slots, masked, image)
        grad = jnp.concatenate(
            [both_ref[image * parts + j, 0].astype(F32) for j in range(parts)], axis=1
        )
        grad = jnp.where(inside, grad, 0.0)
        fill_slots(slots_g, grad, image)
        shifted = jnp.concatenate(
            [both_ref[image * parts + j, 1].astype(F32) for j in range(parts)], axis=1
        )
        shifted = shifted + bias
        result = values + jnp.where(inside, scale * shifted, 0.0)
        result_ref[:, span] = result.astype(BF16)
        weighted = jnp.where(inside, cot_ref[:, span].astype(F32), 0.0)
        small = small + jnp.where(
            lane_c == 64,
            jnp.sum(grad * masked, axis=1, keepdims=True),
            jnp.where(
                lane_c == 65,
                jnp.sum(weighted * shifted, axis=1, keepdims=True),
                jnp.where(lane_c == 66, jnp.sum(weighted, axis=1, keepdims=True), 0.0),
            ),
        )

    def body(group, carry):
        lane = lane_of(SLOT)
        sub = lax.broadcasted_iota(jnp.int32, (SLOT, LANES), 0)
        place = lane % SIDE
        half = lambda ref, c, s: ref[c * SIDE : (c + 1) * SIDE, s * LANES : (s + 1) * LANES]
        stack = lambda ref, c: jnp.concatenate([half(ref, c, s) for s in range(sides)], axis=0)
        for c in range(live):
            row = rows_ref[pl.ds(group * SLOT + c, 1), :]
            build_down(row, c, high_a, low_a, lane, sub)
            for slot, out in ((slots, field), (slots_g, field_g)):
                tiles = load_channel(slot, group, c, lane)
                for s in range(sides):
                    value = jnp.concatenate(tiles[s * PER : (s + 1) * PER], axis=0)
                    at = (slice(c * SIDE, (c + 1) * SIDE), slice(s * LANES, (s + 1) * LANES))
                    out[at] = value.astype(BF16)
        source = field[...]
        tall[...] = dot(high_a[...], source) + dot(low_a[...], source)
        for c in range(live):
            row = rows_ref[pl.ds(group * SLOT + c, 1), :]
            high_b, low_b = build_across(row, True, lane, sub)
            grad = stack(field_g, c)
            flow = dot(
                jnp.concatenate([grad, grad], axis=1), jnp.concatenate([high_b, low_b], axis=0)
            )
            high, low = split(flow)
            for s in range(sides):
                at = (slice(c * SIDE, (c + 1) * SIDE), slice(s * LANES, (s + 1) * LANES))
                high_d[at] = high[s * SIDE : (s + 1) * SIDE]
                low_d[at] = low[s * SIDE : (s + 1) * SIDE]
            high, low = split(stack(tall, c))
            outer = dot(
                jnp.concatenate([grad, grad], axis=0), jnp.concatenate([high, low], axis=0), TN
            )
            total = None
            for part in range(PER):
                value = None
                for i in range(PER):
                    at = i * SIDE + part * SLOT
                    term = jnp.where(lane // SIDE == i, outer[at : at + SLOT], 0.0)
                    value = term if value is None else value + term
                index = part * SLOT + sub - place
                value = jnp.take_along_axis(
                    value, jnp.clip(index, 0, SIDE - 1) + lane // SIDE * SIDE, axis=1
                )
                value = jnp.where(index >= 0, value, 0.0)
                total = value if total is None else total + value
            total = jnp.sum(total, axis=0, keepdims=True)
            total = total + pltpu.roll(total, 64, 1)
            total = total + pltpu.roll(total, 32, 1)
            sums[pl.ds(group * SLOT + c, 1), :] = jnp.where(lane[0:1] // SIDE == 1, total, 0.0)
        high, low = high_d[...], low_d[...]
        back = dot(high_a[...], high, TN) + dot(high_a[...], low, TN) + dot(low_a[...], high, TN)
        wide_ref[...] = back
        outer = dot(high, source, NT) + dot(low, source, NT)
        tall[...] = outer
        for c in range(live):
            value = stack(wide_ref, c)
            tiles = [value[k * SLOT : (k + 1) * SLOT] for k in range(images)]
            store_channel(slots, group, c, tiles, lane)
            total = None
            for turn in range(PER):
                at = c * SIDE + turn * SLOT
                value = tall[at : at + SLOT, c // PER * LANES : (c // PER + 1) * LANES]
                index = PER * sub + turn - lane
                safe = jnp.clip(index, 0, SIDE - 1)
                index_at = (safe % PER) * TILES + safe // PER + c % PER * SIDE
                value = jnp.take_along_axis(value, index_at, axis=1)
                value = jnp.where(index >= 0, value, 0.0)
                total = value if total is None else total + value
            total = jnp.sum(total, axis=0, keepdims=True)
            total = jnp.where(lane[0:1] < SIDE, total, 0.0)
            sums[pl.ds(group * SLOT + c, 1), :] += total
        return carry

    lax.fori_loop(0, slots.shape[0], body, 0)
    skip = rows_ref[0:channels, 2 * SIDE : 2 * SIDE + 1]
    for image in range(images):
        span = slice(image * CELLS, (image + 1) * CELLS)
        inside = image_mask(1, heights[image], widths[image])
        grad = read_slots(slots_g, image, channels)
        value = read_slots(slots, image, channels) + skip * grad
        gfeat_ref[:, span] = cot_ref[:, span].astype(F32) + jnp.where(inside, value, 0.0)
    small_ref[...] = small + sums[0:channels]


def chain_kernel(
    own_ref, other_ref, step_h, step_w, rate_h, rate_w, read_h, read_w, scale_ref,
    gstep_h, grate_h, gread_h, gstep_w, grate_w, gread_w, gskip, gbias, gscale,
):
    total = own_ref[...] + other_ref[...]
    for first, step, rate, read, gstep, grate, gread in (
        (0, step_h, rate_h, read_h, gstep_h, grate_h, gread_h),
        (SIDE, step_w, rate_w, read_w, gstep_w, grate_w, gread_w),
    ):
        pace = jnp.exp(column(step[...]))
        decay = pace * rate[...]
        to_read = jnp.zeros_like(decay)
        to_decay = jnp.zeros_like(decay)
        for lag in range(SIDE):
            term = total[:, first + lag : first + lag + 1] * jnp.exp(-decay * lag)
            to_read = to_read + term
            if lag:
                to_decay = to_decay - float(lag) * term
        to_decay = to_decay * read[...]
        gread[...] = to_read
        grate[...] = pace * to_decay
        gstep[...] = as_row(jnp.sum(to_decay * decay, axis=1, keepdims=True))
    gskip[...] = as_row(total[:, 64:65])
    gscale[...] = as_row(total[:, 65:66])
    gbias[...] = as_row(total[:, 66:67]) * scale_ref[...]


def join_kernel(count, *refs):
    given, outs = refs[:count], refs[count:]
    tall = outs[0].shape[0]
    for index, out in enumerate(outs):
        at = slice(index * tall, (index + 1) * tall)
        total = given[0][at].astype(F32)
        for ref in given[1:]:
            total = total + ref[at].astype(F32)
        out[...] = total.astype(out.dtype)


def relay_kernel(one_ref, two_ref, arrived_ref, first_ref, second_ref, out_one, out_two):
    tall = one_ref.shape[0]
    cut = tall // 2
    one = one_ref[...].astype(F32) + arrived_ref[tall : 2 * tall].astype(F32)
    two = two_ref[...].astype(F32) + arrived_ref[2 * tall : 3 * tall].astype(F32)
    out_one[:cut] = (one[:cut] + first_ref[...].astype(F32)).astype(BF16)
    out_one[cut:] = one[cut:].astype(BF16)
    out_two[:cut] = two[:cut].astype(BF16)
    out_two[cut:] = (two[cut:] + second_ref[...].astype(F32)).astype(BF16)


def finish_kernel(half, mine_ref, other_ref, ggain, gshift, gin, ginb, gout):
    units, count = gin.shape
    channels = ggain.shape[1]
    keep = units // 2
    first = half[0] == 0
    mine, other = mine_ref[...], other_ref[...]
    low = jnp.where(first, mine, other)[:keep]
    high = jnp.where(first, other, mine)[:keep]
    for at, part in ((0, low), (keep, high)):
        gin[at : at + keep] = part[:, :count]
        gout[at : at + keep] = part[:, count : 2 * count]
    bias = jnp.concatenate([low[:, 2 * count :], high[:, 2 * count :]], axis=0)
    ginb[...] = as_row(bias[:, 0:1])
    norms = (mine[:, 2 * count :] + other[:, 2 * count :])[:channels]
    ggain[...] = as_row(norms[:, 1:2])
    gshift[...] = as_row(norms[:, 2:3])


def pack_kernel(half, in_ref, out_ref, bias_ref, gain_ref, shift_ref, pack_ref):
    deep = pack_ref.shape[0]
    own, count = out_ref.shape
    channels = gain_ref.shape[1]
    keep = own // 2
    row = lax.broadcasted_iota(jnp.int32, (deep, own), 0)
    col = lax.broadcasted_iota(jnp.int32, (deep, own), 1)
    pick = jnp.where((col == row + half[0] * keep) & (row < keep), 1.0, 0.0).astype(BF16)
    nt = (((1,), (1,)), ((), ()))
    first = jnp.dot(pick, in_ref[...], preferred_element_type=F32)
    second = jnp.dot(pick, out_ref[...], preferred_element_type=F32)
    bias = jnp.broadcast_to(bias_ref[...], (LANES, own))
    third = lax.dot_general(pick, bias, nt, preferred_element_type=F32)
    row = lax.broadcasted_iota(jnp.int32, (deep, channels), 0)
    col = lax.broadcasted_iota(jnp.int32, (deep, channels), 1)
    pick = jnp.where(col == row, 1.0, 0.0).astype(BF16)
    gain = jnp.broadcast_to(gain_ref[...], (LANES, channels))
    gain = lax.dot_general(pick, gain, nt, preferred_element_type=F32)
    shift = jnp.broadcast_to(shift_ref[...], (LANES, channels))
    shift = lax.dot_general(pick, shift, nt, preferred_element_type=F32)
    lane = lane_of(deep)
    third = jnp.where(lane == 0, third, jnp.where(lane == 1, gain, jnp.where(lane == 2, shift, 0.0)))
    pack_ref[:, :count] = first.astype(BF16)
    pack_ref[:, count : 2 * count] = second.astype(BF16)
    pack_ref[:, 2 * count :] = third.astype(BF16)


ROOT = math.sqrt(2.0 / math.pi)


def mlp_kernel(near, pieces, where_ref, given_ref, *refs):
    own_in, refs = refs[:pieces], refs[pieces:]
    other_in, refs = refs[:pieces], refs[pieces:]
    both_ref, refs = refs[0], refs[1:]
    own_out, refs = refs[:pieces], refs[pieces:]
    gother_ref, active, downs, normal, gains, sum_acc, grad_acc, ext, gext = refs
    count, tokens = normal.shape
    devices, _, channels, _ = both_ref.shape
    spans, rows = [], 0
    for ref in own_in:
        spans.append(slice(rows, rows + ref.shape[0]))
        rows += ref.shape[0]
    deep = rows // devices

    value = jnp.concatenate([given_ref[d, 0].astype(F32) for d in range(devices)], axis=0)
    mean = jnp.mean(value, axis=0, keepdims=True)
    value = value - mean
    inv = lax.rsqrt(jnp.mean(value * value, axis=0, keepdims=True) + EPS)
    normal[...] = value * inv
    value = jnp.concatenate([given_ref[d, 1].astype(F32) for d in range(devices)], axis=0)
    downs[...] = value.astype(BF16)
    for at, ref in zip(spans, own_in):
        ext[at] = ref[:, 2 * count :].astype(F32)
    z, xy = where_ref[0], where_ref[1]
    spots = []
    for d in range(devices):
        spot = ((d % near) ^ xy) * (devices // near) + ((d // near) ^ z)
        spot = pl.multiple_of(spot * deep, deep)
        spots.append(spot)
        gains[d * channels : (d + 1) * channels] = ext[pl.ds(spot, deep), :][:channels]
    active[...] = (normal[...] * gains[:, 1:2] + gains[:, 2:3]).astype(BF16)

    def process(refs, first):
        w_in = jnp.concatenate([ref[:, :count] for ref in refs], axis=0)
        w_out = jnp.concatenate([ref[:, count : 2 * count] for ref in refs], axis=0)
        bias = jnp.concatenate([ref[:, 2 * count :] for ref in refs], axis=0).astype(F32)[:, 0:1]
        act = active[...]
        down = downs[...]
        v = dot(w_in, act) + bias
        square = v * v
        half = 0.5 * jnp.tanh(v * (ROOT * 0.044715 * square + ROOT)) + 0.5
        full = v * half
        hidden = full.astype(BF16)
        slope = half + full * (1.0 - half) * (6.0 * ROOT * 0.044715 * square + 2.0 * ROOT)
        low = (dot(w_out, down) * slope).astype(BF16)
        if first:
            sum_acc[...] = dot(w_out, hidden, TN)
            grad_acc[...] = dot(w_in, low, TN)
        else:
            sum_acc[...] += dot(w_out, hidden, TN)
            grad_acc[...] += dot(w_in, low, TN)
        g_bias = jnp.sum(low.astype(F32), axis=1, keepdims=True)
        g_bias = jnp.where(lane_of(low.shape[0]) == 0, g_bias, 0.0)
        return dot(low, act, NT), dot(hidden, down, NT), g_bias

    g_in, g_out, g_bias = process(other_in, True)
    gother_ref[:, :count] = g_in.astype(BF16)
    gother_ref[:, count : 2 * count] = g_out.astype(BF16)
    gother_ref[:, 2 * count :] = g_bias.astype(BF16)
    g_in, g_out, g_bias = process(own_in, False)
    gext[...] = g_bias
    for at, ref in zip(spans, own_out):
        ref[:, :count] = g_in[at].astype(BF16)
        ref[:, count : 2 * count] = g_out[at].astype(BF16)

    agrad = grad_acc[...]
    norm = normal[...]
    scaled = agrad * gains[:, 1:2]
    first = jnp.mean(scaled, axis=0, keepdims=True)
    second = jnp.mean(scaled * norm, axis=0, keepdims=True)
    mgrad = (scaled - first - norm * second) * inv
    summed = sum_acc[...]
    for d in range(devices):
        both_ref[d, 0] = mgrad[d * channels : (d + 1) * channels].astype(BF16)
        both_ref[d, 1] = summed[d * channels : (d + 1) * channels].astype(BF16)
    lane = lane_of(count)
    tile = jnp.where(lane == 1, jnp.sum(agrad * norm, axis=1, keepdims=True), 0.0)
    tile = jnp.where(lane == 2, jnp.sum(agrad, axis=1, keepdims=True), tile)
    for d in range(devices):
        part = tile[d * channels : (d + 1) * channels]
        if channels < deep:
            part = jnp.concatenate([part, jnp.zeros((deep - channels, LANES), F32)], axis=0)
        gext[pl.ds(spots[d], deep), :] += part
    for at, ref in zip(spans, own_out):
        ref[:, 2 * count :] = gext[at].astype(BF16)


def whole(shape):
    return pl.BlockSpec(shape, lambda i: (0,) * len(shape))


def params(mebibytes):
    return pltpu.CompilerParams(vmem_limit_bytes=mebibytes << 20)


def cost(micros):
    return pl.CostEstimate(flops=0, transcendentals=0, bytes_accessed=micros * 3_000_000)


def join(deep, arrays, count):
    full = pl.BlockSpec(memory_space=pltpu.VMEM)
    width = arrays[0].shape[1]
    return pl.pallas_call(
        partial(join_kernel, len(arrays)),
        out_shape=[
            jax.ShapeDtypeStruct((deep, width), BF16 if i else F32) for i in range(count)
        ],
        in_specs=[full] * len(arrays),
        out_specs=[full] * count,
        compiler_params=params(8),
        cost_estimate=cost(1),
        name="join",
    )(*arrays)


def relay(*arrays):
    full = pl.BlockSpec(memory_space=pltpu.VMEM)
    shape = jax.ShapeDtypeStruct(arrays[0].shape, BF16)
    return pl.pallas_call(
        relay_kernel,
        out_shape=(shape, shape),
        in_specs=[full] * 5,
        out_specs=(full, full),
        compiler_params=params(8),
        cost_estimate=cost(1),
        name="relay",
    )(*arrays)


SMEM = pl.BlockSpec(memory_space=pltpu.SMEM)


def per_device(
    ch, features, cotangent, heights, widths, step_height, rate_height, readout_height,
    step_width, rate_width, readout_width, skip_gain, norm_gain, norm_shift, in_weight,
    in_bias, out_weight, out_bias, layer_scale,
):
    channels, cells = features.shape
    count = in_weight.shape[0]
    pin = lambda v: pltpu.with_memory_space_constraint(v, pltpu.HBM)
    units = in_weight.shape[1]
    states = rate_height.shape[1]
    images = cells // CELLS
    tokens = cells // ch
    parts = CELLS // tokens
    far = 4
    near = ch // far
    deep = -(-(units // 2) // 16) * 16
    width = 2 * count + LANES
    near_groups = [[f * near + i for i in range(near)] for f in range(far)]
    row = lambda v: v.reshape(1, -1)
    exchange = lambda v: lax.ppermute(v, "img", [(0, 1), (1, 0)])
    flip = lambda v, bits: lax.ppermute(v, "ch", [(i, i ^ bits) for i in range(ch)])
    swap = lambda v, groups=None: lax.all_to_all(
        v, "ch", split_axis=0, concat_axis=0, tiled=True, axis_index_groups=groups
    )
    pair = lambda *arrays: lax.optimization_barrier(arrays)
    half = lax.axis_index("img").astype(jnp.int32)
    place = lax.axis_index("ch").astype(jnp.int32)
    full = pl.BlockSpec(memory_space=pltpu.VMEM)

    pack = pl.pallas_call(
        pack_kernel,
        out_shape=jax.ShapeDtypeStruct((deep, width), BF16),
        in_specs=[SMEM] + [full] * 5,
        out_specs=full,
        compiler_params=params(4),
        cost_estimate=cost(2),
        name="pack",
    )(
        half.reshape(1), pin(in_weight.T), pin(out_weight), pin(row(in_bias)), pin(row(norm_gain)),
        pin(row(norm_shift)),
    )
    pack, features_after = lax.optimization_barrier((pack, features))
    shards = [pack] + [flip(pack, bits * near) for bits in range(1, far)]

    groups = -(-channels // SLOT)
    slots = pltpu.VMEM((groups, images * TILES * SLOT, LANES), F32)
    square = (SLOT * SIDE, images // PER * LANES)
    toeplitz = pltpu.VMEM((SLOT * SIDE, SLOT * SIDE), BF16)
    both_shape = (ch, 2, channels, tokens)
    given, taps = pl.pallas_call(
        forward_kernel,
        out_shape=(
            jax.ShapeDtypeStruct(both_shape, BF16),
            jax.ShapeDtypeStruct((groups * SLOT, LANES), F32),
        ),
        in_specs=[SMEM, SMEM] + [full] * 10,
        out_specs=(full, full),
        scratch_shapes=[
            slots, toeplitz, toeplitz, pltpu.VMEM(square, BF16), pltpu.VMEM(square, F32),
        ],
        compiler_params=params(12),
        cost_estimate=cost(6),
        name="mixer_forward",
    )(
        pin(heights), pin(widths), pin(features_after), pin(cotangent), pin(row(layer_scale)),
        pin(row(step_height)), pin(row(step_width)), pin(rate_height), pin(rate_width),
        pin(readout_height), pin(readout_width), pin(row(skip_gain)),
    )
    given, *shards = lax.optimization_barrier((given, *shards))
    given = swap(given)
    shard = jnp.concatenate(shards, axis=0)
    if near == 4:
        cut = far * deep // 2
        beside, above = pair(flip(shard, 1), flip(shard, 2))
        own = [shard, beside, above, flip(beside[:cut], 2), flip(above[cut:], 1)]
        where = jnp.stack([place // near, place % near])
    else:
        own = [swap(jnp.broadcast_to(shard[None], (near,) + shard.shape), near_groups)]
        own = [own[0].reshape(ch * deep, width)]
        where = jnp.stack([place // near, place * 0])
    other = [exchange(piece) for piece in own]

    rows = ch * deep
    pieces = len(own)
    outs = pl.pallas_call(
        partial(mlp_kernel, near, pieces),
        out_shape=[jax.ShapeDtypeStruct(both_shape, BF16)]
        + [jax.ShapeDtypeStruct(piece.shape, BF16) for piece in own]
        + [jax.ShapeDtypeStruct((rows, width), BF16)],
        in_specs=[SMEM] + [full] * (2 * pieces + 1),
        out_specs=[full] * (pieces + 2),
        scratch_shapes=[
            pltpu.VMEM((count, tokens), BF16),
            pltpu.VMEM((count, tokens), BF16),
            pltpu.VMEM((count, tokens), F32),
            pltpu.VMEM((count, LANES), F32),
            pltpu.VMEM((count, tokens), F32),
            pltpu.VMEM((count, tokens), F32),
            pltpu.VMEM((rows, LANES), F32),
            pltpu.VMEM((rows, LANES), F32),
        ],
        compiler_params=params(24),
        cost_estimate=cost(8),
        name="mlp",
    )(where, given, *map(pin, own), *map(pin, other))
    both, gown, gother = outs[0], outs[1:-1], outs[-1]

    arrived = exchange(gother)
    both = swap(both)
    tall = far * deep
    if near == 4:
        cut = tall // 2
        add = lambda v, at: (v.astype(F32) + arrived[at : at + v.shape[0]].astype(F32)).astype(BF16)
        one, two = pair(add(gown[3], 3 * tall), add(gown[4], 3 * tall + cut))
        one, two = pair(flip(one, 2), flip(two, 1))
        one, two = relay(gown[1], gown[2], arrived, one, two)
        first, second, *sent = gown[0], arrived, flip(one, 1), flip(two, 2)
    else:
        total = (gown[0].astype(F32) + arrived.astype(F32)).astype(BF16)
        sent = list(swap(total.reshape(near, tall, width), near_groups))
        first, second, *sent = sent
    landed = [first, second, *sent]
    result, grad_features, small = pl.pallas_call(
        backward_kernel,
        out_shape=(
            jax.ShapeDtypeStruct((channels, cells), BF16),
            jax.ShapeDtypeStruct((channels, cells), F32),
            jax.ShapeDtypeStruct((channels, LANES), F32),
        ),
        in_specs=[SMEM, SMEM] + [full] * 6,
        out_specs=(full,) * 3,
        scratch_shapes=[
            slots, slots, toeplitz, toeplitz, pltpu.VMEM(square, BF16), pltpu.VMEM(square, BF16),
            pltpu.VMEM((SLOT * SIDE, max(SLOT * SIDE, square[1])), F32), pltpu.VMEM(square, BF16),
            pltpu.VMEM(square, BF16), pltpu.VMEM(square, F32),
            pltpu.VMEM((groups * SLOT, LANES), F32),
        ],
        compiler_params=params(16),
        cost_estimate=cost(7),
        name="mixer_backward",
    )(
        pin(heights), pin(widths), pin(features), pin(cotangent), both, taps,
        pin(row(layer_scale)), pin(row(out_bias)),
    )

    *landed, small = lax.optimization_barrier((*landed, small))
    shards = join(deep, landed, far)
    shards = [shards[0]] + [flip(v, (i + 1) * near) for i, v in enumerate(shards[1:])]
    vector_out = jax.ShapeDtypeStruct((1, channels), F32)
    state_out = jax.ShapeDtypeStruct((channels, states), F32)
    chained = pl.pallas_call(
        chain_kernel,
        out_shape=(
            vector_out, state_out, state_out, vector_out, state_out, state_out,
            vector_out, vector_out, vector_out,
        ),
        in_specs=[full] * 9,
        out_specs=(full,) * 9,
        compiler_params=params(4),
        cost_estimate=cost(2),
        name="mixer_chain",
    )(
        small, exchange(small), pin(row(step_height)), pin(row(step_width)), pin(rate_height),
        pin(rate_width), pin(readout_height), pin(readout_width), pin(row(layer_scale)),
    )
    *shards, chained = lax.optimization_barrier((*shards, chained))
    gstep_h, grate_h, gread_h, gstep_w, grate_w, gread_w, gskip, gbias, gscale = chained
    (mine,) = join(deep, shards, 1)
    ggain, gshift, gin, ginb, gout = pl.pallas_call(
        finish_kernel,
        out_shape=(
            vector_out, vector_out, jax.ShapeDtypeStruct((units, count), F32),
            jax.ShapeDtypeStruct((1, units), F32), jax.ShapeDtypeStruct((units, count), F32),
        ),
        in_specs=[SMEM, full, full],
        out_specs=(full,) * 5,
        compiler_params=params(4),
        cost_estimate=cost(1),
        name="finish",
    )(half.reshape(1), mine, exchange(mine))
    flat = lambda v: v.reshape(-1)
    return (
        result, grad_features, flat(gstep_h), grate_h, gread_h, flat(gstep_w), grate_w, gread_w,
        flat(gskip), flat(ggain), flat(gshift), gin.T, flat(ginb), gout, flat(gbias),
        flat(gscale),
    )


def solution(mesh):
    wide, split, tall = P("ch", "img"), P("ch"), P("ch", None)
    return jax.shard_map(
        partial(per_device, mesh.shape["ch"]),
        mesh=mesh,
        in_specs=(
            wide, wide, P("img"), P("img"), split, tall, tall, split, tall, tall, split, split,
            split, P(None, "ch"), split, tall, split, split,
        ),
        out_specs=(
            wide, wide, split, tall, tall, split, tall, tall, split, split, split,
            P(None, "ch"), split, tall, split, split,
        ),
        check_vma=False,
    )
```

time: 146 us -> 103 us (0.71)
  Pallas kernels: 46.6 us -> 27.3 us
  waiting for transfers between devices: 48.1 us -> 36.6 us
  other arithmetic: 8.1 us -> 0.17 us
  starting transfers between devices: 38 us -> 35.7 us
  local copies, waits for them, and re-layouts: 3.89 us -> 1.6 us
    pallas_call x4 -> x7, Pallas kernels: 42.8 us -> 24.1 us  [the longest x1 9.06 us: per_device(): pl.pallas_call(partial(mlp_kernel, near, pieces), out_shape=[jax.ShapeDty...]
    ppermute x12 -> x14, waiting for transfers between devices: 42.7 us -> 28.6 us  [per_device(): lax.ppermute(v, 'ch', [(i, i ^ bits) for i in range(ch)])]
    all_to_all x3 -> x2, starting transfers between devices: 17.6 us -> 11.7 us  [per_device(): lax.all_to_all(v, 'ch', split_axis=0, concat_axis=0, tiled=True, axis_ind...]
    ppermute x12 -> x14, starting transfers between devices: 19.1 us -> 23.2 us  [per_device(): lax.ppermute(v, 'ch', [(i, i ^ bits) for i in range(ch)])]
    all_to_all x3 -> x2, waiting for transfers between devices: 0.01 us -> 3.94 us  [per_device(): lax.all_to_all(v, 'ch', split_axis=0, concat_axis=0, tiled=True, axis_ind...]
    concatenate x4 -> x0, other arithmetic: 2.58 us -> none  [the longest x1 0.92 us: per_device(): even = jnp.concatenate([even, flip(even, 1)], axis=0)]
    add x4 -> x0, other arithmetic: 2.53 us -> none  [the longest x1 1.33 us: per_device(): odd = part[2] + flip(part[3].astype(BF16), 1).astype(F32)]
    convert_element_type x3 -> x1, other arithmetic: 1.7 us -> 0.09 us  [per_device(): (v.astype(F32) + arrived[at:at + v.shape[0]].astype(F32)).astype(BF16)]
  transfers between devices with their start and end apart: 22 -> 24, of which waited for: 12 -> 11; matrix products, arithmetic and copies ran while one was open for 3% -> 0% of each run, Pallas kernels for 22% -> 16%
where the time goes in v3:
time: 103 us; the launch traced here: 102 us
  waiting for transfers between devices  36.6 us (36%)
  starting transfers between devices  35.7 us (35%)
  Pallas kernels  27.3 us (27%)
  local copies, waits for them, and re-layouts  1.6 us (2%)
    ppermute x14, waiting for transfers between devices, per_device(): lax.ppermute(v, 'ch', [(i, i ^ bits) for i in range(ch)])  28.6 us
    ppermute x14, starting transfers between devices, per_device(): lax.ppermute(v, 'ch', [(i, i ^ bits) for i in range(ch)])  23.2 us
    all_to_all x2, starting transfers between devices, per_device(): lax.all_to_all(v, 'ch', split_axis=0, concat_axis=0, tiled=True, axis_ind...  11.7 us
    pallas_call x1, Pallas kernels, per_device(): pl.pallas_call(partial(mlp_kernel, near, pieces), out_shape=[jax.ShapeDty...  9.06 us
    pallas_call x1, Pallas kernels, per_device(): pl.pallas_call(backward_kernel, out_shape=(jax.ShapeDtypeStruct((channels...  7.54 us
    pallas_call x1, Pallas kernels, per_device(): pl.pallas_call(forward_kernel, out_shape=(jax.ShapeDtypeStruct(both_shape...  5.54 us
    ppermute x8, waiting for transfers between devices, per_device(): exchange = lambda v: lax.ppermute(v, 'img', [(0, 1), (1, 0)])  4.11 us
    all_to_all x2, waiting for transfers between devices, per_device(): lax.all_to_all(v, 'ch', split_axis=0, concat_axis=0, tiled=True, axis_ind...  3.94 us
  transfers between devices with their start and end apart: 24, of which 11 were waited for; matrix products, arithmetic and copies ran while one was open for 0% of the time, Pallas kernels for 16%

profile of v3, /device:TPU:0, one launch (start us, length us, event | category | flops | bytes accessed | tf_op | source)
XLA Modules:
  0.0 102.2 jit_solution(16393081304031658680)
XLA Ops:
  0.7 1.2 %pack.1 = bf16[48,896]{1,0:T(8,128)(2,1)S(1)} custom-call(s32[1]{0:T(128)} %bitcast.2.half, bf16[96,384]{1,0:T(8,128)(2,1)} %bitcast.21, bf16[96,384]{1,0:T(8,128)(2,1)} %out_ref.1, bf16[1,96]{1,0:T(2,128)(2,1)} %bitcast.29, bf16[1,24]{1,0:T(2,128)(2,1)} %bitcast.30, bf16[1,24]{1,0:T(2,128)(2,1)} %bitcast.31), custom_call_target="tpu_custom_call" | custom-call | bytes 6000000 | tf_op jit(solution)/shard_map/pack/pallas_call | solution.py:598
  1.8 5.1 %collective-permute-start.2 = (bf16[48,896]{1,0:T(8,128)(2,1)S(1)}, bf16[48,896]{1,0:T(8,128)(2,1)S(1)}, u32[]{:S(2)}, u32[]{:S(2)}) collective-permute-start(bf16[48,896]{1,0:T(8,128)(2,1)S(1)} %pack.1), channel_id=1, source_target_pairs={{0,12},{1,13},{2,14},{3,15},{4,8},{5,9},{6,10},{7,11},{8,4},{9,5},... | collective-permute-start | bytes 258056 | tf_op jit(solution)/shard_map/ppermute | solution.py:589
  6.9 0.0 collective-permute-start.1
  6.9 0.6 collective-permute-start
  7.6 5.5 %mixer_forward.1 = (bf16[16,2,24,512]{3,2,1,0:T(8,128)(2,1)}, f32[24,128]{1,0:T(8,128)S(1)}) custom-call(s32[8]{0:T(128)} %heights.3, s32[8]{0:T(128)} %widths.3, bf16[24,8192]{1,0:T(8,128)(2,1)} %feat_ref.2, bf16[24,8192]{1,0:T(8,128)(2,1)} %cot_ref.3, f32[1,24]{1,0:T(1,128)} %bitcast.22, f32[1,24]{1,0:T(1,128)} %bitcast.25, f32[1,24]{1,0:T(1,128)} %bitcast.27, ...), custom_call_target="tpu_custom_call" | custom-call | bytes 18000000 | tf_op jit(solution)/shard_map/mixer_forward/pallas_call | solution.py:618
  13.1 0.0 collective-permute-done.2
  13.1 1.0 %collective-permute-done.1 = bf16[48,896]{1,0:T(8,128)(2,1)S(1)} collective-permute-done((bf16[48,896]{1,0:T(8,128)(2,1)S(1)}, bf16[48,896]{1,0:T(8,128)(2,1)S(1)}, u32[]{:S(2)}, u32[]{:S(2)}) %collective-permute-start.1) | collective-permute-done | bytes 86048 | tf_op jit(solution)/shard_map/ppermute | solution.py:589
  14.1 0.0 collective-permute-done
  14.1 6.0 %all-to-all-start = ((bf16[16,2,24,512]{3,2,1,0:T(8,128)(2,1)}), bf16[16,2,24,512]{3,2,1,0:T(8,128)(2,1)S(1)}, u32[]{:S(2)}, u32[]{:S(2)}) async-start(bf16[16,2,24,512]{3,2,1,0:T(8,128)(2,1)} %get-tuple-element.82), calls=%async_computation | async-start | bytes 1572864 | tf_op jit(solution)/shard_map/all_to_all | solution.py:590
  20.2 0.0 copy-start.2
  20.3 2.0 %collective-permute-start.4 = (bf16[192,896]{1,0:T(8,128)(2,1)S(1)}, bf16[192,896]{1,0:T(8,128)(2,1)S(1)}, u32[]{:S(2)}, u32[]{:S(2)}) collective-permute-start(bf16[192,896]{1,0:T(8,128)(2,1)S(1)} %constant_dynamic-update-slice_fusion.refs_0_), channel_id=1, source_target_pairs={{0,2},{1,3},{2,0},{3,1},{4,6},{5,7},{6,4},{7,5},{8,10},{9,11},{10,... | collective-permute-start | bytes 1032200 | tf_op jit(solution)/shard_map/ppermute | solution.py:589
  22.2 1.5 %collective-permute-start.3 = (bf16[192,896]{1,0:T(8,128)(2,1)S(1)}, bf16[192,896]{1,0:T(8,128)(2,1)S(1)}, u32[]{:S(2)}, u32[]{:S(2)}) collective-permute-start(bf16[192,896]{1,0:T(8,128)(2,1)S(1)} %constant_dynamic-update-slice_fusion.refs_0_), channel_id=1, source_target_pairs={{0,1},{1,0},{2,3},{3,2},{4,5},{5,4},{6,7},{7,6},{8,9},{9,8},{10,11... | collective-permute-start | bytes 1032200 | tf_op jit(solution)/shard_map/ppermute | solution.py:589
  23.7 0.0 collective-permute-start.7
  23.7 12.6 %collective-permute-done.4.refs_2_ = bf16[192,896]{1,0:T(8,128)(2,1)S(1)} collective-permute-done((bf16[192,896]{1,0:T(8,128)(2,1)S(1)}, bf16[192,896]{1,0:T(8,128)(2,1)S(1)}, u32[]{:S(2)}, u32[]{:S(2)}) %collective-permute-start.4) | collective-permute-done | bytes 344096 | tf_op jit(solution)/shard_map/ppermute | solution.py:589
  36.3 0.0 collective-permute-done.3.refs_1_
  36.3 1.6 %collective-permute-start.6 = (bf16[96,896]{1,0:T(8,128)(2,1)S(1)}, bf16[96,896]{1,0:T(8,128)(2,1)S(1)}, u32[]{:S(2)}, u32[]{:S(2)}) collective-permute-start(bf16[96,896]{1,0:T(8,128)(2,1)S(1)} %slice.13), channel_id=1, source_target_pairs={{0,1},{1,0},{2,3},{3,2},{4,5},{5,4},{6,7},{7,6},{8,9},{9,8},{10,11... | collective-permute-start | bytes 516104 | tf_op jit(solution)/shard_map/ppermute | solution.py:589
  37.9 1.0 %collective-permute-start.5 = (bf16[96,896]{1,0:T(8,128)(2,1)S(1)}, bf16[96,896]{1,0:T(8,128)(2,1)}, u32[]{:S(2)}, u32[]{:S(2)}) collective-permute-start(bf16[96,896]{1,0:T(8,128)(2,1)S(1)} %slice.12), channel_id=1, source_target_pairs={{0,2},{1,3},{2,0},{3,1},{4,6},{5,7},{6,4},{7,5},{8,10},{9,11},{10,... | collective-permute-start | bytes 516104 | tf_op jit(solution)/shard_map/ppermute | solution.py:589
  38.9 0.0 collective-permute-start.8
  38.9 0.5 collective-permute-start.9
  39.4 2.9 %collective-permute-done.6.refs_4_ = bf16[96,896]{1,0:T(8,128)(2,1)S(1)} collective-permute-done((bf16[96,896]{1,0:T(8,128)(2,1)S(1)}, bf16[96,896]{1,0:T(8,128)(2,1)S(1)}, u32[]{:S(2)}, u32[]{:S(2)}) %collective-permute-start.6) | collective-permute-done | bytes 172064 | tf_op jit(solution)/shard_map/ppermute | solution.py:589
  42.3 0.0 collective-permute-start.11
  42.3 1.1 %collective-permute-done.5.refs_3_ = bf16[96,896]{1,0:T(8,128)(2,1)} collective-permute-done((bf16[96,896]{1,0:T(8,128)(2,1)S(1)}, bf16[96,896]{1,0:T(8,128)(2,1)}, u32[]{:S(2)}, u32[]{:S(2)}) %collective-permute-start.5) | collective-permute-done | bytes 172064 | tf_op jit(solution)/shard_map/ppermute | solution.py:589
  43.5 0.0 collective-permute-start.10
  43.5 0.1 pad_add_fusion.where_ref
  43.6 0.0 collective-permute-done.7.refs_5_
  43.6 0.2 collective-permute-done.11.refs_9_
  43.7 1.4 %collective-permute-done.10.refs_8_ = bf16[96,896]{1,0:T(8,128)(2,1)S(1)} collective-permute-done((bf16[96,896]{1,0:T(8,128)(2,1)}, bf16[96,896]{1,0:T(8,128)(2,1)S(1)}, u32[]{:S(2)}, u32[]{:S(2)}) %collective-permute-start.10) | collective-permute-done | bytes 172064 | tf_op jit(solution)/shard_map/ppermute | solution.py:588
  45.1 0.0 collective-permute-done.8.refs_6_
  45.1 0.0 collective-permute-done.9.refs_7_
  45.1 0.0 copy-done.6
  45.1 0.6 copy-done.8
  45.8 0.1 copy-done.4
  45.9 0.7 copy-done.5
  46.6 0.0 all-to-all-done.given_ref
  46.6 0.0 copy-done
  46.7 9.1 %mlp.1 = (bf16[16,2,24,512]{3,2,1,0:T(8,128)(2,1)}, bf16[192,896]{1,0:T(8,128)(2,1)S(1)}, bf16[192,896]{1,0:T(8,128)(2,1)S(1)}, bf16[192,896]{1,0:T(8,128)(2,1)S...) custom-call(s32[2]{0:T(128)S(1)} %pad_add_fusion.where_ref, ...), custom_call_target="tpu_custom_call" | custom-call | bytes 24000000 | tf_op jit(solution)/shard_map/mlp/pallas_call | solution.py:653
  55.7 0.1 collective-permute-start.12
  55.9 5.7 %all-to-all-start.1 = ((bf16[16,2,24,512]{3,2,1,0:T(8,128)(2,1)}), bf16[16,2,24,512]{3,2,1,0:T(8,128)(2,1)S(1)}, u32[]{:S(2)}, u32[]{:S(2)}) async-start(bf16[16,2,24,512]{3,2,1,0:T(8,128)(2,1)} %get-tuple-element.89), calls=%async_computation.1 | async-start | bytes 1572864 | tf_op jit(solution)/shard_map/all_to_all | solution.py:590
  61.6 0.0 collective-permute-done.12.arrived_ref.refs_1_
  61.6 0.1 add_convert_fusion
  61.7 2.0 %collective-permute-start.13 = (bf16[96,896]{1,0:T(8,128)(2,1)S(1)}, bf16[96,896]{1,0:T(8,128)(2,1)S(1)}, u32[]{:S(2)}, u32[]{:S(2)}) collective-permute-start(bf16[96,896]{1,0:T(8,128)(2,1)S(1)} %get-tuple-element.99), channel_id=1, source_target_pairs={{0,2},{1,3},{2,0},{3,1},{4,6},{5,7},{6,4},{7,5},{8,10},{9,11},{10,... | collective-permute-start | bytes 516104 | tf_op jit(solution)/shard_map/ppermute | solution.py:589
  63.7 1.4 %collective-permute-start.14 = (bf16[96,896]{1,0:T(8,128)(2,1)S(1)}, bf16[96,896]{1,0:T(8,128)(2,1)S(1)}, u32[]{:S(2)}, u32[]{:S(2)}) collective-permute-start(bf16[96,896]{1,0:T(8,128)(2,1)S(1)} %get-tuple-element.100), channel_id=1, source_target_pairs={{0,1},{1,0},{2,3},{3,2},{4,5},{5,4},{6,7},{7,6},{8,9},{9,8},{10,11... | collective-permute-start | bytes 516104 | tf_op jit(solution)/shard_map/ppermute | solution.py:589
  65.1 8.7 %collective-permute-done.13.first_ref = bf16[96,896]{1,0:T(8,128)(2,1)S(1)} collective-permute-done((bf16[96,896]{1,0:T(8,128)(2,1)S(1)}, bf16[96,896]{1,0:T(8,128)(2,1)S(1)}, u32[]{:S(2)}, u32[]{:S(2)}) %collective-permute-start.13) | collective-permute-done | bytes 172064 | tf_op jit(solution)/shard_map/ppermute | solution.py:589
  73.8 0.0 collective-permute-done.14.second_ref
  73.8 1.0 relay.1
  74.8 2.0 %collective-permute-start.15 = (bf16[192,896]{1,0:T(8,128)(2,1)}, bf16[192,896]{1,0:T(8,128)(2,1)S(1)}, u32[]{:S(2)}, u32[]{:S(2)}) collective-permute-start(bf16[192,896]{1,0:T(8,128)(2,1)} %get-tuple-element.103), channel_id=1, source_target_pairs={{0,1},{1,0},{2,3},{3,2},{4,5},{5,4},{6,7},{7,6},{8,9},{9,8},{10,11... | collective-permute-start | bytes 1032200 | tf_op jit(solution)/shard_map/ppermute | solution.py:589
  76.8 1.0 collective-permute-start.16
  77.7 3.9 %all-to-all-done.1.both_ref = bf16[16,2,24,512]{3,2,1,0:T(8,128)(2,1)S(1)} async-done(((bf16[16,2,24,512]{3,2,1,0:T(8,128)(2,1)}), bf16[16,2,24,512]{3,2,1,0:T(8,128)(2,1)S(1)}, u32[]{:S(2)}, u32[]{:S(2)}) %all-to-all-start.1) | async-done | bytes 786464 | tf_op jit(solution)/shard_map/all_to_all | solution.py:590
  81.7 7.5 %mixer_backward.1 = (bf16[24,8192]{1,0:T(8,128)(2,1)}, f32[24,8192]{1,0:T(8,128)}, f32[24,128]{1,0:T(8,128)S(1)}) custom-call(s32[8]{0:T(128)} %heights.3, s32[8]{0:T(128)} %widths.3, bf16[24,8192]{1,0:T(8,128)(2,1)} %feat_ref.2, bf16[24,8192]{1,0:T(8,128)(2,1)} %cot_ref.3, bf16[16,2,24,512]{3,2,1,0:T(8,128)(2,1)S(1)} %all-to-all-done.1.both_ref, ...), custom_call_target="tpu_custom_call" | custom-call | bytes 21000000 | tf_op jit(solution)/shard_map/mixer_backward/pallas_call | solution.py:691
  89.2 0.0 collective-permute-done.15.refs_2_
  89.2 0.0 collective-permute-done.16.refs_3_
  89.2 0.2 join.2
  89.4 2.6 %collective-permute-start.17 = (bf16[48,896]{1,0:T(8,128)(2,1)S(1)}, bf16[48,896]{1,0:T(8,128)(2,1)S(1)}, u32[]{:S(2)}, u32[]{:S(2)}) collective-permute-start(bf16[48,896]{1,0:T(8,128)(2,1)S(1)} %get-tuple-element.111), channel_id=1, source_target_pairs={{0,4},{1,5},{2,6},{3,7},{4,0},{5,1},{6,2},{7,3},{8,12},{9,13},{10,... | collective-permute-start | bytes 258056 | tf_op jit(solution)/shard_map/ppermute | solution.py:589
  92.0 0.4 collective-permute-start.18
  92.4 2.0 %collective-permute-start.19 = (bf16[48,896]{1,0:T(8,128)(2,1)S(1)}, bf16[48,896]{1,0:T(8,128)(2,1)S(1)}, u32[]{:S(2)}, u32[]{:S(2)}) collective-permute-start(bf16[48,896]{1,0:T(8,128)(2,1)S(1)} %get-tuple-element.113), channel_id=1, source_target_pairs={{0,12},{1,13},{2,14},{3,15},{4,8},{5,9},{6,10},{7,11},{8,4},{9,5},... | collective-permute-start | bytes 258056 | tf_op jit(solution)/shard_map/ppermute | solution.py:589
  94.4 0.0 collective-permute-start.20
  94.4 1.2 %collective-permute-done.20.other_ref = f32[24,128]{1,0:T(8,128)S(1)} collective-permute-done((f32[24,128]{1,0:T(8,128)S(1)}, f32[24,128]{1,0:T(8,128)S(1)}, u32[]{:S(2)}, u32[]{:S(2)}) %collective-permute-start.20) | collective-permute-done | bytes 12320 | tf_op jit(solution)/shard_map/ppermute | solution.py:588
  95.6 2.0 %mixer_chain.1 = (f32[1,24]{1,0:T(1,128)}, f32[24,64]{1,0:T(8,128)}, f32[24,64]{1,0:T(8,128)}, f32[1,24]{1,0:T(1,128)}, f32[24,64]{1,0:T(8,128)}, /*index=5*/f32...) custom-call(f32[24,128]{1,0:T(8,128)S(1)} %get-tuple-element.114.own_ref, ...), custom_call_target="tpu_custom_call" | custom-call | bytes 6000000 | tf_op jit(solution)/shard_map/mixer_chain/pallas_call | solution.py:719
  97.6 0.0 collective-permute-done.17.refs_1_
  97.6 2.2 %collective-permute-done.18.refs_2_ = bf16[48,896]{1,0:T(8,128)(2,1)S(1)} collective-permute-done((bf16[48,896]{1,0:T(8,128)(2,1)S(1)}, bf16[48,896]{1,0:T(8,128)(2,1)S(1)}, u32[]{:S(2)}, u32[]{:S(2)}) %collective-permute-start.18) | collective-permute-done | bytes 86048 | tf_op jit(solution)/shard_map/ppermute | solution.py:589
  99.9 0.0 collective-permute-done.19.refs_3_
  99.9 0.1 collective-permute-start.21
  100.0 1.4 %collective-permute-done.21.other_ref = f32[48,896]{1,0:T(8,128)S(1)} collective-permute-done((f32[48,896]{1,0:T(8,128)S(1)}, f32[48,896]{1,0:T(8,128)S(1)}, u32[]{:S(2)}, u32[]{:S(2)}) %collective-permute-start.21) | collective-permute-done | bytes 172064 | tf_op jit(solution)/shard_map/ppermute | solution.py:588
  101.4 0.8 finish.1
  (19 shorter events, 0.2 us)
Async XLA Ops:
  1.8 11.3 %collective-permute-start.2 = (bf16[48,896]{1,0:T(8,128)(2,1)S(1)}, bf16[48,896]{1,0:T(8,128)(2,1)S(1)}, u32[]{:S(2)}, u32[]{:S(2)}) collective-permute-start(bf16[48,896]{1,0:T(8,128)(2,1)S(1)} %pack.1), channel_id=1, source_target_pairs={{0,12},{1,13},{2,14},{3,15},{4,8},{5,9},{6,10},{7,11},{8,4},{9,5},... | collective-permute-start | bytes 258056 | tf_op jit(solution)/shard_map/ppermute | solution.py:589
  6.9 7.2 %collective-permute-start.1 = (bf16[48,896]{1,0:T(8,128)(2,1)S(1)}, bf16[48,896]{1,0:T(8,128)(2,1)S(1)}, u32[]{:S(2)}, u32[]{:S(2)}) collective-permute-start(bf16[48,896]{1,0:T(8,128)(2,1)S(1)} %pack.1), channel_id=1, source_target_pairs={{0,8},{1,9},{2,10},{3,11},{4,12},{5,13},{6,14},{7,15},{8,0},{9,1},... | collective-permute-start | bytes 258056 | tf_op jit(solution)/shard_map/ppermute | solution.py:589
  6.9 7.2 %collective-permute-start = (bf16[48,896]{1,0:T(8,128)(2,1)S(1)}, bf16[48,896]{1,0:T(8,128)(2,1)S(1)}, u32[]{:S(2)}, u32[]{:S(2)}) collective-permute-start(bf16[48,896]{1,0:T(8,128)(2,1)S(1)} %pack.1), channel_id=1, source_target_pairs={{0,4},{1,5},{2,6},{3,7},{4,0},{5,1},{6,2},{7,3},{8,12},{9,13},{10,... | collective-permute-start | bytes 258056 | tf_op jit(solution)/shard_map/ppermute | solution.py:589
  14.1 32.5 %all-to-all-start = ((bf16[16,2,24,512]{3,2,1,0:T(8,128)(2,1)}), bf16[16,2,24,512]{3,2,1,0:T(8,128)(2,1)S(1)}, u32[]{:S(2)}, u32[]{:S(2)}) async-start(bf16[16,2,24,512]{3,2,1,0:T(8,128)(2,1)} %get-tuple-element.82), calls=%async_computation | async-start | bytes 1572864 | tf_op jit(solution)/shard_map/all_to_all | solution.py:590
  20.2 26.4 %copy-start.2 = (bf16[192,896]{1,0:T(8,128)(2,1)}, bf16[192,896]{1,0:T(8,128)(2,1)S(1)}, u32[]{:S(2)}) copy-start(bf16[192,896]{1,0:T(8,128)(2,1)S(1)} %constant_dynamic-update-slice_fusion.refs_0_) | copy-start | bytes 1032196
  20.3 16.0 %collective-permute-start.4 = (bf16[192,896]{1,0:T(8,128)(2,1)S(1)}, bf16[192,896]{1,0:T(8,128)(2,1)S(1)}, u32[]{:S(2)}, u32[]{:S(2)}) collective-permute-start(bf16[192,896]{1,0:T(8,128)(2,1)S(1)} %constant_dynamic-update-slice_fusion.refs_0_), channel_id=1, source_target_pairs={{0,2},{1,3},{2,0},{3,1},{4,6},{5,7},{6,4},{7,5},{8,10},{9,11},{10,... | collective-permute-start | bytes 1032200 | tf_op jit(solution)/shard_map/ppermute | solution.py:589
  22.2 14.1 %collective-permute-start.3 = (bf16[192,896]{1,0:T(8,128)(2,1)S(1)}, bf16[192,896]{1,0:T(8,128)(2,1)S(1)}, u32[]{:S(2)}, u32[]{:S(2)}) collective-permute-start(bf16[192,896]{1,0:T(8,128)(2,1)S(1)} %constant_dynamic-update-slice_fusion.refs_0_), channel_id=1, source_target_pairs={{0,1},{1,0},{2,3},{3,2},{4,5},{5,4},{6,7},{7,6},{8,9},{9,8},{10,11... | collective-permute-start | bytes 1032200 | tf_op jit(solution)/shard_map/ppermute | solution.py:589
  23.7 19.9 %collective-permute-start.7 = (bf16[192,896]{1,0:T(8,128)(2,1)S(1)}, bf16[192,896]{1,0:T(8,128)(2,1)S(1)}, u32[]{:S(2)}, u32[]{:S(2)}) collective-permute-start(bf16[192,896]{1,0:T(8,128)(2,1)S(1)} %constant_dynamic-update-slice_fusion.refs_0_), channel_id=1, source_target_pairs={{0,16},{16,0},{1,17},{17,1},{2,18},{18,2},{3,19},{19,3},{4,20},{20... | collective-permute-start | bytes 1032200 | tf_op jit(solution)/shard_map/ppermute | solution.py:588
  36.3 10.3 %copy-start = (bf16[192,896]{1,0:T(8,128)(2,1)}, bf16[192,896]{1,0:T(8,128)(2,1)S(1)}, u32[]{:S(2)}) copy-start(bf16[192,896]{1,0:T(8,128)(2,1)S(1)} %collective-permute-done.4.refs_2_) | copy-start | bytes 1032196
  36.3 10.3 %copy-start.1 = (bf16[192,896]{1,0:T(8,128)(2,1)}, bf16[192,896]{1,0:T(8,128)(2,1)S(1)}, u32[]{:S(2)}) copy-start(bf16[192,896]{1,0:T(8,128)(2,1)S(1)} %collective-permute-done.3.refs_1_) | copy-start | bytes 1032196
  36.3 6.0 %collective-permute-start.6 = (bf16[96,896]{1,0:T(8,128)(2,1)S(1)}, bf16[96,896]{1,0:T(8,128)(2,1)S(1)}, u32[]{:S(2)}, u32[]{:S(2)}) collective-permute-start(bf16[96,896]{1,0:T(8,128)(2,1)S(1)} %slice.13), channel_id=1, source_target_pairs={{0,1},{1,0},{2,3},{3,2},{4,5},{5,4},{6,7},{7,6},{8,9},{9,8},{10,11... | collective-permute-start | bytes 516104 | tf_op jit(solution)/shard_map/ppermute | solution.py:589
  37.9 5.6 %collective-permute-start.5 = (bf16[96,896]{1,0:T(8,128)(2,1)S(1)}, bf16[96,896]{1,0:T(8,128)(2,1)}, u32[]{:S(2)}, u32[]{:S(2)}) collective-permute-start(bf16[96,896]{1,0:T(8,128)(2,1)S(1)} %slice.12), channel_id=1, source_target_pairs={{0,2},{1,3},{2,0},{3,1},{4,6},{5,7},{6,4},{7,5},{8,10},{9,11},{10,... | collective-permute-start | bytes 516104 | tf_op jit(solution)/shard_map/ppermute | solution.py:589
  38.9 6.2 %collective-permute-start.8 = (bf16[192,896]{1,0:T(8,128)(2,1)S(1)}, bf16[192,896]{1,0:T(8,128)(2,1)S(1)}, u32[]{:S(2)}, u32[]{:S(2)}) collective-permute-start(bf16[192,896]{1,0:T(8,128)(2,1)S(1)} %collective-permute-done.3.refs_1_), channel_id=1, source_target_pairs={{0,16},{16,0},{1,17},{17,1},{2,18},{18,2},{3,19},{19,3},{4,20},{20... | collective-permute-start | bytes 1032200 | tf_op jit(solution)/shard_map/ppermute | solution.py:588
  38.9 6.2 %collective-permute-start.9 = (bf16[192,896]{1,0:T(8,128)(2,1)S(1)}, bf16[192,896]{1,0:T(8,128)(2,1)S(1)}, u32[]{:S(2)}, u32[]{:S(2)}) collective-permute-start(bf16[192,896]{1,0:T(8,128)(2,1)S(1)} %collective-permute-done.4.refs_2_), channel_id=1, source_target_pairs={{0,16},{16,0},{1,17},{17,1},{2,18},{18,2},{3,19},{19,3},{4,20},{20... | collective-permute-start | bytes 1032200 | tf_op jit(solution)/shard_map/ppermute | solution.py:588
  42.3 2.8 %copy-start.6 = (bf16[96,896]{1,0:T(8,128)(2,1)}, bf16[96,896]{1,0:T(8,128)(2,1)S(1)}, u32[]{:S(2)}) copy-start(bf16[96,896]{1,0:T(8,128)(2,1)S(1)} %collective-permute-done.6.refs_4_) | copy-start | bytes 516100
  42.3 1.4 %collective-permute-start.11 = (bf16[96,896]{1,0:T(8,128)(2,1)S(1)}, bf16[96,896]{1,0:T(8,128)(2,1)S(1)}, u32[]{:S(2)}, u32[]{:S(2)}) collective-permute-start(bf16[96,896]{1,0:T(8,128)(2,1)S(1)} %collective-permute-done.6.refs_4_), channel_id=1, source_target_pairs={{0,16},{16,0},{1,17},{17,1},{2,18},{18,2},{3,19},{19,3},{4,20},{20... | collective-permute-start | bytes 516104 | tf_op jit(solution)/shard_map/ppermute | solution.py:588
  43.5 1.6 %collective-permute-start.10 = (bf16[96,896]{1,0:T(8,128)(2,1)}, bf16[96,896]{1,0:T(8,128)(2,1)S(1)}, u32[]{:S(2)}, u32[]{:S(2)}) collective-permute-start(bf16[96,896]{1,0:T(8,128)(2,1)} %collective-permute-done.5.refs_3_), channel_id=1, source_target_pairs={{0,16},{16,0},{1,17},{17,1},{2,18},{18,2},{3,19},{19,3},{4,20},{20... | collective-permute-start | bytes 516104 | tf_op jit(solution)/shard_map/ppermute | solution.py:588
  43.6 1.6 %copy-start.3 = (bf16[192,896]{1,0:T(8,128)(2,1)}, bf16[192,896]{1,0:T(8,128)(2,1)S(1)}, u32[]{:S(2)}) copy-start(bf16[192,896]{1,0:T(8,128)(2,1)S(1)} %collective-permute-done.7.refs_5_) | copy-start | bytes 1032196
  43.7 1.4 %copy-start.7 = (bf16[96,896]{1,0:T(8,128)(2,1)}, bf16[96,896]{1,0:T(8,128)(2,1)S(1)}, u32[]{:S(2)}) copy-start(bf16[96,896]{1,0:T(8,128)(2,1)S(1)} %collective-permute-done.11.refs_9_) | copy-start | bytes 516100
  45.1 0.7 copy-start.8
  45.1 0.8 copy-start.4
  45.9 0.7 copy-start.5
  55.7 5.9 %collective-permute-start.12 = (bf16[768,896]{1,0:T(8,128)(2,1)}, bf16[768,896]{1,0:T(8,128)(2,1)S(1)}, u32[]{:S(2)}, u32[]{:S(2)}) collective-permute-start(bf16[768,896]{1,0:T(8,128)(2,1)} %get-tuple-element.94), channel_id=1, source_target_pairs={{0,16},{16,0},{1,17},{17,1},{2,18},{18,2},{3,19},{19,3},{4,20},{20... | collective-permute-start | bytes 4128776 | tf_op jit(solution)/shard_map/ppermute | solution.py:588
  55.9 25.8 %all-to-all-start.1 = ((bf16[16,2,24,512]{3,2,1,0:T(8,128)(2,1)}), bf16[16,2,24,512]{3,2,1,0:T(8,128)(2,1)S(1)}, u32[]{:S(2)}, u32[]{:S(2)}) async-start(bf16[16,2,24,512]{3,2,1,0:T(8,128)(2,1)} %get-tuple-element.89), calls=%async_computation.1 | async-start | bytes 1572864 | tf_op jit(solution)/shard_map/all_to_all | solution.py:590
  61.7 12.1 %collective-permute-start.13 = (bf16[96,896]{1,0:T(8,128)(2,1)S(1)}, bf16[96,896]{1,0:T(8,128)(2,1)S(1)}, u32[]{:S(2)}, u32[]{:S(2)}) collective-permute-start(bf16[96,896]{1,0:T(8,128)(2,1)S(1)} %get-tuple-element.99), channel_id=1, source_target_pairs={{0,2},{1,3},{2,0},{3,1},{4,6},{5,7},{6,4},{7,5},{8,10},{9,11},{10,... | collective-permute-start | bytes 516104 | tf_op jit(solution)/shard_map/ppermute | solution.py:589
  63.7 10.1 %collective-permute-start.14 = (bf16[96,896]{1,0:T(8,128)(2,1)S(1)}, bf16[96,896]{1,0:T(8,128)(2,1)S(1)}, u32[]{:S(2)}, u32[]{:S(2)}) collective-permute-start(bf16[96,896]{1,0:T(8,128)(2,1)S(1)} %get-tuple-element.100), channel_id=1, source_target_pairs={{0,1},{1,0},{2,3},{3,2},{4,5},{5,4},{6,7},{7,6},{8,9},{9,8},{10,11... | collective-permute-start | bytes 516104 | tf_op jit(solution)/shard_map/ppermute | solution.py:589
  74.8 14.4 %collective-permute-start.15 = (bf16[192,896]{1,0:T(8,128)(2,1)}, bf16[192,896]{1,0:T(8,128)(2,1)S(1)}, u32[]{:S(2)}, u32[]{:S(2)}) collective-permute-start(bf16[192,896]{1,0:T(8,128)(2,1)} %get-tuple-element.103), channel_id=1, source_target_pairs={{0,1},{1,0},{2,3},{3,2},{4,5},{5,4},{6,7},{7,6},{8,9},{9,8},{10,11... | collective-permute-start | bytes 1032200 | tf_op jit(solution)/shard_map/ppermute | solution.py:589
  76.8 12.4 %collective-permute-start.16 = (bf16[192,896]{1,0:T(8,128)(2,1)}, bf16[192,896]{1,0:T(8,128)(2,1)S(1)}, u32[]{:S(2)}, u32[]{:S(2)}) collective-permute-start(bf16[192,896]{1,0:T(8,128)(2,1)} %get-tuple-element.104), channel_id=1, source_target_pairs={{0,2},{1,3},{2,0},{3,1},{4,6},{5,7},{6,4},{7,5},{8,10},{9,11},{10,... | collective-permute-start | bytes 1032200 | tf_op jit(solution)/shard_map/ppermute | solution.py:589
  89.4 8.2 %collective-permute-start.17 = (bf16[48,896]{1,0:T(8,128)(2,1)S(1)}, bf16[48,896]{1,0:T(8,128)(2,1)S(1)}, u32[]{:S(2)}, u32[]{:S(2)}) collective-permute-start(bf16[48,896]{1,0:T(8,128)(2,1)S(1)} %get-tuple-element.111), channel_id=1, source_target_pairs={{0,4},{1,5},{2,6},{3,7},{4,0},{5,1},{6,2},{7,3},{8,12},{9,13},{10,... | collective-permute-start | bytes 258056 | tf_op jit(solution)/shard_map/ppermute | solution.py:589
  92.0 7.9 %collective-permute-start.18 = (bf16[48,896]{1,0:T(8,128)(2,1)S(1)}, bf16[48,896]{1,0:T(8,128)(2,1)S(1)}, u32[]{:S(2)}, u32[]{:S(2)}) collective-permute-start(bf16[48,896]{1,0:T(8,128)(2,1)S(1)} %get-tuple-element.112), channel_id=1, source_target_pairs={{0,8},{1,9},{2,10},{3,11},{4,12},{5,13},{6,14},{7,15},{8,0},{9,1},... | collective-permute-start | bytes 258056 | tf_op jit(solution)/shard_map/ppermute | solution.py:589
  92.4 7.5 %collective-permute-start.19 = (bf16[48,896]{1,0:T(8,128)(2,1)S(1)}, bf16[48,896]{1,0:T(8,128)(2,1)S(1)}, u32[]{:S(2)}, u32[]{:S(2)}) collective-permute-start(bf16[48,896]{1,0:T(8,128)(2,1)S(1)} %get-tuple-element.113), channel_id=1, source_target_pairs={{0,12},{1,13},{2,14},{3,15},{4,8},{5,9},{6,10},{7,11},{8,4},{9,5},... | collective-permute-start | bytes 258056 | tf_op jit(solution)/shard_map/ppermute | solution.py:589
  94.4 1.2 %collective-permute-start.20 = (f32[24,128]{1,0:T(8,128)S(1)}, f32[24,128]{1,0:T(8,128)S(1)}, u32[]{:S(2)}, u32[]{:S(2)}) collective-permute-start(f32[24,128]{1,0:T(8,128)S(1)} %get-tuple-element.114.own_ref), channel_id=1, source_target_pairs={{0,16},{16,0},{1,17},{17,1},{2,18},{18,2},{3,19},{19,3},{4,20},{20... | collective-permute-start | bytes 36872 | tf_op jit(solution)/shard_map/ppermute | solution.py:588
  99.9 1.5 %collective-permute-start.21 = (f32[48,896]{1,0:T(8,128)S(1)}, f32[48,896]{1,0:T(8,128)S(1)}, u32[]{:S(2)}, u32[]{:S(2)}) collective-permute-start(f32[48,896]{1,0:T(8,128)S(1)} %join.3.mine_ref), channel_id=1, source_target_pairs={{0,16},{16,0},{1,17},{17,1},{2,18},{18,2},{3,19},{19,3},{4,20},{20... | collective-permute-start | bytes 516104 | tf_op jit(solution)/shard_map/ppermute | solution.py:588

commit v4 on v3

--- a/solution.py
+++ b/solution.py
@@ -209,7 +209,7 @@
 
 def backward_kernel(
     heights, widths, feat_ref, cot_ref, both_ref, rows_ref, scale_ref, bias_ref,
-    result_ref, gfeat_ref, small_ref,
+    step_h, step_w, rate_h, rate_w, read_h, read_w, result_ref, gfeat_ref, small_ref,
     slots, slots_g, high_a, low_a, field, field_g, tall, high_d, low_d, wide_ref, sums,
 ):
     channels, cells = feat_ref.shape
@@ -334,17 +334,19 @@
         grad = read_slots(slots_g, image, channels)
         value = read_slots(slots, image, channels) + skip * grad
         gfeat_ref[:, span] = cot_ref[:, span].astype(F32) + jnp.where(inside, value, 0.0)
-    small_ref[...] = small + sums[0:channels]
-
-
-def chain_kernel(
-    own_ref, other_ref, step_h, step_w, rate_h, rate_w, read_h, read_w, scale_ref,
-    gstep_h, grate_h, gread_h, gstep_w, grate_w, gread_w, gskip, gbias, gscale,
-):
-    total = own_ref[...] + other_ref[...]
-    for first, step, rate, read, gstep, grate, gread in (
-        (0, step_h, rate_h, read_h, gstep_h, grate_h, gread_h),
-        (SIDE, step_w, rate_w, read_w, gstep_w, grate_w, gread_w),
+    small = small + sums[0:channels]
+    states, small = chain(small, step_h, step_w, rate_h, rate_w, read_h, read_w)
+    for index in range(2):
+        pair = jnp.concatenate(states[2 * index : 2 * index + 2], axis=1)
+        small_ref[:, index * pair.shape[1] : (index + 1) * pair.shape[1]] = pair
+    small_ref[:, 2 * pair.shape[1] :] = small
+
+
+def chain(total, step_h, step_w, rate_h, rate_w, read_h, read_w):
+    out, tail = [], total
+    lane = lane_of(total.shape[0])
+    for place, first, step, rate, read in (
+        (67, 0, step_h, rate_h, read_h), (68, SIDE, step_w, rate_w, read_w),
     ):
         pace = jnp.exp(column(step[...]))
         decay = pace * rate[...]
@@ -356,12 +358,9 @@
             if lag:
                 to_decay = to_decay - float(lag) * term
         to_decay = to_decay * read[...]
-        gread[...] = to_read
-        grate[...] = pace * to_decay
-        gstep[...] = as_row(jnp.sum(to_decay * decay, axis=1, keepdims=True))
-    gskip[...] = as_row(total[:, 64:65])
-    gscale[...] = as_row(total[:, 65:66])
-    gbias[...] = as_row(total[:, 66:67]) * scale_ref[...]
+        out += [to_read, pace * to_decay]
+        tail = jnp.where(lane == place, jnp.sum(to_decay * decay, axis=1, keepdims=True), tail)
+    return out, tail
 
 
 def join_kernel(count, *refs):
@@ -375,6 +374,12 @@
         out[...] = total.astype(out.dtype)
 
 
+def cut_kernel(one_ref, two_ref, first_ref, second_ref):
+    cut = first_ref.shape[0]
+    first_ref[...] = one_ref[:cut]
+    second_ref[...] = two_ref[cut:]
+
+
 def relay_kernel(one_ref, two_ref, arrived_ref, first_ref, second_ref, out_one, out_two):
     tall = one_ref.shape[0]
     cut = tall // 2
@@ -386,9 +391,13 @@
     out_two[cut:] = (two[cut:] + second_ref[...].astype(F32)).astype(BF16)
 
 
-def finish_kernel(half, mine_ref, other_ref, ggain, gshift, gin, ginb, gout):
+def finish_kernel(
+    half, mine_ref, other_ref, small_ref, sibling_ref, scale_ref,
+    gstep_h, grate_h, gread_h, gstep_w, grate_w, gread_w, gskip, ggain, gshift, gin, ginb, gout,
+    gbias, gscale,
+):
     units, count = gin.shape
-    channels = ggain.shape[1]
+    channels, states = grate_h.shape
     keep = units // 2
     first = half[0] == 0
     mine, other = mine_ref[...], other_ref[...]
@@ -402,6 +411,15 @@
     norms = (mine[:, 2 * count :] + other[:, 2 * count :])[:channels]
     ggain[...] = as_row(norms[:, 1:2])
     gshift[...] = as_row(norms[:, 2:3])
+    total = small_ref[...] + sibling_ref[...]
+    for index, ref in enumerate((gread_h, grate_h, gread_w, grate_w)):
+        ref[...] = total[:, index * states : (index + 1) * states]
+    total = total[:, 4 * states :]
+    gskip[...] = as_row(total[:, 64:65])
+    gscale[...] = as_row(total[:, 65:66])
+    gbias[...] = as_row(total[:, 66:67]) * scale_ref[...]
+    gstep_h[...] = as_row(total[:, 67:68])
+    gstep_w[...] = as_row(total[:, 68:69])
 
 
 def pack_kernel(half, in_ref, out_ref, bias_ref, gain_ref, shift_ref, pack_ref):
@@ -434,91 +452,107 @@
 ROOT = math.sqrt(2.0 / math.pi)
 
 
-def mlp_kernel(near, pieces, where_ref, given_ref, *refs):
+def perceptron(refs, act, down):
+    count = act.shape[0]
+    w_in = jnp.concatenate([ref[:, :count] for ref in refs], axis=0)
+    w_out = jnp.concatenate([ref[:, count : 2 * count] for ref in refs], axis=0)
+    bias = jnp.concatenate([ref[:, 2 * count :] for ref in refs], axis=0).astype(F32)[:, 0:1]
+    v = dot(w_in, act) + bias
+    square = v * v
+    half = 0.5 * jnp.tanh(v * (ROOT * 0.044715 * square + ROOT)) + 0.5
+    full = v * half
+    hidden = full.astype(BF16)
+    slope = half + full * (1.0 - half) * (6.0 * ROOT * 0.044715 * square + 2.0 * ROOT)
+    low = (dot(w_out, down) * slope).astype(BF16)
+    g_bias = jnp.sum(low.astype(F32), axis=1, keepdims=True)
+    g_bias = jnp.where(lane_of(low.shape[0]) == 0, g_bias, 0.0)
+    grads = (dot(low, act, NT), dot(hidden, down, NT), g_bias)
+    return dot(w_out, hidden, TN), dot(w_in, low, TN), grads
+
+
+def put(ref, grads, start):
+    count = grads[0].shape[1]
+    at = slice(start, start + ref.shape[0])
+    ref[:, :count] = grads[0][at].astype(BF16)
+    ref[:, count : 2 * count] = grads[1][at].astype(BF16)
+    ref[:, 2 * count :] = grads[2][at].astype(BF16)
+    return start + ref.shape[0]
+
+
+def spots_of(near, devices, deep, where_ref):
+    z, xy = where_ref[0], where_ref[1]
+    for d in range(devices):
+        spot = ((d % near) ^ xy) * (devices // near) + ((d // near) ^ z)
+        yield d, pl.multiple_of(spot * deep, deep)
+
+
+def mlp_first(near, pieces, where_ref, given_ref, *refs):
     own_in, refs = refs[:pieces], refs[pieces:]
     other_in, refs = refs[:pieces], refs[pieces:]
-    both_ref, refs = refs[0], refs[1:]
-    own_out, refs = refs[:pieces], refs[pieces:]
-    gother_ref, active, downs, normal, gains, sum_acc, grad_acc, ext, gext = refs
-    count, tokens = normal.shape
-    devices, _, channels, _ = both_ref.shape
-    spans, rows = [], 0
-    for ref in own_in:
-        spans.append(slice(rows, rows + ref.shape[0]))
-        rows += ref.shape[0]
-    deep = rows // devices
+    gother_ref, active, downs, normal, inv_ref, gains, sum_ref, grad_ref, ext = refs
+    devices, _, channels, _ = given_ref.shape
+    deep = ext.shape[0] // devices
+    count = active.shape[0]
 
     value = jnp.concatenate([given_ref[d, 0].astype(F32) for d in range(devices)], axis=0)
     mean = jnp.mean(value, axis=0, keepdims=True)
     value = value - mean
     inv = lax.rsqrt(jnp.mean(value * value, axis=0, keepdims=True) + EPS)
-    normal[...] = value * inv
-    value = jnp.concatenate([given_ref[d, 1].astype(F32) for d in range(devices)], axis=0)
-    downs[...] = value.astype(BF16)
-    for at, ref in zip(spans, own_in):
-        ext[at] = ref[:, 2 * count :].astype(F32)
-    z, xy = where_ref[0], where_ref[1]
-    spots = []
-    for d in range(devices):
-        spot = ((d % near) ^ xy) * (devices // near) + ((d // near) ^ z)
-        spot = pl.multiple_of(spot * deep, deep)
-        spots.append(spot)
+    value = value * inv
+    normal[...] = value
+    inv_ref[...] = inv
+    down = jnp.concatenate([given_ref[d, 1].astype(F32) for d in range(devices)], axis=0)
+    downs[...] = down.astype(BF16)
+    at = 0
+    for ref in own_in:
+        ext[at : at + ref.shape[0]] = ref[:, 2 * count :].astype(F32)
+        at += ref.shape[0]
+    for d, spot in spots_of(near, devices, deep, where_ref):
         gains[d * channels : (d + 1) * channels] = ext[pl.ds(spot, deep), :][:channels]
-    active[...] = (normal[...] * gains[:, 1:2] + gains[:, 2:3]).astype(BF16)
-
-    def process(refs, first):
-        w_in = jnp.concatenate([ref[:, :count] for ref in refs], axis=0)
-        w_out = jnp.concatenate([ref[:, count : 2 * count] for ref in refs], axis=0)
-        bias = jnp.concatenate([ref[:, 2 * count :] for ref in refs], axis=0).astype(F32)[:, 0:1]
-        act = active[...]
-        down = downs[...]
-        v = dot(w_in, act) + bias
-        square = v * v
-        half = 0.5 * jnp.tanh(v * (ROOT * 0.044715 * square + ROOT)) + 0.5
-        full = v * half
-        hidden = full.astype(BF16)
-        slope = half + full * (1.0 - half) * (6.0 * ROOT * 0.044715 * square + 2.0 * ROOT)
-        low = (dot(w_out, down) * slope).astype(BF16)
-        if first:
-            sum_acc[...] = dot(w_out, hidden, TN)
-            grad_acc[...] = dot(w_in, low, TN)
-        else:
-            sum_acc[...] += dot(w_out, hidden, TN)
-            grad_acc[...] += dot(w_in, low, TN)
-        g_bias = jnp.sum(low.astype(F32), axis=1, keepdims=True)
-        g_bias = jnp.where(lane_of(low.shape[0]) == 0, g_bias, 0.0)
-        return dot(low, act, NT), dot(hidden, down, NT), g_bias
-
-    g_in, g_out, g_bias = process(other_in, True)
-    gother_ref[:, :count] = g_in.astype(BF16)
-    gother_ref[:, count : 2 * count] = g_out.astype(BF16)
-    gother_ref[:, 2 * count :] = g_bias.astype(BF16)
-    g_in, g_out, g_bias = process(own_in, False)
-    gext[...] = g_bias
-    for at, ref in zip(spans, own_out):
-        ref[:, :count] = g_in[at].astype(BF16)
-        ref[:, count : 2 * count] = g_out[at].astype(BF16)
-
-    agrad = grad_acc[...]
-    norm = normal[...]
+    active[...] = (value * gains[:, 1:2] + gains[:, 2:3]).astype(BF16)
+    sums, total, grads = perceptron(other_in, active[...], downs[...])
+    put(gother_ref, grads, 0)
+    sum_ref[...] = sums
+    grad_ref[...] = total
+
+
+def mlp_second(
+    near, pieces, where_ref, active, downs, normal_ref, inv_ref, gains, sum_ref, grad_ref, *refs
+):
+    own_in, refs = refs[:pieces], refs[pieces:]
+    both_ref, refs = refs[0], refs[1:]
+    own_out, (gext,) = refs[:pieces], refs[pieces:]
+    count = active.shape[0]
+    devices, _, channels, _ = both_ref.shape
+    deep = gext.shape[0] // devices
+
+    sums, total, grads = perceptron(own_in, active[...], downs[...])
+    gext[...] = grads[2]
+    start = 0
+    for ref in own_out:
+        start = put(ref, grads, start)
+    summed = sum_ref[...] + sums
+    agrad = grad_ref[...] + total
+    norm = normal_ref[...]
     scaled = agrad * gains[:, 1:2]
     first = jnp.mean(scaled, axis=0, keepdims=True)
     second = jnp.mean(scaled * norm, axis=0, keepdims=True)
-    mgrad = (scaled - first - norm * second) * inv
-    summed = sum_acc[...]
+    mgrad = (scaled - first - norm * second) * inv_ref[...]
     for d in range(devices):
         both_ref[d, 0] = mgrad[d * channels : (d + 1) * channels].astype(BF16)
         both_ref[d, 1] = summed[d * channels : (d + 1) * channels].astype(BF16)
     lane = lane_of(count)
     tile = jnp.where(lane == 1, jnp.sum(agrad * norm, axis=1, keepdims=True), 0.0)
     tile = jnp.where(lane == 2, jnp.sum(agrad, axis=1, keepdims=True), tile)
-    for d in range(devices):
+    for d, spot in spots_of(near, devices, deep, where_ref):
         part = tile[d * channels : (d + 1) * channels]
         if channels < deep:
             part = jnp.concatenate([part, jnp.zeros((deep - channels, LANES), F32)], axis=0)
-        gext[pl.ds(spots[d], deep), :] += part
-    for at, ref in zip(spans, own_out):
-        ref[:, 2 * count :] = gext[at].astype(BF16)
+        gext[pl.ds(spot, deep), :] += part
+    start = 0
+    for ref in own_out:
+        ref[:, 2 * count :] = gext[start : start + ref.shape[0]].astype(BF16)
+        start += ref.shape[0]
 
 
 def whole(shape):
@@ -544,7 +578,7 @@
         in_specs=[full] * len(arrays),
         out_specs=[full] * count,
         compiler_params=params(8),
-        cost_estimate=cost(1),
+        cost_estimate=pl.CostEstimate(flops=1 if count > 1 else 1, transcendentals=0, bytes_accessed=1_000_000),
         name="join",
     )(*arrays)
 
@@ -558,7 +592,7 @@
         in_specs=[full] * 5,
         out_specs=(full, full),
         compiler_params=params(8),
-        cost_estimate=cost(1),
+        cost_estimate=pl.CostEstimate(flops=100_000_000_000, transcendentals=0, bytes_accessed=1_000_000),
         name="relay",
     )(*arrays)
 
@@ -607,13 +641,13 @@
         half.reshape(1), pin(in_weight.T), pin(out_weight), pin(row(in_bias)), pin(row(norm_gain)),
         pin(row(norm_shift)),
     )
-    pack, features_after = lax.optimization_barrier((pack, features))
+    pack, features_after = pair(pack, features)
     shards = [pack] + [flip(pack, bits * near) for bits in range(1, far)]
 
     groups = -(-channels // SLOT)
-    slots = pltpu.VMEM((groups, images * TILES * SLOT, LANES), F32)
     square = (SLOT * SIDE, images // PER * LANES)
     toeplitz = pltpu.VMEM((SLOT * SIDE, SLOT * SIDE), BF16)
+    slots = pltpu.VMEM((groups, images * TILES * SLOT, LANES), F32)
     both_shape = (ch, 2, channels, tokens)
     given, taps = pl.pallas_call(
         forward_kernel,
@@ -634,13 +668,22 @@
         pin(row(step_height)), pin(row(step_width)), pin(rate_height), pin(rate_width),
         pin(readout_height), pin(readout_width), pin(row(skip_gain)),
     )
-    given, *shards = lax.optimization_barrier((given, *shards))
+    given, *shards = pair(given, *shards)
     given = swap(given)
     shard = jnp.concatenate(shards, axis=0)
     if near == 4:
         cut = far * deep // 2
         beside, above = pair(flip(shard, 1), flip(shard, 2))
-        own = [shard, beside, above, flip(beside[:cut], 2), flip(above[cut:], 1)]
+        ends = pl.pallas_call(
+            cut_kernel,
+            out_shape=[jax.ShapeDtypeStruct((cut, width), BF16)] * 2,
+            in_specs=[full] * 2,
+            out_specs=[full] * 2,
+            compiler_params=params(4),
+            cost_estimate=pl.CostEstimate(flops=100_000_000_000, transcendentals=0, bytes_accessed=1_000_000),
+            name="ends",
+        )(beside, above)
+        own = [shard, beside, above, flip(ends[0], 2), flip(ends[1], 1)]
         where = jnp.stack([place // near, place % near])
     else:
         own = [swap(jnp.broadcast_to(shard[None], (near,) + shard.shape), near_groups)]
@@ -650,30 +693,34 @@
 
     rows = ch * deep
     pieces = len(own)
-    outs = pl.pallas_call(
-        partial(mlp_kernel, near, pieces),
+    plane = jax.ShapeDtypeStruct((count, tokens), F32)
+    token_low = jax.ShapeDtypeStruct((count, tokens), BF16)
+    gother, *state = pl.pallas_call(
+        partial(mlp_first, near, pieces),
+        out_shape=[
+            jax.ShapeDtypeStruct((rows, width), BF16), token_low, token_low, plane,
+            jax.ShapeDtypeStruct((1, tokens), F32), jax.ShapeDtypeStruct((count, LANES), F32),
+            plane, plane,
+        ],
+        in_specs=[SMEM] + [full] * (1 + 2 * pieces),
+        out_specs=[full] * 8,
+        scratch_shapes=[pltpu.VMEM((rows, LANES), F32)],
+        compiler_params=params(16),
+        cost_estimate=cost(5),
+        name="mlp_first",
+    )(where, given, *own, *map(pin, other))
+    arrived = exchange(gother)
+    both, *gown = pl.pallas_call(
+        partial(mlp_second, near, pieces),
         out_shape=[jax.ShapeDtypeStruct(both_shape, BF16)]
-        + [jax.ShapeDtypeStruct(piece.shape, BF16) for piece in own]
-        + [jax.ShapeDtypeStruct((rows, width), BF16)],
-        in_specs=[SMEM] + [full] * (2 * pieces + 1),
-        out_specs=[full] * (pieces + 2),
-        scratch_shapes=[
-            pltpu.VMEM((count, tokens), BF16),
-            pltpu.VMEM((count, tokens), BF16),
-            pltpu.VMEM((count, tokens), F32),
-            pltpu.VMEM((count, LANES), F32),
-            pltpu.VMEM((count, tokens), F32),
-            pltpu.VMEM((count, tokens), F32),
-            pltpu.VMEM((rows, LANES), F32),
-            pltpu.VMEM((rows, LANES), F32),
-        ],
-        compiler_params=params(24),
-        cost_estimate=cost(8),
-        name="mlp",
-    )(where, given, *map(pin, own), *map(pin, other))
-    both, gown, gother = outs[0], outs[1:-1], outs[-1]
-
-    arrived = exchange(gother)
+        + [jax.ShapeDtypeStruct(piece.shape, BF16) for piece in own],
+        in_specs=[SMEM] + [full] * (7 + pieces),
+        out_specs=[full] * (1 + pieces),
+        scratch_shapes=[pltpu.VMEM((rows, LANES), F32)],
+        compiler_params=params(16),
+        cost_estimate=cost(5),
+        name="mlp_second",
+    )(where, *state, *own)
     both = swap(both)
     tall = far * deep
     if near == 4:
@@ -688,19 +735,21 @@
         sent = list(swap(total.reshape(near, tall, width), near_groups))
         first, second, *sent = sent
     landed = [first, second, *sent]
+    shards = join(deep, landed, far)
+    shards = [shards[0]] + [flip(v, (i + 1) * near) for i, v in enumerate(shards[1:])]
     result, grad_features, small = pl.pallas_call(
         backward_kernel,
         out_shape=(
             jax.ShapeDtypeStruct((channels, cells), BF16),
             jax.ShapeDtypeStruct((channels, cells), F32),
-            jax.ShapeDtypeStruct((channels, LANES), F32),
+            jax.ShapeDtypeStruct((channels, LANES + 4 * states), F32),
         ),
-        in_specs=[SMEM, SMEM] + [full] * 6,
+        in_specs=[SMEM, SMEM] + [full] * 12,
         out_specs=(full,) * 3,
         scratch_shapes=[
-            slots, slots, toeplitz, toeplitz, pltpu.VMEM(square, BF16), pltpu.VMEM(square, BF16),
-            pltpu.VMEM((SLOT * SIDE, max(SLOT * SIDE, square[1])), F32), pltpu.VMEM(square, BF16),
-            pltpu.VMEM(square, BF16), pltpu.VMEM(square, F32),
+            slots, slots, toeplitz, toeplitz, pltpu.VMEM(square, BF16),
+            pltpu.VMEM(square, BF16), pltpu.VMEM((SLOT * SIDE, max(SLOT * SIDE, square[1])), F32),
+            pltpu.VMEM(square, BF16), pltpu.VMEM(square, BF16), pltpu.VMEM(square, F32),
             pltpu.VMEM((groups * SLOT, LANES), F32),
         ],
         compiler_params=params(16),
@@ -708,50 +757,30 @@
         name="mixer_backward",
     )(
         pin(heights), pin(widths), pin(features), pin(cotangent), both, taps,
-        pin(row(layer_scale)), pin(row(out_bias)),
+        pin(row(layer_scale)), pin(row(out_bias)), pin(row(step_height)), pin(row(step_width)),
+        pin(rate_height), pin(rate_width), pin(readout_height), pin(readout_width),
     )
-
-    *landed, small = lax.optimization_barrier((*landed, small))
-    shards = join(deep, landed, far)
-    shards = [shards[0]] + [flip(v, (i + 1) * near) for i, v in enumerate(shards[1:])]
+    *shards, small = pair(*shards, small)
+    (mine,) = join(deep, shards, 1)
     vector_out = jax.ShapeDtypeStruct((1, channels), F32)
     state_out = jax.ShapeDtypeStruct((channels, states), F32)
-    chained = pl.pallas_call(
-        chain_kernel,
-        out_shape=(
-            vector_out, state_out, state_out, vector_out, state_out, state_out,
-            vector_out, vector_out, vector_out,
-        ),
-        in_specs=[full] * 9,
-        out_specs=(full,) * 9,
-        compiler_params=params(4),
-        cost_estimate=cost(2),
-        name="mixer_chain",
-    )(
-        small, exchange(small), pin(row(step_height)), pin(row(step_width)), pin(rate_height),
-        pin(rate_width), pin(readout_height), pin(readout_width), pin(row(layer_scale)),
-    )
-    *shards, chained = lax.optimization_barrier((*shards, chained))
-    gstep_h, grate_h, gread_h, gstep_w, grate_w, gread_w, gskip, gbias, gscale = chained
-    (mine,) = join(deep, shards, 1)
-    ggain, gshift, gin, ginb, gout = pl.pallas_call(
+    weight_out = jax.ShapeDtypeStruct((units, count), F32)
+    outs = pl.pallas_call(
         finish_kernel,
         out_shape=(
-            vector_out, vector_out, jax.ShapeDtypeStruct((units, count), F32),
-            jax.ShapeDtypeStruct((1, units), F32), jax.ShapeDtypeStruct((units, count), F32),
+            vector_out, state_out, state_out, vector_out, state_out, state_out, vector_out,
+            vector_out, vector_out, weight_out, jax.ShapeDtypeStruct((1, units), F32), weight_out,
+            vector_out, vector_out,
         ),
-        in_specs=[SMEM, full, full],
-        out_specs=(full,) * 5,
+        in_specs=[SMEM] + [full] * 5,
+        out_specs=(full,) * 14,
         compiler_params=params(4),
         cost_estimate=cost(1),
         name="finish",
-    )(half.reshape(1), mine, exchange(mine))
-    flat = lambda v: v.reshape(-1)
-    return (
-        result, grad_features, flat(gstep_h), grate_h, gread_h, flat(gstep_w), grate_w, gread_w,
-        flat(gskip), flat(ggain), flat(gshift), gin.T, flat(ginb), gout, flat(gbias),
-        flat(gscale),
-    )
+    )(half.reshape(1), mine, exchange(mine), small, exchange(small), pin(row(layer_scale)))
+    outs = [v.reshape(-1) if v.shape[0] == 1 else v for v in outs]
+    outs[9] = outs[9].T
+    return (result, grad_features, *outs)
 
 
 def solution(mesh):

time: 103 us -> 92.9 us (0.902)
  starting transfers between devices: 35.7 us -> 31 us
  waiting for transfers between devices: 36.6 us -> 33.1 us
  local copies, waits for them, and re-layouts: 1.6 us -> 0.08 us
    ppermute x14, waiting for transfers between devices: 28.6 us -> 25.3 us  [per_device(): lax.ppermute(v, 'ch', [(i, i ^ bits) for i in range(ch)])]
    ppermute x14, starting transfers between devices: 23.2 us -> 20.1 us  [per_device(): lax.ppermute(v, 'ch', [(i, i ^ bits) for i in range(ch)])]
    all_to_all x2, starting transfers between devices: 11.7 us -> 9.22 us  [per_device(): lax.all_to_all(v, 'ch', split_axis=0, concat_axis=0, tiled=True, axis_ind...]
    ppermute x8, waiting for transfers between devices: 4.11 us -> 2.02 us  [per_device(): exchange = lambda v: lax.ppermute(v, 'img', [(0, 1), (1, 0)])]
    all_to_all x2, waiting for transfers between devices: 3.94 us -> 5.78 us  [per_device(): lax.all_to_all(v, 'ch', split_axis=0, concat_axis=0, tiled=True, axis_ind...]
    unnamed x21 -> x15, local copies, waits for them, and re-layouts: 1.56 us -> 0.06 us
    pallas_call x3 -> x4, Pallas kernels: 11.9 us -> 10.7 us  [the longest x1 4.75 us: per_device(): pl.pallas_call(partial(mlp_second, near, pieces), out_shape=[jax.ShapeDty...]
  transfers between devices with their start and end apart: 24 -> 24, of which waited for: 11 -> 11; matrix products, arithmetic and copies ran while one was open for 0% -> 0% of each run, Pallas kernels for 16% -> 21%
where the time goes in v4:
time: 92.9 us; the launch traced here: 92.4 us
  waiting for transfers between devices  33.1 us (36%)
  starting transfers between devices  31 us (33%)
  Pallas kernels  26.4 us (28%)
  between operations  0.95 us (1%)
    ppermute x14, waiting for transfers between devices, per_device(): lax.ppermute(v, 'ch', [(i, i ^ bits) for i in range(ch)])  25.3 us
    ppermute x14, starting transfers between devices, per_device(): lax.ppermute(v, 'ch', [(i, i ^ bits) for i in range(ch)])  20.1 us
    all_to_all x2, starting transfers between devices, per_device(): lax.all_to_all(v, 'ch', split_axis=0, concat_axis=0, tiled=True, axis_ind...  9.22 us
    pallas_call x1, Pallas kernels, per_device(): pl.pallas_call(backward_kernel, out_shape=(jax.ShapeDtypeStruct((channels...  7.62 us
    all_to_all x2, waiting for transfers between devices, per_device(): lax.all_to_all(v, 'ch', split_axis=0, concat_axis=0, tiled=True, axis_ind...  5.78 us
    pallas_call x1, Pallas kernels, per_device(): pl.pallas_call(forward_kernel, out_shape=(jax.ShapeDtypeStruct(both_shape...  5.54 us
    pallas_call x1, Pallas kernels, per_device(): pl.pallas_call(partial(mlp_second, near, pieces), out_shape=[jax.ShapeDty...  4.75 us
    pallas_call x1, Pallas kernels, per_device(): pl.pallas_call(partial(mlp_first, near, pieces), out_shape=[jax.ShapeDtyp...  4.49 us
  transfers between devices with their start and end apart: 24, of which 11 were waited for; matrix products, arithmetic and copies ran while one was open for 0% of the time, Pallas kernels for 21%

profile of v4, /device:TPU:0, one launch (start us, length us, event | category | flops | bytes accessed | tf_op | source)
XLA Modules:
  0.0 92.4 jit_solution(14254103563778310781)
XLA Ops:
  0.7 1.2 %pack.1 = bf16[48,896]{1,0:T(8,128)(2,1)S(1)} custom-call(s32[1]{0:T(128)} %bitcast.2.half, bf16[96,384]{1,0:T(8,128)(2,1)} %bitcast.21, bf16[96,384]{1,0:T(8,128)(2,1)} %out_ref.1, bf16[1,96]{1,0:T(2,128)(2,1)} %bitcast.29, bf16[1,24]{1,0:T(2,128)(2,1)} %bitcast.30, bf16[1,24]{1,0:T(2,128)(2,1)} %bitcast.31), custom_call_target="tpu_custom_call" | custom-call | bytes 6000000 | tf_op jit(solution)/shard_map/pack/pallas_call | solution.py:632
  1.8 5.1 %collective-permute-start.2 = (bf16[48,896]{1,0:T(8,128)(2,1)S(1)}, bf16[48,896]{1,0:T(8,128)(2,1)S(1)}, u32[]{:S(2)}, u32[]{:S(2)}) collective-permute-start(bf16[48,896]{1,0:T(8,128)(2,1)S(1)} %pack.1), channel_id=1, source_target_pairs={{0,12},{1,13},{2,14},{3,15},{4,8},{5,9},{6,10},{7,11},{8,4},{9,5},... | collective-permute-start | bytes 258056 | tf_op jit(solution)/shard_map/ppermute | solution.py:623
  6.9 0.0 collective-permute-start.1
  6.9 0.6 collective-permute-start
  7.6 5.5 %mixer_forward.1 = (bf16[16,2,24,512]{3,2,1,0:T(8,128)(2,1)}, f32[24,128]{1,0:T(8,128)S(1)}) custom-call(s32[8]{0:T(128)} %heights.3, s32[8]{0:T(128)} %widths.3, bf16[24,8192]{1,0:T(8,128)(2,1)} %feat_ref.2, bf16[24,8192]{1,0:T(8,128)(2,1)} %cot_ref.3, f32[1,24]{1,0:T(1,128)} %bitcast.22, f32[1,24]{1,0:T(1,128)} %bitcast.25, f32[1,24]{1,0:T(1,128)} %bitcast.27, ...), custom_call_target="tpu_custom_call" | custom-call | bytes 18000000 | tf_op jit(solution)/shard_map/mixer_forward/pallas_call | solution.py:652
  13.1 0.0 collective-permute-done.2
  13.1 1.0 %collective-permute-done.1 = bf16[48,896]{1,0:T(8,128)(2,1)S(1)} collective-permute-done((bf16[48,896]{1,0:T(8,128)(2,1)S(1)}, bf16[48,896]{1,0:T(8,128)(2,1)S(1)}, u32[]{:S(2)}, u32[]{:S(2)}) %collective-permute-start.1) | collective-permute-done | bytes 86048 | tf_op jit(solution)/shard_map/ppermute | solution.py:623
  14.1 0.0 collective-permute-done
  14.2 1.6 %collective-permute-start.4 = (bf16[192,896]{1,0:T(8,128)(2,1)S(1)}, bf16[192,896]{1,0:T(8,128)(2,1)S(1)}, u32[]{:S(2)}, u32[]{:S(2)}) collective-permute-start(bf16[192,896]{1,0:T(8,128)(2,1)S(1)} %constant_dynamic-update-slice_fusion.refs_0_), channel_id=1, source_target_pairs={{0,2},{1,3},{2,0},{3,1},{4,6},{5,7},{6,4},{7,5},{8,10},{9,11},{10,... | collective-permute-start | bytes 1032200 | tf_op jit(solution)/shard_map/ppermute | solution.py:623
  15.8 1.5 %collective-permute-start.3 = (bf16[192,896]{1,0:T(8,128)(2,1)S(1)}, bf16[192,896]{1,0:T(8,128)(2,1)S(1)}, u32[]{:S(2)}, u32[]{:S(2)}) collective-permute-start(bf16[192,896]{1,0:T(8,128)(2,1)S(1)} %constant_dynamic-update-slice_fusion.refs_0_), channel_id=1, source_target_pairs={{0,1},{1,0},{2,3},{3,2},{4,5},{5,4},{6,7},{7,6},{8,9},{9,8},{10,11... | collective-permute-start | bytes 1032200 | tf_op jit(solution)/shard_map/ppermute | solution.py:623
  17.3 0.0 collective-permute-start.7
  17.3 4.1 %all-to-all-start = ((bf16[16,2,24,512]{3,2,1,0:T(8,128)(2,1)}), bf16[16,2,24,512]{3,2,1,0:T(8,128)(2,1)S(1)}, u32[]{:S(2)}, u32[]{:S(2)}) async-start(bf16[16,2,24,512]{3,2,1,0:T(8,128)(2,1)} %get-tuple-element.78), calls=%async_computation | async-start | bytes 1572864 | tf_op jit(solution)/shard_map/all_to_all | solution.py:624
  21.4 2.0 %collective-permute-done.4.two_ref.refs_2_ = bf16[192,896]{1,0:T(8,128)(2,1)S(1)} collective-permute-done((bf16[192,896]{1,0:T(8,128)(2,1)S(1)}, bf16[192,896]{1,0:T(8,128)(2,1)S(1)}, u32[]{:S(2)}, u32[]{:S(2)}) %collective-permute-start.4) | collective-permute-done | bytes 344096 | tf_op jit(solution)/shard_map/ppermute | solution.py:623
  23.5 1.7 %collective-permute-done.3.one_ref.refs_1_ = bf16[192,896]{1,0:T(8,128)(2,1)S(1)} collective-permute-done((bf16[192,896]{1,0:T(8,128)(2,1)S(1)}, bf16[192,896]{1,0:T(8,128)(2,1)S(1)}, u32[]{:S(2)}, u32[]{:S(2)}) %collective-permute-start.3) | collective-permute-done | bytes 344096 | tf_op jit(solution)/shard_map/ppermute | solution.py:623
  25.2 0.2 collective-permute-start.5
  25.5 2.0 %collective-permute-start.6 = (bf16[96,896]{1,0:T(8,128)(2,1)S(1)}, bf16[96,896]{1,0:T(8,128)(2,1)S(1)}, u32[]{:S(2)}, u32[]{:S(2)}) collective-permute-start(bf16[96,896]{1,0:T(8,128)(2,1)S(1)} %get-tuple-element.86), channel_id=1, source_target_pairs={{0,1},{1,0},{2,3},{3,2},{4,5},{5,4},{6,7},{7,6},{8,9},{9,8},{10,11... | collective-permute-start | bytes 516104 | tf_op jit(solution)/shard_map/ppermute | solution.py:623
  27.5 0.0 collective-permute-start.8
  27.5 0.5 collective-permute-start.9
  28.0 6.0 %collective-permute-done.5.refs_3_ = bf16[96,896]{1,0:T(8,128)(2,1)S(1)} collective-permute-done((bf16[96,896]{1,0:T(8,128)(2,1)S(1)}, bf16[96,896]{1,0:T(8,128)(2,1)S(1)}, u32[]{:S(2)}, u32[]{:S(2)}) %collective-permute-start.5) | collective-permute-done | bytes 172064 | tf_op jit(solution)/shard_map/ppermute | solution.py:623
  34.1 0.0 collective-permute-start.10
  34.1 0.0 collective-permute-done.6.refs_4_
  34.1 0.5 collective-permute-start.11
  34.6 0.1 pad_add_fusion.where_ref
  34.6 0.0 collective-permute-done.7.refs_5_
  34.6 0.8 collective-permute-done.10.refs_8_
  35.5 0.2 collective-permute-done.11.refs_9_
  35.7 0.0 collective-permute-done.8.refs_6_
  35.7 0.0 collective-permute-done.9.refs_7_
  35.7 5.8 %all-to-all-done.given_ref = bf16[16,2,24,512]{3,2,1,0:T(8,128)(2,1)S(1)} async-done(((bf16[16,2,24,512]{3,2,1,0:T(8,128)(2,1)}), bf16[16,2,24,512]{3,2,1,0:T(8,128)(2,1)S(1)}, u32[]{:S(2)}, u32[]{:S(2)}) %all-to-all-start) | async-done | bytes 786464 | tf_op jit(solution)/shard_map/all_to_all | solution.py:624
  41.5 0.0 copy-done.2
  41.5 0.0 copy-done.4
  41.5 0.0 copy-done.5
  41.5 0.0 copy-done.3
  41.5 4.5 %mlp_first.1 = (bf16[768,896]{1,0:T(8,128)(2,1)S(1)}, bf16[384,512]{1,0:T(8,128)(2,1)S(1)}, bf16[384,512]{1,0:T(8,128)(2,1)S(1)}, f32[384,512]{1,0:T(8,128)S(1)}...) custom-call(s32[2]{0:T(128)S(1)} %pad_add_fusion.where_ref, ...), custom_call_target="tpu_custom_call" | custom-call | bytes 15000000 | tf_op jit(solution)/shard_map/mlp_first/pallas_call | solution.py:698
  46.0 0.1 collective-permute-start.12
  46.1 4.7 %mlp_second.1 = (bf16[16,2,24,512]{3,2,1,0:T(8,128)(2,1)}, bf16[192,896]{1,0:T(8,128)(2,1)S(1)}, bf16[192,896]{1,0:T(8,128)(2,1)S(1)}, bf16[192,896]{1,0:T(8,128...) custom-call(s32[2]{0:T(128)S(1)} %pad_add_fusion.where_ref, ...), custom_call_target="tpu_custom_call" | custom-call | bytes 15000000 | tf_op jit(solution)/shard_map/mlp_second/pallas_call | solution.py:713
  50.8 0.0 collective-permute-done.12.arrived_ref.refs_1_
  50.8 0.8 add_convert_fusion
  51.7 0.0 copy-done
  51.7 1.6 %collective-permute-start.13 = (bf16[96,896]{1,0:T(8,128)(2,1)}, bf16[96,896]{1,0:T(8,128)(2,1)S(1)}, u32[]{:S(2)}, u32[]{:S(2)}) collective-permute-start(bf16[96,896]{1,0:T(8,128)(2,1)} %get-tuple-element.104), channel_id=1, source_target_pairs={{0,2},{1,3},{2,0},{3,1},{4,6},{5,7},{6,4},{7,5},{8,10},{9,11},{10,... | collective-permute-start | bytes 516104 | tf_op jit(solution)/shard_map/ppermute | solution.py:623
  53.3 0.6 collective-permute-start.14
  53.9 5.1 %all-to-all-start.1 = ((bf16[16,2,24,512]{3,2,1,0:T(8,128)(2,1)}), bf16[16,2,24,512]{3,2,1,0:T(8,128)(2,1)S(1)}, u32[]{:S(2)}, u32[]{:S(2)}) async-start(bf16[16,2,24,512]{3,2,1,0:T(8,128)(2,1)} %get-tuple-element.94), calls=%async_computation.1 | async-start | bytes 1572864 | tf_op jit(solution)/shard_map/all_to_all | solution.py:624
  59.0 0.0 collective-permute-done.13.first_ref
  59.0 1.1 %collective-permute-done.14.second_ref = bf16[96,896]{1,0:T(8,128)(2,1)} collective-permute-done((bf16[96,896]{1,0:T(8,128)(2,1)}, bf16[96,896]{1,0:T(8,128)(2,1)}, u32[]{:S(2)}, u32[]{:S(2)}) %collective-permute-start.14) | collective-permute-done | bytes 172064 | tf_op jit(solution)/shard_map/ppermute | solution.py:623
  60.1 0.0 copy-done.1
  60.1 1.1 %relay.1 = (bf16[192,896]{1,0:T(8,128)(2,1)S(1)}, bf16[192,896]{1,0:T(8,128)(2,1)S(1)}) custom-call(bf16[192,896]{1,0:T(8,128)(2,1)S(1)} %get-tuple-element.100.one_ref, bf16[192,896]{1,0:T(8,128)(2,1)S(1)} %copy-done.1, bf16[768,896]{1,0:T(8,128)(2,1)S(1)} %collective-permute-done.12.arrived_ref.refs_1_, ...), custom_call_target="tpu_custom_call" | custom-call | flops 99999997952 | bytes 1000000 | tf_op jit(solution)/shard_map/relay/pallas_call | solution.py:589
  61.2 0.9 collective-permute-start.15
  62.1 1.5 %collective-permute-start.16 = (bf16[192,896]{1,0:T(8,128)(2,1)S(1)}, bf16[192,896]{1,0:T(8,128)(2,1)S(1)}, u32[]{:S(2)}, u32[]{:S(2)}) collective-permute-start(bf16[192,896]{1,0:T(8,128)(2,1)S(1)} %get-tuple-element.109), channel_id=1, source_target_pairs={{0,2},{1,3},{2,0},{3,1},{4,6},{5,7},{6,4},{7,5},{8,10},{9,11},{10,... | collective-permute-start | bytes 1032200 | tf_op jit(solution)/shard_map/ppermute | solution.py:623
  63.6 12.2 %collective-permute-done.15.refs_2_ = bf16[192,896]{1,0:T(8,128)(2,1)S(1)} collective-permute-done((bf16[192,896]{1,0:T(8,128)(2,1)S(1)}, bf16[192,896]{1,0:T(8,128)(2,1)S(1)}, u32[]{:S(2)}, u32[]{:S(2)}) %collective-permute-start.15) | collective-permute-done | bytes 344096 | tf_op jit(solution)/shard_map/ppermute | solution.py:623
  75.8 1.2 %collective-permute-done.16.refs_3_ = bf16[192,896]{1,0:T(8,128)(2,1)S(1)} collective-permute-done((bf16[192,896]{1,0:T(8,128)(2,1)S(1)}, bf16[192,896]{1,0:T(8,128)(2,1)S(1)}, u32[]{:S(2)}, u32[]{:S(2)}) %collective-permute-start.16) | collective-permute-done | bytes 344096 | tf_op jit(solution)/shard_map/ppermute | solution.py:623
  77.0 0.2 join.2
  77.1 1.3 %collective-permute-start.17 = (bf16[48,896]{1,0:T(8,128)(2,1)S(1)}, bf16[48,896]{1,0:T(8,128)(2,1)S(1)}, u32[]{:S(2)}, u32[]{:S(2)}) collective-permute-start(bf16[48,896]{1,0:T(8,128)(2,1)S(1)} %get-tuple-element.111), channel_id=1, source_target_pairs={{0,4},{1,5},{2,6},{3,7},{4,0},{5,1},{6,2},{7,3},{8,12},{9,13},{10,... | collective-permute-start | bytes 258056 | tf_op jit(solution)/shard_map/ppermute | solution.py:623
  78.4 2.8 %collective-permute-start.18 = (bf16[48,896]{1,0:T(8,128)(2,1)S(1)}, bf16[48,896]{1,0:T(8,128)(2,1)S(1)}, u32[]{:S(2)}, u32[]{:S(2)}) collective-permute-start(bf16[48,896]{1,0:T(8,128)(2,1)S(1)} %get-tuple-element.112), channel_id=1, source_target_pairs={{0,8},{1,9},{2,10},{3,11},{4,12},{5,13},{6,14},{7,15},{8,0},{9,1},... | collective-permute-start | bytes 258056 | tf_op jit(solution)/shard_map/ppermute | solution.py:623
  81.2 0.4 collective-permute-start.19
  81.6 0.0 all-to-all-done.1.both_ref
  81.6 7.6 %mixer_backward.1 = (bf16[24,8192]{1,0:T(8,128)(2,1)}, f32[24,8192]{1,0:T(8,128)}, f32[24,384]{1,0:T(8,128)S(1)}) custom-call(s32[8]{0:T(128)} %heights.3, s32[8]{0:T(128)} %widths.3, bf16[24,8192]{1,0:T(8,128)(2,1)} %feat_ref.2, bf16[24,8192]{1,0:T(8,128)(2,1)} %cot_ref.3, bf16[16,2,24,512]{3,2,1,0:T(8,128)(2,1)S(1)} %all-to-all-done.1.both_ref, ...), custom_call_target="tpu_custom_call" | custom-call | bytes 21000000 | tf_op jit(solution)/shard_map/mixer_backward/pallas_call | solution.py:740
  89.2 0.0 collective-permute-done.17.refs_1_
  89.2 0.0 collective-permute-done.18.refs_2_
  89.2 0.0 collective-permute-done.19.refs_3_
  89.3 0.1 collective-permute-start.20
  89.4 0.5 collective-permute-start.21
  89.8 0.9 %collective-permute-done.21.sibling_ref = f32[24,384]{1,0:T(8,128)S(1)} collective-permute-done((f32[24,384]{1,0:T(8,128)S(1)}, f32[24,384]{1,0:T(8,128)S(1)}, u32[]{:S(2)}, u32[]{:S(2)}) %collective-permute-start.21) | collective-permute-done | bytes 36896 | tf_op jit(solution)/shard_map/ppermute | solution.py:622
  90.8 0.0 collective-permute-done.20.other_ref
  90.8 1.5 %finish.1 = (f32[1,24]{1,0:T(1,128)}, f32[24,64]{1,0:T(8,128)}, f32[24,64]{1,0:T(8,128)}, f32[1,24]{1,0:T(1,128)}, f32[24,64]{1,0:T(8,128)}, /*index=5*/f32[24,6...) custom-call(s32[1]{0:T(128)} %bitcast.2.half, ...), custom_call_target="tpu_custom_call" | custom-call | bytes 3000000 | tf_op jit(solution)/shard_map/finish/pallas_call | solution.py:768
  (12 shorter events, 0.1 us)
Async XLA Ops:
  1.8 11.3 %collective-permute-start.2 = (bf16[48,896]{1,0:T(8,128)(2,1)S(1)}, bf16[48,896]{1,0:T(8,128)(2,1)S(1)}, u32[]{:S(2)}, u32[]{:S(2)}) collective-permute-start(bf16[48,896]{1,0:T(8,128)(2,1)S(1)} %pack.1), channel_id=1, source_target_pairs={{0,12},{1,13},{2,14},{3,15},{4,8},{5,9},{6,10},{7,11},{8,4},{9,5},... | collective-permute-start | bytes 258056 | tf_op jit(solution)/shard_map/ppermute | solution.py:623
  6.9 7.2 %collective-permute-start.1 = (bf16[48,896]{1,0:T(8,128)(2,1)S(1)}, bf16[48,896]{1,0:T(8,128)(2,1)S(1)}, u32[]{:S(2)}, u32[]{:S(2)}) collective-permute-start(bf16[48,896]{1,0:T(8,128)(2,1)S(1)} %pack.1), channel_id=1, source_target_pairs={{0,8},{1,9},{2,10},{3,11},{4,12},{5,13},{6,14},{7,15},{8,0},{9,1},... | collective-permute-start | bytes 258056 | tf_op jit(solution)/shard_map/ppermute | solution.py:623
  6.9 7.2 %collective-permute-start = (bf16[48,896]{1,0:T(8,128)(2,1)S(1)}, bf16[48,896]{1,0:T(8,128)(2,1)S(1)}, u32[]{:S(2)}, u32[]{:S(2)}) collective-permute-start(bf16[48,896]{1,0:T(8,128)(2,1)S(1)} %pack.1), channel_id=1, source_target_pairs={{0,4},{1,5},{2,6},{3,7},{4,0},{5,1},{6,2},{7,3},{8,12},{9,13},{10,... | collective-permute-start | bytes 258056 | tf_op jit(solution)/shard_map/ppermute | solution.py:623
  14.2 9.2 %collective-permute-start.4 = (bf16[192,896]{1,0:T(8,128)(2,1)S(1)}, bf16[192,896]{1,0:T(8,128)(2,1)S(1)}, u32[]{:S(2)}, u32[]{:S(2)}) collective-permute-start(bf16[192,896]{1,0:T(8,128)(2,1)S(1)} %constant_dynamic-update-slice_fusion.refs_0_), channel_id=1, source_target_pairs={{0,2},{1,3},{2,0},{3,1},{4,6},{5,7},{6,4},{7,5},{8,10},{9,11},{10,... | collective-permute-start | bytes 1032200 | tf_op jit(solution)/shard_map/ppermute | solution.py:623
  15.8 9.4 %collective-permute-start.3 = (bf16[192,896]{1,0:T(8,128)(2,1)S(1)}, bf16[192,896]{1,0:T(8,128)(2,1)S(1)}, u32[]{:S(2)}, u32[]{:S(2)}) collective-permute-start(bf16[192,896]{1,0:T(8,128)(2,1)S(1)} %constant_dynamic-update-slice_fusion.refs_0_), channel_id=1, source_target_pairs={{0,1},{1,0},{2,3},{3,2},{4,5},{5,4},{6,7},{7,6},{8,9},{9,8},{10,11... | collective-permute-start | bytes 1032200 | tf_op jit(solution)/shard_map/ppermute | solution.py:623
  17.3 17.3 %collective-permute-start.7 = (bf16[192,896]{1,0:T(8,128)(2,1)S(1)}, bf16[192,896]{1,0:T(8,128)(2,1)S(1)}, u32[]{:S(2)}, u32[]{:S(2)}) collective-permute-start(bf16[192,896]{1,0:T(8,128)(2,1)S(1)} %constant_dynamic-update-slice_fusion.refs_0_), channel_id=1, source_target_pairs={{0,16},{16,0},{1,17},{17,1},{2,18},{18,2},{3,19},{19,3},{4,20},{20... | collective-permute-start | bytes 1032200 | tf_op jit(solution)/shard_map/ppermute | solution.py:622
  17.3 24.2 %all-to-all-start = ((bf16[16,2,24,512]{3,2,1,0:T(8,128)(2,1)}), bf16[16,2,24,512]{3,2,1,0:T(8,128)(2,1)S(1)}, u32[]{:S(2)}, u32[]{:S(2)}) async-start(bf16[16,2,24,512]{3,2,1,0:T(8,128)(2,1)} %get-tuple-element.78), calls=%async_computation | async-start | bytes 1572864 | tf_op jit(solution)/shard_map/all_to_all | solution.py:624
  25.2 8.8 %collective-permute-start.5 = (bf16[96,896]{1,0:T(8,128)(2,1)S(1)}, bf16[96,896]{1,0:T(8,128)(2,1)S(1)}, u32[]{:S(2)}, u32[]{:S(2)}) collective-permute-start(bf16[96,896]{1,0:T(8,128)(2,1)S(1)} %get-tuple-element.85), channel_id=1, source_target_pairs={{0,2},{1,3},{2,0},{3,1},{4,6},{5,7},{6,4},{7,5},{8,10},{9,11},{10,... | collective-permute-start | bytes 516104 | tf_op jit(solution)/shard_map/ppermute | solution.py:623
  25.5 8.6 %collective-permute-start.6 = (bf16[96,896]{1,0:T(8,128)(2,1)S(1)}, bf16[96,896]{1,0:T(8,128)(2,1)S(1)}, u32[]{:S(2)}, u32[]{:S(2)}) collective-permute-start(bf16[96,896]{1,0:T(8,128)(2,1)S(1)} %get-tuple-element.86), channel_id=1, source_target_pairs={{0,1},{1,0},{2,3},{3,2},{4,5},{5,4},{6,7},{7,6},{8,9},{9,8},{10,11... | collective-permute-start | bytes 516104 | tf_op jit(solution)/shard_map/ppermute | solution.py:623
  27.5 8.2 %collective-permute-start.8 = (bf16[192,896]{1,0:T(8,128)(2,1)S(1)}, bf16[192,896]{1,0:T(8,128)(2,1)S(1)}, u32[]{:S(2)}, u32[]{:S(2)}) collective-permute-start(bf16[192,896]{1,0:T(8,128)(2,1)S(1)} %collective-permute-done.3.one_ref.refs_1_), channel_id=1, source_target_pairs={{0,16},{16,0},{1,17},{17,1},{2,18},{18,2},{3,19},{19,3},{4,20},{20... | collective-permute-start | bytes 1032200 | tf_op jit(solution)/shard_map/ppermute | solution.py:622
  27.5 8.2 %collective-permute-start.9 = (bf16[192,896]{1,0:T(8,128)(2,1)S(1)}, bf16[192,896]{1,0:T(8,128)(2,1)}, u32[]{:S(2)}, u32[]{:S(2)}) collective-permute-start(bf16[192,896]{1,0:T(8,128)(2,1)S(1)} %collective-permute-done.4.two_ref.refs_2_), channel_id=1, source_target_pairs={{0,16},{16,0},{1,17},{17,1},{2,18},{18,2},{3,19},{19,3},{4,20},{20... | collective-permute-start | bytes 1032200 | tf_op jit(solution)/shard_map/ppermute | solution.py:622
  34.1 1.4 %collective-permute-start.10 = (bf16[96,896]{1,0:T(8,128)(2,1)S(1)}, bf16[96,896]{1,0:T(8,128)(2,1)S(1)}, u32[]{:S(2)}, u32[]{:S(2)}) collective-permute-start(bf16[96,896]{1,0:T(8,128)(2,1)S(1)} %collective-permute-done.5.refs_3_), channel_id=1, source_target_pairs={{0,16},{16,0},{1,17},{17,1},{2,18},{18,2},{3,19},{19,3},{4,20},{20... | collective-permute-start | bytes 516104 | tf_op jit(solution)/shard_map/ppermute | solution.py:622
  34.1 1.6 %collective-permute-start.11 = (bf16[96,896]{1,0:T(8,128)(2,1)S(1)}, bf16[96,896]{1,0:T(8,128)(2,1)S(1)}, u32[]{:S(2)}, u32[]{:S(2)}) collective-permute-start(bf16[96,896]{1,0:T(8,128)(2,1)S(1)} %collective-permute-done.6.refs_4_), channel_id=1, source_target_pairs={{0,16},{16,0},{1,17},{17,1},{2,18},{18,2},{3,19},{19,3},{4,20},{20... | collective-permute-start | bytes 516104 | tf_op jit(solution)/shard_map/ppermute | solution.py:622
  34.6 6.9 %copy-start.2 = (bf16[192,896]{1,0:T(8,128)(2,1)}, bf16[192,896]{1,0:T(8,128)(2,1)S(1)}, u32[]{:S(2)}) copy-start(bf16[192,896]{1,0:T(8,128)(2,1)S(1)} %collective-permute-done.7.refs_5_) | copy-start | bytes 1032196
  35.5 6.0 %copy-start.4 = (bf16[96,896]{1,0:T(8,128)(2,1)}, bf16[96,896]{1,0:T(8,128)(2,1)S(1)}, u32[]{:S(2)}) copy-start(bf16[96,896]{1,0:T(8,128)(2,1)S(1)} %collective-permute-done.10.refs_8_) | copy-start | bytes 516100
  35.7 5.8 %copy-start.5 = (bf16[96,896]{1,0:T(8,128)(2,1)}, bf16[96,896]{1,0:T(8,128)(2,1)S(1)}, u32[]{:S(2)}) copy-start(bf16[96,896]{1,0:T(8,128)(2,1)S(1)} %collective-permute-done.11.refs_9_) | copy-start | bytes 516100
  35.7 5.8 %copy-start.3 = (bf16[192,896]{1,0:T(8,128)(2,1)}, bf16[192,896]{1,0:T(8,128)(2,1)S(1)}, u32[]{:S(2)}) copy-start(bf16[192,896]{1,0:T(8,128)(2,1)S(1)} %collective-permute-done.8.refs_6_) | copy-start | bytes 1032196
  46.0 4.8 %collective-permute-start.12 = (bf16[768,896]{1,0:T(8,128)(2,1)S(1)}, bf16[768,896]{1,0:T(8,128)(2,1)S(1)}, u32[]{:S(2)}, u32[]{:S(2)}) collective-permute-start(bf16[768,896]{1,0:T(8,128)(2,1)S(1)} %get-tuple-element.99), channel_id=1, source_target_pairs={{0,16},{16,0},{1,17},{17,1},{2,18},{18,2},{3,19},{19,3},{4,20},{20... | collective-permute-start | bytes 4128776 | tf_op jit(solution)/shard_map/ppermute | solution.py:622
  50.8 0.8 copy-start
  51.7 8.4 %copy-start.1 = (bf16[192,896]{1,0:T(8,128)(2,1)S(1)}, bf16[192,896]{1,0:T(8,128)(2,1)}, u32[]{:S(2)}) copy-start(bf16[192,896]{1,0:T(8,128)(2,1)} %copy-done) | copy-start | bytes 1032196
  51.7 7.3 %collective-permute-start.13 = (bf16[96,896]{1,0:T(8,128)(2,1)}, bf16[96,896]{1,0:T(8,128)(2,1)S(1)}, u32[]{:S(2)}, u32[]{:S(2)}) collective-permute-start(bf16[96,896]{1,0:T(8,128)(2,1)} %get-tuple-element.104), channel_id=1, source_target_pairs={{0,2},{1,3},{2,0},{3,1},{4,6},{5,7},{6,4},{7,5},{8,10},{9,11},{10,... | collective-permute-start | bytes 516104 | tf_op jit(solution)/shard_map/ppermute | solution.py:623
  53.3 6.8 %collective-permute-start.14 = (bf16[96,896]{1,0:T(8,128)(2,1)}, bf16[96,896]{1,0:T(8,128)(2,1)}, u32[]{:S(2)}, u32[]{:S(2)}) collective-permute-start(bf16[96,896]{1,0:T(8,128)(2,1)} %get-tuple-element.105), channel_id=1, source_target_pairs={{0,1},{1,0},{2,3},{3,2},{4,5},{5,4},{6,7},{7,6},{8,9},{9,8},{10,11... | collective-permute-start | bytes 516104 | tf_op jit(solution)/shard_map/ppermute | solution.py:623
  53.9 27.7 %all-to-all-start.1 = ((bf16[16,2,24,512]{3,2,1,0:T(8,128)(2,1)}), bf16[16,2,24,512]{3,2,1,0:T(8,128)(2,1)S(1)}, u32[]{:S(2)}, u32[]{:S(2)}) async-start(bf16[16,2,24,512]{3,2,1,0:T(8,128)(2,1)} %get-tuple-element.94), calls=%async_computation.1 | async-start | bytes 1572864 | tf_op jit(solution)/shard_map/all_to_all | solution.py:624
  61.2 14.5 %collective-permute-start.15 = (bf16[192,896]{1,0:T(8,128)(2,1)S(1)}, bf16[192,896]{1,0:T(8,128)(2,1)S(1)}, u32[]{:S(2)}, u32[]{:S(2)}) collective-permute-start(bf16[192,896]{1,0:T(8,128)(2,1)S(1)} %get-tuple-element.108), channel_id=1, source_target_pairs={{0,1},{1,0},{2,3},{3,2},{4,5},{5,4},{6,7},{7,6},{8,9},{9,8},{10,11... | collective-permute-start | bytes 1032200 | tf_op jit(solution)/shard_map/ppermute | solution.py:623
  62.1 14.8 %collective-permute-start.16 = (bf16[192,896]{1,0:T(8,128)(2,1)S(1)}, bf16[192,896]{1,0:T(8,128)(2,1)S(1)}, u32[]{:S(2)}, u32[]{:S(2)}) collective-permute-start(bf16[192,896]{1,0:T(8,128)(2,1)S(1)} %get-tuple-element.109), channel_id=1, source_target_pairs={{0,2},{1,3},{2,0},{3,1},{4,6},{5,7},{6,4},{7,5},{8,10},{9,11},{10,... | collective-permute-start | bytes 1032200 | tf_op jit(solution)/shard_map/ppermute | solution.py:623
  77.1 12.1 %collective-permute-start.17 = (bf16[48,896]{1,0:T(8,128)(2,1)S(1)}, bf16[48,896]{1,0:T(8,128)(2,1)S(1)}, u32[]{:S(2)}, u32[]{:S(2)}) collective-permute-start(bf16[48,896]{1,0:T(8,128)(2,1)S(1)} %get-tuple-element.111), channel_id=1, source_target_pairs={{0,4},{1,5},{2,6},{3,7},{4,0},{5,1},{6,2},{7,3},{8,12},{9,13},{10,... | collective-permute-start | bytes 258056 | tf_op jit(solution)/shard_map/ppermute | solution.py:623
  78.4 10.8 %collective-permute-start.18 = (bf16[48,896]{1,0:T(8,128)(2,1)S(1)}, bf16[48,896]{1,0:T(8,128)(2,1)S(1)}, u32[]{:S(2)}, u32[]{:S(2)}) collective-permute-start(bf16[48,896]{1,0:T(8,128)(2,1)S(1)} %get-tuple-element.112), channel_id=1, source_target_pairs={{0,8},{1,9},{2,10},{3,11},{4,12},{5,13},{6,14},{7,15},{8,0},{9,1},... | collective-permute-start | bytes 258056 | tf_op jit(solution)/shard_map/ppermute | solution.py:623
  81.2 8.0 %collective-permute-start.19 = (bf16[48,896]{1,0:T(8,128)(2,1)S(1)}, bf16[48,896]{1,0:T(8,128)(2,1)S(1)}, u32[]{:S(2)}, u32[]{:S(2)}) collective-permute-start(bf16[48,896]{1,0:T(8,128)(2,1)S(1)} %get-tuple-element.113), channel_id=1, source_target_pairs={{0,12},{1,13},{2,14},{3,15},{4,8},{5,9},{6,10},{7,11},{8,4},{9,5},... | collective-permute-start | bytes 258056 | tf_op jit(solution)/shard_map/ppermute | solution.py:623
  89.3 1.5 %collective-permute-start.20 = (f32[48,896]{1,0:T(8,128)S(1)}, f32[48,896]{1,0:T(8,128)S(1)}, u32[]{:S(2)}, u32[]{:S(2)}) collective-permute-start(f32[48,896]{1,0:T(8,128)S(1)} %join.3.mine_ref), channel_id=1, source_target_pairs={{0,16},{16,0},{1,17},{17,1},{2,18},{18,2},{3,19},{19,3},{4,20},{20... | collective-permute-start | bytes 516104 | tf_op jit(solution)/shard_map/ppermute | solution.py:622
  89.4 1.4 %collective-permute-start.21 = (f32[24,384]{1,0:T(8,128)S(1)}, f32[24,384]{1,0:T(8,128)S(1)}, u32[]{:S(2)}, u32[]{:S(2)}) collective-permute-start(f32[24,384]{1,0:T(8,128)S(1)} %get-tuple-element.119.small_ref), channel_id=1, source_target_pairs={{0,16},{16,0},{1,17},{17,1},{2,18},{18,2},{3,19},{19,3},{4,20},{20... | collective-permute-start | bytes 110600 | tf_op jit(solution)/shard_map/ppermute | solution.py:622

commit v5 on v4

--- a/solution.py
+++ b/solution.py
@@ -207,10 +207,50 @@
             out_ref[image * parts + j, 1] = down[:, j * wide : (j + 1) * wide]
 
 
+def prepare_kernel(
+    heights, widths, feat_ref, rows_ref, field_ref, high_a, low_a, high_s, low_s, slots, tall
+):
+    channels, cells = feat_ref.shape
+    images = cells // CELLS
+    live = min(SLOT, channels)
+    sides = images // PER
+    for ref in (field_ref, high_a, low_a):
+        ref[...] = jnp.zeros_like(ref)
+    for image in range(images):
+        inside = image_mask(1, heights[image], widths[image])
+        value = feat_ref[:, image * CELLS : (image + 1) * CELLS].astype(F32)
+        fill_slots(slots, jnp.where(inside, value, 0.0), image)
+
+    def body(group, carry):
+        lane = lane_of(SLOT)
+        sub = lax.broadcasted_iota(jnp.int32, (SLOT, LANES), 0)
+        for c in range(live):
+            row = rows_ref[pl.ds(group * SLOT + c, 1), :]
+            build_down(row, c, high_a.at[group], low_a.at[group], lane, sub)
+            tiles = load_channel(slots, group, c, lane)
+            for s in range(sides):
+                value = jnp.concatenate(tiles[s * PER : (s + 1) * PER], axis=0)
+                at = (group, slice(c * SIDE, (c + 1) * SIDE), slice(s * LANES, (s + 1) * LANES))
+                field_ref[at] = value.astype(BF16)
+        source = field_ref[group]
+        tall[...] = dot(high_a[group], source) + dot(low_a[group], source)
+        for c in range(live):
+            value = jnp.concatenate(
+                [tall[c * SIDE : (c + 1) * SIDE, s * LANES : (s + 1) * LANES] for s in range(sides)],
+                axis=0,
+            )
+            high, low = split(value)
+            high_s[group, c] = high
+            low_s[group, c] = low
+        return carry
+
+    lax.fori_loop(0, slots.shape[0], body, 0)
+
+
 def backward_kernel(
     heights, widths, feat_ref, cot_ref, both_ref, rows_ref, scale_ref, bias_ref,
-    step_h, step_w, rate_h, rate_w, read_h, read_w, result_ref, gfeat_ref, small_ref,
-    slots, slots_g, high_a, low_a, field, field_g, tall, high_d, low_d, wide_ref, sums,
+    step_h, step_w, rate_h, rate_w, read_h, read_w, field_ref, high_a, low_a, high_s, low_s,
+    result_ref, gfeat_ref, small_ref, slots, slots_g, field_g, outer_ref, high_d, low_d, wide_ref, sums,
 ):
     channels, cells = feat_ref.shape
     images = cells // CELLS
@@ -218,7 +258,7 @@
     sides = images // PER
     wide = both_ref.shape[3]
     parts = CELLS // wide
-    for ref in (high_a, low_a, sums, field, field_g, high_d, low_d):
+    for ref in (sums, field_g, high_d, low_d):
         ref[...] = jnp.zeros_like(ref)
     lane_c = lane_of(channels)
     scale = column(scale_ref[...])
@@ -228,8 +268,6 @@
         span = slice(image * CELLS, (image + 1) * CELLS)
         inside = image_mask(1, heights[image], widths[image])
         values = feat_ref[:, span].astype(F32)
-        masked = jnp.where(inside, values, 0.0)
-        fill_slots(slots, masked, image)
         grad = jnp.concatenate(
             [both_ref[image * parts + j, 0].astype(F32) for j in range(parts)], axis=1
         )
@@ -244,11 +282,11 @@
         weighted = jnp.where(inside, cot_ref[:, span].astype(F32), 0.0)
         small = small + jnp.where(
             lane_c == 64,
-            jnp.sum(grad * masked, axis=1, keepdims=True),
+            jnp.sum(grad * values, axis=1, keepdims=True),
             jnp.where(
                 lane_c == 65,
                 jnp.sum(weighted * shifted, axis=1, keepdims=True),
-                jnp.where(lane_c == 66, jnp.sum(weighted, axis=1, keepdims=True), 0.0),
+                jnp.where(lane_c == 66, scale * jnp.sum(weighted, axis=1, keepdims=True), 0.0),
             ),
         )
 
@@ -259,16 +297,11 @@
         half = lambda ref, c, s: ref[c * SIDE : (c + 1) * SIDE, s * LANES : (s + 1) * LANES]
         stack = lambda ref, c: jnp.concatenate([half(ref, c, s) for s in range(sides)], axis=0)
         for c in range(live):
-            row = rows_ref[pl.ds(group * SLOT + c, 1), :]
-            build_down(row, c, high_a, low_a, lane, sub)
-            for slot, out in ((slots, field), (slots_g, field_g)):
-                tiles = load_channel(slot, group, c, lane)
-                for s in range(sides):
-                    value = jnp.concatenate(tiles[s * PER : (s + 1) * PER], axis=0)
-                    at = (slice(c * SIDE, (c + 1) * SIDE), slice(s * LANES, (s + 1) * LANES))
-                    out[at] = value.astype(BF16)
-        source = field[...]
-        tall[...] = dot(high_a[...], source) + dot(low_a[...], source)
+            tiles = load_channel(slots_g, group, c, lane)
+            for s in range(sides):
+                value = jnp.concatenate(tiles[s * PER : (s + 1) * PER], axis=0)
+                at = (slice(c * SIDE, (c + 1) * SIDE), slice(s * LANES, (s + 1) * LANES))
+                field_g[at] = value.astype(BF16)
         for c in range(live):
             row = rows_ref[pl.ds(group * SLOT + c, 1), :]
             high_b, low_b = build_across(row, True, lane, sub)
@@ -281,9 +314,10 @@
                 at = (slice(c * SIDE, (c + 1) * SIDE), slice(s * LANES, (s + 1) * LANES))
                 high_d[at] = high[s * SIDE : (s + 1) * SIDE]
                 low_d[at] = low[s * SIDE : (s + 1) * SIDE]
-            high, low = split(stack(tall, c))
             outer = dot(
-                jnp.concatenate([grad, grad], axis=0), jnp.concatenate([high, low], axis=0), TN
+                jnp.concatenate([grad, grad], axis=0),
+                jnp.concatenate([high_s[group, c], low_s[group, c]], axis=0),
+                TN,
             )
             total = None
             for part in range(PER):
@@ -303,10 +337,11 @@
             total = total + pltpu.roll(total, 32, 1)
             sums[pl.ds(group * SLOT + c, 1), :] = jnp.where(lane[0:1] // SIDE == 1, total, 0.0)
         high, low = high_d[...], low_d[...]
-        back = dot(high_a[...], high, TN) + dot(high_a[...], low, TN) + dot(low_a[...], high, TN)
+        down = high_a[group]
+        back = dot(down, high, TN) + dot(down, low, TN) + dot(low_a[group], high, TN)
         wide_ref[...] = back
-        outer = dot(high, source, NT) + dot(low, source, NT)
-        tall[...] = outer
+        source = field_ref[group]
+        outer_ref[...] = dot(high, source, NT) + dot(low, source, NT)
         for c in range(live):
             value = stack(wide_ref, c)
             tiles = [value[k * SLOT : (k + 1) * SLOT] for k in range(images)]
@@ -314,7 +349,7 @@
             total = None
             for turn in range(PER):
                 at = c * SIDE + turn * SLOT
-                value = tall[at : at + SLOT, c // PER * LANES : (c // PER + 1) * LANES]
+                value = outer_ref[at : at + SLOT, c // PER * LANES : (c // PER + 1) * LANES]
                 index = PER * sub + turn - lane
                 safe = jnp.clip(index, 0, SIDE - 1)
                 index_at = (safe % PER) * TILES + safe // PER + c % PER * SIDE
@@ -392,7 +427,7 @@
 
 
 def finish_kernel(
-    half, mine_ref, other_ref, small_ref, sibling_ref, scale_ref,
+    half, mine_ref, other_ref, small_ref, sibling_ref,
     gstep_h, grate_h, gread_h, gstep_w, grate_w, gread_w, gskip, ggain, gshift, gin, ginb, gout,
     gbias, gscale,
 ):
@@ -417,7 +452,7 @@
     total = total[:, 4 * states :]
     gskip[...] = as_row(total[:, 64:65])
     gscale[...] = as_row(total[:, 65:66])
-    gbias[...] = as_row(total[:, 66:67]) * scale_ref[...]
+    gbias[...] = as_row(total[:, 66:67])
     gstep_h[...] = as_row(total[:, 67:68])
     gstep_w[...] = as_row(total[:, 68:69])
 
@@ -729,12 +764,29 @@
         one, two = pair(add(gown[3], 3 * tall), add(gown[4], 3 * tall + cut))
         one, two = pair(flip(one, 2), flip(two, 1))
         one, two = relay(gown[1], gown[2], arrived, one, two)
+        features_last, one, two = pair(features, one, two)
         first, second, *sent = gown[0], arrived, flip(one, 1), flip(two, 2)
     else:
+        features_last = features
         total = (gown[0].astype(F32) + arrived.astype(F32)).astype(BF16)
         sent = list(swap(total.reshape(near, tall, width), near_groups))
         first, second, *sent = sent
     landed = [first, second, *sent]
+    table = pltpu.HBM((groups,) + toeplitz.shape, BF16)
+    strip = pltpu.HBM((groups, SLOT, images * SLOT, LANES), BF16)
+    prepared = pl.pallas_call(
+        prepare_kernel,
+        out_shape=(
+            pltpu.HBM((groups,) + square, BF16), table, table, strip, strip,
+        ),
+        in_specs=[SMEM, SMEM, full, full],
+        out_specs=(full,) * 5,
+        scratch_shapes=[slots, pltpu.VMEM(square, F32)],
+        compiler_params=params(12),
+        cost_estimate=cost(4),
+        name="mixer_prepare",
+    )(pin(heights), pin(widths), pin(features_last), taps)
+    *landed, _ = pair(*landed, prepared[0])
     shards = join(deep, landed, far)
     shards = [shards[0]] + [flip(v, (i + 1) * near) for i, v in enumerate(shards[1:])]
     result, grad_features, small = pl.pallas_call(
@@ -744,12 +796,12 @@
             jax.ShapeDtypeStruct((channels, cells), F32),
             jax.ShapeDtypeStruct((channels, LANES + 4 * states), F32),
         ),
-        in_specs=[SMEM, SMEM] + [full] * 12,
+        in_specs=[SMEM, SMEM] + [full] * 17,
         out_specs=(full,) * 3,
         scratch_shapes=[
-            slots, slots, toeplitz, toeplitz, pltpu.VMEM(square, BF16),
-            pltpu.VMEM(square, BF16), pltpu.VMEM((SLOT * SIDE, max(SLOT * SIDE, square[1])), F32),
-            pltpu.VMEM(square, BF16), pltpu.VMEM(square, BF16), pltpu.VMEM(square, F32),
+            slots, slots, pltpu.VMEM(square, BF16),
+            pltpu.VMEM((SLOT * SIDE, SLOT * SIDE), F32), pltpu.VMEM(square, BF16),
+            pltpu.VMEM(square, BF16), pltpu.VMEM(square, F32),
             pltpu.VMEM((groups * SLOT, LANES), F32),
         ],
         compiler_params=params(16),
@@ -759,6 +811,7 @@
         pin(heights), pin(widths), pin(features), pin(cotangent), both, taps,
         pin(row(layer_scale)), pin(row(out_bias)), pin(row(step_height)), pin(row(step_width)),
         pin(rate_height), pin(rate_width), pin(readout_height), pin(readout_width),
+        *map(pin, prepared),
     )
     *shards, small = pair(*shards, small)
     (mine,) = join(deep, shards, 1)
@@ -772,12 +825,12 @@
             vector_out, vector_out, weight_out, jax.ShapeDtypeStruct((1, units), F32), weight_out,
             vector_out, vector_out,
         ),
-        in_specs=[SMEM] + [full] * 5,
+        in_specs=[SMEM] + [full] * 4,
         out_specs=(full,) * 14,
         compiler_params=params(4),
         cost_estimate=cost(1),
         name="finish",
-    )(half.reshape(1), mine, exchange(mine), small, exchange(small), pin(row(layer_scale)))
+    )(half.reshape(1), mine, exchange(mine), small, exchange(small))
     outs = [v.reshape(-1) if v.shape[0] == 1 else v for v in outs]
     outs[9] = outs[9].T
     return (result, grad_features, *outs)

time: 92.9 us -> 91.5 us (0.985)
  waiting for transfers between devices: 33.1 us -> 29.6 us
  Pallas kernels: 26.4 us -> 28.5 us
    ppermute x14, waiting for transfers between devices: 25.3 us -> 21.8 us  [per_device(): lax.ppermute(v, 'ch', [(i, i ^ bits) for i in range(ch)])]
    pallas_call x0 -> x1, Pallas kernels: none -> 3.57 us  [per_device(): pl.pallas_call(prepare_kernel, out_shape=(pltpu.HBM((groups,) + square, B...]
  transfers between devices with their start and end apart: 24 -> 24, of which waited for: 11 -> 11; matrix products, arithmetic and copies ran while one was open for 0% -> 0% of each run, Pallas kernels for 21% -> 24%
where the time goes in v5:
time: 91.5 us; the launch traced here: 91 us
  starting transfers between devices  31 us (34%)
  waiting for transfers between devices  29.6 us (32%)
  Pallas kernels  28.5 us (31%)
  between operations  0.96 us (1%)
  other arithmetic  0.92 us (1%)
    ppermute x14, waiting for transfers between devices, per_device(): lax.ppermute(v, 'ch', [(i, i ^ bits) for i in range(ch)])  21.8 us
    ppermute x14, starting transfers between devices, per_device(): lax.ppermute(v, 'ch', [(i, i ^ bits) for i in range(ch)])  20.1 us
    all_to_all x2, starting transfers between devices, per_device(): lax.all_to_all(v, 'ch', split_axis=0, concat_axis=0, tiled=True, axis_ind...  9.22 us
    pallas_call x1, Pallas kernels, per_device(): pl.pallas_call(backward_kernel, out_shape=(jax.ShapeDtypeStruct((channels...  6.85 us
    all_to_all x2, waiting for transfers between devices, per_device(): lax.all_to_all(v, 'ch', split_axis=0, concat_axis=0, tiled=True, axis_ind...  5.78 us
    pallas_call x1, Pallas kernels, per_device(): pl.pallas_call(forward_kernel, out_shape=(jax.ShapeDtypeStruct(both_shape...  5.54 us
    pallas_call x1, Pallas kernels, per_device(): pl.pallas_call(partial(mlp_second, near, pieces), out_shape=[jax.ShapeDty...  4.74 us
    pallas_call x1, Pallas kernels, per_device(): pl.pallas_call(partial(mlp_first, near, pieces), out_shape=[jax.ShapeDtyp...  4.49 us
  transfers between devices with their start and end apart: 24, of which 11 were waited for; matrix products, arithmetic and copies ran while one was open for 0% of the time, Pallas kernels for 24%

profile of v5, /device:TPU:0, one launch (start us, length us, event | category | flops | bytes accessed | tf_op | source)
XLA Modules:
  0.0 91.0 jit_solution(11543044523485800013)
XLA Ops:
  0.7 1.2 %pack.1 = bf16[48,896]{1,0:T(8,128)(2,1)S(1)} custom-call(s32[1]{0:T(128)} %bitcast.2.half, bf16[96,384]{1,0:T(8,128)(2,1)} %bitcast.21, bf16[96,384]{1,0:T(8,128)(2,1)} %out_ref.1, bf16[1,96]{1,0:T(2,128)(2,1)} %bitcast.28, bf16[1,24]{1,0:T(2,128)(2,1)} %bitcast.29, bf16[1,24]{1,0:T(2,128)(2,1)} %bitcast.30), custom_call_target="tpu_custom_call" | custom-call | bytes 6000000 | tf_op jit(solution)/shard_map/pack/pallas_call | solution.py:667
  1.8 5.1 %collective-permute-start.2 = (bf16[48,896]{1,0:T(8,128)(2,1)S(1)}, bf16[48,896]{1,0:T(8,128)(2,1)S(1)}, u32[]{:S(2)}, u32[]{:S(2)}) collective-permute-start(bf16[48,896]{1,0:T(8,128)(2,1)S(1)} %pack.1), channel_id=1, source_target_pairs={{0,12},{1,13},{2,14},{3,15},{4,8},{5,9},{6,10},{7,11},{8,4},{9,5},... | collective-permute-start | bytes 258056 | tf_op jit(solution)/shard_map/ppermute | solution.py:658
  6.9 0.0 collective-permute-start.1
  6.9 0.6 collective-permute-start
  7.6 5.5 %mixer_forward.1 = (bf16[16,2,24,512]{3,2,1,0:T(8,128)(2,1)}, f32[24,128]{1,0:T(8,128)S(1)}) custom-call(s32[8]{0:T(128)} %heights.5, s32[8]{0:T(128)} %widths.5, bf16[24,8192]{1,0:T(8,128)(2,1)} %feat_ref.3, bf16[24,8192]{1,0:T(8,128)(2,1)} %cot_ref.3, f32[1,24]{1,0:T(1,128)} %bitcast.22, f32[1,24]{1,0:T(1,128)} %bitcast.24, f32[1,24]{1,0:T(1,128)} %bitcast.26, ...), custom_call_target="tpu_custom_call" | custom-call | bytes 18000000 | tf_op jit(solution)/shard_map/mixer_forward/pallas_call | solution.py:687
  13.1 0.0 collective-permute-done.2
  13.1 1.0 %collective-permute-done.1 = bf16[48,896]{1,0:T(8,128)(2,1)S(1)} collective-permute-done((bf16[48,896]{1,0:T(8,128)(2,1)S(1)}, bf16[48,896]{1,0:T(8,128)(2,1)S(1)}, u32[]{:S(2)}, u32[]{:S(2)}) %collective-permute-start.1) | collective-permute-done | bytes 86048 | tf_op jit(solution)/shard_map/ppermute | solution.py:658
  14.1 0.0 collective-permute-done
  14.2 1.6 %collective-permute-start.4 = (bf16[192,896]{1,0:T(8,128)(2,1)S(1)}, bf16[192,896]{1,0:T(8,128)(2,1)S(1)}, u32[]{:S(2)}, u32[]{:S(2)}) collective-permute-start(bf16[192,896]{1,0:T(8,128)(2,1)S(1)} %constant_dynamic-update-slice_fusion.refs_0_), channel_id=1, source_target_pairs={{0,2},{1,3},{2,0},{3,1},{4,6},{5,7},{6,4},{7,5},{8,10},{9,11},{10,... | collective-permute-start | bytes 1032200 | tf_op jit(solution)/shard_map/ppermute | solution.py:658
  15.8 1.5 %collective-permute-start.3 = (bf16[192,896]{1,0:T(8,128)(2,1)S(1)}, bf16[192,896]{1,0:T(8,128)(2,1)S(1)}, u32[]{:S(2)}, u32[]{:S(2)}) collective-permute-start(bf16[192,896]{1,0:T(8,128)(2,1)S(1)} %constant_dynamic-update-slice_fusion.refs_0_), channel_id=1, source_target_pairs={{0,1},{1,0},{2,3},{3,2},{4,5},{5,4},{6,7},{7,6},{8,9},{9,8},{10,11... | collective-permute-start | bytes 1032200 | tf_op jit(solution)/shard_map/ppermute | solution.py:658
  17.3 0.0 collective-permute-start.7
  17.3 4.1 %all-to-all-start = ((bf16[16,2,24,512]{3,2,1,0:T(8,128)(2,1)}), bf16[16,2,24,512]{3,2,1,0:T(8,128)(2,1)S(1)}, u32[]{:S(2)}, u32[]{:S(2)}) async-start(bf16[16,2,24,512]{3,2,1,0:T(8,128)(2,1)} %get-tuple-element.90), calls=%async_computation | async-start | bytes 1572864 | tf_op jit(solution)/shard_map/all_to_all | solution.py:659
  21.4 2.0 %collective-permute-done.4.two_ref.refs_2_ = bf16[192,896]{1,0:T(8,128)(2,1)S(1)} collective-permute-done((bf16[192,896]{1,0:T(8,128)(2,1)S(1)}, bf16[192,896]{1,0:T(8,128)(2,1)S(1)}, u32[]{:S(2)}, u32[]{:S(2)}) %collective-permute-start.4) | collective-permute-done | bytes 344096 | tf_op jit(solution)/shard_map/ppermute | solution.py:658
  23.5 1.7 %collective-permute-done.3.one_ref.refs_1_ = bf16[192,896]{1,0:T(8,128)(2,1)S(1)} collective-permute-done((bf16[192,896]{1,0:T(8,128)(2,1)S(1)}, bf16[192,896]{1,0:T(8,128)(2,1)S(1)}, u32[]{:S(2)}, u32[]{:S(2)}) %collective-permute-start.3) | collective-permute-done | bytes 344096 | tf_op jit(solution)/shard_map/ppermute | solution.py:658
  25.2 0.2 collective-permute-start.5
  25.5 2.0 %collective-permute-start.6 = (bf16[96,896]{1,0:T(8,128)(2,1)S(1)}, bf16[96,896]{1,0:T(8,128)(2,1)S(1)}, u32[]{:S(2)}, u32[]{:S(2)}) collective-permute-start(bf16[96,896]{1,0:T(8,128)(2,1)S(1)} %get-tuple-element.98), channel_id=1, source_target_pairs={{0,1},{1,0},{2,3},{3,2},{4,5},{5,4},{6,7},{7,6},{8,9},{9,8},{10,11... | collective-permute-start | bytes 516104 | tf_op jit(solution)/shard_map/ppermute | solution.py:658
  27.5 0.0 collective-permute-start.8
  27.5 0.5 collective-permute-start.9
  28.0 6.0 %collective-permute-done.5.refs_3_ = bf16[96,896]{1,0:T(8,128)(2,1)S(1)} collective-permute-done((bf16[96,896]{1,0:T(8,128)(2,1)S(1)}, bf16[96,896]{1,0:T(8,128)(2,1)S(1)}, u32[]{:S(2)}, u32[]{:S(2)}) %collective-permute-start.5) | collective-permute-done | bytes 172064 | tf_op jit(solution)/shard_map/ppermute | solution.py:658
  34.0 0.0 collective-permute-start.10
  34.1 0.0 collective-permute-done.6.refs_4_
  34.1 0.5 collective-permute-start.11
  34.6 0.1 pad_add_fusion.where_ref
  34.6 0.0 collective-permute-done.7.refs_5_
  34.6 0.8 collective-permute-done.10.refs_8_
  35.5 0.2 collective-permute-done.11.refs_9_
  35.7 0.0 collective-permute-done.8.refs_6_
  35.7 0.0 collective-permute-done.9.refs_7_
  35.7 5.8 %all-to-all-done.given_ref = bf16[16,2,24,512]{3,2,1,0:T(8,128)(2,1)S(1)} async-done(((bf16[16,2,24,512]{3,2,1,0:T(8,128)(2,1)}), bf16[16,2,24,512]{3,2,1,0:T(8,128)(2,1)S(1)}, u32[]{:S(2)}, u32[]{:S(2)}) %all-to-all-start) | async-done | bytes 786464 | tf_op jit(solution)/shard_map/all_to_all | solution.py:659
  41.5 0.0 copy-done.2
  41.5 0.0 copy-done.4
  41.5 0.0 copy-done.5
  41.5 0.0 copy-done.3
  41.5 4.5 %mlp_first.1 = (bf16[768,896]{1,0:T(8,128)(2,1)S(1)}, bf16[384,512]{1,0:T(8,128)(2,1)S(1)}, bf16[384,512]{1,0:T(8,128)(2,1)S(1)}, f32[384,512]{1,0:T(8,128)S(1)}...) custom-call(s32[2]{0:T(128)S(1)} %pad_add_fusion.where_ref, ...), custom_call_target="tpu_custom_call" | custom-call | bytes 15000000 | tf_op jit(solution)/shard_map/mlp_first/pallas_call | solution.py:733
  46.0 0.1 collective-permute-start.12
  46.1 4.7 %mlp_second.1 = (bf16[16,2,24,512]{3,2,1,0:T(8,128)(2,1)}, bf16[192,896]{1,0:T(8,128)(2,1)S(1)}, bf16[192,896]{1,0:T(8,128)(2,1)S(1)}, bf16[192,896]{1,0:T(8,128...) custom-call(s32[2]{0:T(128)S(1)} %pad_add_fusion.where_ref, ...), custom_call_target="tpu_custom_call" | custom-call | bytes 15000000 | tf_op jit(solution)/shard_map/mlp_second/pallas_call | solution.py:748
  50.8 0.0 collective-permute-done.12.arrived_ref.refs_1_
  50.8 0.8 add_convert_fusion
  51.7 0.0 copy-done
  51.7 1.6 %collective-permute-start.13 = (bf16[96,896]{1,0:T(8,128)(2,1)}, bf16[96,896]{1,0:T(8,128)(2,1)S(1)}, u32[]{:S(2)}, u32[]{:S(2)}) collective-permute-start(bf16[96,896]{1,0:T(8,128)(2,1)} %get-tuple-element.113), channel_id=1, source_target_pairs={{0,2},{1,3},{2,0},{3,1},{4,6},{5,7},{6,4},{7,5},{8,10},{9,11},{10,... | collective-permute-start | bytes 516104 | tf_op jit(solution)/shard_map/ppermute | solution.py:658
  53.3 0.6 collective-permute-start.14
  53.9 5.1 %all-to-all-start.1 = ((bf16[16,2,24,512]{3,2,1,0:T(8,128)(2,1)}), bf16[16,2,24,512]{3,2,1,0:T(8,128)(2,1)S(1)}, u32[]{:S(2)}, u32[]{:S(2)}) async-start(bf16[16,2,24,512]{3,2,1,0:T(8,128)(2,1)} %get-tuple-element.106), calls=%async_computation.1 | async-start | bytes 1572864 | tf_op jit(solution)/shard_map/all_to_all | solution.py:659
  59.0 0.0 collective-permute-done.13.first_ref
  59.0 1.1 %collective-permute-done.14.second_ref = bf16[96,896]{1,0:T(8,128)(2,1)} collective-permute-done((bf16[96,896]{1,0:T(8,128)(2,1)}, bf16[96,896]{1,0:T(8,128)(2,1)}, u32[]{:S(2)}, u32[]{:S(2)}) %collective-permute-start.14) | collective-permute-done | bytes 172064 | tf_op jit(solution)/shard_map/ppermute | solution.py:658
  60.1 1.1 %relay.1 = (bf16[192,896]{1,0:T(8,128)(2,1)S(1)}, bf16[192,896]{1,0:T(8,128)(2,1)S(1)}) custom-call(bf16[192,896]{1,0:T(8,128)(2,1)S(1)} %get-tuple-element.108.one_ref, bf16[192,896]{1,0:T(8,128)(2,1)S(1)} %copy-done.1, bf16[768,896]{1,0:T(8,128)(2,1)S(1)} %collective-permute-done.12.arrived_ref.refs_1_, ...), custom_call_target="tpu_custom_call" | custom-call | flops 99999997952 | bytes 1000000 | tf_op jit(solution)/shard_map/relay/pallas_call | solution.py:624
  61.2 0.9 collective-permute-start.15
  62.1 1.5 %collective-permute-start.16 = (bf16[192,896]{1,0:T(8,128)(2,1)S(1)}, bf16[192,896]{1,0:T(8,128)(2,1)S(1)}, u32[]{:S(2)}, u32[]{:S(2)}) collective-permute-start(bf16[192,896]{1,0:T(8,128)(2,1)S(1)} %get-tuple-element.129), channel_id=1, source_target_pairs={{0,2},{1,3},{2,0},{3,1},{4,6},{5,7},{6,4},{7,5},{8,10},{9,11},{10,... | collective-permute-start | bytes 1032200 | tf_op jit(solution)/shard_map/ppermute | solution.py:658
  63.6 3.6 %mixer_prepare.1 = (bf16[3,256,256]{2,1,0:T(8,128)(2,1)}, bf16[3,256,256]{2,1,0:T(8,128)(2,1)}, bf16[3,256,256]{2,1,0:T(8,128)(2,1)}, bf16[3,8,64,128]{3,2,1,0:T(8,128)(2,1)}, bf16[3,8,64,128]{3,2,1,0:T(8,128)(2,1)}) custom-call(s32[8]{0:T(128)} %heights.5, s32[8]{0:T(128)} %widths.5, bf16[24,8192]{1,0:T(8,128)(2,1)} %feat_ref.3, ...), custom_call_target="tpu_custom_call" | custom-call | bytes 12000000 | tf_op jit(solution)/shard_map/mixer_prepare/pallas_call | solution.py:777
  67.2 8.6 %collective-permute-done.15.refs_2_ = bf16[192,896]{1,0:T(8,128)(2,1)S(1)} collective-permute-done((bf16[192,896]{1,0:T(8,128)(2,1)S(1)}, bf16[192,896]{1,0:T(8,128)(2,1)S(1)}, u32[]{:S(2)}, u32[]{:S(2)}) %collective-permute-start.15) | collective-permute-done | bytes 344096 | tf_op jit(solution)/shard_map/ppermute | solution.py:658
  75.8 1.2 %collective-permute-done.16.refs_3_ = bf16[192,896]{1,0:T(8,128)(2,1)S(1)} collective-permute-done((bf16[192,896]{1,0:T(8,128)(2,1)S(1)}, bf16[192,896]{1,0:T(8,128)(2,1)S(1)}, u32[]{:S(2)}, u32[]{:S(2)}) %collective-permute-start.16) | collective-permute-done | bytes 344096 | tf_op jit(solution)/shard_map/ppermute | solution.py:658
  77.0 0.2 join.2
  77.1 1.3 %collective-permute-start.17 = (bf16[48,896]{1,0:T(8,128)(2,1)S(1)}, bf16[48,896]{1,0:T(8,128)(2,1)S(1)}, u32[]{:S(2)}, u32[]{:S(2)}) collective-permute-start(bf16[48,896]{1,0:T(8,128)(2,1)S(1)} %get-tuple-element.135), channel_id=1, source_target_pairs={{0,4},{1,5},{2,6},{3,7},{4,0},{5,1},{6,2},{7,3},{8,12},{9,13},{10,... | collective-permute-start | bytes 258056 | tf_op jit(solution)/shard_map/ppermute | solution.py:658
  78.4 2.8 %collective-permute-start.18 = (bf16[48,896]{1,0:T(8,128)(2,1)S(1)}, bf16[48,896]{1,0:T(8,128)(2,1)S(1)}, u32[]{:S(2)}, u32[]{:S(2)}) collective-permute-start(bf16[48,896]{1,0:T(8,128)(2,1)S(1)} %get-tuple-element.136), channel_id=1, source_target_pairs={{0,8},{1,9},{2,10},{3,11},{4,12},{5,13},{6,14},{7,15},{8,0},{9,1},... | collective-permute-start | bytes 258056 | tf_op jit(solution)/shard_map/ppermute | solution.py:658
  81.2 0.4 collective-permute-start.19
  81.6 0.0 all-to-all-done.1.both_ref
  81.6 6.9 %mixer_backward.1 = (bf16[24,8192]{1,0:T(8,128)(2,1)}, f32[24,8192]{1,0:T(8,128)}, f32[24,384]{1,0:T(8,128)S(1)}) custom-call(s32[8]{0:T(128)} %heights.5, s32[8]{0:T(128)} %widths.5, bf16[24,8192]{1,0:T(8,128)(2,1)} %feat_ref.3, bf16[24,8192]{1,0:T(8,128)(2,1)} %cot_ref.3, bf16[16,2,24,512]{3,2,1,0:T(8,128)(2,1)S(1)} %all-to-all-done.1.both_ref, ...), custom_call_target="tpu_custom_call" | custom-call | bytes 21000000 | tf_op jit(solution)/shard_map/mixer_backward/pallas_call | solution.py:792
  88.4 0.0 collective-permute-done.17.refs_1_
  88.5 0.0 collective-permute-done.18.refs_2_
  88.5 0.0 collective-permute-done.19.refs_3_
  88.5 0.1 collective-permute-start.20
  88.6 0.5 collective-permute-start.21
  89.1 0.9 %collective-permute-done.21.sibling_ref = f32[24,384]{1,0:T(8,128)S(1)} collective-permute-done((f32[24,384]{1,0:T(8,128)S(1)}, f32[24,384]{1,0:T(8,128)S(1)}, u32[]{:S(2)}, u32[]{:S(2)}) %collective-permute-start.21) | collective-permute-done | bytes 36896 | tf_op jit(solution)/shard_map/ppermute | solution.py:657
  90.1 0.0 collective-permute-done.20.other_ref
  90.1 0.8 finish.1
  (13 shorter events, 0.1 us)
Async XLA Ops:
  1.8 11.3 %collective-permute-start.2 = (bf16[48,896]{1,0:T(8,128)(2,1)S(1)}, bf16[48,896]{1,0:T(8,128)(2,1)S(1)}, u32[]{:S(2)}, u32[]{:S(2)}) collective-permute-start(bf16[48,896]{1,0:T(8,128)(2,1)S(1)} %pack.1), channel_id=1, source_target_pairs={{0,12},{1,13},{2,14},{3,15},{4,8},{5,9},{6,10},{7,11},{8,4},{9,5},... | collective-permute-start | bytes 258056 | tf_op jit(solution)/shard_map/ppermute | solution.py:658
  6.9 7.2 %collective-permute-start.1 = (bf16[48,896]{1,0:T(8,128)(2,1)S(1)}, bf16[48,896]{1,0:T(8,128)(2,1)S(1)}, u32[]{:S(2)}, u32[]{:S(2)}) collective-permute-start(bf16[48,896]{1,0:T(8,128)(2,1)S(1)} %pack.1), channel_id=1, source_target_pairs={{0,8},{1,9},{2,10},{3,11},{4,12},{5,13},{6,14},{7,15},{8,0},{9,1},... | collective-permute-start | bytes 258056 | tf_op jit(solution)/shard_map/ppermute | solution.py:658
  6.9 7.2 %collective-permute-start = (bf16[48,896]{1,0:T(8,128)(2,1)S(1)}, bf16[48,896]{1,0:T(8,128)(2,1)S(1)}, u32[]{:S(2)}, u32[]{:S(2)}) collective-permute-start(bf16[48,896]{1,0:T(8,128)(2,1)S(1)} %pack.1), channel_id=1, source_target_pairs={{0,4},{1,5},{2,6},{3,7},{4,0},{5,1},{6,2},{7,3},{8,12},{9,13},{10,... | collective-permute-start | bytes 258056 | tf_op jit(solution)/shard_map/ppermute | solution.py:658
  14.2 9.2 %collective-permute-start.4 = (bf16[192,896]{1,0:T(8,128)(2,1)S(1)}, bf16[192,896]{1,0:T(8,128)(2,1)S(1)}, u32[]{:S(2)}, u32[]{:S(2)}) collective-permute-start(bf16[192,896]{1,0:T(8,128)(2,1)S(1)} %constant_dynamic-update-slice_fusion.refs_0_), channel_id=1, source_target_pairs={{0,2},{1,3},{2,0},{3,1},{4,6},{5,7},{6,4},{7,5},{8,10},{9,11},{10,... | collective-permute-start | bytes 1032200 | tf_op jit(solution)/shard_map/ppermute | solution.py:658
  15.8 9.4 %collective-permute-start.3 = (bf16[192,896]{1,0:T(8,128)(2,1)S(1)}, bf16[192,896]{1,0:T(8,128)(2,1)S(1)}, u32[]{:S(2)}, u32[]{:S(2)}) collective-permute-start(bf16[192,896]{1,0:T(8,128)(2,1)S(1)} %constant_dynamic-update-slice_fusion.refs_0_), channel_id=1, source_target_pairs={{0,1},{1,0},{2,3},{3,2},{4,5},{5,4},{6,7},{7,6},{8,9},{9,8},{10,11... | collective-permute-start | bytes 1032200 | tf_op jit(solution)/shard_map/ppermute | solution.py:658
  17.3 17.3 %collective-permute-start.7 = (bf16[192,896]{1,0:T(8,128)(2,1)S(1)}, bf16[192,896]{1,0:T(8,128)(2,1)S(1)}, u32[]{:S(2)}, u32[]{:S(2)}) collective-permute-start(bf16[192,896]{1,0:T(8,128)(2,1)S(1)} %constant_dynamic-update-slice_fusion.refs_0_), channel_id=1, source_target_pairs={{0,16},{16,0},{1,17},{17,1},{2,18},{18,2},{3,19},{19,3},{4,20},{20... | collective-permute-start | bytes 1032200 | tf_op jit(solution)/shard_map/ppermute | solution.py:657
  17.3 24.2 %all-to-all-start = ((bf16[16,2,24,512]{3,2,1,0:T(8,128)(2,1)}), bf16[16,2,24,512]{3,2,1,0:T(8,128)(2,1)S(1)}, u32[]{:S(2)}, u32[]{:S(2)}) async-start(bf16[16,2,24,512]{3,2,1,0:T(8,128)(2,1)} %get-tuple-element.90), calls=%async_computation | async-start | bytes 1572864 | tf_op jit(solution)/shard_map/all_to_all | solution.py:659
  25.2 8.8 %collective-permute-start.5 = (bf16[96,896]{1,0:T(8,128)(2,1)S(1)}, bf16[96,896]{1,0:T(8,128)(2,1)S(1)}, u32[]{:S(2)}, u32[]{:S(2)}) collective-permute-start(bf16[96,896]{1,0:T(8,128)(2,1)S(1)} %get-tuple-element.97), channel_id=1, source_target_pairs={{0,2},{1,3},{2,0},{3,1},{4,6},{5,7},{6,4},{7,5},{8,10},{9,11},{10,... | collective-permute-start | bytes 516104 | tf_op jit(solution)/shard_map/ppermute | solution.py:658
  25.5 8.6 %collective-permute-start.6 = (bf16[96,896]{1,0:T(8,128)(2,1)S(1)}, bf16[96,896]{1,0:T(8,128)(2,1)S(1)}, u32[]{:S(2)}, u32[]{:S(2)}) collective-permute-start(bf16[96,896]{1,0:T(8,128)(2,1)S(1)} %get-tuple-element.98), channel_id=1, source_target_pairs={{0,1},{1,0},{2,3},{3,2},{4,5},{5,4},{6,7},{7,6},{8,9},{9,8},{10,11... | collective-permute-start | bytes 516104 | tf_op jit(solution)/shard_map/ppermute | solution.py:658
  27.5 8.2 %collective-permute-start.8 = (bf16[192,896]{1,0:T(8,128)(2,1)S(1)}, bf16[192,896]{1,0:T(8,128)(2,1)S(1)}, u32[]{:S(2)}, u32[]{:S(2)}) collective-permute-start(bf16[192,896]{1,0:T(8,128)(2,1)S(1)} %collective-permute-done.3.one_ref.refs_1_), channel_id=1, source_target_pairs={{0,16},{16,0},{1,17},{17,1},{2,18},{18,2},{3,19},{19,3},{4,20},{20... | collective-permute-start | bytes 1032200 | tf_op jit(solution)/shard_map/ppermute | solution.py:657
  27.5 8.2 %collective-permute-start.9 = (bf16[192,896]{1,0:T(8,128)(2,1)S(1)}, bf16[192,896]{1,0:T(8,128)(2,1)}, u32[]{:S(2)}, u32[]{:S(2)}) collective-permute-start(bf16[192,896]{1,0:T(8,128)(2,1)S(1)} %collective-permute-done.4.two_ref.refs_2_), channel_id=1, source_target_pairs={{0,16},{16,0},{1,17},{17,1},{2,18},{18,2},{3,19},{19,3},{4,20},{20... | collective-permute-start | bytes 1032200 | tf_op jit(solution)/shard_map/ppermute | solution.py:657
  34.0 1.4 %collective-permute-start.10 = (bf16[96,896]{1,0:T(8,128)(2,1)S(1)}, bf16[96,896]{1,0:T(8,128)(2,1)S(1)}, u32[]{:S(2)}, u32[]{:S(2)}) collective-permute-start(bf16[96,896]{1,0:T(8,128)(2,1)S(1)} %collective-permute-done.5.refs_3_), channel_id=1, source_target_pairs={{0,16},{16,0},{1,17},{17,1},{2,18},{18,2},{3,19},{19,3},{4,20},{20... | collective-permute-start | bytes 516104 | tf_op jit(solution)/shard_map/ppermute | solution.py:657
  34.1 1.6 %collective-permute-start.11 = (bf16[96,896]{1,0:T(8,128)(2,1)S(1)}, bf16[96,896]{1,0:T(8,128)(2,1)S(1)}, u32[]{:S(2)}, u32[]{:S(2)}) collective-permute-start(bf16[96,896]{1,0:T(8,128)(2,1)S(1)} %collective-permute-done.6.refs_4_), channel_id=1, source_target_pairs={{0,16},{16,0},{1,17},{17,1},{2,18},{18,2},{3,19},{19,3},{4,20},{20... | collective-permute-start | bytes 516104 | tf_op jit(solution)/shard_map/ppermute | solution.py:657
  34.6 6.9 %copy-start.2 = (bf16[192,896]{1,0:T(8,128)(2,1)}, bf16[192,896]{1,0:T(8,128)(2,1)S(1)}, u32[]{:S(2)}) copy-start(bf16[192,896]{1,0:T(8,128)(2,1)S(1)} %collective-permute-done.7.refs_5_) | copy-start | bytes 1032196
  35.5 6.0 %copy-start.4 = (bf16[96,896]{1,0:T(8,128)(2,1)}, bf16[96,896]{1,0:T(8,128)(2,1)S(1)}, u32[]{:S(2)}) copy-start(bf16[96,896]{1,0:T(8,128)(2,1)S(1)} %collective-permute-done.10.refs_8_) | copy-start | bytes 516100
  35.7 5.8 %copy-start.5 = (bf16[96,896]{1,0:T(8,128)(2,1)}, bf16[96,896]{1,0:T(8,128)(2,1)S(1)}, u32[]{:S(2)}) copy-start(bf16[96,896]{1,0:T(8,128)(2,1)S(1)} %collective-permute-done.11.refs_9_) | copy-start | bytes 516100
  35.7 5.8 %copy-start.3 = (bf16[192,896]{1,0:T(8,128)(2,1)}, bf16[192,896]{1,0:T(8,128)(2,1)S(1)}, u32[]{:S(2)}) copy-start(bf16[192,896]{1,0:T(8,128)(2,1)S(1)} %collective-permute-done.8.refs_6_) | copy-start | bytes 1032196
  46.0 4.8 %collective-permute-start.12 = (bf16[768,896]{1,0:T(8,128)(2,1)S(1)}, bf16[768,896]{1,0:T(8,128)(2,1)S(1)}, u32[]{:S(2)}, u32[]{:S(2)}) collective-permute-start(bf16[768,896]{1,0:T(8,128)(2,1)S(1)} %get-tuple-element.110), channel_id=1, source_target_pairs={{0,16},{16,0},{1,17},{17,1},{2,18},{18,2},{3,19},{19,3},{4,20},{20... | collective-permute-start | bytes 4128776 | tf_op jit(solution)/shard_map/ppermute | solution.py:657
  50.8 0.8 copy-start
  51.7 8.4 %copy-start.1 = (bf16[192,896]{1,0:T(8,128)(2,1)S(1)}, bf16[192,896]{1,0:T(8,128)(2,1)}, u32[]{:S(2)}) copy-start(bf16[192,896]{1,0:T(8,128)(2,1)} %copy-done) | copy-start | bytes 1032196
  51.7 7.3 %collective-permute-start.13 = (bf16[96,896]{1,0:T(8,128)(2,1)}, bf16[96,896]{1,0:T(8,128)(2,1)S(1)}, u32[]{:S(2)}, u32[]{:S(2)}) collective-permute-start(bf16[96,896]{1,0:T(8,128)(2,1)} %get-tuple-element.113), channel_id=1, source_target_pairs={{0,2},{1,3},{2,0},{3,1},{4,6},{5,7},{6,4},{7,5},{8,10},{9,11},{10,... | collective-permute-start | bytes 516104 | tf_op jit(solution)/shard_map/ppermute | solution.py:658
  53.3 6.8 %collective-permute-start.14 = (bf16[96,896]{1,0:T(8,128)(2,1)}, bf16[96,896]{1,0:T(8,128)(2,1)}, u32[]{:S(2)}, u32[]{:S(2)}) collective-permute-start(bf16[96,896]{1,0:T(8,128)(2,1)} %get-tuple-element.114), channel_id=1, source_target_pairs={{0,1},{1,0},{2,3},{3,2},{4,5},{5,4},{6,7},{7,6},{8,9},{9,8},{10,11... | collective-permute-start | bytes 516104 | tf_op jit(solution)/shard_map/ppermute | solution.py:658
  53.9 27.7 %all-to-all-start.1 = ((bf16[16,2,24,512]{3,2,1,0:T(8,128)(2,1)}), bf16[16,2,24,512]{3,2,1,0:T(8,128)(2,1)S(1)}, u32[]{:S(2)}, u32[]{:S(2)}) async-start(bf16[16,2,24,512]{3,2,1,0:T(8,128)(2,1)} %get-tuple-element.106), calls=%async_computation.1 | async-start | bytes 1572864 | tf_op jit(solution)/shard_map/all_to_all | solution.py:659
  61.2 14.6 %collective-permute-start.15 = (bf16[192,896]{1,0:T(8,128)(2,1)S(1)}, bf16[192,896]{1,0:T(8,128)(2,1)S(1)}, u32[]{:S(2)}, u32[]{:S(2)}) collective-permute-start(bf16[192,896]{1,0:T(8,128)(2,1)S(1)} %get-tuple-element.128), channel_id=1, source_target_pairs={{0,1},{1,0},{2,3},{3,2},{4,5},{5,4},{6,7},{7,6},{8,9},{9,8},{10,11... | collective-permute-start | bytes 1032200 | tf_op jit(solution)/shard_map/ppermute | solution.py:658
  62.1 14.8 %collective-permute-start.16 = (bf16[192,896]{1,0:T(8,128)(2,1)S(1)}, bf16[192,896]{1,0:T(8,128)(2,1)S(1)}, u32[]{:S(2)}, u32[]{:S(2)}) collective-permute-start(bf16[192,896]{1,0:T(8,128)(2,1)S(1)} %get-tuple-element.129), channel_id=1, source_target_pairs={{0,2},{1,3},{2,0},{3,1},{4,6},{5,7},{6,4},{7,5},{8,10},{9,11},{10,... | collective-permute-start | bytes 1032200 | tf_op jit(solution)/shard_map/ppermute | solution.py:658
  77.1 11.3 %collective-permute-start.17 = (bf16[48,896]{1,0:T(8,128)(2,1)S(1)}, bf16[48,896]{1,0:T(8,128)(2,1)S(1)}, u32[]{:S(2)}, u32[]{:S(2)}) collective-permute-start(bf16[48,896]{1,0:T(8,128)(2,1)S(1)} %get-tuple-element.135), channel_id=1, source_target_pairs={{0,4},{1,5},{2,6},{3,7},{4,0},{5,1},{6,2},{7,3},{8,12},{9,13},{10,... | collective-permute-start | bytes 258056 | tf_op jit(solution)/shard_map/ppermute | solution.py:658
  78.4 10.0 %collective-permute-start.18 = (bf16[48,896]{1,0:T(8,128)(2,1)S(1)}, bf16[48,896]{1,0:T(8,128)(2,1)S(1)}, u32[]{:S(2)}, u32[]{:S(2)}) collective-permute-start(bf16[48,896]{1,0:T(8,128)(2,1)S(1)} %get-tuple-element.136), channel_id=1, source_target_pairs={{0,8},{1,9},{2,10},{3,11},{4,12},{5,13},{6,14},{7,15},{8,0},{9,1},... | collective-permute-start | bytes 258056 | tf_op jit(solution)/shard_map/ppermute | solution.py:658
  81.2 7.2 %collective-permute-start.19 = (bf16[48,896]{1,0:T(8,128)(2,1)S(1)}, bf16[48,896]{1,0:T(8,128)(2,1)S(1)}, u32[]{:S(2)}, u32[]{:S(2)}) collective-permute-start(bf16[48,896]{1,0:T(8,128)(2,1)S(1)} %get-tuple-element.137), channel_id=1, source_target_pairs={{0,12},{1,13},{2,14},{3,15},{4,8},{5,9},{6,10},{7,11},{8,4},{9,5},... | collective-permute-start | bytes 258056 | tf_op jit(solution)/shard_map/ppermute | solution.py:658
  88.5 1.5 %collective-permute-start.20 = (f32[48,896]{1,0:T(8,128)S(1)}, f32[48,896]{1,0:T(8,128)S(1)}, u32[]{:S(2)}, u32[]{:S(2)}) collective-permute-start(f32[48,896]{1,0:T(8,128)S(1)} %join.3.mine_ref), channel_id=1, source_target_pairs={{0,16},{16,0},{1,17},{17,1},{2,18},{18,2},{3,19},{19,3},{4,20},{20... | collective-permute-start | bytes 516104 | tf_op jit(solution)/shard_map/ppermute | solution.py:657
  88.6 1.4 %collective-permute-start.21 = (f32[24,384]{1,0:T(8,128)S(1)}, f32[24,384]{1,0:T(8,128)S(1)}, u32[]{:S(2)}, u32[]{:S(2)}) collective-permute-start(f32[24,384]{1,0:T(8,128)S(1)} %get-tuple-element.143.small_ref), channel_id=1, source_target_pairs={{0,16},{16,0},{1,17},{17,1},{2,18},{18,2},{3,19},{19,3},{4,20},{20... | collective-permute-start | bytes 110600 | tf_op jit(solution)/shard_map/ppermute | solution.py:657

commit v6 on v5

--- a/solution.py
+++ b/solution.py
@@ -13,6 +13,7 @@
 LANES = 128
 PER = LANES // SIDE
 SLOT = 8
+EDGE = 16
 TILES = CELLS // LANES
 EPS = 1e-06
 F32 = jnp.float32
@@ -415,6 +416,14 @@
     second_ref[...] = two_ref[cut:]
 
 
+def start_kernel(one_ref, two_ref, arrived_ref, out_one, out_two):
+    cut = one_ref.shape[0]
+    at = arrived_ref.shape[0] - 2 * cut
+    for start, ref, out in ((at, one_ref, out_one), (at + cut, two_ref, out_two)):
+        total = ref[...].astype(F32) + arrived_ref[start : start + cut].astype(F32)
+        out[...] = total.astype(BF16)
+
+
 def relay_kernel(one_ref, two_ref, arrived_ref, first_ref, second_ref, out_one, out_two):
     tall = one_ref.shape[0]
     cut = tall // 2
@@ -434,18 +443,20 @@
     units, count = gin.shape
     channels, states = grate_h.shape
     keep = units // 2
+    deep = deep_of(mine_ref, count)
     first = half[0] == 0
     mine, other = mine_ref[...], other_ref[...]
-    low = jnp.where(first, mine, other)[:keep]
-    high = jnp.where(first, other, mine)[:keep]
-    for at, part in ((0, low), (keep, high)):
-        gin[at : at + keep] = part[:, :count]
-        gout[at : at + keep] = part[:, count : 2 * count]
-    bias = jnp.concatenate([low[:, 2 * count :], high[:, 2 * count :]], axis=0)
-    ginb[...] = as_row(bias[:, 0:1])
-    norms = (mine[:, 2 * count :] + other[:, 2 * count :])[:channels]
-    ggain[...] = as_row(norms[:, 1:2])
-    gshift[...] = as_row(norms[:, 2:3])
+    bias = []
+    for at, part in ((0, jnp.where(first, mine, other)), (keep, jnp.where(first, other, mine))):
+        for index in range(2 * count // LANES):
+            out = gin if index < count // LANES else gout
+            lanes = pl.ds(index * LANES % count, LANES)
+            out[at : at + keep, lanes] = part[index * deep : index * deep + keep]
+        bias.append(unfold(part[-EDGE:], 0, deep)[:keep])
+    ginb[...] = as_row(jnp.concatenate(bias, axis=0))
+    norms = mine[-EDGE:] + other[-EDGE:]
+    ggain[...] = as_row(unfold(norms, 1, deep)[:channels])
+    gshift[...] = as_row(unfold(norms, 2, deep)[:channels])
     total = small_ref[...] + sibling_ref[...]
     for index, ref in enumerate((gread_h, grate_h, gread_w, grate_w)):
         ref[...] = total[:, index * states : (index + 1) * states]
@@ -457,42 +468,79 @@
     gstep_w[...] = as_row(total[:, 68:69])
 
 
+def deep_of(ref, count, shards=1):
+    return (ref.shape[0] // shards - EDGE) * LANES // (2 * count)
+
+
+def fold(columns, deep):
+    lane = lane_of(EDGE)
+    pieces = deep // EDGE
+    tile = jnp.zeros((EDGE, LANES), F32)
+    for index, value in enumerate(columns):
+        if value is not None:
+            for p in range(pieces):
+                part = value[p * EDGE : (p + 1) * EDGE]
+                tile = jnp.where(lane == index * pieces + p, part, tile)
+    return tile
+
+
+def unfold(tile, index, deep):
+    pieces = deep // EDGE
+    first = index * pieces
+    return jnp.concatenate([tile[:, first + p : first + p + 1] for p in range(pieces)], axis=0)
+
+
 def pack_kernel(half, in_ref, out_ref, bias_ref, gain_ref, shift_ref, pack_ref):
-    deep = pack_ref.shape[0]
     own, count = out_ref.shape
+    deep = deep_of(pack_ref, count)
     channels = gain_ref.shape[1]
     keep = own // 2
     row = lax.broadcasted_iota(jnp.int32, (deep, own), 0)
     col = lax.broadcasted_iota(jnp.int32, (deep, own), 1)
     pick = jnp.where((col == row + half[0] * keep) & (row < keep), 1.0, 0.0).astype(BF16)
-    nt = (((1,), (1,)), ((), ()))
-    first = jnp.dot(pick, in_ref[...], preferred_element_type=F32)
-    second = jnp.dot(pick, out_ref[...], preferred_element_type=F32)
-    bias = jnp.broadcast_to(bias_ref[...], (LANES, own))
-    third = lax.dot_general(pick, bias, nt, preferred_element_type=F32)
+    first = dot(pick, in_ref[...]).astype(BF16)
+    second = dot(pick, out_ref[...]).astype(BF16)
+    bias = dot(pick, jnp.broadcast_to(bias_ref[...], (LANES, own)), NT)
     row = lax.broadcasted_iota(jnp.int32, (deep, channels), 0)
     col = lax.broadcasted_iota(jnp.int32, (deep, channels), 1)
     pick = jnp.where(col == row, 1.0, 0.0).astype(BF16)
-    gain = jnp.broadcast_to(gain_ref[...], (LANES, channels))
-    gain = lax.dot_general(pick, gain, nt, preferred_element_type=F32)
-    shift = jnp.broadcast_to(shift_ref[...], (LANES, channels))
-    shift = lax.dot_general(pick, shift, nt, preferred_element_type=F32)
-    lane = lane_of(deep)
-    third = jnp.where(lane == 0, third, jnp.where(lane == 1, gain, jnp.where(lane == 2, shift, 0.0)))
-    pack_ref[:, :count] = first.astype(BF16)
-    pack_ref[:, count : 2 * count] = second.astype(BF16)
-    pack_ref[:, 2 * count :] = third.astype(BF16)
+    gain = dot(pick, jnp.broadcast_to(gain_ref[...], (LANES, channels)), NT)
+    shift = dot(pick, jnp.broadcast_to(shift_ref[...], (LANES, channels)), NT)
+    half_tiles = count // LANES
+    for index in range(2 * half_tiles):
+        source = first if index < half_tiles else second
+        lanes = slice(index % half_tiles * LANES, (index % half_tiles + 1) * LANES)
+        pack_ref[index * deep : (index + 1) * deep] = source[:, lanes]
+    pack_ref[2 * half_tiles * deep :] = fold((bias, gain, shift), deep).astype(BF16)
 
 
 ROOT = math.sqrt(2.0 / math.pi)
 
 
-def perceptron(refs, act, down):
+def shards_of(ref, count, deep):
+    height = 2 * count // LANES * deep + EDGE
+    return range(0, ref.shape[0], height)
+
+
+def perceptron(refs, act, down, deep):
     count = act.shape[0]
-    w_in = jnp.concatenate([ref[:, :count] for ref in refs], axis=0)
-    w_out = jnp.concatenate([ref[:, count : 2 * count] for ref in refs], axis=0)
-    bias = jnp.concatenate([ref[:, 2 * count :] for ref in refs], axis=0).astype(F32)[:, 0:1]
-    v = dot(w_in, act) + bias
+    tiles = count // LANES
+
+    def matrix(first):
+        rows = []
+        for ref in refs:
+            for base in shards_of(ref, count, deep):
+                starts = [base + (first + j) * deep for j in range(tiles)]
+                rows.append(jnp.concatenate([ref[at : at + deep] for at in starts], axis=1))
+        return jnp.concatenate(rows, axis=0)
+
+    bias = []
+    for ref in refs:
+        for base in shards_of(ref, count, deep):
+            at = base + 2 * tiles * deep
+            bias.append(unfold(ref[at : at + EDGE].astype(F32), 0, deep))
+    w_in, w_out = matrix(0), matrix(tiles)
+    v = dot(w_in, act) + jnp.concatenate(bias, axis=0)
     square = v * v
     half = 0.5 * jnp.tanh(v * (ROOT * 0.044715 * square + ROOT)) + 0.5
     full = v * half
@@ -500,33 +548,41 @@
     slope = half + full * (1.0 - half) * (6.0 * ROOT * 0.044715 * square + 2.0 * ROOT)
     low = (dot(w_out, down) * slope).astype(BF16)
     g_bias = jnp.sum(low.astype(F32), axis=1, keepdims=True)
-    g_bias = jnp.where(lane_of(low.shape[0]) == 0, g_bias, 0.0)
-    grads = (dot(low, act, NT), dot(hidden, down, NT), g_bias)
+    grads = (dot(low, act, NT).astype(BF16), dot(hidden, down, NT).astype(BF16), g_bias)
     return dot(w_out, hidden, TN), dot(w_in, low, TN), grads
 
 
-def put(ref, grads, start):
+def put(ref, grads, start, deep, edges=None):
     count = grads[0].shape[1]
-    at = slice(start, start + ref.shape[0])
-    ref[:, :count] = grads[0][at].astype(BF16)
-    ref[:, count : 2 * count] = grads[1][at].astype(BF16)
-    ref[:, 2 * count :] = grads[2][at].astype(BF16)
-    return start + ref.shape[0]
-
-
-def spots_of(near, devices, deep, where_ref):
+    tiles = count // LANES
+    for base in shards_of(ref, count, deep):
+        for index in range(2 * tiles):
+            lanes = slice(index % tiles * LANES, (index % tiles + 1) * LANES)
+            at = base + index * deep
+            ref[at : at + deep] = grads[index // tiles][start : start + deep, lanes]
+        edge = fold((grads[2][start : start + deep],), deep)
+        if edges is None:
+            at = base + 2 * tiles * deep
+            ref[at : at + EDGE] = edge.astype(BF16)
+        else:
+            at = start // deep * EDGE
+            edges[at : at + EDGE] = edge
+        start += deep
+    return start
+
+
+def spots_of(near, devices, where_ref):
     z, xy = where_ref[0], where_ref[1]
     for d in range(devices):
         spot = ((d % near) ^ xy) * (devices // near) + ((d // near) ^ z)
-        yield d, pl.multiple_of(spot * deep, deep)
-
-
-def mlp_first(near, pieces, where_ref, given_ref, *refs):
+        yield d, pl.multiple_of(spot * EDGE, EDGE)
+
+
+def mlp_first(near, pieces, deep, where_ref, given_ref, *refs):
     own_in, refs = refs[:pieces], refs[pieces:]
     other_in, refs = refs[:pieces], refs[pieces:]
     gother_ref, active, downs, normal, inv_ref, gains, sum_ref, grad_ref, ext = refs
     devices, _, channels, _ = given_ref.shape
-    deep = ext.shape[0] // devices
     count = active.shape[0]
 
     value = jnp.concatenate([given_ref[d, 0].astype(F32) for d in range(devices)], axis=0)
@@ -540,32 +596,37 @@
     downs[...] = down.astype(BF16)
     at = 0
     for ref in own_in:
-        ext[at : at + ref.shape[0]] = ref[:, 2 * count :].astype(F32)
-        at += ref.shape[0]
-    for d, spot in spots_of(near, devices, deep, where_ref):
-        gains[d * channels : (d + 1) * channels] = ext[pl.ds(spot, deep), :][:channels]
+        for base in shards_of(ref, count, deep):
+            edge = base + 2 * count // LANES * deep
+            ext[at : at + EDGE] = ref[edge : edge + EDGE].astype(F32)
+            at += EDGE
+    lane = lane_of(channels)
+    for d, spot in spots_of(near, devices, where_ref):
+        tile = ext[pl.ds(spot, EDGE), :]
+        gain, shift = (unfold(tile, index, deep)[:channels] for index in (1, 2))
+        pair = jnp.where(lane == 1, gain, jnp.where(lane == 2, shift, 0.0))
+        gains[d * channels : (d + 1) * channels] = pair
     active[...] = (value * gains[:, 1:2] + gains[:, 2:3]).astype(BF16)
-    sums, total, grads = perceptron(other_in, active[...], downs[...])
-    put(gother_ref, grads, 0)
+    sums, total, grads = perceptron(other_in, active[...], downs[...], deep)
+    put(gother_ref, grads, 0, deep)
     sum_ref[...] = sums
     grad_ref[...] = total
 
 
 def mlp_second(
-    near, pieces, where_ref, active, downs, normal_ref, inv_ref, gains, sum_ref, grad_ref, *refs
+    near, pieces, deep, where_ref, active, downs, normal_ref, inv_ref, gains, sum_ref, grad_ref,
+    *refs,
 ):
     own_in, refs = refs[:pieces], refs[pieces:]
     both_ref, refs = refs[0], refs[1:]
     own_out, (gext,) = refs[:pieces], refs[pieces:]
     count = active.shape[0]
     devices, _, channels, _ = both_ref.shape
-    deep = gext.shape[0] // devices
-
-    sums, total, grads = perceptron(own_in, active[...], downs[...])
-    gext[...] = grads[2]
+
+    sums, total, grads = perceptron(own_in, active[...], downs[...], deep)
     start = 0
     for ref in own_out:
-        start = put(ref, grads, start)
+        start = put(ref, grads, start, deep, gext)
     summed = sum_ref[...] + sums
     agrad = grad_ref[...] + total
     norm = normal_ref[...]
@@ -576,18 +637,22 @@
     for d in range(devices):
         both_ref[d, 0] = mgrad[d * channels : (d + 1) * channels].astype(BF16)
         both_ref[d, 1] = summed[d * channels : (d + 1) * channels].astype(BF16)
-    lane = lane_of(count)
-    tile = jnp.where(lane == 1, jnp.sum(agrad * norm, axis=1, keepdims=True), 0.0)
-    tile = jnp.where(lane == 2, jnp.sum(agrad, axis=1, keepdims=True), tile)
-    for d, spot in spots_of(near, devices, deep, where_ref):
-        part = tile[d * channels : (d + 1) * channels]
-        if channels < deep:
-            part = jnp.concatenate([part, jnp.zeros((deep - channels, LANES), F32)], axis=0)
-        gext[pl.ds(spot, deep), :] += part
-    start = 0
+    by_gain = jnp.sum(agrad * norm, axis=1, keepdims=True)
+    by_shift = jnp.sum(agrad, axis=1, keepdims=True)
+    for d, spot in spots_of(near, devices, where_ref):
+        parts = []
+        for value in (by_gain, by_shift):
+            value = value[d * channels : (d + 1) * channels]
+            if channels < deep:
+                value = jnp.concatenate([value, jnp.zeros((deep - channels, 1), F32)], axis=0)
+            parts.append(value)
+        gext[pl.ds(spot, EDGE), :] += fold((None, *parts), deep)
+    at = 0
     for ref in own_out:
-        ref[:, 2 * count :] = gext[start : start + ref.shape[0]].astype(BF16)
-        start += ref.shape[0]
+        for base in shards_of(ref, count, deep):
+            edge = base + 2 * count // LANES * deep
+            ref[edge : edge + EDGE] = gext[at : at + EDGE].astype(BF16)
+            at += EDGE
 
 
 def whole(shape):
@@ -608,11 +673,11 @@
     return pl.pallas_call(
         partial(join_kernel, len(arrays)),
         out_shape=[
-            jax.ShapeDtypeStruct((deep, width), BF16 if i else F32) for i in range(count)
+            pltpu.VMEM((deep, width), BF16 if i else F32) for i in range(count)
         ],
         in_specs=[full] * len(arrays),
         out_specs=[full] * count,
-        compiler_params=params(8),
+        compiler_params=params(16),
         cost_estimate=pl.CostEstimate(flops=1 if count > 1 else 1, transcendentals=0, bytes_accessed=1_000_000),
         name="join",
     )(*arrays)
@@ -620,13 +685,13 @@
 
 def relay(*arrays):
     full = pl.BlockSpec(memory_space=pltpu.VMEM)
-    shape = jax.ShapeDtypeStruct(arrays[0].shape, BF16)
+    shape = pltpu.VMEM(arrays[0].shape, BF16)
     return pl.pallas_call(
         relay_kernel,
         out_shape=(shape, shape),
         in_specs=[full] * 5,
         out_specs=(full, full),
-        compiler_params=params(8),
+        compiler_params=params(16),
         cost_estimate=pl.CostEstimate(flops=100_000_000_000, transcendentals=0, bytes_accessed=1_000_000),
         name="relay",
     )(*arrays)
@@ -651,7 +716,8 @@
     far = 4
     near = ch // far
     deep = -(-(units // 2) // 16) * 16
-    width = 2 * count + LANES
+    tall_one = 2 * count // LANES * deep + EDGE
+    width = LANES
     near_groups = [[f * near + i for i in range(near)] for f in range(far)]
     row = lambda v: v.reshape(1, -1)
     exchange = lambda v: lax.ppermute(v, "img", [(0, 1), (1, 0)])
@@ -666,10 +732,10 @@
 
     pack = pl.pallas_call(
         pack_kernel,
-        out_shape=jax.ShapeDtypeStruct((deep, width), BF16),
+        out_shape=jax.ShapeDtypeStruct((tall_one, width), BF16),
         in_specs=[SMEM] + [full] * 5,
         out_specs=full,
-        compiler_params=params(4),
+        compiler_params=params(16),
         cost_estimate=cost(2),
         name="pack",
     )(
@@ -695,7 +761,7 @@
         scratch_shapes=[
             slots, toeplitz, toeplitz, pltpu.VMEM(square, BF16), pltpu.VMEM(square, F32),
         ],
-        compiler_params=params(12),
+        compiler_params=params(16),
         cost_estimate=cost(6),
         name="mixer_forward",
     )(
@@ -707,14 +773,14 @@
     given = swap(given)
     shard = jnp.concatenate(shards, axis=0)
     if near == 4:
-        cut = far * deep // 2
+        cut = far * tall_one // 2
         beside, above = pair(flip(shard, 1), flip(shard, 2))
         ends = pl.pallas_call(
             cut_kernel,
             out_shape=[jax.ShapeDtypeStruct((cut, width), BF16)] * 2,
             in_specs=[full] * 2,
             out_specs=[full] * 2,
-            compiler_params=params(4),
+            compiler_params=params(16),
             cost_estimate=pl.CostEstimate(flops=100_000_000_000, transcendentals=0, bytes_accessed=1_000_000),
             name="ends",
         )(beside, above)
@@ -722,16 +788,16 @@
         where = jnp.stack([place // near, place % near])
     else:
         own = [swap(jnp.broadcast_to(shard[None], (near,) + shard.shape), near_groups)]
-        own = [own[0].reshape(ch * deep, width)]
+        own = [own[0].reshape(ch * tall_one, width)]
         where = jnp.stack([place // near, place * 0])
     other = [exchange(piece) for piece in own]
 
-    rows = ch * deep
+    rows = ch * tall_one
     pieces = len(own)
     plane = jax.ShapeDtypeStruct((count, tokens), F32)
     token_low = jax.ShapeDtypeStruct((count, tokens), BF16)
     gother, *state = pl.pallas_call(
-        partial(mlp_first, near, pieces),
+        partial(mlp_first, near, pieces, deep),
         out_shape=[
             jax.ShapeDtypeStruct((rows, width), BF16), token_low, token_low, plane,
             jax.ShapeDtypeStruct((1, tokens), F32), jax.ShapeDtypeStruct((count, LANES), F32),
@@ -739,29 +805,37 @@
         ],
         in_specs=[SMEM] + [full] * (1 + 2 * pieces),
         out_specs=[full] * 8,
-        scratch_shapes=[pltpu.VMEM((rows, LANES), F32)],
+        scratch_shapes=[pltpu.VMEM((ch * EDGE, LANES), F32)],
         compiler_params=params(16),
         cost_estimate=cost(5),
         name="mlp_first",
-    )(where, given, *own, *map(pin, other))
+    )(where, given, *own, *other)
     arrived = exchange(gother)
     both, *gown = pl.pallas_call(
-        partial(mlp_second, near, pieces),
+        partial(mlp_second, near, pieces, deep),
         out_shape=[jax.ShapeDtypeStruct(both_shape, BF16)]
         + [jax.ShapeDtypeStruct(piece.shape, BF16) for piece in own],
         in_specs=[SMEM] + [full] * (7 + pieces),
         out_specs=[full] * (1 + pieces),
-        scratch_shapes=[pltpu.VMEM((rows, LANES), F32)],
+        scratch_shapes=[pltpu.VMEM((ch * EDGE, LANES), F32)],
         compiler_params=params(16),
         cost_estimate=cost(5),
         name="mlp_second",
     )(where, *state, *own)
     both = swap(both)
-    tall = far * deep
+    tall = far * tall_one
     if near == 4:
         cut = tall // 2
-        add = lambda v, at: (v.astype(F32) + arrived[at : at + v.shape[0]].astype(F32)).astype(BF16)
-        one, two = pair(add(gown[3], 3 * tall), add(gown[4], 3 * tall + cut))
+        part = pltpu.VMEM(gown[3].shape, BF16)
+        one, two = pl.pallas_call(
+            start_kernel,
+            out_shape=(part, part),
+            in_specs=[full] * 3,
+            out_specs=(full, full),
+            compiler_params=params(16),
+            cost_estimate=cost(1),
+            name="start",
+        )(gown[3], gown[4], arrived)
         one, two = pair(flip(one, 2), flip(two, 1))
         one, two = relay(gown[1], gown[2], arrived, one, two)
         features_last, one, two = pair(features, one, two)
@@ -782,12 +856,12 @@
         in_specs=[SMEM, SMEM, full, full],
         out_specs=(full,) * 5,
         scratch_shapes=[slots, pltpu.VMEM(square, F32)],
-        compiler_params=params(12),
+        compiler_params=params(16),
         cost_estimate=cost(4),
         name="mixer_prepare",
     )(pin(heights), pin(widths), pin(features_last), taps)
     *landed, _ = pair(*landed, prepared[0])
-    shards = join(deep, landed, far)
+    shards = join(tall_one, landed, far)
     shards = [shards[0]] + [flip(v, (i + 1) * near) for i, v in enumerate(shards[1:])]
     result, grad_features, small = pl.pallas_call(
         backward_kernel,
@@ -814,7 +888,7 @@
         *map(pin, prepared),
     )
     *shards, small = pair(*shards, small)
-    (mine,) = join(deep, shards, 1)
+    (mine,) = join(tall_one, shards, 1)
     vector_out = jax.ShapeDtypeStruct((1, channels), F32)
     state_out = jax.ShapeDtypeStruct((channels, states), F32)
     weight_out = jax.ShapeDtypeStruct((units, count), F32)
@@ -827,7 +901,7 @@
         ),
         in_specs=[SMEM] + [full] * 4,
         out_specs=(full,) * 14,
-        compiler_params=params(4),
+        compiler_params=params(16),
         cost_estimate=cost(1),
         name="finish",
     )(half.reshape(1), mine, exchange(mine), small, exchange(small))

time: 91.5 us -> 89.4 us (0.977)
  waiting for transfers between devices: 29.6 us -> 27.3 us
  starting transfers between devices: 31 us -> 32 us
    ppermute x14, waiting for transfers between devices: 21.8 us -> 18.8 us  [per_device(): lax.ppermute(v, 'ch', [(i, i ^ bits) for i in range(ch)])]
    pallas_call x5 -> x6, Pallas kernels: 10.6 us -> 10.7 us  [the longest x1 4.89 us: per_device(): pl.pallas_call(partial(mlp_second, near, pieces, deep), out_shape=[jax.Sh...]
  transfers between devices with their start and end apart: 24 -> 24, of which waited for: 11 -> 11; matrix products, arithmetic and copies ran while one was open for 0% -> 0% of each run, Pallas kernels for 24% -> 25%
where the time goes in v6:
time: 89.4 us; the launch traced here: 89 us
  starting transfers between devices  32 us (36%)
  Pallas kernels  28.6 us (32%)
  waiting for transfers between devices  27.3 us (31%)
  between operations  0.94 us (1%)
    ppermute x14, starting transfers between devices, per_device(): lax.ppermute(v, 'ch', [(i, i ^ bits) for i in range(ch)])  20.4 us
    ppermute x14, waiting for transfers between devices, per_device(): lax.ppermute(v, 'ch', [(i, i ^ bits) for i in range(ch)])  18.8 us
    all_to_all x2, starting transfers between devices, per_device(): lax.all_to_all(v, 'ch', split_axis=0, concat_axis=0, tiled=True, axis_ind...  9.9 us
    pallas_call x1, Pallas kernels, per_device(): pl.pallas_call(backward_kernel, out_shape=(jax.ShapeDtypeStruct((channels...  6.85 us
    all_to_all x2, waiting for transfers between devices, per_device(): lax.all_to_all(v, 'ch', split_axis=0, concat_axis=0, tiled=True, axis_ind...  6.6 us
    pallas_call x1, Pallas kernels, per_device(): pl.pallas_call(forward_kernel, out_shape=(jax.ShapeDtypeStruct(both_shape...  5.54 us
    pallas_call x1, Pallas kernels, per_device(): pl.pallas_call(partial(mlp_second, near, pieces, deep), out_shape=[jax.Sh...  4.89 us
    pallas_call x1, Pallas kernels, per_device(): pl.pallas_call(partial(mlp_first, near, pieces, deep), out_shape=[jax.Sha...  3.75 us
  transfers between devices with their start and end apart: 24, of which 11 were waited for; matrix products, arithmetic and copies ran while one was open for 0% of the time, Pallas kernels for 25%

profile of v6, /device:TPU:0, one launch (start us, length us, event | category | flops | bytes accessed | tf_op | source)
XLA Modules:
  0.0 89.0 jit_solution(4153294501088673836)
XLA Ops:
  0.7 1.2 %pack.1 = bf16[304,128]{1,0:T(8,128)(2,1)S(1)} custom-call(s32[1]{0:T(128)} %bitcast.2.half, bf16[96,384]{1,0:T(8,128)(2,1)} %bitcast.21, bf16[96,384]{1,0:T(8,128)(2,1)} %out_ref.1, bf16[1,96]{1,0:T(2,128)(2,1)} %bitcast.28, bf16[1,24]{1,0:T(2,128)(2,1)} %bitcast.29, bf16[1,24]{1,0:T(2,128)(2,1)} %bitcast.30), custom_call_target="tpu_custom_call" | custom-call | bytes 6000000 | tf_op jit(solution)/shard_map/pack/pallas_call | solution.py:733
  1.8 5.1 %collective-permute-start.2 = (bf16[304,128]{1,0:T(8,128)(2,1)S(1)}, bf16[304,128]{1,0:T(8,128)(2,1)S(1)}, u32[]{:S(2)}, u32[]{:S(2)}) collective-permute-start(bf16[304,128]{1,0:T(8,128)(2,1)S(1)} %pack.1), channel_id=1, source_target_pairs={{0,12},{1,13},{2,14},{3,15},{4,8},{5,9},{6,10},{7,11},{8,4},{9,5},... | collective-permute-start | bytes 233480 | tf_op jit(solution)/shard_map/ppermute | solution.py:724
  6.9 0.0 collective-permute-start.1
  6.9 0.6 collective-permute-start
  7.6 5.5 %mixer_forward.1 = (bf16[16,2,24,512]{3,2,1,0:T(8,128)(2,1)}, f32[24,128]{1,0:T(8,128)S(1)}) custom-call(s32[8]{0:T(128)} %heights.5, s32[8]{0:T(128)} %widths.5, bf16[24,8192]{1,0:T(8,128)(2,1)} %feat_ref.3, bf16[24,8192]{1,0:T(8,128)(2,1)} %cot_ref.3, f32[1,24]{1,0:T(1,128)} %bitcast.22, f32[1,24]{1,0:T(1,128)} %bitcast.24, f32[1,24]{1,0:T(1,128)} %bitcast.26, ...), custom_call_target="tpu_custom_call" | custom-call | bytes 18000000 | tf_op jit(solution)/shard_map/mixer_forward/pallas_call | solution.py:753
  13.1 0.0 collective-permute-done.2
  13.1 0.3 collective-permute-done.1
  13.5 0.0 collective-permute-done
  13.5 1.6 %collective-permute-start.4 = (bf16[1216,128]{1,0:T(8,128)(2,1)S(1)}, bf16[1216,128]{1,0:T(8,128)(2,1)S(1)}, u32[]{:S(2)}, u32[]{:S(2)}) collective-permute-start(bf16[1216,128]{1,0:T(8,128)(2,1)S(1)} %constant_dynamic-update-slice_fusion.refs_0_), channel_id=1, source_target_pairs={{0,2},{1,3},{2,0},{3,1},{4,6},{5,7},{6,4},{7,5},{8,10},{9,11},{10,... | collective-permute-start | bytes 933896 | tf_op jit(solution)/shard_map/ppermute | solution.py:724
  15.1 1.5 %collective-permute-start.3 = (bf16[1216,128]{1,0:T(8,128)(2,1)S(1)}, bf16[1216,128]{1,0:T(8,128)(2,1)S(1)}, u32[]{:S(2)}, u32[]{:S(2)}) collective-permute-start(bf16[1216,128]{1,0:T(8,128)(2,1)S(1)} %constant_dynamic-update-slice_fusion.refs_0_), channel_id=1, source_target_pairs={{0,1},{1,0},{2,3},{3,2},{4,5},{5,4},{6,7},{7,6},{8,9},{9,8},{10,11... | collective-permute-start | bytes 933896 | tf_op jit(solution)/shard_map/ppermute | solution.py:724
  16.6 0.0 collective-permute-start.7
  16.6 4.8 %all-to-all-start = ((bf16[16,2,24,512]{3,2,1,0:T(8,128)(2,1)}), bf16[16,2,24,512]{3,2,1,0:T(8,128)(2,1)S(1)}, u32[]{:S(2)}, u32[]{:S(2)}) async-start(bf16[16,2,24,512]{3,2,1,0:T(8,128)(2,1)} %get-tuple-element.90), calls=%async_computation | async-start | bytes 1572864 | tf_op jit(solution)/shard_map/all_to_all | solution.py:725
  21.4 0.8 collective-permute-done.4.two_ref.refs_2_
  22.2 1.4 %collective-permute-done.3.one_ref.refs_1_ = bf16[1216,128]{1,0:T(8,128)(2,1)S(1)} collective-permute-done((bf16[1216,128]{1,0:T(8,128)(2,1)S(1)}, bf16[1216,128]{1,0:T(8,128)(2,1)S(1)}, u32[]{:S(2)}, u32[]{:S(2)}) %collective-permute-start.3) | collective-permute-done | bytes 311328 | tf_op jit(solution)/shard_map/ppermute | solution.py:724
  23.7 0.4 collective-permute-start.5
  24.1 1.6 %collective-permute-start.6 = (bf16[608,128]{1,0:T(8,128)(2,1)S(1)}, bf16[608,128]{1,0:T(8,128)(2,1)S(1)}, u32[]{:S(2)}, u32[]{:S(2)}) collective-permute-start(bf16[608,128]{1,0:T(8,128)(2,1)S(1)} %get-tuple-element.98), channel_id=1, source_target_pairs={{0,1},{1,0},{2,3},{3,2},{4,5},{5,4},{6,7},{7,6},{8,9},{9,8},{10,11... | collective-permute-start | bytes 466952 | tf_op jit(solution)/shard_map/ppermute | solution.py:724
  25.8 0.0 collective-permute-start.8
  25.8 0.5 collective-permute-start.9
  26.3 7.0 %collective-permute-done.5.refs_3_ = bf16[608,128]{1,0:T(8,128)(2,1)S(1)} collective-permute-done((bf16[608,128]{1,0:T(8,128)(2,1)S(1)}, bf16[608,128]{1,0:T(8,128)(2,1)S(1)}, u32[]{:S(2)}, u32[]{:S(2)}) %collective-permute-start.5) | collective-permute-done | bytes 155680 | tf_op jit(solution)/shard_map/ppermute | solution.py:724
  33.3 0.0 collective-permute-start.10
  33.3 0.0 collective-permute-done.6.refs_4_
  33.3 0.5 collective-permute-start.11
  33.8 0.1 pad_add_fusion.where_ref
  33.9 0.0 collective-permute-done.7.refs_5_
  33.9 0.8 collective-permute-done.10.refs_8_
  34.7 0.2 collective-permute-done.11.refs_9_
  34.9 0.0 collective-permute-done.8.refs_6_
  34.9 0.0 collective-permute-done.9.refs_7_
  34.9 6.6 %all-to-all-done.given_ref = bf16[16,2,24,512]{3,2,1,0:T(8,128)(2,1)S(1)} async-done(((bf16[16,2,24,512]{3,2,1,0:T(8,128)(2,1)}), bf16[16,2,24,512]{3,2,1,0:T(8,128)(2,1)S(1)}, u32[]{:S(2)}, u32[]{:S(2)}) %all-to-all-start) | async-done | bytes 786464 | tf_op jit(solution)/shard_map/all_to_all | solution.py:725
  41.5 3.7 %mlp_first.1 = (bf16[4864,128]{1,0:T(8,128)(2,1)S(1)}, bf16[384,512]{1,0:T(8,128)(2,1)S(1)}, bf16[384,512]{1,0:T(8,128)(2,1)S(1)}, f32[384,512]{1,0:T(8,128)S(1)...) custom-call(s32[2]{0:T(128)S(1)} %pad_add_fusion.where_ref, ...), custom_call_target="tpu_custom_call" | custom-call | bytes 15000000 | tf_op jit(solution)/shard_map/mlp_first/pallas_call | solution.py:799
  45.2 0.1 collective-permute-start.12
  45.3 4.9 %mlp_second.1 = (bf16[16,2,24,512]{3,2,1,0:T(8,128)(2,1)}, bf16[1216,128]{1,0:T(8,128)(2,1)S(1)}, bf16[1216,128]{1,0:T(8,128)(2,1)S(1)}, bf16[1216,128]{1,0:T(8,...) custom-call(s32[2]{0:T(128)S(1)} %pad_add_fusion.where_ref, ...), custom_call_target="tpu_custom_call" | custom-call | bytes 15000000 | tf_op jit(solution)/shard_map/mlp_second/pallas_call | solution.py:814
  50.2 0.0 collective-permute-done.12.arrived_ref.refs_1_
  50.2 0.7 start.1
  50.9 1.6 %collective-permute-start.13 = (bf16[608,128]{1,0:T(8,128)(2,1)}, bf16[608,128]{1,0:T(8,128)(2,1)S(1)}, u32[]{:S(2)}, u32[]{:S(2)}) collective-permute-start(bf16[608,128]{1,0:T(8,128)(2,1)} %get-tuple-element.113), channel_id=1, source_target_pairs={{0,2},{1,3},{2,0},{3,1},{4,6},{5,7},{6,4},{7,5},{8,10},{9,11},{10,... | collective-permute-start | bytes 466952 | tf_op jit(solution)/shard_map/ppermute | solution.py:724
  52.5 0.6 collective-permute-start.14
  53.1 5.1 %all-to-all-start.1 = ((bf16[16,2,24,512]{3,2,1,0:T(8,128)(2,1)}), bf16[16,2,24,512]{3,2,1,0:T(8,128)(2,1)S(1)}, u32[]{:S(2)}, u32[]{:S(2)}) async-start(bf16[16,2,24,512]{3,2,1,0:T(8,128)(2,1)} %get-tuple-element.106), calls=%async_computation.1 | async-start | bytes 1572864 | tf_op jit(solution)/shard_map/all_to_all | solution.py:725
  58.2 0.0 collective-permute-done.13.first_ref
  58.2 0.6 collective-permute-done.14.second_ref
  58.8 1.1 %relay.1 = (bf16[1216,128]{1,0:T(8,128)(2,1)S(1)}, bf16[1216,128]{1,0:T(8,128)(2,1)S(1)}) custom-call(bf16[1216,128]{1,0:T(8,128)(2,1)S(1)} %get-tuple-element.108.one_ref, bf16[1216,128]{1,0:T(8,128)(2,1)S(1)} %get-tuple-element.109.two_ref, bf16[4864,128]{1,0:T(8,128)(2,1)S(1)} %collective-permute-done.12.arrived_ref.refs_1_, ...), custom_call_target="tpu_custom_call" | custom-call | flops 99999997952 | bytes 1000000 | tf_op jit(solution)/shard_map/relay/pallas_call | solution.py:689
  59.9 1.4 %collective-permute-start.15 = (bf16[1216,128]{1,0:T(8,128)(2,1)S(1)}, bf16[1216,128]{1,0:T(8,128)(2,1)S(1)}, u32[]{:S(2)}, u32[]{:S(2)}) collective-permute-start(bf16[1216,128]{1,0:T(8,128)(2,1)S(1)} %get-tuple-element.128), channel_id=1, source_target_pairs={{0,1},{1,0},{2,3},{3,2},{4,5},{5,4},{6,7},{7,6},{8,9},{9,8},{10,11... | collective-permute-start | bytes 933896 | tf_op jit(solution)/shard_map/ppermute | solution.py:724
  61.3 1.5 %collective-permute-start.16 = (bf16[1216,128]{1,0:T(8,128)(2,1)S(1)}, bf16[1216,128]{1,0:T(8,128)(2,1)S(1)}, u32[]{:S(2)}, u32[]{:S(2)}) collective-permute-start(bf16[1216,128]{1,0:T(8,128)(2,1)S(1)} %get-tuple-element.129), channel_id=1, source_target_pairs={{0,2},{1,3},{2,0},{3,1},{4,6},{5,7},{6,4},{7,5},{8,10},{9,11},{10,... | collective-permute-start | bytes 933896 | tf_op jit(solution)/shard_map/ppermute | solution.py:724
  62.8 3.5 %mixer_prepare.1 = (bf16[3,256,256]{2,1,0:T(8,128)(2,1)}, bf16[3,256,256]{2,1,0:T(8,128)(2,1)}, bf16[3,256,256]{2,1,0:T(8,128)(2,1)}, bf16[3,8,64,128]{3,2,1,0:T(8,128)(2,1)}, bf16[3,8,64,128]{3,2,1,0:T(8,128)(2,1)}) custom-call(s32[8]{0:T(128)} %heights.5, s32[8]{0:T(128)} %widths.5, bf16[24,8192]{1,0:T(8,128)(2,1)} %feat_ref.3, ...), custom_call_target="tpu_custom_call" | custom-call | bytes 12000000 | tf_op jit(solution)/shard_map/mixer_prepare/pallas_call | solution.py:851
  66.3 7.8 %collective-permute-done.15.refs_2_ = bf16[1216,128]{1,0:T(8,128)(2,1)S(1)} collective-permute-done((bf16[1216,128]{1,0:T(8,128)(2,1)S(1)}, bf16[1216,128]{1,0:T(8,128)(2,1)S(1)}, u32[]{:S(2)}, u32[]{:S(2)}) %collective-permute-start.15) | collective-permute-done | bytes 311328 | tf_op jit(solution)/shard_map/ppermute | solution.py:724
  74.1 0.8 collective-permute-done.16.refs_3_
  74.9 0.2 join.2
  75.1 1.9 %collective-permute-start.17 = (bf16[304,128]{1,0:T(8,128)(2,1)S(1)}, bf16[304,128]{1,0:T(8,128)(2,1)S(1)}, u32[]{:S(2)}, u32[]{:S(2)}) collective-permute-start(bf16[304,128]{1,0:T(8,128)(2,1)S(1)} %get-tuple-element.135), channel_id=1, source_target_pairs={{0,4},{1,5},{2,6},{3,7},{4,0},{5,1},{6,2},{7,3},{8,12},{9,13},{10,... | collective-permute-start | bytes 233480 | tf_op jit(solution)/shard_map/ppermute | solution.py:724
  77.0 2.3 %collective-permute-start.18 = (bf16[304,128]{1,0:T(8,128)(2,1)S(1)}, bf16[304,128]{1,0:T(8,128)(2,1)S(1)}, u32[]{:S(2)}, u32[]{:S(2)}) collective-permute-start(bf16[304,128]{1,0:T(8,128)(2,1)S(1)} %get-tuple-element.136), channel_id=1, source_target_pairs={{0,8},{1,9},{2,10},{3,11},{4,12},{5,13},{6,14},{7,15},{8,0},{9,1},... | collective-permute-start | bytes 233480 | tf_op jit(solution)/shard_map/ppermute | solution.py:724
  79.3 0.2 collective-permute-start.19
  79.5 0.0 all-to-all-done.1.both_ref
  79.5 6.9 %mixer_backward.1 = (bf16[24,8192]{1,0:T(8,128)(2,1)}, f32[24,8192]{1,0:T(8,128)}, f32[24,384]{1,0:T(8,128)S(1)}) custom-call(s32[8]{0:T(128)} %heights.5, s32[8]{0:T(128)} %widths.5, bf16[24,8192]{1,0:T(8,128)(2,1)} %feat_ref.3, bf16[24,8192]{1,0:T(8,128)(2,1)} %cot_ref.3, bf16[16,2,24,512]{3,2,1,0:T(8,128)(2,1)S(1)} %all-to-all-done.1.both_ref, ...), custom_call_target="tpu_custom_call" | custom-call | bytes 21000000 | tf_op jit(solution)/shard_map/mixer_backward/pallas_call | solution.py:866
  86.4 0.0 collective-permute-done.17.refs_1_
  86.4 0.0 collective-permute-done.18.refs_2_
  86.4 0.0 collective-permute-done.19.refs_3_
  86.5 0.1 collective-permute-start.20
  86.5 0.5 collective-permute-start.21
  87.0 0.9 %collective-permute-done.21.sibling_ref = f32[24,384]{1,0:T(8,128)S(1)} collective-permute-done((f32[24,384]{1,0:T(8,128)S(1)}, f32[24,384]{1,0:T(8,128)S(1)}, u32[]{:S(2)}, u32[]{:S(2)}) %collective-permute-start.21) | collective-permute-done | bytes 36896 | tf_op jit(solution)/shard_map/ppermute | solution.py:723
  88.0 0.0 collective-permute-done.20.other_ref
  88.0 0.9 finish.1
  (6 shorter events, 0.1 us)
Async XLA Ops:
  1.8 11.3 %collective-permute-start.2 = (bf16[304,128]{1,0:T(8,128)(2,1)S(1)}, bf16[304,128]{1,0:T(8,128)(2,1)S(1)}, u32[]{:S(2)}, u32[]{:S(2)}) collective-permute-start(bf16[304,128]{1,0:T(8,128)(2,1)S(1)} %pack.1), channel_id=1, source_target_pairs={{0,12},{1,13},{2,14},{3,15},{4,8},{5,9},{6,10},{7,11},{8,4},{9,5},... | collective-permute-start | bytes 233480 | tf_op jit(solution)/shard_map/ppermute | solution.py:724
  6.9 6.5 %collective-permute-start.1 = (bf16[304,128]{1,0:T(8,128)(2,1)S(1)}, bf16[304,128]{1,0:T(8,128)(2,1)S(1)}, u32[]{:S(2)}, u32[]{:S(2)}) collective-permute-start(bf16[304,128]{1,0:T(8,128)(2,1)S(1)} %pack.1), channel_id=1, source_target_pairs={{0,8},{1,9},{2,10},{3,11},{4,12},{5,13},{6,14},{7,15},{8,0},{9,1},... | collective-permute-start | bytes 233480 | tf_op jit(solution)/shard_map/ppermute | solution.py:724
  6.9 6.5 %collective-permute-start = (bf16[304,128]{1,0:T(8,128)(2,1)S(1)}, bf16[304,128]{1,0:T(8,128)(2,1)S(1)}, u32[]{:S(2)}, u32[]{:S(2)}) collective-permute-start(bf16[304,128]{1,0:T(8,128)(2,1)S(1)} %pack.1), channel_id=1, source_target_pairs={{0,4},{1,5},{2,6},{3,7},{4,0},{5,1},{6,2},{7,3},{8,12},{9,13},{10,... | collective-permute-start | bytes 233480 | tf_op jit(solution)/shard_map/ppermute | solution.py:724
  13.5 8.7 %collective-permute-start.4 = (bf16[1216,128]{1,0:T(8,128)(2,1)S(1)}, bf16[1216,128]{1,0:T(8,128)(2,1)S(1)}, u32[]{:S(2)}, u32[]{:S(2)}) collective-permute-start(bf16[1216,128]{1,0:T(8,128)(2,1)S(1)} %constant_dynamic-update-slice_fusion.refs_0_), channel_id=1, source_target_pairs={{0,2},{1,3},{2,0},{3,1},{4,6},{5,7},{6,4},{7,5},{8,10},{9,11},{10,... | collective-permute-start | bytes 933896 | tf_op jit(solution)/shard_map/ppermute | solution.py:724
  15.1 8.6 %collective-permute-start.3 = (bf16[1216,128]{1,0:T(8,128)(2,1)S(1)}, bf16[1216,128]{1,0:T(8,128)(2,1)S(1)}, u32[]{:S(2)}, u32[]{:S(2)}) collective-permute-start(bf16[1216,128]{1,0:T(8,128)(2,1)S(1)} %constant_dynamic-update-slice_fusion.refs_0_), channel_id=1, source_target_pairs={{0,1},{1,0},{2,3},{3,2},{4,5},{5,4},{6,7},{7,6},{8,9},{9,8},{10,11... | collective-permute-start | bytes 933896 | tf_op jit(solution)/shard_map/ppermute | solution.py:724
  16.6 17.3 %collective-permute-start.7 = (bf16[1216,128]{1,0:T(8,128)(2,1)S(1)}, bf16[1216,128]{1,0:T(8,128)(2,1)S(1)}, u32[]{:S(2)}, u32[]{:S(2)}) collective-permute-start(bf16[1216,128]{1,0:T(8,128)(2,1)S(1)} %constant_dynamic-update-slice_fusion.refs_0_), channel_id=1, source_target_pairs={{0,16},{16,0},{1,17},{17,1},{2,18},{18,2},{3,19},{19,3},{4,20},{20... | collective-permute-start | bytes 933896 | tf_op jit(solution)/shard_map/ppermute | solution.py:723
  16.6 24.9 %all-to-all-start = ((bf16[16,2,24,512]{3,2,1,0:T(8,128)(2,1)}), bf16[16,2,24,512]{3,2,1,0:T(8,128)(2,1)S(1)}, u32[]{:S(2)}, u32[]{:S(2)}) async-start(bf16[16,2,24,512]{3,2,1,0:T(8,128)(2,1)} %get-tuple-element.90), calls=%async_computation | async-start | bytes 1572864 | tf_op jit(solution)/shard_map/all_to_all | solution.py:725
  23.7 9.6 %collective-permute-start.5 = (bf16[608,128]{1,0:T(8,128)(2,1)S(1)}, bf16[608,128]{1,0:T(8,128)(2,1)S(1)}, u32[]{:S(2)}, u32[]{:S(2)}) collective-permute-start(bf16[608,128]{1,0:T(8,128)(2,1)S(1)} %get-tuple-element.97), channel_id=1, source_target_pairs={{0,2},{1,3},{2,0},{3,1},{4,6},{5,7},{6,4},{7,5},{8,10},{9,11},{10,... | collective-permute-start | bytes 466952 | tf_op jit(solution)/shard_map/ppermute | solution.py:724
  24.1 9.2 %collective-permute-start.6 = (bf16[608,128]{1,0:T(8,128)(2,1)S(1)}, bf16[608,128]{1,0:T(8,128)(2,1)S(1)}, u32[]{:S(2)}, u32[]{:S(2)}) collective-permute-start(bf16[608,128]{1,0:T(8,128)(2,1)S(1)} %get-tuple-element.98), channel_id=1, source_target_pairs={{0,1},{1,0},{2,3},{3,2},{4,5},{5,4},{6,7},{7,6},{8,9},{9,8},{10,11... | collective-permute-start | bytes 466952 | tf_op jit(solution)/shard_map/ppermute | solution.py:724
  25.8 9.1 %collective-permute-start.8 = (bf16[1216,128]{1,0:T(8,128)(2,1)S(1)}, bf16[1216,128]{1,0:T(8,128)(2,1)S(1)}, u32[]{:S(2)}, u32[]{:S(2)}) collective-permute-start(bf16[1216,128]{1,0:T(8,128)(2,1)S(1)} %collective-permute-done.3.one_ref.refs_1_), channel_id=1, source_target_pairs={{0,16},{16,0},{1,17},{17,1},{2,18},{18,2},{3,19},{19,3},{4,20},{20... | collective-permute-start | bytes 933896 | tf_op jit(solution)/shard_map/ppermute | solution.py:723
  25.8 9.1 %collective-permute-start.9 = (bf16[1216,128]{1,0:T(8,128)(2,1)S(1)}, bf16[1216,128]{1,0:T(8,128)(2,1)S(1)}, u32[]{:S(2)}, u32[]{:S(2)}) collective-permute-start(bf16[1216,128]{1,0:T(8,128)(2,1)S(1)} %collective-permute-done.4.two_ref.refs_2_), channel_id=1, source_target_pairs={{0,16},{16,0},{1,17},{17,1},{2,18},{18,2},{3,19},{19,3},{4,20},{20... | collective-permute-start | bytes 933896 | tf_op jit(solution)/shard_map/ppermute | solution.py:723
  33.3 1.4 %collective-permute-start.10 = (bf16[608,128]{1,0:T(8,128)(2,1)S(1)}, bf16[608,128]{1,0:T(8,128)(2,1)S(1)}, u32[]{:S(2)}, u32[]{:S(2)}) collective-permute-start(bf16[608,128]{1,0:T(8,128)(2,1)S(1)} %collective-permute-done.5.refs_3_), channel_id=1, source_target_pairs={{0,16},{16,0},{1,17},{17,1},{2,18},{18,2},{3,19},{19,3},{4,20},{20... | collective-permute-start | bytes 466952 | tf_op jit(solution)/shard_map/ppermute | solution.py:723
  33.3 1.6 %collective-permute-start.11 = (bf16[608,128]{1,0:T(8,128)(2,1)S(1)}, bf16[608,128]{1,0:T(8,128)(2,1)S(1)}, u32[]{:S(2)}, u32[]{:S(2)}) collective-permute-start(bf16[608,128]{1,0:T(8,128)(2,1)S(1)} %collective-permute-done.6.refs_4_), channel_id=1, source_target_pairs={{0,16},{16,0},{1,17},{17,1},{2,18},{18,2},{3,19},{19,3},{4,20},{20... | collective-permute-start | bytes 466952 | tf_op jit(solution)/shard_map/ppermute | solution.py:723
  45.2 5.0 %collective-permute-start.12 = (bf16[4864,128]{1,0:T(8,128)(2,1)S(1)}, bf16[4864,128]{1,0:T(8,128)(2,1)S(1)}, u32[]{:S(2)}, u32[]{:S(2)}) collective-permute-start(bf16[4864,128]{1,0:T(8,128)(2,1)S(1)} %get-tuple-element.110), channel_id=1, source_target_pairs={{0,16},{16,0},{1,17},{17,1},{2,18},{18,2},{3,19},{19,3},{4,20},{20... | collective-permute-start | bytes 3735560 | tf_op jit(solution)/shard_map/ppermute | solution.py:723
  50.9 7.3 %collective-permute-start.13 = (bf16[608,128]{1,0:T(8,128)(2,1)}, bf16[608,128]{1,0:T(8,128)(2,1)S(1)}, u32[]{:S(2)}, u32[]{:S(2)}) collective-permute-start(bf16[608,128]{1,0:T(8,128)(2,1)} %get-tuple-element.113), channel_id=1, source_target_pairs={{0,2},{1,3},{2,0},{3,1},{4,6},{5,7},{6,4},{7,5},{8,10},{9,11},{10,... | collective-permute-start | bytes 466952 | tf_op jit(solution)/shard_map/ppermute | solution.py:724
  52.5 6.2 %collective-permute-start.14 = (bf16[608,128]{1,0:T(8,128)(2,1)S(1)}, bf16[608,128]{1,0:T(8,128)(2,1)}, u32[]{:S(2)}, u32[]{:S(2)}) collective-permute-start(bf16[608,128]{1,0:T(8,128)(2,1)S(1)} %get-tuple-element.114), channel_id=1, source_target_pairs={{0,1},{1,0},{2,3},{3,2},{4,5},{5,4},{6,7},{7,6},{8,9},{9,8},{10,11... | collective-permute-start | bytes 466952 | tf_op jit(solution)/shard_map/ppermute | solution.py:724
  53.1 26.4 %all-to-all-start.1 = ((bf16[16,2,24,512]{3,2,1,0:T(8,128)(2,1)}), bf16[16,2,24,512]{3,2,1,0:T(8,128)(2,1)S(1)}, u32[]{:S(2)}, u32[]{:S(2)}) async-start(bf16[16,2,24,512]{3,2,1,0:T(8,128)(2,1)} %get-tuple-element.106), calls=%async_computation.1 | async-start | bytes 1572864 | tf_op jit(solution)/shard_map/all_to_all | solution.py:725
  59.9 14.3 %collective-permute-start.15 = (bf16[1216,128]{1,0:T(8,128)(2,1)S(1)}, bf16[1216,128]{1,0:T(8,128)(2,1)S(1)}, u32[]{:S(2)}, u32[]{:S(2)}) collective-permute-start(bf16[1216,128]{1,0:T(8,128)(2,1)S(1)} %get-tuple-element.128), channel_id=1, source_target_pairs={{0,1},{1,0},{2,3},{3,2},{4,5},{5,4},{6,7},{7,6},{8,9},{9,8},{10,11... | collective-permute-start | bytes 933896 | tf_op jit(solution)/shard_map/ppermute | solution.py:724
  61.3 13.6 %collective-permute-start.16 = (bf16[1216,128]{1,0:T(8,128)(2,1)S(1)}, bf16[1216,128]{1,0:T(8,128)(2,1)S(1)}, u32[]{:S(2)}, u32[]{:S(2)}) collective-permute-start(bf16[1216,128]{1,0:T(8,128)(2,1)S(1)} %get-tuple-element.129), channel_id=1, source_target_pairs={{0,2},{1,3},{2,0},{3,1},{4,6},{5,7},{6,4},{7,5},{8,10},{9,11},{10,... | collective-permute-start | bytes 933896 | tf_op jit(solution)/shard_map/ppermute | solution.py:724
  75.1 11.3 %collective-permute-start.17 = (bf16[304,128]{1,0:T(8,128)(2,1)S(1)}, bf16[304,128]{1,0:T(8,128)(2,1)S(1)}, u32[]{:S(2)}, u32[]{:S(2)}) collective-permute-start(bf16[304,128]{1,0:T(8,128)(2,1)S(1)} %get-tuple-element.135), channel_id=1, source_target_pairs={{0,4},{1,5},{2,6},{3,7},{4,0},{5,1},{6,2},{7,3},{8,12},{9,13},{10,... | collective-permute-start | bytes 233480 | tf_op jit(solution)/shard_map/ppermute | solution.py:724
  77.0 9.4 %collective-permute-start.18 = (bf16[304,128]{1,0:T(8,128)(2,1)S(1)}, bf16[304,128]{1,0:T(8,128)(2,1)S(1)}, u32[]{:S(2)}, u32[]{:S(2)}) collective-permute-start(bf16[304,128]{1,0:T(8,128)(2,1)S(1)} %get-tuple-element.136), channel_id=1, source_target_pairs={{0,8},{1,9},{2,10},{3,11},{4,12},{5,13},{6,14},{7,15},{8,0},{9,1},... | collective-permute-start | bytes 233480 | tf_op jit(solution)/shard_map/ppermute | solution.py:724
  79.3 7.1 %collective-permute-start.19 = (bf16[304,128]{1,0:T(8,128)(2,1)S(1)}, bf16[304,128]{1,0:T(8,128)(2,1)S(1)}, u32[]{:S(2)}, u32[]{:S(2)}) collective-permute-start(bf16[304,128]{1,0:T(8,128)(2,1)S(1)} %get-tuple-element.137), channel_id=1, source_target_pairs={{0,12},{1,13},{2,14},{3,15},{4,8},{5,9},{6,10},{7,11},{8,4},{9,5},... | collective-permute-start | bytes 233480 | tf_op jit(solution)/shard_map/ppermute | solution.py:724
  86.5 1.5 %collective-permute-start.20 = (f32[304,128]{1,0:T(8,128)S(1)}, f32[304,128]{1,0:T(8,128)S(1)}, u32[]{:S(2)}, u32[]{:S(2)}) collective-permute-start(f32[304,128]{1,0:T(8,128)S(1)} %join.3.mine_ref), channel_id=1, source_target_pairs={{0,16},{16,0},{1,17},{17,1},{2,18},{18,2},{3,19},{19,3},{4,20},{20... | collective-permute-start | bytes 466952 | tf_op jit(solution)/shard_map/ppermute | solution.py:723
  86.5 1.4 %collective-permute-start.21 = (f32[24,384]{1,0:T(8,128)S(1)}, f32[24,384]{1,0:T(8,128)S(1)}, u32[]{:S(2)}, u32[]{:S(2)}) collective-permute-start(f32[24,384]{1,0:T(8,128)S(1)} %get-tuple-element.143.small_ref), channel_id=1, source_target_pairs={{0,16},{16,0},{1,17},{17,1},{2,18},{18,2},{3,19},{19,3},{4,20},{20... | collective-permute-start | bytes 110600 | tf_op jit(solution)/shard_map/ppermute | solution.py:723

commit v7 on v6

--- a/solution.py
+++ b/solution.py
@@ -33,8 +33,9 @@
 
 
 def image_mask(rows, height, width):
-    cell = lax.broadcasted_iota(jnp.int32, (rows, CELLS), 1)
-    return (cell // SIDE < height) & (cell % SIDE < width)
+    cell = lax.broadcasted_iota(jnp.int32, (SLOT, CELLS), 1)
+    inside = jnp.where((cell // SIDE < height) & (cell % SIDE < width), 1.0, 0.0)
+    return jnp.concatenate([inside] * -(-rows // SLOT), axis=0)[:rows]
 
 
 def lane_of(rows):
@@ -157,13 +158,16 @@
     for ref in (high_a, low_a, field):
         ref[...] = jnp.zeros_like(ref)
     for image in range(images):
-        inside = image_mask(1, heights[image], widths[image])
+        inside = image_mask(channels, heights[image], widths[image])
         value = feat_ref[:, image * CELLS : (image + 1) * CELLS].astype(F32)
-        fill_slots(slots, jnp.where(inside, value, 0.0), image)
+        fill_slots(slots, value * inside, image)
     live = min(SLOT, channels)
     sides = images // PER
 
+    scratch = (high_a, low_a, field, tall)
+
     def body(group, carry):
+        high_a, low_a, field, tall = (ref.at[group] for ref in scratch)
         lane = lane_of(SLOT)
         sub = lax.broadcasted_iota(jnp.int32, (SLOT, LANES), 0)
         for c in range(live):
@@ -191,18 +195,19 @@
             store_channel(slots, group, c, tiles, lane)
         return carry
 
-    lax.fori_loop(0, slots.shape[0], body, 0)
+    for group in range(slots.shape[0]):
+        body(group, 0)
     wide = out_ref.shape[3]
     parts = CELLS // wide
     skip = rows_ref[0:channels, 2 * SIDE : 2 * SIDE + 1]
     scale = column(scale_ref[...])
     for image in range(images):
         span = slice(image * CELLS, (image + 1) * CELLS)
-        inside = image_mask(1, heights[image], widths[image])
+        inside = image_mask(channels, heights[image], widths[image])
         value = read_slots(slots, image, channels) + skip * feat_ref[:, span].astype(F32)
-        value = jnp.where(inside, value, 0.0).astype(BF16)
+        value = (value * inside).astype(BF16)
         down = cot_ref[:, span].astype(F32) * scale
-        down = jnp.where(inside, down, 0.0).astype(BF16)
+        down = (down * inside).astype(BF16)
         for j in range(parts):
             out_ref[image * parts + j, 0] = value[:, j * wide : (j + 1) * wide]
             out_ref[image * parts + j, 1] = down[:, j * wide : (j + 1) * wide]
@@ -218,9 +223,9 @@
     for ref in (field_ref, high_a, low_a):
         ref[...] = jnp.zeros_like(ref)
     for image in range(images):
-        inside = image_mask(1, heights[image], widths[image])
+        inside = image_mask(channels, heights[image], widths[image])
         value = feat_ref[:, image * CELLS : (image + 1) * CELLS].astype(F32)
-        fill_slots(slots, jnp.where(inside, value, 0.0), image)
+        fill_slots(slots, value * inside, image)
 
     def body(group, carry):
         lane = lane_of(SLOT)
@@ -267,20 +272,20 @@
     small = jnp.zeros((channels, LANES), F32)
     for image in range(images):
         span = slice(image * CELLS, (image + 1) * CELLS)
-        inside = image_mask(1, heights[image], widths[image])
+        inside = image_mask(channels, heights[image], widths[image])
         values = feat_ref[:, span].astype(F32)
         grad = jnp.concatenate(
             [both_ref[image * parts + j, 0].astype(F32) for j in range(parts)], axis=1
         )
-        grad = jnp.where(inside, grad, 0.0)
+        grad = grad * inside
         fill_slots(slots_g, grad, image)
         shifted = jnp.concatenate(
             [both_ref[image * parts + j, 1].astype(F32) for j in range(parts)], axis=1
         )
         shifted = shifted + bias
-        result = values + jnp.where(inside, scale * shifted, 0.0)
+        result = values + inside * (scale * shifted)
         result_ref[:, span] = result.astype(BF16)
-        weighted = jnp.where(inside, cot_ref[:, span].astype(F32), 0.0)
+        weighted = cot_ref[:, span].astype(F32) * inside
         small = small + jnp.where(
             lane_c == 64,
             jnp.sum(grad * values, axis=1, keepdims=True),
@@ -366,10 +371,10 @@
     skip = rows_ref[0:channels, 2 * SIDE : 2 * SIDE + 1]
     for image in range(images):
         span = slice(image * CELLS, (image + 1) * CELLS)
-        inside = image_mask(1, heights[image], widths[image])
+        inside = image_mask(channels, heights[image], widths[image])
         grad = read_slots(slots_g, image, channels)
         value = read_slots(slots, image, channels) + skip * grad
-        gfeat_ref[:, span] = cot_ref[:, span].astype(F32) + jnp.where(inside, value, 0.0)
+        gfeat_ref[:, span] = cot_ref[:, span].astype(F32) + value * inside
     small = small + sums[0:channels]
     states, small = chain(small, step_h, step_w, rate_h, rate_w, read_h, read_w)
     for index in range(2):
@@ -522,7 +527,7 @@
     return range(0, ref.shape[0], height)
 
 
-def perceptron(refs, act, down, deep):
+def perceptron(refs, act, down, deep, sums_first):
     count = act.shape[0]
     tiles = count // LANES
 
@@ -548,8 +553,12 @@
     slope = half + full * (1.0 - half) * (6.0 * ROOT * 0.044715 * square + 2.0 * ROOT)
     low = (dot(w_out, down) * slope).astype(BF16)
     g_bias = jnp.sum(low.astype(F32), axis=1, keepdims=True)
+    if sums_first:
+        sums, total = dot(w_out, hidden, TN), dot(w_in, low, TN)
     grads = (dot(low, act, NT).astype(BF16), dot(hidden, down, NT).astype(BF16), g_bias)
-    return dot(w_out, hidden, TN), dot(w_in, low, TN), grads
+    if not sums_first:
+        sums, total = dot(w_out, hidden, TN), dot(w_in, low, TN)
+    return sums, total, grads
 
 
 def put(ref, grads, start, deep, edges=None):
@@ -578,6 +587,19 @@
         yield d, pl.multiple_of(spot * EDGE, EDGE)
 
 
+def piece_of(rows, channels):
+    return lax.broadcasted_iota(jnp.int32, (rows, LANES), 0) % channels // EDGE
+
+
+def spread_of(tiles, index, channels, deep):
+    piece = piece_of(tiles.shape[0], channels)[:, 0:1]
+    first = index * (deep // EDGE)
+    out = tiles[:, first : first + 1]
+    for p in range(1, -(-channels // EDGE)):
+        out = jnp.where(piece == p, tiles[:, first + p : first + p + 1], out)
+    return out
+
+
 def mlp_first(near, pieces, deep, where_ref, given_ref, *refs):
     own_in, refs = refs[:pieces], refs[pieces:]
     other_in, refs = refs[:pieces], refs[pieces:]
@@ -600,14 +622,15 @@
             edge = base + 2 * count // LANES * deep
             ext[at : at + EDGE] = ref[edge : edge + EDGE].astype(F32)
             at += EDGE
-    lane = lane_of(channels)
     for d, spot in spots_of(near, devices, where_ref):
         tile = ext[pl.ds(spot, EDGE), :]
-        gain, shift = (unfold(tile, index, deep)[:channels] for index in (1, 2))
-        pair = jnp.where(lane == 1, gain, jnp.where(lane == 2, shift, 0.0))
-        gains[d * channels : (d + 1) * channels] = pair
-    active[...] = (value * gains[:, 1:2] + gains[:, 2:3]).astype(BF16)
-    sums, total, grads = perceptron(other_in, active[...], downs[...], deep)
+        for at in range(0, channels, EDGE):
+            rows = min(EDGE, channels - at)
+            gains[d * channels + at : d * channels + at + rows] = tile[:rows]
+    gain, shift = (spread_of(gains[...], index, channels, deep) for index in (1, 2))
+    gains[...] = jnp.broadcast_to(gain, gains.shape)
+    active[...] = (value * gain + shift).astype(BF16)
+    sums, total, grads = perceptron(other_in, active[...], downs[...], deep, False)
     put(gother_ref, grads, 0, deep)
     sum_ref[...] = sums
     grad_ref[...] = total
@@ -623,14 +646,14 @@
     count = active.shape[0]
     devices, _, channels, _ = both_ref.shape
 
-    sums, total, grads = perceptron(own_in, active[...], downs[...], deep)
+    sums, total, grads = perceptron(own_in, active[...], downs[...], deep, True)
     start = 0
     for ref in own_out:
         start = put(ref, grads, start, deep, gext)
     summed = sum_ref[...] + sums
     agrad = grad_ref[...] + total
     norm = normal_ref[...]
-    scaled = agrad * gains[:, 1:2]
+    scaled = agrad * gains[:, 0:1]
     first = jnp.mean(scaled, axis=0, keepdims=True)
     second = jnp.mean(scaled * norm, axis=0, keepdims=True)
     mgrad = (scaled - first - norm * second) * inv_ref[...]
@@ -639,14 +662,19 @@
         both_ref[d, 1] = summed[d * channels : (d + 1) * channels].astype(BF16)
     by_gain = jnp.sum(agrad * norm, axis=1, keepdims=True)
     by_shift = jnp.sum(agrad, axis=1, keepdims=True)
+    lane, piece = lane_of(count), piece_of(count, channels)
+    base = deep // EDGE
+    tile = jnp.where(lane == base + piece, by_gain, 0.0)
+    tile = jnp.where(lane == 2 * base + piece, by_shift, tile)
     for d, spot in spots_of(near, devices, where_ref):
-        parts = []
-        for value in (by_gain, by_shift):
-            value = value[d * channels : (d + 1) * channels]
-            if channels < deep:
-                value = jnp.concatenate([value, jnp.zeros((deep - channels, 1), F32)], axis=0)
-            parts.append(value)
-        gext[pl.ds(spot, EDGE), :] += fold((None, *parts), deep)
+        edge = None
+        for at in range(0, channels, EDGE):
+            rows = min(EDGE, channels - at)
+            part = tile[d * channels + at : d * channels + at + rows]
+            if rows < EDGE:
+                part = jnp.concatenate([part, jnp.zeros((EDGE - rows, LANES), F32)], axis=0)
+            edge = part if edge is None else edge + part
+        gext[pl.ds(spot, EDGE), :] += edge
     at = 0
     for ref in own_out:
         for base in shards_of(ref, count, deep):
@@ -759,7 +787,9 @@
         in_specs=[SMEM, SMEM] + [full] * 10,
         out_specs=(full, full),
         scratch_shapes=[
-            slots, toeplitz, toeplitz, pltpu.VMEM(square, BF16), pltpu.VMEM(square, F32),
+            slots, pltpu.VMEM((groups,) + toeplitz.shape, BF16),
+            pltpu.VMEM((groups,) + toeplitz.shape, BF16), pltpu.VMEM((groups,) + square, BF16),
+            pltpu.VMEM((groups,) + square, F32),
         ],
         compiler_params=params(16),
         cost_estimate=cost(6),

time: 89.4 us -> 88.5 us (0.990)
  Pallas kernels: 28.6 us -> 27.7 us
  transfers between devices with their start and end apart: 24 -> 24, of which waited for: 11 -> 11; matrix products, arithmetic and copies ran while one was open for 0% -> 0% of each run, Pallas kernels for 25% -> 24%
where the time goes in v7:
time: 88.5 us; the launch traced here: 88 us
  starting transfers between devices  32 us (36%)
  Pallas kernels  27.7 us (31%)
  waiting for transfers between devices  27.3 us (31%)
  between operations  0.94 us (1%)
    ppermute x14, starting transfers between devices, per_device(): lax.ppermute(v, 'ch', [(i, i ^ bits) for i in range(ch)])  20.7 us
    ppermute x14, waiting for transfers between devices, per_device(): lax.ppermute(v, 'ch', [(i, i ^ bits) for i in range(ch)])  19 us
    all_to_all x2, starting transfers between devices, per_device(): lax.all_to_all(v, 'ch', split_axis=0, concat_axis=0, tiled=True, axis_ind...  9.64 us
    pallas_call x1, Pallas kernels, per_device(): pl.pallas_call(backward_kernel, out_shape=(jax.ShapeDtypeStruct((channels...  6.79 us
    all_to_all x2, waiting for transfers between devices, per_device(): lax.all_to_all(v, 'ch', split_axis=0, concat_axis=0, tiled=True, axis_ind...  6.39 us
    pallas_call x1, Pallas kernels, per_device(): pl.pallas_call(forward_kernel, out_shape=(jax.ShapeDtypeStruct(both_shape...  5.28 us
    pallas_call x1, Pallas kernels, per_device(): pl.pallas_call(partial(mlp_second, near, pieces, deep), out_shape=[jax.Sh...  4.18 us
    pallas_call x1, Pallas kernels, per_device(): pl.pallas_call(partial(mlp_first, near, pieces, deep), out_shape=[jax.Sha...  3.85 us
  transfers between devices with their start and end apart: 24, of which 11 were waited for; matrix products, arithmetic and copies ran while one was open for 0% of the time, Pallas kernels for 24%

profile of v7, /device:TPU:0, one launch (start us, length us, event | category | flops | bytes accessed | tf_op | source)
XLA Modules:
  0.0 88.0 jit_solution(13701984486236135188)
XLA Ops:
  0.7 1.2 %pack.1 = bf16[304,128]{1,0:T(8,128)(2,1)S(1)} custom-call(s32[1]{0:T(128)} %bitcast.2.half, bf16[96,384]{1,0:T(8,128)(2,1)} %bitcast.21, bf16[96,384]{1,0:T(8,128)(2,1)} %out_ref.1, bf16[1,96]{1,0:T(2,128)(2,1)} %bitcast.28, bf16[1,24]{1,0:T(2,128)(2,1)} %bitcast.29, bf16[1,24]{1,0:T(2,128)(2,1)} %bitcast.30), custom_call_target="tpu_custom_call" | custom-call | bytes 6000000 | tf_op jit(solution)/shard_map/pack/pallas_call | solution.py:761
  1.8 5.1 %collective-permute-start.2 = (bf16[304,128]{1,0:T(8,128)(2,1)S(1)}, bf16[304,128]{1,0:T(8,128)(2,1)S(1)}, u32[]{:S(2)}, u32[]{:S(2)}) collective-permute-start(bf16[304,128]{1,0:T(8,128)(2,1)S(1)} %pack.1), channel_id=1, source_target_pairs={{0,12},{1,13},{2,14},{3,15},{4,8},{5,9},{6,10},{7,11},{8,4},{9,5},... | collective-permute-start | bytes 233480 | tf_op jit(solution)/shard_map/ppermute | solution.py:752
  6.9 0.0 collective-permute-start.1
  6.9 0.6 collective-permute-start
  7.6 5.3 %mixer_forward.1 = (bf16[16,2,24,512]{3,2,1,0:T(8,128)(2,1)}, f32[24,128]{1,0:T(8,128)S(1)}) custom-call(s32[8]{0:T(128)} %heights.5, s32[8]{0:T(128)} %widths.5, bf16[24,8192]{1,0:T(8,128)(2,1)} %feat_ref.3, bf16[24,8192]{1,0:T(8,128)(2,1)} %cot_ref.3, f32[1,24]{1,0:T(1,128)} %bitcast.22, f32[1,24]{1,0:T(1,128)} %bitcast.24, f32[1,24]{1,0:T(1,128)} %bitcast.26, ...), custom_call_target="tpu_custom_call" | custom-call | bytes 18000000 | tf_op jit(solution)/shard_map/mixer_forward/pallas_call | solution.py:781
  12.8 0.0 collective-permute-done.2
  12.9 0.6 collective-permute-done.1
  13.5 0.0 collective-permute-done
  13.5 1.6 %collective-permute-start.4 = (bf16[1216,128]{1,0:T(8,128)(2,1)S(1)}, bf16[1216,128]{1,0:T(8,128)(2,1)S(1)}, u32[]{:S(2)}, u32[]{:S(2)}) collective-permute-start(bf16[1216,128]{1,0:T(8,128)(2,1)S(1)} %constant_dynamic-update-slice_fusion.refs_0_), channel_id=1, source_target_pairs={{0,2},{1,3},{2,0},{3,1},{4,6},{5,7},{6,4},{7,5},{8,10},{9,11},{10,... | collective-permute-start | bytes 933896 | tf_op jit(solution)/shard_map/ppermute | solution.py:752
  15.1 1.5 %collective-permute-start.3 = (bf16[1216,128]{1,0:T(8,128)(2,1)S(1)}, bf16[1216,128]{1,0:T(8,128)(2,1)S(1)}, u32[]{:S(2)}, u32[]{:S(2)}) collective-permute-start(bf16[1216,128]{1,0:T(8,128)(2,1)S(1)} %constant_dynamic-update-slice_fusion.refs_0_), channel_id=1, source_target_pairs={{0,1},{1,0},{2,3},{3,2},{4,5},{5,4},{6,7},{7,6},{8,9},{9,8},{10,11... | collective-permute-start | bytes 933896 | tf_op jit(solution)/shard_map/ppermute | solution.py:752
  16.6 0.0 collective-permute-start.7
  16.6 4.5 %all-to-all-start = ((bf16[16,2,24,512]{3,2,1,0:T(8,128)(2,1)}), bf16[16,2,24,512]{3,2,1,0:T(8,128)(2,1)S(1)}, u32[]{:S(2)}, u32[]{:S(2)}) async-start(bf16[16,2,24,512]{3,2,1,0:T(8,128)(2,1)} %get-tuple-element.90), calls=%async_computation | async-start | bytes 1572864 | tf_op jit(solution)/shard_map/all_to_all | solution.py:753
  21.2 1.1 %collective-permute-done.4.two_ref.refs_2_ = bf16[1216,128]{1,0:T(8,128)(2,1)S(1)} collective-permute-done((bf16[1216,128]{1,0:T(8,128)(2,1)S(1)}, bf16[1216,128]{1,0:T(8,128)(2,1)S(1)}, u32[]{:S(2)}, u32[]{:S(2)}) %collective-permute-start.4) | collective-permute-done | bytes 311328 | tf_op jit(solution)/shard_map/ppermute | solution.py:752
  22.2 1.4 %collective-permute-done.3.one_ref.refs_1_ = bf16[1216,128]{1,0:T(8,128)(2,1)S(1)} collective-permute-done((bf16[1216,128]{1,0:T(8,128)(2,1)S(1)}, bf16[1216,128]{1,0:T(8,128)(2,1)S(1)}, u32[]{:S(2)}, u32[]{:S(2)}) %collective-permute-start.3) | collective-permute-done | bytes 311328 | tf_op jit(solution)/shard_map/ppermute | solution.py:752
  23.7 0.4 collective-permute-start.5
  24.1 1.9 %collective-permute-start.6 = (bf16[608,128]{1,0:T(8,128)(2,1)S(1)}, bf16[608,128]{1,0:T(8,128)(2,1)S(1)}, u32[]{:S(2)}, u32[]{:S(2)}) collective-permute-start(bf16[608,128]{1,0:T(8,128)(2,1)S(1)} %get-tuple-element.98), channel_id=1, source_target_pairs={{0,1},{1,0},{2,3},{3,2},{4,5},{5,4},{6,7},{7,6},{8,9},{9,8},{10,11... | collective-permute-start | bytes 466952 | tf_op jit(solution)/shard_map/ppermute | solution.py:752
  26.0 0.0 collective-permute-start.8
  26.0 0.5 collective-permute-start.9
  26.5 6.7 %collective-permute-done.5.refs_3_ = bf16[608,128]{1,0:T(8,128)(2,1)S(1)} collective-permute-done((bf16[608,128]{1,0:T(8,128)(2,1)S(1)}, bf16[608,128]{1,0:T(8,128)(2,1)S(1)}, u32[]{:S(2)}, u32[]{:S(2)}) %collective-permute-start.5) | collective-permute-done | bytes 155680 | tf_op jit(solution)/shard_map/ppermute | solution.py:752
  33.2 0.0 collective-permute-start.10
  33.2 0.0 collective-permute-done.6.refs_4_
  33.2 0.5 collective-permute-start.11
  33.7 0.1 pad_add_fusion.where_ref
  33.8 0.0 collective-permute-done.7.refs_5_
  33.8 0.8 collective-permute-done.10.refs_8_
  34.6 0.2 collective-permute-done.11.refs_9_
  34.8 0.0 collective-permute-done.8.refs_6_
  34.8 0.0 collective-permute-done.9.refs_7_
  34.8 6.4 %all-to-all-done.given_ref = bf16[16,2,24,512]{3,2,1,0:T(8,128)(2,1)S(1)} async-done(((bf16[16,2,24,512]{3,2,1,0:T(8,128)(2,1)}), bf16[16,2,24,512]{3,2,1,0:T(8,128)(2,1)S(1)}, u32[]{:S(2)}, u32[]{:S(2)}) %all-to-all-start) | async-done | bytes 786464 | tf_op jit(solution)/shard_map/all_to_all | solution.py:753
  41.2 3.8 %mlp_first.1 = (bf16[4864,128]{1,0:T(8,128)(2,1)S(1)}, bf16[384,512]{1,0:T(8,128)(2,1)S(1)}, bf16[384,512]{1,0:T(8,128)(2,1)S(1)}, f32[384,512]{1,0:T(8,128)S(1)...) custom-call(s32[2]{0:T(128)S(1)} %pad_add_fusion.where_ref, ...), custom_call_target="tpu_custom_call" | custom-call | bytes 15000000 | tf_op jit(solution)/shard_map/mlp_first/pallas_call | solution.py:829
  45.1 0.1 collective-permute-start.12
  45.2 4.2 %mlp_second.1 = (bf16[16,2,24,512]{3,2,1,0:T(8,128)(2,1)}, bf16[1216,128]{1,0:T(8,128)(2,1)S(1)}, bf16[1216,128]{1,0:T(8,128)(2,1)S(1)}, bf16[1216,128]{1,0:T(8,...) custom-call(s32[2]{0:T(128)S(1)} %pad_add_fusion.where_ref, ...), custom_call_target="tpu_custom_call" | custom-call | bytes 15000000 | tf_op jit(solution)/shard_map/mlp_second/pallas_call | solution.py:844
  49.3 0.0 collective-permute-done.12.arrived_ref.refs_1_
  49.4 0.7 start.1
  50.1 1.6 %collective-permute-start.13 = (bf16[608,128]{1,0:T(8,128)(2,1)}, bf16[608,128]{1,0:T(8,128)(2,1)S(1)}, u32[]{:S(2)}, u32[]{:S(2)}) collective-permute-start(bf16[608,128]{1,0:T(8,128)(2,1)} %get-tuple-element.113), channel_id=1, source_target_pairs={{0,2},{1,3},{2,0},{3,1},{4,6},{5,7},{6,4},{7,5},{8,10},{9,11},{10,... | collective-permute-start | bytes 466952 | tf_op jit(solution)/shard_map/ppermute | solution.py:752
  51.7 0.6 collective-permute-start.14
  52.2 5.1 %all-to-all-start.1 = ((bf16[16,2,24,512]{3,2,1,0:T(8,128)(2,1)}), bf16[16,2,24,512]{3,2,1,0:T(8,128)(2,1)S(1)}, u32[]{:S(2)}, u32[]{:S(2)}) async-start(bf16[16,2,24,512]{3,2,1,0:T(8,128)(2,1)} %get-tuple-element.106), calls=%async_computation.1 | async-start | bytes 1572864 | tf_op jit(solution)/shard_map/all_to_all | solution.py:753
  57.3 0.0 collective-permute-done.13.first_ref
  57.4 0.6 collective-permute-done.14.second_ref
  57.9 1.1 %relay.1 = (bf16[1216,128]{1,0:T(8,128)(2,1)S(1)}, bf16[1216,128]{1,0:T(8,128)(2,1)S(1)}) custom-call(bf16[1216,128]{1,0:T(8,128)(2,1)S(1)} %get-tuple-element.108.one_ref, bf16[1216,128]{1,0:T(8,128)(2,1)S(1)} %get-tuple-element.109.two_ref, bf16[4864,128]{1,0:T(8,128)(2,1)S(1)} %collective-permute-done.12.arrived_ref.refs_1_, ...), custom_call_target="tpu_custom_call" | custom-call | flops 99999997952 | bytes 1000000 | tf_op jit(solution)/shard_map/relay/pallas_call | solution.py:717
  59.0 1.4 %collective-permute-start.15 = (bf16[1216,128]{1,0:T(8,128)(2,1)S(1)}, bf16[1216,128]{1,0:T(8,128)(2,1)S(1)}, u32[]{:S(2)}, u32[]{:S(2)}) collective-permute-start(bf16[1216,128]{1,0:T(8,128)(2,1)S(1)} %get-tuple-element.128), channel_id=1, source_target_pairs={{0,1},{1,0},{2,3},{3,2},{4,5},{5,4},{6,7},{7,6},{8,9},{9,8},{10,11... | collective-permute-start | bytes 933896 | tf_op jit(solution)/shard_map/ppermute | solution.py:752
  60.4 1.5 %collective-permute-start.16 = (bf16[1216,128]{1,0:T(8,128)(2,1)S(1)}, bf16[1216,128]{1,0:T(8,128)(2,1)S(1)}, u32[]{:S(2)}, u32[]{:S(2)}) collective-permute-start(bf16[1216,128]{1,0:T(8,128)(2,1)S(1)} %get-tuple-element.129), channel_id=1, source_target_pairs={{0,2},{1,3},{2,0},{3,1},{4,6},{5,7},{6,4},{7,5},{8,10},{9,11},{10,... | collective-permute-start | bytes 933896 | tf_op jit(solution)/shard_map/ppermute | solution.py:752
  61.9 3.5 %mixer_prepare.1 = (bf16[3,256,256]{2,1,0:T(8,128)(2,1)}, bf16[3,256,256]{2,1,0:T(8,128)(2,1)}, bf16[3,256,256]{2,1,0:T(8,128)(2,1)}, bf16[3,8,64,128]{3,2,1,0:T(8,128)(2,1)}, bf16[3,8,64,128]{3,2,1,0:T(8,128)(2,1)}) custom-call(s32[8]{0:T(128)} %heights.5, s32[8]{0:T(128)} %widths.5, bf16[24,8192]{1,0:T(8,128)(2,1)} %feat_ref.3, ...), custom_call_target="tpu_custom_call" | custom-call | bytes 12000000 | tf_op jit(solution)/shard_map/mixer_prepare/pallas_call | solution.py:881
  65.5 7.8 %collective-permute-done.15.refs_2_ = bf16[1216,128]{1,0:T(8,128)(2,1)S(1)} collective-permute-done((bf16[1216,128]{1,0:T(8,128)(2,1)S(1)}, bf16[1216,128]{1,0:T(8,128)(2,1)S(1)}, u32[]{:S(2)}, u32[]{:S(2)}) %collective-permute-start.15) | collective-permute-done | bytes 311328 | tf_op jit(solution)/shard_map/ppermute | solution.py:752
  73.3 0.8 collective-permute-done.16.refs_3_
  74.1 0.2 join.2
  74.2 1.9 %collective-permute-start.17 = (bf16[304,128]{1,0:T(8,128)(2,1)S(1)}, bf16[304,128]{1,0:T(8,128)(2,1)S(1)}, u32[]{:S(2)}, u32[]{:S(2)}) collective-permute-start(bf16[304,128]{1,0:T(8,128)(2,1)S(1)} %get-tuple-element.135), channel_id=1, source_target_pairs={{0,4},{1,5},{2,6},{3,7},{4,0},{5,1},{6,2},{7,3},{8,12},{9,13},{10,... | collective-permute-start | bytes 233480 | tf_op jit(solution)/shard_map/ppermute | solution.py:752
  76.2 2.3 %collective-permute-start.18 = (bf16[304,128]{1,0:T(8,128)(2,1)S(1)}, bf16[304,128]{1,0:T(8,128)(2,1)S(1)}, u32[]{:S(2)}, u32[]{:S(2)}) collective-permute-start(bf16[304,128]{1,0:T(8,128)(2,1)S(1)} %get-tuple-element.136), channel_id=1, source_target_pairs={{0,8},{1,9},{2,10},{3,11},{4,12},{5,13},{6,14},{7,15},{8,0},{9,1},... | collective-permute-start | bytes 233480 | tf_op jit(solution)/shard_map/ppermute | solution.py:752
  78.5 0.2 collective-permute-start.19
  78.7 0.0 all-to-all-done.1.both_ref
  78.7 6.8 %mixer_backward.1 = (bf16[24,8192]{1,0:T(8,128)(2,1)}, f32[24,8192]{1,0:T(8,128)}, f32[24,384]{1,0:T(8,128)S(1)}) custom-call(s32[8]{0:T(128)} %heights.5, s32[8]{0:T(128)} %widths.5, bf16[24,8192]{1,0:T(8,128)(2,1)} %feat_ref.3, bf16[24,8192]{1,0:T(8,128)(2,1)} %cot_ref.3, bf16[16,2,24,512]{3,2,1,0:T(8,128)(2,1)S(1)} %all-to-all-done.1.both_ref, ...), custom_call_target="tpu_custom_call" | custom-call | bytes 21000000 | tf_op jit(solution)/shard_map/mixer_backward/pallas_call | solution.py:896
  85.5 0.0 collective-permute-done.17.refs_1_
  85.5 0.0 collective-permute-done.18.refs_2_
  85.5 0.0 collective-permute-done.19.refs_3_
  85.5 0.1 collective-permute-start.20
  85.6 0.5 collective-permute-start.21
  86.1 0.9 %collective-permute-done.21.sibling_ref = f32[24,384]{1,0:T(8,128)S(1)} collective-permute-done((f32[24,384]{1,0:T(8,128)S(1)}, f32[24,384]{1,0:T(8,128)S(1)}, u32[]{:S(2)}, u32[]{:S(2)}) %collective-permute-start.21) | collective-permute-done | bytes 36896 | tf_op jit(solution)/shard_map/ppermute | solution.py:751
  87.0 0.0 collective-permute-done.20.other_ref
  87.0 0.9 finish.1
  (6 shorter events, 0.1 us)
Async XLA Ops:
  1.8 11.0 %collective-permute-start.2 = (bf16[304,128]{1,0:T(8,128)(2,1)S(1)}, bf16[304,128]{1,0:T(8,128)(2,1)S(1)}, u32[]{:S(2)}, u32[]{:S(2)}) collective-permute-start(bf16[304,128]{1,0:T(8,128)(2,1)S(1)} %pack.1), channel_id=1, source_target_pairs={{0,12},{1,13},{2,14},{3,15},{4,8},{5,9},{6,10},{7,11},{8,4},{9,5},... | collective-permute-start | bytes 233480 | tf_op jit(solution)/shard_map/ppermute | solution.py:752
  6.9 6.5 %collective-permute-start.1 = (bf16[304,128]{1,0:T(8,128)(2,1)S(1)}, bf16[304,128]{1,0:T(8,128)(2,1)S(1)}, u32[]{:S(2)}, u32[]{:S(2)}) collective-permute-start(bf16[304,128]{1,0:T(8,128)(2,1)S(1)} %pack.1), channel_id=1, source_target_pairs={{0,8},{1,9},{2,10},{3,11},{4,12},{5,13},{6,14},{7,15},{8,0},{9,1},... | collective-permute-start | bytes 233480 | tf_op jit(solution)/shard_map/ppermute | solution.py:752
  6.9 6.5 %collective-permute-start = (bf16[304,128]{1,0:T(8,128)(2,1)S(1)}, bf16[304,128]{1,0:T(8,128)(2,1)S(1)}, u32[]{:S(2)}, u32[]{:S(2)}) collective-permute-start(bf16[304,128]{1,0:T(8,128)(2,1)S(1)} %pack.1), channel_id=1, source_target_pairs={{0,4},{1,5},{2,6},{3,7},{4,0},{5,1},{6,2},{7,3},{8,12},{9,13},{10,... | collective-permute-start | bytes 233480 | tf_op jit(solution)/shard_map/ppermute | solution.py:752
  13.5 8.7 %collective-permute-start.4 = (bf16[1216,128]{1,0:T(8,128)(2,1)S(1)}, bf16[1216,128]{1,0:T(8,128)(2,1)S(1)}, u32[]{:S(2)}, u32[]{:S(2)}) collective-permute-start(bf16[1216,128]{1,0:T(8,128)(2,1)S(1)} %constant_dynamic-update-slice_fusion.refs_0_), channel_id=1, source_target_pairs={{0,2},{1,3},{2,0},{3,1},{4,6},{5,7},{6,4},{7,5},{8,10},{9,11},{10,... | collective-permute-start | bytes 933896 | tf_op jit(solution)/shard_map/ppermute | solution.py:752
  15.1 8.6 %collective-permute-start.3 = (bf16[1216,128]{1,0:T(8,128)(2,1)S(1)}, bf16[1216,128]{1,0:T(8,128)(2,1)S(1)}, u32[]{:S(2)}, u32[]{:S(2)}) collective-permute-start(bf16[1216,128]{1,0:T(8,128)(2,1)S(1)} %constant_dynamic-update-slice_fusion.refs_0_), channel_id=1, source_target_pairs={{0,1},{1,0},{2,3},{3,2},{4,5},{5,4},{6,7},{7,6},{8,9},{9,8},{10,11... | collective-permute-start | bytes 933896 | tf_op jit(solution)/shard_map/ppermute | solution.py:752
  16.6 17.2 %collective-permute-start.7 = (bf16[1216,128]{1,0:T(8,128)(2,1)S(1)}, bf16[1216,128]{1,0:T(8,128)(2,1)S(1)}, u32[]{:S(2)}, u32[]{:S(2)}) collective-permute-start(bf16[1216,128]{1,0:T(8,128)(2,1)S(1)} %constant_dynamic-update-slice_fusion.refs_0_), channel_id=1, source_target_pairs={{0,16},{16,0},{1,17},{17,1},{2,18},{18,2},{3,19},{19,3},{4,20},{20... | collective-permute-start | bytes 933896 | tf_op jit(solution)/shard_map/ppermute | solution.py:751
  16.6 24.6 %all-to-all-start = ((bf16[16,2,24,512]{3,2,1,0:T(8,128)(2,1)}), bf16[16,2,24,512]{3,2,1,0:T(8,128)(2,1)S(1)}, u32[]{:S(2)}, u32[]{:S(2)}) async-start(bf16[16,2,24,512]{3,2,1,0:T(8,128)(2,1)} %get-tuple-element.90), calls=%async_computation | async-start | bytes 1572864 | tf_op jit(solution)/shard_map/all_to_all | solution.py:753
  23.7 9.5 %collective-permute-start.5 = (bf16[608,128]{1,0:T(8,128)(2,1)S(1)}, bf16[608,128]{1,0:T(8,128)(2,1)S(1)}, u32[]{:S(2)}, u32[]{:S(2)}) collective-permute-start(bf16[608,128]{1,0:T(8,128)(2,1)S(1)} %get-tuple-element.97), channel_id=1, source_target_pairs={{0,2},{1,3},{2,0},{3,1},{4,6},{5,7},{6,4},{7,5},{8,10},{9,11},{10,... | collective-permute-start | bytes 466952 | tf_op jit(solution)/shard_map/ppermute | solution.py:752
  24.1 9.1 %collective-permute-start.6 = (bf16[608,128]{1,0:T(8,128)(2,1)S(1)}, bf16[608,128]{1,0:T(8,128)(2,1)S(1)}, u32[]{:S(2)}, u32[]{:S(2)}) collective-permute-start(bf16[608,128]{1,0:T(8,128)(2,1)S(1)} %get-tuple-element.98), channel_id=1, source_target_pairs={{0,1},{1,0},{2,3},{3,2},{4,5},{5,4},{6,7},{7,6},{8,9},{9,8},{10,11... | collective-permute-start | bytes 466952 | tf_op jit(solution)/shard_map/ppermute | solution.py:752
  26.0 8.8 %collective-permute-start.8 = (bf16[1216,128]{1,0:T(8,128)(2,1)S(1)}, bf16[1216,128]{1,0:T(8,128)(2,1)S(1)}, u32[]{:S(2)}, u32[]{:S(2)}) collective-permute-start(bf16[1216,128]{1,0:T(8,128)(2,1)S(1)} %collective-permute-done.3.one_ref.refs_1_), channel_id=1, source_target_pairs={{0,16},{16,0},{1,17},{17,1},{2,18},{18,2},{3,19},{19,3},{4,20},{20... | collective-permute-start | bytes 933896 | tf_op jit(solution)/shard_map/ppermute | solution.py:751
  26.0 8.8 %collective-permute-start.9 = (bf16[1216,128]{1,0:T(8,128)(2,1)S(1)}, bf16[1216,128]{1,0:T(8,128)(2,1)S(1)}, u32[]{:S(2)}, u32[]{:S(2)}) collective-permute-start(bf16[1216,128]{1,0:T(8,128)(2,1)S(1)} %collective-permute-done.4.two_ref.refs_2_), channel_id=1, source_target_pairs={{0,16},{16,0},{1,17},{17,1},{2,18},{18,2},{3,19},{19,3},{4,20},{20... | collective-permute-start | bytes 933896 | tf_op jit(solution)/shard_map/ppermute | solution.py:751
  33.2 1.4 %collective-permute-start.10 = (bf16[608,128]{1,0:T(8,128)(2,1)S(1)}, bf16[608,128]{1,0:T(8,128)(2,1)S(1)}, u32[]{:S(2)}, u32[]{:S(2)}) collective-permute-start(bf16[608,128]{1,0:T(8,128)(2,1)S(1)} %collective-permute-done.5.refs_3_), channel_id=1, source_target_pairs={{0,16},{16,0},{1,17},{17,1},{2,18},{18,2},{3,19},{19,3},{4,20},{20... | collective-permute-start | bytes 466952 | tf_op jit(solution)/shard_map/ppermute | solution.py:751
  33.2 1.6 %collective-permute-start.11 = (bf16[608,128]{1,0:T(8,128)(2,1)S(1)}, bf16[608,128]{1,0:T(8,128)(2,1)S(1)}, u32[]{:S(2)}, u32[]{:S(2)}) collective-permute-start(bf16[608,128]{1,0:T(8,128)(2,1)S(1)} %collective-permute-done.6.refs_4_), channel_id=1, source_target_pairs={{0,16},{16,0},{1,17},{17,1},{2,18},{18,2},{3,19},{19,3},{4,20},{20... | collective-permute-start | bytes 466952 | tf_op jit(solution)/shard_map/ppermute | solution.py:751
  45.1 4.3 %collective-permute-start.12 = (bf16[4864,128]{1,0:T(8,128)(2,1)S(1)}, bf16[4864,128]{1,0:T(8,128)(2,1)S(1)}, u32[]{:S(2)}, u32[]{:S(2)}) collective-permute-start(bf16[4864,128]{1,0:T(8,128)(2,1)S(1)} %get-tuple-element.110), channel_id=1, source_target_pairs={{0,16},{16,0},{1,17},{17,1},{2,18},{18,2},{3,19},{19,3},{4,20},{20... | collective-permute-start | bytes 3735560 | tf_op jit(solution)/shard_map/ppermute | solution.py:751
  50.1 7.3 %collective-permute-start.13 = (bf16[608,128]{1,0:T(8,128)(2,1)}, bf16[608,128]{1,0:T(8,128)(2,1)S(1)}, u32[]{:S(2)}, u32[]{:S(2)}) collective-permute-start(bf16[608,128]{1,0:T(8,128)(2,1)} %get-tuple-element.113), channel_id=1, source_target_pairs={{0,2},{1,3},{2,0},{3,1},{4,6},{5,7},{6,4},{7,5},{8,10},{9,11},{10,... | collective-permute-start | bytes 466952 | tf_op jit(solution)/shard_map/ppermute | solution.py:752
  51.7 6.2 %collective-permute-start.14 = (bf16[608,128]{1,0:T(8,128)(2,1)S(1)}, bf16[608,128]{1,0:T(8,128)(2,1)}, u32[]{:S(2)}, u32[]{:S(2)}) collective-permute-start(bf16[608,128]{1,0:T(8,128)(2,1)S(1)} %get-tuple-element.114), channel_id=1, source_target_pairs={{0,1},{1,0},{2,3},{3,2},{4,5},{5,4},{6,7},{7,6},{8,9},{9,8},{10,11... | collective-permute-start | bytes 466952 | tf_op jit(solution)/shard_map/ppermute | solution.py:752
  52.2 26.4 %all-to-all-start.1 = ((bf16[16,2,24,512]{3,2,1,0:T(8,128)(2,1)}), bf16[16,2,24,512]{3,2,1,0:T(8,128)(2,1)S(1)}, u32[]{:S(2)}, u32[]{:S(2)}) async-start(bf16[16,2,24,512]{3,2,1,0:T(8,128)(2,1)} %get-tuple-element.106), calls=%async_computation.1 | async-start | bytes 1572864 | tf_op jit(solution)/shard_map/all_to_all | solution.py:753
  59.0 14.3 %collective-permute-start.15 = (bf16[1216,128]{1,0:T(8,128)(2,1)S(1)}, bf16[1216,128]{1,0:T(8,128)(2,1)S(1)}, u32[]{:S(2)}, u32[]{:S(2)}) collective-permute-start(bf16[1216,128]{1,0:T(8,128)(2,1)S(1)} %get-tuple-element.128), channel_id=1, source_target_pairs={{0,1},{1,0},{2,3},{3,2},{4,5},{5,4},{6,7},{7,6},{8,9},{9,8},{10,11... | collective-permute-start | bytes 933896 | tf_op jit(solution)/shard_map/ppermute | solution.py:752
  60.4 13.6 %collective-permute-start.16 = (bf16[1216,128]{1,0:T(8,128)(2,1)S(1)}, bf16[1216,128]{1,0:T(8,128)(2,1)S(1)}, u32[]{:S(2)}, u32[]{:S(2)}) collective-permute-start(bf16[1216,128]{1,0:T(8,128)(2,1)S(1)} %get-tuple-element.129), channel_id=1, source_target_pairs={{0,2},{1,3},{2,0},{3,1},{4,6},{5,7},{6,4},{7,5},{8,10},{9,11},{10,... | collective-permute-start | bytes 933896 | tf_op jit(solution)/shard_map/ppermute | solution.py:752
  74.2 11.2 %collective-permute-start.17 = (bf16[304,128]{1,0:T(8,128)(2,1)S(1)}, bf16[304,128]{1,0:T(8,128)(2,1)S(1)}, u32[]{:S(2)}, u32[]{:S(2)}) collective-permute-start(bf16[304,128]{1,0:T(8,128)(2,1)S(1)} %get-tuple-element.135), channel_id=1, source_target_pairs={{0,4},{1,5},{2,6},{3,7},{4,0},{5,1},{6,2},{7,3},{8,12},{9,13},{10,... | collective-permute-start | bytes 233480 | tf_op jit(solution)/shard_map/ppermute | solution.py:752
  76.2 9.3 %collective-permute-start.18 = (bf16[304,128]{1,0:T(8,128)(2,1)S(1)}, bf16[304,128]{1,0:T(8,128)(2,1)S(1)}, u32[]{:S(2)}, u32[]{:S(2)}) collective-permute-start(bf16[304,128]{1,0:T(8,128)(2,1)S(1)} %get-tuple-element.136), channel_id=1, source_target_pairs={{0,8},{1,9},{2,10},{3,11},{4,12},{5,13},{6,14},{7,15},{8,0},{9,1},... | collective-permute-start | bytes 233480 | tf_op jit(solution)/shard_map/ppermute | solution.py:752
  78.5 7.0 %collective-permute-start.19 = (bf16[304,128]{1,0:T(8,128)(2,1)S(1)}, bf16[304,128]{1,0:T(8,128)(2,1)S(1)}, u32[]{:S(2)}, u32[]{:S(2)}) collective-permute-start(bf16[304,128]{1,0:T(8,128)(2,1)S(1)} %get-tuple-element.137), channel_id=1, source_target_pairs={{0,12},{1,13},{2,14},{3,15},{4,8},{5,9},{6,10},{7,11},{8,4},{9,5},... | collective-permute-start | bytes 233480 | tf_op jit(solution)/shard_map/ppermute | solution.py:752
  85.5 1.5 %collective-permute-start.20 = (f32[304,128]{1,0:T(8,128)S(1)}, f32[304,128]{1,0:T(8,128)S(1)}, u32[]{:S(2)}, u32[]{:S(2)}) collective-permute-start(f32[304,128]{1,0:T(8,128)S(1)} %join.3.mine_ref), channel_id=1, source_target_pairs={{0,16},{16,0},{1,17},{17,1},{2,18},{18,2},{3,19},{19,3},{4,20},{20... | collective-permute-start | bytes 466952 | tf_op jit(solution)/shard_map/ppermute | solution.py:751
  85.6 1.4 %collective-permute-start.21 = (f32[24,384]{1,0:T(8,128)S(1)}, f32[24,384]{1,0:T(8,128)S(1)}, u32[]{:S(2)}, u32[]{:S(2)}) collective-permute-start(f32[24,384]{1,0:T(8,128)S(1)} %get-tuple-element.143.small_ref), channel_id=1, source_target_pairs={{0,16},{16,0},{1,17},{17,1},{2,18},{18,2},{3,19},{19,3},{4,20},{20... | collective-permute-start | bytes 110600 | tf_op jit(solution)/shard_map/ppermute | solution.py:751

commit v8 on v7

--- a/solution.py
+++ b/solution.py
@@ -844,7 +844,8 @@
     both, *gown = pl.pallas_call(
         partial(mlp_second, near, pieces, deep),
         out_shape=[jax.ShapeDtypeStruct(both_shape, BF16)]
-        + [jax.ShapeDtypeStruct(piece.shape, BF16) for piece in own],
+        + [pltpu.HBM(own[0].shape, BF16)]
+        + [jax.ShapeDtypeStruct(piece.shape, BF16) for piece in own[1:]],
         in_specs=[SMEM] + [full] * (7 + pieces),
         out_specs=[full] * (1 + pieces),
         scratch_shapes=[pltpu.VMEM((ch * EDGE, LANES), F32)],
@@ -856,32 +857,23 @@
     tall = far * tall_one
     if near == 4:
         cut = tall // 2
-        part = pltpu.VMEM(gown[3].shape, BF16)
-        one, two = pl.pallas_call(
-            start_kernel,
-            out_shape=(part, part),
-            in_specs=[full] * 3,
-            out_specs=(full, full),
-            compiler_params=params(16),
-            cost_estimate=cost(1),
-            name="start",
-        )(gown[3], gown[4], arrived)
+        add = lambda v, at: (v.astype(F32) + arrived[at : at + v.shape[0]].astype(F32)).astype(BF16)
+        one, two = pair(add(gown[3], 3 * tall), add(gown[4], 3 * tall + cut))
         one, two = pair(flip(one, 2), flip(two, 1))
         one, two = relay(gown[1], gown[2], arrived, one, two)
-        features_last, one, two = pair(features, one, two)
-        first, second, *sent = gown[0], arrived, flip(one, 1), flip(two, 2)
+        features_last, first, one, two = pair(features, gown[0], one, two)
+        landed = [*join(tall, [pin(first), arrived], 1), flip(one, 1), flip(two, 2)]
     else:
         features_last = features
         total = (gown[0].astype(F32) + arrived.astype(F32)).astype(BF16)
         sent = list(swap(total.reshape(near, tall, width), near_groups))
-        first, second, *sent = sent
-    landed = [first, second, *sent]
-    table = pltpu.HBM((groups,) + toeplitz.shape, BF16)
-    strip = pltpu.HBM((groups, SLOT, images * SLOT, LANES), BF16)
+        landed = sent
+    table = jax.ShapeDtypeStruct((groups,) + toeplitz.shape, BF16)
+    strip = jax.ShapeDtypeStruct((groups, SLOT, images * SLOT, LANES), BF16)
     prepared = pl.pallas_call(
         prepare_kernel,
         out_shape=(
-            pltpu.HBM((groups,) + square, BF16), table, table, strip, strip,
+            jax.ShapeDtypeStruct((groups,) + square, BF16), table, table, strip, strip,
         ),
         in_specs=[SMEM, SMEM, full, full],
         out_specs=(full,) * 5,
@@ -915,7 +907,7 @@
         pin(heights), pin(widths), pin(features), pin(cotangent), both, taps,
         pin(row(layer_scale)), pin(row(out_bias)), pin(row(step_height)), pin(row(step_width)),
         pin(rate_height), pin(rate_width), pin(readout_height), pin(readout_width),
-        *map(pin, prepared),
+        *prepared,
     )
     *shards, small = pair(*shards, small)
     (mine,) = join(tall_one, shards, 1)

time: 88.5 us -> 87.5 us (0.989)
  Pallas kernels: 27.7 us -> 25.6 us
    pallas_call x2 -> x1, Pallas kernels: 4.25 us -> 2.5 us  [per_device(): pl.pallas_call(prepare_kernel, out_shape=(jax.ShapeDtypeStruct((groups,)...]
    pallas_call x2 -> x3, Pallas kernels: 0.19 us -> 1.18 us  [join(): pl.pallas_call(partial(join_kernel, len(arrays)), out_shape=[pltpu.VMEM((...]
    pallas_call x1, Pallas kernels: 1.1 us -> 0.19 us  [relay(): pl.pallas_call(relay_kernel, out_shape=(shape, shape), in_specs=[full] *...]
  transfers between devices with their start and end apart: 24 -> 24, of which waited for: 11 -> 11; matrix products, arithmetic and copies ran while one was open for 0% -> 0% of each run, Pallas kernels for 24% -> 23%
where the time goes in v8:
time: 87.5 us; the launch traced here: 87 us
  starting transfers between devices  32.2 us (37%)
  waiting for transfers between devices  28.1 us (32%)
  Pallas kernels  25.6 us (29%)
  between operations  0.95 us (1%)
    ppermute x14, starting transfers between devices, per_device(): lax.ppermute(v, 'ch', [(i, i ^ bits) for i in range(ch)])  20.9 us
    ppermute x14, waiting for transfers between devices, per_device(): lax.ppermute(v, 'ch', [(i, i ^ bits) for i in range(ch)])  19.7 us
    all_to_all x2, starting transfers between devices, per_device(): lax.all_to_all(v, 'ch', split_axis=0, concat_axis=0, tiled=True, axis_ind...  9.66 us
    all_to_all x2, waiting for transfers between devices, per_device(): lax.all_to_all(v, 'ch', split_axis=0, concat_axis=0, tiled=True, axis_ind...  6.39 us
    pallas_call x1, Pallas kernels, per_device(): pl.pallas_call(backward_kernel, out_shape=(jax.ShapeDtypeStruct((channels...  6.18 us
    pallas_call x1, Pallas kernels, per_device(): pl.pallas_call(forward_kernel, out_shape=(jax.ShapeDtypeStruct(both_shape...  5.28 us
    pallas_call x1, Pallas kernels, per_device(): pl.pallas_call(partial(mlp_second, near, pieces, deep), out_shape=[jax.Sh...  4.36 us
    pallas_call x1, Pallas kernels, per_device(): pl.pallas_call(partial(mlp_first, near, pieces, deep), out_shape=[jax.Sha...  3.85 us
  transfers between devices with their start and end apart: 24, of which 11 were waited for; matrix products, arithmetic and copies ran while one was open for 0% of the time, Pallas kernels for 23%

profile of v8, /device:TPU:0, one launch (start us, length us, event | category | flops | bytes accessed | tf_op | source)
XLA Modules:
  0.0 87.0 jit_solution(11983332213349989816)
XLA Ops:
  0.7 1.2 %pack.1 = bf16[304,128]{1,0:T(8,128)(2,1)S(1)} custom-call(s32[1]{0:T(128)} %bitcast.2.half, bf16[96,384]{1,0:T(8,128)(2,1)} %bitcast.21, bf16[96,384]{1,0:T(8,128)(2,1)} %out_ref.1, bf16[1,96]{1,0:T(2,128)(2,1)} %bitcast.28, bf16[1,24]{1,0:T(2,128)(2,1)} %bitcast.29, bf16[1,24]{1,0:T(2,128)(2,1)} %bitcast.30), custom_call_target="tpu_custom_call" | custom-call | bytes 6000000 | tf_op jit(solution)/shard_map/pack/pallas_call | solution.py:761
  1.8 5.1 %collective-permute-start.2 = (bf16[304,128]{1,0:T(8,128)(2,1)S(1)}, bf16[304,128]{1,0:T(8,128)(2,1)S(1)}, u32[]{:S(2)}, u32[]{:S(2)}) collective-permute-start(bf16[304,128]{1,0:T(8,128)(2,1)S(1)} %pack.1), channel_id=1, source_target_pairs={{0,12},{1,13},{2,14},{3,15},{4,8},{5,9},{6,10},{7,11},{8,4},{9,5},... | collective-permute-start | bytes 233480 | tf_op jit(solution)/shard_map/ppermute | solution.py:752
  6.9 0.0 collective-permute-start.1
  6.9 0.6 collective-permute-start
  7.6 5.3 %mixer_forward.1 = (bf16[16,2,24,512]{3,2,1,0:T(8,128)(2,1)}, f32[24,128]{1,0:T(8,128)S(1)}) custom-call(s32[8]{0:T(128)} %heights.5, s32[8]{0:T(128)} %widths.5, bf16[24,8192]{1,0:T(8,128)(2,1)} %feat_ref.3, bf16[24,8192]{1,0:T(8,128)(2,1)} %cot_ref.3, f32[1,24]{1,0:T(1,128)} %bitcast.22, f32[1,24]{1,0:T(1,128)} %bitcast.24, f32[1,24]{1,0:T(1,128)} %bitcast.26, ...), custom_call_target="tpu_custom_call" | custom-call | bytes 18000000 | tf_op jit(solution)/shard_map/mixer_forward/pallas_call | solution.py:781
  12.8 0.0 collective-permute-done.2
  12.9 0.6 collective-permute-done.1
  13.5 0.0 collective-permute-done
  13.5 1.6 %collective-permute-start.4 = (bf16[1216,128]{1,0:T(8,128)(2,1)S(1)}, bf16[1216,128]{1,0:T(8,128)(2,1)S(1)}, u32[]{:S(2)}, u32[]{:S(2)}) collective-permute-start(bf16[1216,128]{1,0:T(8,128)(2,1)S(1)} %constant_dynamic-update-slice_fusion.refs_0_), channel_id=1, source_target_pairs={{0,2},{1,3},{2,0},{3,1},{4,6},{5,7},{6,4},{7,5},{8,10},{9,11},{10,... | collective-permute-start | bytes 933896 | tf_op jit(solution)/shard_map/ppermute | solution.py:752
  15.1 1.5 %collective-permute-start.3 = (bf16[1216,128]{1,0:T(8,128)(2,1)S(1)}, bf16[1216,128]{1,0:T(8,128)(2,1)S(1)}, u32[]{:S(2)}, u32[]{:S(2)}) collective-permute-start(bf16[1216,128]{1,0:T(8,128)(2,1)S(1)} %constant_dynamic-update-slice_fusion.refs_0_), channel_id=1, source_target_pairs={{0,1},{1,0},{2,3},{3,2},{4,5},{5,4},{6,7},{7,6},{8,9},{9,8},{10,11... | collective-permute-start | bytes 933896 | tf_op jit(solution)/shard_map/ppermute | solution.py:752
  16.6 0.0 collective-permute-start.7
  16.6 4.5 %all-to-all-start = ((bf16[16,2,24,512]{3,2,1,0:T(8,128)(2,1)}), bf16[16,2,24,512]{3,2,1,0:T(8,128)(2,1)S(1)}, u32[]{:S(2)}, u32[]{:S(2)}) async-start(bf16[16,2,24,512]{3,2,1,0:T(8,128)(2,1)} %get-tuple-element.90), calls=%async_computation | async-start | bytes 1572864 | tf_op jit(solution)/shard_map/all_to_all | solution.py:753
  21.2 1.1 %collective-permute-done.4.two_ref.refs_2_ = bf16[1216,128]{1,0:T(8,128)(2,1)S(1)} collective-permute-done((bf16[1216,128]{1,0:T(8,128)(2,1)S(1)}, bf16[1216,128]{1,0:T(8,128)(2,1)S(1)}, u32[]{:S(2)}, u32[]{:S(2)}) %collective-permute-start.4) | collective-permute-done | bytes 311328 | tf_op jit(solution)/shard_map/ppermute | solution.py:752
  22.2 1.4 %collective-permute-done.3.one_ref.refs_1_ = bf16[1216,128]{1,0:T(8,128)(2,1)S(1)} collective-permute-done((bf16[1216,128]{1,0:T(8,128)(2,1)S(1)}, bf16[1216,128]{1,0:T(8,128)(2,1)S(1)}, u32[]{:S(2)}, u32[]{:S(2)}) %collective-permute-start.3) | collective-permute-done | bytes 311328 | tf_op jit(solution)/shard_map/ppermute | solution.py:752
  23.7 0.4 collective-permute-start.5
  24.1 1.9 %collective-permute-start.6 = (bf16[608,128]{1,0:T(8,128)(2,1)S(1)}, bf16[608,128]{1,0:T(8,128)(2,1)S(1)}, u32[]{:S(2)}, u32[]{:S(2)}) collective-permute-start(bf16[608,128]{1,0:T(8,128)(2,1)S(1)} %get-tuple-element.98), channel_id=1, source_target_pairs={{0,1},{1,0},{2,3},{3,2},{4,5},{5,4},{6,7},{7,6},{8,9},{9,8},{10,11... | collective-permute-start | bytes 466952 | tf_op jit(solution)/shard_map/ppermute | solution.py:752
  26.0 0.0 collective-permute-start.8
  26.0 0.5 collective-permute-start.9
  26.5 6.7 %collective-permute-done.5.refs_3_ = bf16[608,128]{1,0:T(8,128)(2,1)S(1)} collective-permute-done((bf16[608,128]{1,0:T(8,128)(2,1)S(1)}, bf16[608,128]{1,0:T(8,128)(2,1)S(1)}, u32[]{:S(2)}, u32[]{:S(2)}) %collective-permute-start.5) | collective-permute-done | bytes 155680 | tf_op jit(solution)/shard_map/ppermute | solution.py:752
  33.2 0.0 collective-permute-start.10
  33.2 0.0 collective-permute-done.6.refs_4_
  33.2 0.5 collective-permute-start.11
  33.7 0.1 pad_add_fusion.where_ref
  33.8 0.0 collective-permute-done.7.refs_5_
  33.8 0.8 collective-permute-done.10.refs_8_
  34.6 0.2 collective-permute-done.11.refs_9_
  34.8 0.0 collective-permute-done.8.refs_6_
  34.8 0.0 collective-permute-done.9.refs_7_
  34.8 6.4 %all-to-all-done.given_ref = bf16[16,2,24,512]{3,2,1,0:T(8,128)(2,1)S(1)} async-done(((bf16[16,2,24,512]{3,2,1,0:T(8,128)(2,1)}), bf16[16,2,24,512]{3,2,1,0:T(8,128)(2,1)S(1)}, u32[]{:S(2)}, u32[]{:S(2)}) %all-to-all-start) | async-done | bytes 786464 | tf_op jit(solution)/shard_map/all_to_all | solution.py:753
  41.2 3.8 %mlp_first.1 = (bf16[4864,128]{1,0:T(8,128)(2,1)S(1)}, bf16[384,512]{1,0:T(8,128)(2,1)S(1)}, bf16[384,512]{1,0:T(8,128)(2,1)S(1)}, f32[384,512]{1,0:T(8,128)S(1)...) custom-call(s32[2]{0:T(128)S(1)} %pad_add_fusion.where_ref, ...), custom_call_target="tpu_custom_call" | custom-call | bytes 15000000 | tf_op jit(solution)/shard_map/mlp_first/pallas_call | solution.py:829
  45.1 0.1 collective-permute-start.12
  45.2 4.4 %mlp_second.1 = (bf16[16,2,24,512]{3,2,1,0:T(8,128)(2,1)}, bf16[1216,128]{1,0:T(8,128)(2,1)}, bf16[1216,128]{1,0:T(8,128)(2,1)S(1)}, bf16[1216,128]{1,0:T(8,128)...) custom-call(s32[2]{0:T(128)S(1)} %pad_add_fusion.where_ref, ...), custom_call_target="tpu_custom_call" | custom-call | bytes 15000000 | tf_op jit(solution)/shard_map/mlp_second/pallas_call | solution.py:844
  49.5 0.0 collective-permute-done.12.arrived_ref.refs_1_
  49.5 0.1 add_convert_fusion
  49.6 1.7 %collective-permute-start.13 = (bf16[608,128]{1,0:T(8,128)(2,1)S(1)}, bf16[608,128]{1,0:T(8,128)(2,1)S(1)}, u32[]{:S(2)}, u32[]{:S(2)}) collective-permute-start(bf16[608,128]{1,0:T(8,128)(2,1)S(1)} %get-tuple-element.114), channel_id=1, source_target_pairs={{0,2},{1,3},{2,0},{3,1},{4,6},{5,7},{6,4},{7,5},{8,10},{9,11},{10,... | collective-permute-start | bytes 466952 | tf_op jit(solution)/shard_map/ppermute | solution.py:752
  51.3 0.6 collective-permute-start.14
  51.9 5.1 %all-to-all-start.1 = ((bf16[16,2,24,512]{3,2,1,0:T(8,128)(2,1)}), bf16[16,2,24,512]{3,2,1,0:T(8,128)(2,1)S(1)}, u32[]{:S(2)}, u32[]{:S(2)}) async-start(bf16[16,2,24,512]{3,2,1,0:T(8,128)(2,1)} %get-tuple-element.106), calls=%async_computation.1 | async-start | bytes 1572864 | tf_op jit(solution)/shard_map/all_to_all | solution.py:753
  57.0 0.0 collective-permute-done.13.first_ref
  57.0 0.4 collective-permute-done.14.second_ref
  57.4 0.2 relay.1
  57.6 1.6 %collective-permute-start.15 = (bf16[1216,128]{1,0:T(8,128)(2,1)S(1)}, bf16[1216,128]{1,0:T(8,128)(2,1)S(1)}, u32[]{:S(2)}, u32[]{:S(2)}) collective-permute-start(bf16[1216,128]{1,0:T(8,128)(2,1)S(1)} %get-tuple-element.129), channel_id=1, source_target_pairs={{0,1},{1,0},{2,3},{3,2},{4,5},{5,4},{6,7},{7,6},{8,9},{9,8},{10,11... | collective-permute-start | bytes 933896 | tf_op jit(solution)/shard_map/ppermute | solution.py:752
  59.2 1.5 %collective-permute-start.16 = (bf16[1216,128]{1,0:T(8,128)(2,1)S(1)}, bf16[1216,128]{1,0:T(8,128)(2,1)S(1)}, u32[]{:S(2)}, u32[]{:S(2)}) collective-permute-start(bf16[1216,128]{1,0:T(8,128)(2,1)S(1)} %get-tuple-element.130), channel_id=1, source_target_pairs={{0,2},{1,3},{2,0},{3,1},{4,6},{5,7},{6,4},{7,5},{8,10},{9,11},{10,... | collective-permute-start | bytes 933896 | tf_op jit(solution)/shard_map/ppermute | solution.py:752
  60.7 1.0 %join.3.refs_0_ = f32[1216,128]{1,0:T(8,128)S(1)} custom-call(bf16[1216,128]{1,0:T(8,128)(2,1)} %get-tuple-element.128.refs_0_, bf16[4864,128]{1,0:T(8,128)(2,1)S(1)} %collective-permute-done.12.arrived_ref.refs_1_), custom_call_target="tpu_custom_call" | custom-call | flops 1 | bytes 1000000 | tf_op jit(solution)/shard_map/join/pallas_call | solution.py:701
  61.7 2.5 %mixer_prepare.1 = (bf16[3,256,256]{2,1,0:T(8,128)(2,1)S(1)}, bf16[3,256,256]{2,1,0:T(8,128)(2,1)S(1)}, bf16[3,256,256]{2,1,0:T(8,128)(2,1)S(1)}, bf16[3,8,64,12...) custom-call(s32[8]{0:T(128)} %heights.5, s32[8]{0:T(128)} %widths.5, bf16[24,8192]{1,0:T(8,128)(2,1)} %feat_ref.3, ...), custom_call_target="tpu_custom_call" | custom-call | bytes 12000000 | tf_op jit(solution)/shard_map/mixer_prepare/pallas_call | solution.py:873
  64.2 8.3 %collective-permute-done.15.refs_1_ = bf16[1216,128]{1,0:T(8,128)(2,1)S(1)} collective-permute-done((bf16[1216,128]{1,0:T(8,128)(2,1)S(1)}, bf16[1216,128]{1,0:T(8,128)(2,1)S(1)}, u32[]{:S(2)}, u32[]{:S(2)}) %collective-permute-start.15) | collective-permute-done | bytes 311328 | tf_op jit(solution)/shard_map/ppermute | solution.py:752
  72.6 1.1 %collective-permute-done.16.refs_2_ = bf16[1216,128]{1,0:T(8,128)(2,1)S(1)} collective-permute-done((bf16[1216,128]{1,0:T(8,128)(2,1)S(1)}, bf16[1216,128]{1,0:T(8,128)(2,1)S(1)}, u32[]{:S(2)}, u32[]{:S(2)}) %collective-permute-start.16) | collective-permute-done | bytes 311328 | tf_op jit(solution)/shard_map/ppermute | solution.py:752
  73.7 0.1 join.4
  73.8 1.6 %collective-permute-start.17 = (bf16[304,128]{1,0:T(8,128)(2,1)S(1)}, bf16[304,128]{1,0:T(8,128)(2,1)S(1)}, u32[]{:S(2)}, u32[]{:S(2)}) collective-permute-start(bf16[304,128]{1,0:T(8,128)(2,1)S(1)} %get-tuple-element.135), channel_id=1, source_target_pairs={{0,4},{1,5},{2,6},{3,7},{4,0},{5,1},{6,2},{7,3},{8,12},{9,13},{10,... | collective-permute-start | bytes 233480 | tf_op jit(solution)/shard_map/ppermute | solution.py:752
  75.4 2.7 %collective-permute-start.18 = (bf16[304,128]{1,0:T(8,128)(2,1)S(1)}, bf16[304,128]{1,0:T(8,128)(2,1)S(1)}, u32[]{:S(2)}, u32[]{:S(2)}) collective-permute-start(bf16[304,128]{1,0:T(8,128)(2,1)S(1)} %get-tuple-element.136), channel_id=1, source_target_pairs={{0,8},{1,9},{2,10},{3,11},{4,12},{5,13},{6,14},{7,15},{8,0},{9,1},... | collective-permute-start | bytes 233480 | tf_op jit(solution)/shard_map/ppermute | solution.py:752
  78.1 0.2 collective-permute-start.19
  78.3 0.0 all-to-all-done.1.both_ref
  78.3 6.2 %mixer_backward.1 = (bf16[24,8192]{1,0:T(8,128)(2,1)}, f32[24,8192]{1,0:T(8,128)}, f32[24,384]{1,0:T(8,128)S(1)}) custom-call(s32[8]{0:T(128)} %heights.5, s32[8]{0:T(128)} %widths.5, bf16[24,8192]{1,0:T(8,128)(2,1)} %feat_ref.3, bf16[24,8192]{1,0:T(8,128)(2,1)} %cot_ref.3, bf16[16,2,24,512]{3,2,1,0:T(8,128)(2,1)S(1)} %all-to-all-done.1.both_ref, ...), custom_call_target="tpu_custom_call" | custom-call | bytes 21000000 | tf_op jit(solution)/shard_map/mixer_backward/pallas_call | solution.py:888
  84.4 0.0 collective-permute-done.17.refs_1_
  84.4 0.0 collective-permute-done.18.refs_2_
  84.4 0.0 collective-permute-done.19.refs_3_
  84.5 0.1 collective-permute-start.20
  84.6 0.5 collective-permute-start.21
  85.1 0.9 %collective-permute-done.21.sibling_ref = f32[24,384]{1,0:T(8,128)S(1)} collective-permute-done((f32[24,384]{1,0:T(8,128)S(1)}, f32[24,384]{1,0:T(8,128)S(1)}, u32[]{:S(2)}, u32[]{:S(2)}) %collective-permute-start.21) | collective-permute-done | bytes 36896 | tf_op jit(solution)/shard_map/ppermute | solution.py:751
  86.0 0.0 collective-permute-done.20.other_ref
  86.0 0.9 finish.1
  (6 shorter events, 0.1 us)
Async XLA Ops:
  1.8 11.0 %collective-permute-start.2 = (bf16[304,128]{1,0:T(8,128)(2,1)S(1)}, bf16[304,128]{1,0:T(8,128)(2,1)S(1)}, u32[]{:S(2)}, u32[]{:S(2)}) collective-permute-start(bf16[304,128]{1,0:T(8,128)(2,1)S(1)} %pack.1), channel_id=1, source_target_pairs={{0,12},{1,13},{2,14},{3,15},{4,8},{5,9},{6,10},{7,11},{8,4},{9,5},... | collective-permute-start | bytes 233480 | tf_op jit(solution)/shard_map/ppermute | solution.py:752
  6.9 6.5 %collective-permute-start.1 = (bf16[304,128]{1,0:T(8,128)(2,1)S(1)}, bf16[304,128]{1,0:T(8,128)(2,1)S(1)}, u32[]{:S(2)}, u32[]{:S(2)}) collective-permute-start(bf16[304,128]{1,0:T(8,128)(2,1)S(1)} %pack.1), channel_id=1, source_target_pairs={{0,8},{1,9},{2,10},{3,11},{4,12},{5,13},{6,14},{7,15},{8,0},{9,1},... | collective-permute-start | bytes 233480 | tf_op jit(solution)/shard_map/ppermute | solution.py:752
  6.9 6.5 %collective-permute-start = (bf16[304,128]{1,0:T(8,128)(2,1)S(1)}, bf16[304,128]{1,0:T(8,128)(2,1)S(1)}, u32[]{:S(2)}, u32[]{:S(2)}) collective-permute-start(bf16[304,128]{1,0:T(8,128)(2,1)S(1)} %pack.1), channel_id=1, source_target_pairs={{0,4},{1,5},{2,6},{3,7},{4,0},{5,1},{6,2},{7,3},{8,12},{9,13},{10,... | collective-permute-start | bytes 233480 | tf_op jit(solution)/shard_map/ppermute | solution.py:752
  13.5 8.7 %collective-permute-start.4 = (bf16[1216,128]{1,0:T(8,128)(2,1)S(1)}, bf16[1216,128]{1,0:T(8,128)(2,1)S(1)}, u32[]{:S(2)}, u32[]{:S(2)}) collective-permute-start(bf16[1216,128]{1,0:T(8,128)(2,1)S(1)} %constant_dynamic-update-slice_fusion.refs_0_), channel_id=1, source_target_pairs={{0,2},{1,3},{2,0},{3,1},{4,6},{5,7},{6,4},{7,5},{8,10},{9,11},{10,... | collective-permute-start | bytes 933896 | tf_op jit(solution)/shard_map/ppermute | solution.py:752
  15.1 8.6 %collective-permute-start.3 = (bf16[1216,128]{1,0:T(8,128)(2,1)S(1)}, bf16[1216,128]{1,0:T(8,128)(2,1)S(1)}, u32[]{:S(2)}, u32[]{:S(2)}) collective-permute-start(bf16[1216,128]{1,0:T(8,128)(2,1)S(1)} %constant_dynamic-update-slice_fusion.refs_0_), channel_id=1, source_target_pairs={{0,1},{1,0},{2,3},{3,2},{4,5},{5,4},{6,7},{7,6},{8,9},{9,8},{10,11... | collective-permute-start | bytes 933896 | tf_op jit(solution)/shard_map/ppermute | solution.py:752
  16.6 17.2 %collective-permute-start.7 = (bf16[1216,128]{1,0:T(8,128)(2,1)S(1)}, bf16[1216,128]{1,0:T(8,128)(2,1)S(1)}, u32[]{:S(2)}, u32[]{:S(2)}) collective-permute-start(bf16[1216,128]{1,0:T(8,128)(2,1)S(1)} %constant_dynamic-update-slice_fusion.refs_0_), channel_id=1, source_target_pairs={{0,16},{16,0},{1,17},{17,1},{2,18},{18,2},{3,19},{19,3},{4,20},{20... | collective-permute-start | bytes 933896 | tf_op jit(solution)/shard_map/ppermute | solution.py:751
  16.6 24.6 %all-to-all-start = ((bf16[16,2,24,512]{3,2,1,0:T(8,128)(2,1)}), bf16[16,2,24,512]{3,2,1,0:T(8,128)(2,1)S(1)}, u32[]{:S(2)}, u32[]{:S(2)}) async-start(bf16[16,2,24,512]{3,2,1,0:T(8,128)(2,1)} %get-tuple-element.90), calls=%async_computation | async-start | bytes 1572864 | tf_op jit(solution)/shard_map/all_to_all | solution.py:753
  23.7 9.5 %collective-permute-start.5 = (bf16[608,128]{1,0:T(8,128)(2,1)S(1)}, bf16[608,128]{1,0:T(8,128)(2,1)S(1)}, u32[]{:S(2)}, u32[]{:S(2)}) collective-permute-start(bf16[608,128]{1,0:T(8,128)(2,1)S(1)} %get-tuple-element.97), channel_id=1, source_target_pairs={{0,2},{1,3},{2,0},{3,1},{4,6},{5,7},{6,4},{7,5},{8,10},{9,11},{10,... | collective-permute-start | bytes 466952 | tf_op jit(solution)/shard_map/ppermute | solution.py:752
  24.1 9.1 %collective-permute-start.6 = (bf16[608,128]{1,0:T(8,128)(2,1)S(1)}, bf16[608,128]{1,0:T(8,128)(2,1)S(1)}, u32[]{:S(2)}, u32[]{:S(2)}) collective-permute-start(bf16[608,128]{1,0:T(8,128)(2,1)S(1)} %get-tuple-element.98), channel_id=1, source_target_pairs={{0,1},{1,0},{2,3},{3,2},{4,5},{5,4},{6,7},{7,6},{8,9},{9,8},{10,11... | collective-permute-start | bytes 466952 | tf_op jit(solution)/shard_map/ppermute | solution.py:752
  26.0 8.8 %collective-permute-start.8 = (bf16[1216,128]{1,0:T(8,128)(2,1)S(1)}, bf16[1216,128]{1,0:T(8,128)(2,1)S(1)}, u32[]{:S(2)}, u32[]{:S(2)}) collective-permute-start(bf16[1216,128]{1,0:T(8,128)(2,1)S(1)} %collective-permute-done.3.one_ref.refs_1_), channel_id=1, source_target_pairs={{0,16},{16,0},{1,17},{17,1},{2,18},{18,2},{3,19},{19,3},{4,20},{20... | collective-permute-start | bytes 933896 | tf_op jit(solution)/shard_map/ppermute | solution.py:751
  26.0 8.8 %collective-permute-start.9 = (bf16[1216,128]{1,0:T(8,128)(2,1)S(1)}, bf16[1216,128]{1,0:T(8,128)(2,1)S(1)}, u32[]{:S(2)}, u32[]{:S(2)}) collective-permute-start(bf16[1216,128]{1,0:T(8,128)(2,1)S(1)} %collective-permute-done.4.two_ref.refs_2_), channel_id=1, source_target_pairs={{0,16},{16,0},{1,17},{17,1},{2,18},{18,2},{3,19},{19,3},{4,20},{20... | collective-permute-start | bytes 933896 | tf_op jit(solution)/shard_map/ppermute | solution.py:751
  33.2 1.4 %collective-permute-start.10 = (bf16[608,128]{1,0:T(8,128)(2,1)S(1)}, bf16[608,128]{1,0:T(8,128)(2,1)S(1)}, u32[]{:S(2)}, u32[]{:S(2)}) collective-permute-start(bf16[608,128]{1,0:T(8,128)(2,1)S(1)} %collective-permute-done.5.refs_3_), channel_id=1, source_target_pairs={{0,16},{16,0},{1,17},{17,1},{2,18},{18,2},{3,19},{19,3},{4,20},{20... | collective-permute-start | bytes 466952 | tf_op jit(solution)/shard_map/ppermute | solution.py:751
  33.2 1.6 %collective-permute-start.11 = (bf16[608,128]{1,0:T(8,128)(2,1)S(1)}, bf16[608,128]{1,0:T(8,128)(2,1)S(1)}, u32[]{:S(2)}, u32[]{:S(2)}) collective-permute-start(bf16[608,128]{1,0:T(8,128)(2,1)S(1)} %collective-permute-done.6.refs_4_), channel_id=1, source_target_pairs={{0,16},{16,0},{1,17},{17,1},{2,18},{18,2},{3,19},{19,3},{4,20},{20... | collective-permute-start | bytes 466952 | tf_op jit(solution)/shard_map/ppermute | solution.py:751
  45.1 4.4 %collective-permute-start.12 = (bf16[4864,128]{1,0:T(8,128)(2,1)S(1)}, bf16[4864,128]{1,0:T(8,128)(2,1)S(1)}, u32[]{:S(2)}, u32[]{:S(2)}) collective-permute-start(bf16[4864,128]{1,0:T(8,128)(2,1)S(1)} %get-tuple-element.111), channel_id=1, source_target_pairs={{0,16},{16,0},{1,17},{17,1},{2,18},{18,2},{3,19},{19,3},{4,20},{20... | collective-permute-start | bytes 3735560 | tf_op jit(solution)/shard_map/ppermute | solution.py:751
  49.6 7.4 %collective-permute-start.13 = (bf16[608,128]{1,0:T(8,128)(2,1)S(1)}, bf16[608,128]{1,0:T(8,128)(2,1)S(1)}, u32[]{:S(2)}, u32[]{:S(2)}) collective-permute-start(bf16[608,128]{1,0:T(8,128)(2,1)S(1)} %get-tuple-element.114), channel_id=1, source_target_pairs={{0,2},{1,3},{2,0},{3,1},{4,6},{5,7},{6,4},{7,5},{8,10},{9,11},{10,... | collective-permute-start | bytes 466952 | tf_op jit(solution)/shard_map/ppermute | solution.py:752
  51.3 6.1 %collective-permute-start.14 = (bf16[608,128]{1,0:T(8,128)(2,1)S(1)}, bf16[608,128]{1,0:T(8,128)(2,1)S(1)}, u32[]{:S(2)}, u32[]{:S(2)}) collective-permute-start(bf16[608,128]{1,0:T(8,128)(2,1)S(1)} %get-tuple-element.115), channel_id=1, source_target_pairs={{0,1},{1,0},{2,3},{3,2},{4,5},{5,4},{6,7},{7,6},{8,9},{9,8},{10,11... | collective-permute-start | bytes 466952 | tf_op jit(solution)/shard_map/ppermute | solution.py:752
  51.9 26.4 %all-to-all-start.1 = ((bf16[16,2,24,512]{3,2,1,0:T(8,128)(2,1)}), bf16[16,2,24,512]{3,2,1,0:T(8,128)(2,1)S(1)}, u32[]{:S(2)}, u32[]{:S(2)}) async-start(bf16[16,2,24,512]{3,2,1,0:T(8,128)(2,1)} %get-tuple-element.106), calls=%async_computation.1 | async-start | bytes 1572864 | tf_op jit(solution)/shard_map/all_to_all | solution.py:753
  57.6 14.9 %collective-permute-start.15 = (bf16[1216,128]{1,0:T(8,128)(2,1)S(1)}, bf16[1216,128]{1,0:T(8,128)(2,1)S(1)}, u32[]{:S(2)}, u32[]{:S(2)}) collective-permute-start(bf16[1216,128]{1,0:T(8,128)(2,1)S(1)} %get-tuple-element.129), channel_id=1, source_target_pairs={{0,1},{1,0},{2,3},{3,2},{4,5},{5,4},{6,7},{7,6},{8,9},{9,8},{10,11... | collective-permute-start | bytes 933896 | tf_op jit(solution)/shard_map/ppermute | solution.py:752
  59.2 14.5 %collective-permute-start.16 = (bf16[1216,128]{1,0:T(8,128)(2,1)S(1)}, bf16[1216,128]{1,0:T(8,128)(2,1)S(1)}, u32[]{:S(2)}, u32[]{:S(2)}) collective-permute-start(bf16[1216,128]{1,0:T(8,128)(2,1)S(1)} %get-tuple-element.130), channel_id=1, source_target_pairs={{0,2},{1,3},{2,0},{3,1},{4,6},{5,7},{6,4},{7,5},{8,10},{9,11},{10,... | collective-permute-start | bytes 933896 | tf_op jit(solution)/shard_map/ppermute | solution.py:752
  73.8 10.6 %collective-permute-start.17 = (bf16[304,128]{1,0:T(8,128)(2,1)S(1)}, bf16[304,128]{1,0:T(8,128)(2,1)S(1)}, u32[]{:S(2)}, u32[]{:S(2)}) collective-permute-start(bf16[304,128]{1,0:T(8,128)(2,1)S(1)} %get-tuple-element.135), channel_id=1, source_target_pairs={{0,4},{1,5},{2,6},{3,7},{4,0},{5,1},{6,2},{7,3},{8,12},{9,13},{10,... | collective-permute-start | bytes 233480 | tf_op jit(solution)/shard_map/ppermute | solution.py:752
  75.4 9.1 %collective-permute-start.18 = (bf16[304,128]{1,0:T(8,128)(2,1)S(1)}, bf16[304,128]{1,0:T(8,128)(2,1)S(1)}, u32[]{:S(2)}, u32[]{:S(2)}) collective-permute-start(bf16[304,128]{1,0:T(8,128)(2,1)S(1)} %get-tuple-element.136), channel_id=1, source_target_pairs={{0,8},{1,9},{2,10},{3,11},{4,12},{5,13},{6,14},{7,15},{8,0},{9,1},... | collective-permute-start | bytes 233480 | tf_op jit(solution)/shard_map/ppermute | solution.py:752
  78.1 6.4 %collective-permute-start.19 = (bf16[304,128]{1,0:T(8,128)(2,1)S(1)}, bf16[304,128]{1,0:T(8,128)(2,1)S(1)}, u32[]{:S(2)}, u32[]{:S(2)}) collective-permute-start(bf16[304,128]{1,0:T(8,128)(2,1)S(1)} %get-tuple-element.137), channel_id=1, source_target_pairs={{0,12},{1,13},{2,14},{3,15},{4,8},{5,9},{6,10},{7,11},{8,4},{9,5},... | collective-permute-start | bytes 233480 | tf_op jit(solution)/shard_map/ppermute | solution.py:752
  84.5 1.5 %collective-permute-start.20 = (f32[304,128]{1,0:T(8,128)S(1)}, f32[304,128]{1,0:T(8,128)S(1)}, u32[]{:S(2)}, u32[]{:S(2)}) collective-permute-start(f32[304,128]{1,0:T(8,128)S(1)} %join.5.mine_ref), channel_id=1, source_target_pairs={{0,16},{16,0},{1,17},{17,1},{2,18},{18,2},{3,19},{19,3},{4,20},{20... | collective-permute-start | bytes 466952 | tf_op jit(solution)/shard_map/ppermute | solution.py:751
  84.6 1.4 %collective-permute-start.21 = (f32[24,384]{1,0:T(8,128)S(1)}, f32[24,384]{1,0:T(8,128)S(1)}, u32[]{:S(2)}, u32[]{:S(2)}) collective-permute-start(f32[24,384]{1,0:T(8,128)S(1)} %get-tuple-element.143.small_ref), channel_id=1, source_target_pairs={{0,16},{16,0},{1,17},{17,1},{2,18},{18,2},{3,19},{19,3},{4,20},{20... | collective-permute-start | bytes 110600 | tf_op jit(solution)/shard_map/ppermute | solution.py:751

commit v9 on v8

--- a/solution.py
+++ b/solution.py
@@ -404,6 +404,13 @@
     return out, tail
 
 
+def stack_kernel(*refs):
+    out = refs[-1]
+    tall = refs[0].shape[0]
+    for index, ref in enumerate(refs[:-1]):
+        out[index * tall : (index + 1) * tall] = ref[...]
+
+
 def join_kernel(count, *refs):
     given, outs = refs[:count], refs[count:]
     tall = outs[0].shape[0]
@@ -771,7 +778,8 @@
         pin(row(norm_shift)),
     )
     pack, features_after = pair(pack, features)
-    shards = [pack] + [flip(pack, bits * near) for bits in range(1, far)]
+    shards = [flip(pack, bits * near) for bits in range(far - 1, 0, -1)]
+    shards = [pack] + shards[::-1]
 
     groups = -(-channels // SLOT)
     square = (SLOT * SIDE, images // PER * LANES)
@@ -801,7 +809,15 @@
     )
     given, *shards = pair(given, *shards)
     given = swap(given)
-    shard = jnp.concatenate(shards, axis=0)
+    shard = pl.pallas_call(
+        stack_kernel,
+        out_shape=pltpu.VMEM((far * tall_one, width), BF16),
+        in_specs=[full] * far,
+        out_specs=full,
+        compiler_params=params(16),
+        cost_estimate=cost(1),
+        name="stack",
+    )(*shards)
     if near == 4:
         cut = far * tall_one // 2
         beside, above = pair(flip(shard, 1), flip(shard, 2))

time: 87.5 us -> 87.4 us (level)
  no operation moved by 1% of the time
where the time goes in v9:
time: 87.4 us; the launch traced here: 87 us
  starting transfers between devices  32.2 us (37%)
  waiting for transfers between devices  28.1 us (32%)
  Pallas kernels  25.6 us (29%)
  between operations  0.93 us (1%)
    ppermute x14, starting transfers between devices, per_device(): lax.ppermute(v, 'ch', [(i, i ^ bits) for i in range(ch)])  20.8 us
    ppermute x14, waiting for transfers between devices, per_device(): lax.ppermute(v, 'ch', [(i, i ^ bits) for i in range(ch)])  19.8 us
    all_to_all x2, starting transfers between devices, per_device(): lax.all_to_all(v, 'ch', split_axis=0, concat_axis=0, tiled=True, axis_ind...  9.66 us
    all_to_all x2, waiting for transfers between devices, per_device(): lax.all_to_all(v, 'ch', split_axis=0, concat_axis=0, tiled=True, axis_ind...  6.39 us
    pallas_call x1, Pallas kernels, per_device(): pl.pallas_call(backward_kernel, out_shape=(jax.ShapeDtypeStruct((channels...  6.18 us
    pallas_call x1, Pallas kernels, per_device(): pl.pallas_call(forward_kernel, out_shape=(jax.ShapeDtypeStruct(both_shape...  5.28 us
    pallas_call x1, Pallas kernels, per_device(): pl.pallas_call(partial(mlp_second, near, pieces, deep), out_shape=[jax.Sh...  4.37 us
    pallas_call x1, Pallas kernels, per_device(): pl.pallas_call(partial(mlp_first, near, pieces, deep), out_shape=[jax.Sha...  3.85 us
  transfers between devices with their start and end apart: 24, of which 11 were waited for; matrix products, arithmetic and copies ran while one was open for 0% of the time, Pallas kernels for 23%

profile of v9, /device:TPU:0, one launch (start us, length us, event | category | flops | bytes accessed | tf_op | source)
XLA Modules:
  0.0 87.0 jit_solution(2457091579947521800)
XLA Ops:
  0.7 1.2 %pack.1.refs_0_ = bf16[304,128]{1,0:T(8,128)(2,1)S(1)} custom-call(s32[1]{0:T(128)} %bitcast.2.half, bf16[96,384]{1,0:T(8,128)(2,1)} %bitcast.21, bf16[96,384]{1,0:T(8,128)(2,1)} %out_ref.1, bf16[1,96]{1,0:T(2,128)(2,1)} %bitcast.28, bf16[1,24]{1,0:T(2,128)(2,1)} %bitcast.29, bf16[1,24]{1,0:T(2,128)(2,1)} %bitcast.30), custom_call_target="tpu_custom_call" | custom-call | bytes 6000000 | tf_op jit(solution)/shard_map/pack/pallas_call | solution.py:768
  1.8 5.1 %collective-permute-start.2 = (bf16[304,128]{1,0:T(8,128)(2,1)S(1)}, bf16[304,128]{1,0:T(8,128)(2,1)S(1)}, u32[]{:S(2)}, u32[]{:S(2)}) collective-permute-start(bf16[304,128]{1,0:T(8,128)(2,1)S(1)} %pack.1.refs_0_), channel_id=1, source_target_pairs={{0,12},{1,13},{2,14},{3,15},{4,8},{5,9},{6,10},{7,11},{8,4},{9,5},... | collective-permute-start | bytes 233480 | tf_op jit(solution)/shard_map/ppermute | solution.py:759
  6.9 0.0 collective-permute-start.1
  6.9 0.6 collective-permute-start
  7.6 5.3 %mixer_forward.1 = (bf16[16,2,24,512]{3,2,1,0:T(8,128)(2,1)}, f32[24,128]{1,0:T(8,128)S(1)}) custom-call(s32[8]{0:T(128)} %heights.5, s32[8]{0:T(128)} %widths.5, bf16[24,8192]{1,0:T(8,128)(2,1)} %feat_ref.3, bf16[24,8192]{1,0:T(8,128)(2,1)} %cot_ref.3, f32[1,24]{1,0:T(1,128)} %bitcast.22, f32[1,24]{1,0:T(1,128)} %bitcast.24, f32[1,24]{1,0:T(1,128)} %bitcast.26, ...), custom_call_target="tpu_custom_call" | custom-call | bytes 18000000 | tf_op jit(solution)/shard_map/mixer_forward/pallas_call | solution.py:789
  12.8 0.0 collective-permute-done.2.refs_3_
  12.9 0.6 collective-permute-done.1.refs_2_
  13.5 0.0 collective-permute-done.refs_1_
  13.5 1.6 %collective-permute-start.4 = (bf16[1216,128]{1,0:T(8,128)(2,1)S(1)}, bf16[1216,128]{1,0:T(8,128)(2,1)S(1)}, u32[]{:S(2)}, u32[]{:S(2)}) collective-permute-start(bf16[1216,128]{1,0:T(8,128)(2,1)S(1)} %stack.13.refs_0_), channel_id=1, source_target_pairs={{0,2},{1,3},{2,0},{3,1},{4,6},{5,7},{6,4},{7,5},{8,10},{9,11},{10,... | collective-permute-start | bytes 933896 | tf_op jit(solution)/shard_map/ppermute | solution.py:759
  15.1 1.5 %collective-permute-start.3 = (bf16[1216,128]{1,0:T(8,128)(2,1)S(1)}, bf16[1216,128]{1,0:T(8,128)(2,1)S(1)}, u32[]{:S(2)}, u32[]{:S(2)}) collective-permute-start(bf16[1216,128]{1,0:T(8,128)(2,1)S(1)} %stack.13.refs_0_), channel_id=1, source_target_pairs={{0,1},{1,0},{2,3},{3,2},{4,5},{5,4},{6,7},{7,6},{8,9},{9,8},{10,11... | collective-permute-start | bytes 933896 | tf_op jit(solution)/shard_map/ppermute | solution.py:759
  16.6 0.0 collective-permute-start.7
  16.6 4.5 %all-to-all-start = ((bf16[16,2,24,512]{3,2,1,0:T(8,128)(2,1)}), bf16[16,2,24,512]{3,2,1,0:T(8,128)(2,1)S(1)}, u32[]{:S(2)}, u32[]{:S(2)}) async-start(bf16[16,2,24,512]{3,2,1,0:T(8,128)(2,1)} %get-tuple-element.90), calls=%async_computation | async-start | bytes 1572864 | tf_op jit(solution)/shard_map/all_to_all | solution.py:760
  21.1 1.1 %collective-permute-done.4.two_ref.refs_2_ = bf16[1216,128]{1,0:T(8,128)(2,1)S(1)} collective-permute-done((bf16[1216,128]{1,0:T(8,128)(2,1)S(1)}, bf16[1216,128]{1,0:T(8,128)(2,1)S(1)}, u32[]{:S(2)}, u32[]{:S(2)}) %collective-permute-start.4) | collective-permute-done | bytes 311328 | tf_op jit(solution)/shard_map/ppermute | solution.py:759
  22.2 1.4 %collective-permute-done.3.one_ref.refs_1_ = bf16[1216,128]{1,0:T(8,128)(2,1)S(1)} collective-permute-done((bf16[1216,128]{1,0:T(8,128)(2,1)S(1)}, bf16[1216,128]{1,0:T(8,128)(2,1)S(1)}, u32[]{:S(2)}, u32[]{:S(2)}) %collective-permute-start.3) | collective-permute-done | bytes 311328 | tf_op jit(solution)/shard_map/ppermute | solution.py:759
  23.6 0.4 collective-permute-start.5
  24.1 1.9 %collective-permute-start.6 = (bf16[608,128]{1,0:T(8,128)(2,1)S(1)}, bf16[608,128]{1,0:T(8,128)(2,1)S(1)}, u32[]{:S(2)}, u32[]{:S(2)}) collective-permute-start(bf16[608,128]{1,0:T(8,128)(2,1)S(1)} %get-tuple-element.98), channel_id=1, source_target_pairs={{0,1},{1,0},{2,3},{3,2},{4,5},{5,4},{6,7},{7,6},{8,9},{9,8},{10,11... | collective-permute-start | bytes 466952 | tf_op jit(solution)/shard_map/ppermute | solution.py:759
  26.0 0.0 collective-permute-start.8
  26.0 0.5 collective-permute-start.9
  26.5 6.7 %collective-permute-done.5.refs_3_ = bf16[608,128]{1,0:T(8,128)(2,1)S(1)} collective-permute-done((bf16[608,128]{1,0:T(8,128)(2,1)S(1)}, bf16[608,128]{1,0:T(8,128)(2,1)S(1)}, u32[]{:S(2)}, u32[]{:S(2)}) %collective-permute-start.5) | collective-permute-done | bytes 155680 | tf_op jit(solution)/shard_map/ppermute | solution.py:759
  33.2 0.0 collective-permute-start.10
  33.2 0.0 collective-permute-done.6.refs_4_
  33.2 0.5 collective-permute-start.11
  33.7 0.1 pad_add_fusion.where_ref
  33.8 0.0 collective-permute-done.7.refs_5_
  33.8 0.8 collective-permute-done.10.refs_8_
  34.6 0.2 collective-permute-done.11.refs_9_
  34.8 0.0 collective-permute-done.8.refs_6_
  34.8 0.0 collective-permute-done.9.refs_7_
  34.8 6.4 %all-to-all-done.given_ref = bf16[16,2,24,512]{3,2,1,0:T(8,128)(2,1)S(1)} async-done(((bf16[16,2,24,512]{3,2,1,0:T(8,128)(2,1)}), bf16[16,2,24,512]{3,2,1,0:T(8,128)(2,1)S(1)}, u32[]{:S(2)}, u32[]{:S(2)}) %all-to-all-start) | async-done | bytes 786464 | tf_op jit(solution)/shard_map/all_to_all | solution.py:760
  41.2 3.8 %mlp_first.1 = (bf16[4864,128]{1,0:T(8,128)(2,1)S(1)}, bf16[384,512]{1,0:T(8,128)(2,1)S(1)}, bf16[384,512]{1,0:T(8,128)(2,1)S(1)}, f32[384,512]{1,0:T(8,128)S(1)...) custom-call(s32[2]{0:T(128)S(1)} %pad_add_fusion.where_ref, ...), custom_call_target="tpu_custom_call" | custom-call | bytes 15000000 | tf_op jit(solution)/shard_map/mlp_first/pallas_call | solution.py:845
  45.0 0.1 collective-permute-start.12
  45.1 4.4 %mlp_second.1 = (bf16[16,2,24,512]{3,2,1,0:T(8,128)(2,1)}, bf16[1216,128]{1,0:T(8,128)(2,1)}, bf16[1216,128]{1,0:T(8,128)(2,1)S(1)}, bf16[1216,128]{1,0:T(8,128)...) custom-call(s32[2]{0:T(128)S(1)} %pad_add_fusion.where_ref, ...), custom_call_target="tpu_custom_call" | custom-call | bytes 15000000 | tf_op jit(solution)/shard_map/mlp_second/pallas_call | solution.py:860
  49.5 0.0 collective-permute-done.12.arrived_ref.refs_1_
  49.5 0.1 add_convert_fusion
  49.6 1.7 %collective-permute-start.13 = (bf16[608,128]{1,0:T(8,128)(2,1)S(1)}, bf16[608,128]{1,0:T(8,128)(2,1)S(1)}, u32[]{:S(2)}, u32[]{:S(2)}) collective-permute-start(bf16[608,128]{1,0:T(8,128)(2,1)S(1)} %get-tuple-element.114), channel_id=1, source_target_pairs={{0,2},{1,3},{2,0},{3,1},{4,6},{5,7},{6,4},{7,5},{8,10},{9,11},{10,... | collective-permute-start | bytes 466952 | tf_op jit(solution)/shard_map/ppermute | solution.py:759
  51.3 0.6 collective-permute-start.14
  51.8 5.1 %all-to-all-start.1 = ((bf16[16,2,24,512]{3,2,1,0:T(8,128)(2,1)}), bf16[16,2,24,512]{3,2,1,0:T(8,128)(2,1)S(1)}, u32[]{:S(2)}, u32[]{:S(2)}) async-start(bf16[16,2,24,512]{3,2,1,0:T(8,128)(2,1)} %get-tuple-element.106), calls=%async_computation.1 | async-start | bytes 1572864 | tf_op jit(solution)/shard_map/all_to_all | solution.py:760
  56.9 0.0 collective-permute-done.13.first_ref
  57.0 0.5 collective-permute-done.14.second_ref
  57.4 0.2 relay.1
  57.6 1.5 %collective-permute-start.15 = (bf16[1216,128]{1,0:T(8,128)(2,1)S(1)}, bf16[1216,128]{1,0:T(8,128)(2,1)S(1)}, u32[]{:S(2)}, u32[]{:S(2)}) collective-permute-start(bf16[1216,128]{1,0:T(8,128)(2,1)S(1)} %get-tuple-element.129), channel_id=1, source_target_pairs={{0,1},{1,0},{2,3},{3,2},{4,5},{5,4},{6,7},{7,6},{8,9},{9,8},{10,11... | collective-permute-start | bytes 933896 | tf_op jit(solution)/shard_map/ppermute | solution.py:759
  59.1 1.5 %collective-permute-start.16 = (bf16[1216,128]{1,0:T(8,128)(2,1)S(1)}, bf16[1216,128]{1,0:T(8,128)(2,1)S(1)}, u32[]{:S(2)}, u32[]{:S(2)}) collective-permute-start(bf16[1216,128]{1,0:T(8,128)(2,1)S(1)} %get-tuple-element.130), channel_id=1, source_target_pairs={{0,2},{1,3},{2,0},{3,1},{4,6},{5,7},{6,4},{7,5},{8,10},{9,11},{10,... | collective-permute-start | bytes 933896 | tf_op jit(solution)/shard_map/ppermute | solution.py:759
  60.6 1.0 %join.3.refs_0_ = f32[1216,128]{1,0:T(8,128)S(1)} custom-call(bf16[1216,128]{1,0:T(8,128)(2,1)} %get-tuple-element.128.refs_0_, bf16[4864,128]{1,0:T(8,128)(2,1)S(1)} %collective-permute-done.12.arrived_ref.refs_1_), custom_call_target="tpu_custom_call" | custom-call | flops 1 | bytes 1000000 | tf_op jit(solution)/shard_map/join/pallas_call | solution.py:708
  61.6 2.5 %mixer_prepare.1 = (bf16[3,256,256]{2,1,0:T(8,128)(2,1)S(1)}, bf16[3,256,256]{2,1,0:T(8,128)(2,1)S(1)}, bf16[3,256,256]{2,1,0:T(8,128)(2,1)S(1)}, bf16[3,8,64,12...) custom-call(s32[8]{0:T(128)} %heights.5, s32[8]{0:T(128)} %widths.5, bf16[24,8192]{1,0:T(8,128)(2,1)} %feat_ref.3, ...), custom_call_target="tpu_custom_call" | custom-call | bytes 12000000 | tf_op jit(solution)/shard_map/mixer_prepare/pallas_call | solution.py:889
  64.1 8.4 %collective-permute-done.15.refs_1_ = bf16[1216,128]{1,0:T(8,128)(2,1)S(1)} collective-permute-done((bf16[1216,128]{1,0:T(8,128)(2,1)S(1)}, bf16[1216,128]{1,0:T(8,128)(2,1)S(1)}, u32[]{:S(2)}, u32[]{:S(2)}) %collective-permute-start.15) | collective-permute-done | bytes 311328 | tf_op jit(solution)/shard_map/ppermute | solution.py:759
  72.5 1.1 %collective-permute-done.16.refs_2_ = bf16[1216,128]{1,0:T(8,128)(2,1)S(1)} collective-permute-done((bf16[1216,128]{1,0:T(8,128)(2,1)S(1)}, bf16[1216,128]{1,0:T(8,128)(2,1)S(1)}, u32[]{:S(2)}, u32[]{:S(2)}) %collective-permute-start.16) | collective-permute-done | bytes 311328 | tf_op jit(solution)/shard_map/ppermute | solution.py:759
  73.6 0.1 join.4
  73.8 1.6 %collective-permute-start.17 = (bf16[304,128]{1,0:T(8,128)(2,1)S(1)}, bf16[304,128]{1,0:T(8,128)(2,1)S(1)}, u32[]{:S(2)}, u32[]{:S(2)}) collective-permute-start(bf16[304,128]{1,0:T(8,128)(2,1)S(1)} %get-tuple-element.135), channel_id=1, source_target_pairs={{0,4},{1,5},{2,6},{3,7},{4,0},{5,1},{6,2},{7,3},{8,12},{9,13},{10,... | collective-permute-start | bytes 233480 | tf_op jit(solution)/shard_map/ppermute | solution.py:759
  75.3 2.7 %collective-permute-start.18 = (bf16[304,128]{1,0:T(8,128)(2,1)S(1)}, bf16[304,128]{1,0:T(8,128)(2,1)S(1)}, u32[]{:S(2)}, u32[]{:S(2)}) collective-permute-start(bf16[304,128]{1,0:T(8,128)(2,1)S(1)} %get-tuple-element.136), channel_id=1, source_target_pairs={{0,8},{1,9},{2,10},{3,11},{4,12},{5,13},{6,14},{7,15},{8,0},{9,1},... | collective-permute-start | bytes 233480 | tf_op jit(solution)/shard_map/ppermute | solution.py:759
  78.0 0.2 collective-permute-start.19
  78.2 0.0 all-to-all-done.1.both_ref
  78.2 6.2 %mixer_backward.1 = (bf16[24,8192]{1,0:T(8,128)(2,1)}, f32[24,8192]{1,0:T(8,128)}, f32[24,384]{1,0:T(8,128)S(1)}) custom-call(s32[8]{0:T(128)} %heights.5, s32[8]{0:T(128)} %widths.5, bf16[24,8192]{1,0:T(8,128)(2,1)} %feat_ref.3, bf16[24,8192]{1,0:T(8,128)(2,1)} %cot_ref.3, bf16[16,2,24,512]{3,2,1,0:T(8,128)(2,1)S(1)} %all-to-all-done.1.both_ref, ...), custom_call_target="tpu_custom_call" | custom-call | bytes 21000000 | tf_op jit(solution)/shard_map/mixer_backward/pallas_call | solution.py:904
  84.4 0.0 collective-permute-done.17.refs_1_
  84.4 0.0 collective-permute-done.18.refs_2_
  84.4 0.0 collective-permute-done.19.refs_3_
  84.5 0.1 collective-permute-start.20
  84.5 0.5 collective-permute-start.21
  85.0 0.9 %collective-permute-done.21.sibling_ref = f32[24,384]{1,0:T(8,128)S(1)} collective-permute-done((f32[24,384]{1,0:T(8,128)S(1)}, f32[24,384]{1,0:T(8,128)S(1)}, u32[]{:S(2)}, u32[]{:S(2)}) %collective-permute-start.21) | collective-permute-done | bytes 36896 | tf_op jit(solution)/shard_map/ppermute | solution.py:758
  86.0 0.0 collective-permute-done.20.other_ref
  86.0 0.9 finish.1
  (3 shorter events, 0.1 us)
Async XLA Ops:
  1.8 11.0 %collective-permute-start.2 = (bf16[304,128]{1,0:T(8,128)(2,1)S(1)}, bf16[304,128]{1,0:T(8,128)(2,1)S(1)}, u32[]{:S(2)}, u32[]{:S(2)}) collective-permute-start(bf16[304,128]{1,0:T(8,128)(2,1)S(1)} %pack.1.refs_0_), channel_id=1, source_target_pairs={{0,12},{1,13},{2,14},{3,15},{4,8},{5,9},{6,10},{7,11},{8,4},{9,5},... | collective-permute-start | bytes 233480 | tf_op jit(solution)/shard_map/ppermute | solution.py:759
  6.9 6.5 %collective-permute-start.1 = (bf16[304,128]{1,0:T(8,128)(2,1)S(1)}, bf16[304,128]{1,0:T(8,128)(2,1)S(1)}, u32[]{:S(2)}, u32[]{:S(2)}) collective-permute-start(bf16[304,128]{1,0:T(8,128)(2,1)S(1)} %pack.1.refs_0_), channel_id=1, source_target_pairs={{0,8},{1,9},{2,10},{3,11},{4,12},{5,13},{6,14},{7,15},{8,0},{9,1},... | collective-permute-start | bytes 233480 | tf_op jit(solution)/shard_map/ppermute | solution.py:759
  6.9 6.5 %collective-permute-start = (bf16[304,128]{1,0:T(8,128)(2,1)S(1)}, bf16[304,128]{1,0:T(8,128)(2,1)S(1)}, u32[]{:S(2)}, u32[]{:S(2)}) collective-permute-start(bf16[304,128]{1,0:T(8,128)(2,1)S(1)} %pack.1.refs_0_), channel_id=1, source_target_pairs={{0,4},{1,5},{2,6},{3,7},{4,0},{5,1},{6,2},{7,3},{8,12},{9,13},{10,... | collective-permute-start | bytes 233480 | tf_op jit(solution)/shard_map/ppermute | solution.py:759
  13.5 8.7 %collective-permute-start.4 = (bf16[1216,128]{1,0:T(8,128)(2,1)S(1)}, bf16[1216,128]{1,0:T(8,128)(2,1)S(1)}, u32[]{:S(2)}, u32[]{:S(2)}) collective-permute-start(bf16[1216,128]{1,0:T(8,128)(2,1)S(1)} %stack.13.refs_0_), channel_id=1, source_target_pairs={{0,2},{1,3},{2,0},{3,1},{4,6},{5,7},{6,4},{7,5},{8,10},{9,11},{10,... | collective-permute-start | bytes 933896 | tf_op jit(solution)/shard_map/ppermute | solution.py:759
  15.1 8.6 %collective-permute-start.3 = (bf16[1216,128]{1,0:T(8,128)(2,1)S(1)}, bf16[1216,128]{1,0:T(8,128)(2,1)S(1)}, u32[]{:S(2)}, u32[]{:S(2)}) collective-permute-start(bf16[1216,128]{1,0:T(8,128)(2,1)S(1)} %stack.13.refs_0_), channel_id=1, source_target_pairs={{0,1},{1,0},{2,3},{3,2},{4,5},{5,4},{6,7},{7,6},{8,9},{9,8},{10,11... | collective-permute-start | bytes 933896 | tf_op jit(solution)/shard_map/ppermute | solution.py:759
  16.6 17.2 %collective-permute-start.7 = (bf16[1216,128]{1,0:T(8,128)(2,1)S(1)}, bf16[1216,128]{1,0:T(8,128)(2,1)S(1)}, u32[]{:S(2)}, u32[]{:S(2)}) collective-permute-start(bf16[1216,128]{1,0:T(8,128)(2,1)S(1)} %stack.13.refs_0_), channel_id=1, source_target_pairs={{0,16},{16,0},{1,17},{17,1},{2,18},{18,2},{3,19},{19,3},{4,20},{20... | collective-permute-start | bytes 933896 | tf_op jit(solution)/shard_map/ppermute | solution.py:758
  16.6 24.6 %all-to-all-start = ((bf16[16,2,24,512]{3,2,1,0:T(8,128)(2,1)}), bf16[16,2,24,512]{3,2,1,0:T(8,128)(2,1)S(1)}, u32[]{:S(2)}, u32[]{:S(2)}) async-start(bf16[16,2,24,512]{3,2,1,0:T(8,128)(2,1)} %get-tuple-element.90), calls=%async_computation | async-start | bytes 1572864 | tf_op jit(solution)/shard_map/all_to_all | solution.py:760
  23.6 9.5 %collective-permute-start.5 = (bf16[608,128]{1,0:T(8,128)(2,1)S(1)}, bf16[608,128]{1,0:T(8,128)(2,1)S(1)}, u32[]{:S(2)}, u32[]{:S(2)}) collective-permute-start(bf16[608,128]{1,0:T(8,128)(2,1)S(1)} %get-tuple-element.97), channel_id=1, source_target_pairs={{0,2},{1,3},{2,0},{3,1},{4,6},{5,7},{6,4},{7,5},{8,10},{9,11},{10,... | collective-permute-start | bytes 466952 | tf_op jit(solution)/shard_map/ppermute | solution.py:759
  24.1 9.1 %collective-permute-start.6 = (bf16[608,128]{1,0:T(8,128)(2,1)S(1)}, bf16[608,128]{1,0:T(8,128)(2,1)S(1)}, u32[]{:S(2)}, u32[]{:S(2)}) collective-permute-start(bf16[608,128]{1,0:T(8,128)(2,1)S(1)} %get-tuple-element.98), channel_id=1, source_target_pairs={{0,1},{1,0},{2,3},{3,2},{4,5},{5,4},{6,7},{7,6},{8,9},{9,8},{10,11... | collective-permute-start | bytes 466952 | tf_op jit(solution)/shard_map/ppermute | solution.py:759
  26.0 8.8 %collective-permute-start.8 = (bf16[1216,128]{1,0:T(8,128)(2,1)S(1)}, bf16[1216,128]{1,0:T(8,128)(2,1)S(1)}, u32[]{:S(2)}, u32[]{:S(2)}) collective-permute-start(bf16[1216,128]{1,0:T(8,128)(2,1)S(1)} %collective-permute-done.3.one_ref.refs_1_), channel_id=1, source_target_pairs={{0,16},{16,0},{1,17},{17,1},{2,18},{18,2},{3,19},{19,3},{4,20},{20... | collective-permute-start | bytes 933896 | tf_op jit(solution)/shard_map/ppermute | solution.py:758
  26.0 8.8 %collective-permute-start.9 = (bf16[1216,128]{1,0:T(8,128)(2,1)S(1)}, bf16[1216,128]{1,0:T(8,128)(2,1)S(1)}, u32[]{:S(2)}, u32[]{:S(2)}) collective-permute-start(bf16[1216,128]{1,0:T(8,128)(2,1)S(1)} %collective-permute-done.4.two_ref.refs_2_), channel_id=1, source_target_pairs={{0,16},{16,0},{1,17},{17,1},{2,18},{18,2},{3,19},{19,3},{4,20},{20... | collective-permute-start | bytes 933896 | tf_op jit(solution)/shard_map/ppermute | solution.py:758
  33.2 1.4 %collective-permute-start.10 = (bf16[608,128]{1,0:T(8,128)(2,1)S(1)}, bf16[608,128]{1,0:T(8,128)(2,1)S(1)}, u32[]{:S(2)}, u32[]{:S(2)}) collective-permute-start(bf16[608,128]{1,0:T(8,128)(2,1)S(1)} %collective-permute-done.5.refs_3_), channel_id=1, source_target_pairs={{0,16},{16,0},{1,17},{17,1},{2,18},{18,2},{3,19},{19,3},{4,20},{20... | collective-permute-start | bytes 466952 | tf_op jit(solution)/shard_map/ppermute | solution.py:758
  33.2 1.6 %collective-permute-start.11 = (bf16[608,128]{1,0:T(8,128)(2,1)S(1)}, bf16[608,128]{1,0:T(8,128)(2,1)S(1)}, u32[]{:S(2)}, u32[]{:S(2)}) collective-permute-start(bf16[608,128]{1,0:T(8,128)(2,1)S(1)} %collective-permute-done.6.refs_4_), channel_id=1, source_target_pairs={{0,16},{16,0},{1,17},{17,1},{2,18},{18,2},{3,19},{19,3},{4,20},{20... | collective-permute-start | bytes 466952 | tf_op jit(solution)/shard_map/ppermute | solution.py:758
  45.0 4.5 %collective-permute-start.12 = (bf16[4864,128]{1,0:T(8,128)(2,1)S(1)}, bf16[4864,128]{1,0:T(8,128)(2,1)S(1)}, u32[]{:S(2)}, u32[]{:S(2)}) collective-permute-start(bf16[4864,128]{1,0:T(8,128)(2,1)S(1)} %get-tuple-element.111), channel_id=1, source_target_pairs={{0,16},{16,0},{1,17},{17,1},{2,18},{18,2},{3,19},{19,3},{4,20},{20... | collective-permute-start | bytes 3735560 | tf_op jit(solution)/shard_map/ppermute | solution.py:758
  49.6 7.4 %collective-permute-start.13 = (bf16[608,128]{1,0:T(8,128)(2,1)S(1)}, bf16[608,128]{1,0:T(8,128)(2,1)S(1)}, u32[]{:S(2)}, u32[]{:S(2)}) collective-permute-start(bf16[608,128]{1,0:T(8,128)(2,1)S(1)} %get-tuple-element.114), channel_id=1, source_target_pairs={{0,2},{1,3},{2,0},{3,1},{4,6},{5,7},{6,4},{7,5},{8,10},{9,11},{10,... | collective-permute-start | bytes 466952 | tf_op jit(solution)/shard_map/ppermute | solution.py:759
  51.3 6.1 %collective-permute-start.14 = (bf16[608,128]{1,0:T(8,128)(2,1)S(1)}, bf16[608,128]{1,0:T(8,128)(2,1)S(1)}, u32[]{:S(2)}, u32[]{:S(2)}) collective-permute-start(bf16[608,128]{1,0:T(8,128)(2,1)S(1)} %get-tuple-element.115), channel_id=1, source_target_pairs={{0,1},{1,0},{2,3},{3,2},{4,5},{5,4},{6,7},{7,6},{8,9},{9,8},{10,11... | collective-permute-start | bytes 466952 | tf_op jit(solution)/shard_map/ppermute | solution.py:759
  51.8 26.4 %all-to-all-start.1 = ((bf16[16,2,24,512]{3,2,1,0:T(8,128)(2,1)}), bf16[16,2,24,512]{3,2,1,0:T(8,128)(2,1)S(1)}, u32[]{:S(2)}, u32[]{:S(2)}) async-start(bf16[16,2,24,512]{3,2,1,0:T(8,128)(2,1)} %get-tuple-element.106), calls=%async_computation.1 | async-start | bytes 1572864 | tf_op jit(solution)/shard_map/all_to_all | solution.py:760
  57.6 14.9 %collective-permute-start.15 = (bf16[1216,128]{1,0:T(8,128)(2,1)S(1)}, bf16[1216,128]{1,0:T(8,128)(2,1)S(1)}, u32[]{:S(2)}, u32[]{:S(2)}) collective-permute-start(bf16[1216,128]{1,0:T(8,128)(2,1)S(1)} %get-tuple-element.129), channel_id=1, source_target_pairs={{0,1},{1,0},{2,3},{3,2},{4,5},{5,4},{6,7},{7,6},{8,9},{9,8},{10,11... | collective-permute-start | bytes 933896 | tf_op jit(solution)/shard_map/ppermute | solution.py:759
  59.1 14.5 %collective-permute-start.16 = (bf16[1216,128]{1,0:T(8,128)(2,1)S(1)}, bf16[1216,128]{1,0:T(8,128)(2,1)S(1)}, u32[]{:S(2)}, u32[]{:S(2)}) collective-permute-start(bf16[1216,128]{1,0:T(8,128)(2,1)S(1)} %get-tuple-element.130), channel_id=1, source_target_pairs={{0,2},{1,3},{2,0},{3,1},{4,6},{5,7},{6,4},{7,5},{8,10},{9,11},{10,... | collective-permute-start | bytes 933896 | tf_op jit(solution)/shard_map/ppermute | solution.py:759
  73.8 10.6 %collective-permute-start.17 = (bf16[304,128]{1,0:T(8,128)(2,1)S(1)}, bf16[304,128]{1,0:T(8,128)(2,1)S(1)}, u32[]{:S(2)}, u32[]{:S(2)}) collective-permute-start(bf16[304,128]{1,0:T(8,128)(2,1)S(1)} %get-tuple-element.135), channel_id=1, source_target_pairs={{0,4},{1,5},{2,6},{3,7},{4,0},{5,1},{6,2},{7,3},{8,12},{9,13},{10,... | collective-permute-start | bytes 233480 | tf_op jit(solution)/shard_map/ppermute | solution.py:759
  75.3 9.1 %collective-permute-start.18 = (bf16[304,128]{1,0:T(8,128)(2,1)S(1)}, bf16[304,128]{1,0:T(8,128)(2,1)S(1)}, u32[]{:S(2)}, u32[]{:S(2)}) collective-permute-start(bf16[304,128]{1,0:T(8,128)(2,1)S(1)} %get-tuple-element.136), channel_id=1, source_target_pairs={{0,8},{1,9},{2,10},{3,11},{4,12},{5,13},{6,14},{7,15},{8,0},{9,1},... | collective-permute-start | bytes 233480 | tf_op jit(solution)/shard_map/ppermute | solution.py:759
  78.0 6.4 %collective-permute-start.19 = (bf16[304,128]{1,0:T(8,128)(2,1)S(1)}, bf16[304,128]{1,0:T(8,128)(2,1)S(1)}, u32[]{:S(2)}, u32[]{:S(2)}) collective-permute-start(bf16[304,128]{1,0:T(8,128)(2,1)S(1)} %get-tuple-element.137), channel_id=1, source_target_pairs={{0,12},{1,13},{2,14},{3,15},{4,8},{5,9},{6,10},{7,11},{8,4},{9,5},... | collective-permute-start | bytes 233480 | tf_op jit(solution)/shard_map/ppermute | solution.py:759
  84.5 1.5 %collective-permute-start.20 = (f32[304,128]{1,0:T(8,128)S(1)}, f32[304,128]{1,0:T(8,128)S(1)}, u32[]{:S(2)}, u32[]{:S(2)}) collective-permute-start(f32[304,128]{1,0:T(8,128)S(1)} %join.5.mine_ref), channel_id=1, source_target_pairs={{0,16},{16,0},{1,17},{17,1},{2,18},{18,2},{3,19},{19,3},{4,20},{20... | collective-permute-start | bytes 466952 | tf_op jit(solution)/shard_map/ppermute | solution.py:758
  84.5 1.4 %collective-permute-start.21 = (f32[24,384]{1,0:T(8,128)S(1)}, f32[24,384]{1,0:T(8,128)S(1)}, u32[]{:S(2)}, u32[]{:S(2)}) collective-permute-start(f32[24,384]{1,0:T(8,128)S(1)} %get-tuple-element.143.small_ref), channel_id=1, source_target_pairs={{0,16},{16,0},{1,17},{17,1},{2,18},{18,2},{3,19},{19,3},{4,20},{20... | collective-permute-start | bytes 110600 | tf_op jit(solution)/shard_map/ppermute | solution.py:758
